TPU v7x, 256 devices: a whole 4x4x8 slice. The times are simulated.
256 devices in a mesh: section: 8 (over z), dp: 32 (over y, x, core).
Axes of the slice: x: 4, y: 4, z: 8, core: 2. Of those that a mesh axis runs over, the one named last changes fastest.
Arguments:
- layer_input_states: bfloat16 [8, 32, 128, 8192], P('section', 'dp'), may hold values from -11 to 11, as said below
- frozen_reference_states: bfloat16 [8, 32, 128, 8192], P('section', None, None, 'dp'), may hold values from -11 to 11
- adapter_down_weight: bfloat16 [8, 16, 8192], P('section'), may hold values from -0.0625 to 0.0625
- adapter_up_weight: bfloat16 [8, 16, 8192], P('section'), may hold values from -0.1796875 to 0.1796875
- layer_norm_gain: float32 [8, 8192], P('section'), may hold values from 0.5 to 1.5
- tile_reference_position: int32 [32], replicated, may hold values from 0 to 31, each once
- tile_harmful_flag: int32 [32], P('dp'), may hold values from 0 to 1, as said below
- tile_valid_count: int32 [32], P('dp'), may hold values from 32 to 128
Outputs:
- grad_down: float32 [8, 16, 8192], P('section')
- grad_up: float32 [8, 16, 8192], P('section')
Inputs may be any that keep to these rules, and one draw needn't show every extreme that they name: layer_input_states and frozen_reference_states are bounded. `tile_harmful_flag`: both harmful and retain tiles occur.
All inputs are finite; a program needn't handle non-finite values.
Results may differ from a plain program's by a relative error of at most 0.0012.
Values may be sent and summed in bfloat16 or wider, within the bound.
No kernel may reach another device: no remote copies, remote signals or barrier semaphores. Data moves between devices by JAX's collectives and lax.ppermute only.
A program may use at most 64 MiB of HBM per device.

v0:
```python
import jax
import jax.numpy as jnp
from jax import lax
from jax.sharding import PartitionSpec as P

norm_eps = 1e-05
stat_eps = 1e-06
coef_reroute = 64.0
coef_retain = 1.0
loss_scale = 2048.0


def shifted(value, axis, by):
    count = lax.axis_size(axis)
    pairs = [(i, i + by) for i in range(count) if 0 <= i + by < count]
    return lax.ppermute(value, axis, pairs)


def contract_last(left, right):
    return lax.dot_general(
        left, right, (((1,), (1,)), ((), ())), preferred_element_type=jnp.float32
    )


def contract_first(left, right):
    return lax.dot_general(
        left, right, (((0,), (0,)), ((), ())), preferred_element_type=jnp.float32
    )


def section_forward(inputs, down_projection_rows, up_projection_rows, gains):
    stream = inputs.astype(jnp.float32)
    inverse_rms = lax.rsqrt(jnp.mean(stream * stream, axis=-1, keepdims=True) + norm_eps)
    normed = (stream * inverse_rms * gains).astype(jnp.bfloat16)
    low_rank = contract_last(normed, down_projection_rows).astype(jnp.bfloat16)
    output = stream + jnp.dot(low_rank, up_projection_rows, preferred_element_type=jnp.float32)
    return (stream, inverse_rms, normed, low_rank, output)


def token_stats(output, references):
    difference = output - references
    out_sq = jnp.sum(output * output, axis=-1, keepdims=True)
    ref_sq = jnp.sum(references * references, axis=-1, keepdims=True)
    cross_sum = jnp.sum(output * references, axis=-1, keepdims=True)
    diff_sq = jnp.sum(difference * difference, axis=-1, keepdims=True)
    return (out_sq, ref_sq, cross_sum, diff_sq)


def loss_grad(
    output,
    references,
    out_sq,
    ref_sq,
    cross_sum,
    diff_sq,
    is_harm,
    is_valid,
    weight_harm,
    weight_keep,
):
    out_norm = jnp.sqrt(out_sq + stat_eps)
    ref_norm = jnp.sqrt(ref_sq + stat_eps)
    diff_norm = jnp.sqrt(diff_sq + stat_eps)
    cosine = cross_sum / (out_norm * ref_norm)
    reroute = jnp.where(
        cosine > 0, references / (out_norm * ref_norm) - cosine * output / (out_sq + stat_eps), 0.0
    )
    retain = (output - references) / diff_norm
    return is_valid * (is_harm * weight_harm * reroute + (1.0 - is_harm) * weight_keep * retain)


def back_input(gradient, stream, inverse_rms, down_projection_rows, up_projection_rows, gains):
    grad_bf = gradient.astype(jnp.bfloat16)
    low_grad = contract_last(grad_bf, up_projection_rows).astype(jnp.bfloat16)
    norm_grad = jnp.dot(low_grad, down_projection_rows, preferred_element_type=jnp.float32) * gains
    scaled = stream * inverse_rms
    return gradient + inverse_rms * (
        norm_grad - scaled * jnp.mean(norm_grad * scaled, axis=-1, keepdims=True)
    )


def shards(
    layer_input_states,
    frozen_reference_states,
    adapter_down_weight,
    adapter_up_weight,
    layer_norm_gain,
    tile_reference_position,
    tile_harmful_flag,
    tile_valid_count,
):
    tiles_dev = layer_input_states.shape[1]
    tile_rows = layer_input_states.shape[2]
    features = layer_input_states.shape[3]
    tokens = tiles_dev * tile_rows
    down_projection_rows = adapter_down_weight[0]
    up_projection_rows = adapter_up_weight[0]
    gains = layer_norm_gain[0]
    positions = jnp.arange(tile_rows, dtype=jnp.int32)
    is_valid = (
        (positions[None, :] < tile_valid_count[:, None]).astype(jnp.float32).reshape(tokens, 1)
    )
    is_harm = jnp.broadcast_to(
        tile_harmful_flag.astype(jnp.float32)[:, None], (tiles_dev, tile_rows)
    ).reshape(tokens, 1)
    count_harm, count_keep = lax.psum(
        (jnp.sum(is_valid * is_harm), jnp.sum(is_valid * (1.0 - is_harm))), "dp"
    )
    weight_harm = loss_scale * coef_reroute / count_harm
    weight_keep = loss_scale * coef_retain / count_keep
    stream, inverse_rms, normed, low_rank, output = section_forward(
        layer_input_states[0].reshape(tokens, features),
        down_projection_rows,
        up_projection_rows,
        gains,
    )
    ordered = jnp.take(frozen_reference_states[0], tile_reference_position, axis=0)
    fetched = lax.all_to_all(ordered, "dp", split_axis=0, concat_axis=2, tiled=True)
    references = fetched.reshape(tokens, features).astype(jnp.float32)
    out_sq, ref_sq, cross_sum, diff_sq = token_stats(output, references)
    own = loss_grad(
        output,
        references,
        out_sq,
        ref_sq,
        cross_sum,
        diff_sq,
        is_harm,
        is_valid,
        weight_harm,
        weight_keep,
    )
    rounds = lax.axis_size("section") - 1
    incoming = jnp.zeros((tokens, features), jnp.bfloat16)
    for round_index in range(rounds):
        gradient = own + incoming.astype(jnp.float32)
        passed = back_input(
            gradient, stream, inverse_rms, down_projection_rows, up_projection_rows, gains
        )
        incoming = shifted(passed.astype(jnp.bfloat16), "section", -1)
    gradient = own + incoming.astype(jnp.float32)
    grad_bf = gradient.astype(jnp.bfloat16)
    low_grad = contract_last(grad_bf, up_projection_rows).astype(jnp.bfloat16)
    local_up = contract_first(low_rank, grad_bf)
    local_down = contract_first(low_grad, normed)
    total_down, total_up = lax.psum((local_down, local_up), "dp")
    return (total_down[None], total_up[None])


def solution(mesh):
    return jax.shard_map(
        shards,
        mesh=mesh,
        in_specs=(
            P("section", "dp", None, None),
            P("section", None, None, "dp"),
            P("section", None, None),
            P("section", None, None),
            P("section", None),
            P(),
            P("dp"),
            P("dp"),
        ),
        out_specs=(P("section", None, None), P("section", None, None)),
        check_vma=False,
    )
```

profile of v0, /device:TPU:1, one launch (start us, length us, event | category | flops | bytes accessed | tf_op | source)
XLA Modules:
  0.0 680.9 jit_solution(3945017062348272659)
XLA Ops:
  7.2 0.8 compare_and_fusion
  8.0 0.7 compare_select_fusion
  8.8 2.0 gather_fusion
  10.8 3.3 broadcast_select_fusion
  14.0 8.8 %all-to-all-start = ((bf16[32,128,256]{2,1,0:T(8,128)(2,1)}), bf16[32,128,256]{2,1,0:T(8,128)(2,1)}, u32[]{:S(2)}, u32[]{:S(2)}) async-start(bf16[32,128,256]{2,1,0:T(8,128)(2,1)} %broadcast_select_fusion), calls=%async_computation | async-start | bytes 4194304 | tf_op jit(solution)/shard_map/all_to_all | solution.py:118
  24.2 0.6 fusion.148
  24.8 80.3 %all-reduce = (f32[]{:T(128)}, f32[]{:T(128)}) all-reduce(f32[]{:T(128)} %get-tuple-element.33, f32[]{:T(128)} %get-tuple-element.32), channel_id=1, replica_groups=mesh['section'=8,'dp'=32] {'dp'}, use_global_device_ids=true, to_apply=%region_7.8 | all-reduce | flops 2 | bytes 16 | tf_op jit(solution)/shard_map/psum | solution.py:106
  106.4 0.5 fusion.53
  107.0 0.7 fusion.120
  107.7 2.1 fusion.178
  109.8 0.4 copy.12
  110.3 0.5 copy-done.4
  110.8 1.9 multiply_reduce_fusion.2
  112.7 2.1 fusion.56
  114.8 3.0 add_multiply_fusion
  117.8 6.5 fusion.17
  124.3 4.6 fusion.21
  128.9 1.3 collective-permute-start
  130.2 45.8 %collective-permute-done = bf16[128,8192]{1,0:T(8,128)(2,1)} collective-permute-done((bf16[128,8192]{1,0:T(8,128)(2,1)S(1)}, bf16[128,8192]{1,0:T(8,128)(2,1)}, u32[]{:S(2)}, u32[]{:S(2)}) %collective-permute-start) | collective-permute-done | bytes 2097184 | tf_op jit(solution)/shard_map/ppermute | solution.py:16
  176.0 7.2 %fusion.22 = (f32[128]{0:T(128)S(1)}, f32[128,8192]{1,0:T(8,128)}) fusion(bf16[1,1,128,8192]{3,2,1,0:T(8,128)(2,1)S(1)} %copy-done.3, f32[128]{0:T(128)S(1)} %add_rsqrt_fusion, f32[8192]{0:T(1024)S(1)} %bitcast.220, bf16[1,16,8192]{2,1,0:T(8,128)(2,1)S(1)} %copy-done.5, f32[128,8192]{1,0:T(8,128)} %add_multiply_fusion, ...), kind=kOutput, calls=%fused_computation.37 | convolution fusion | flops 75499392 | bytes 13140992 | tf_op jit(solution)/shard_map/dot_general | solution.py:75
  183.2 5.4 fusion.26
  188.6 1.5 collective-permute-start.1
  190.1 44.9 %collective-permute-done.1 = bf16[128,8192]{1,0:T(8,128)(2,1)} collective-permute-done((bf16[128,8192]{1,0:T(8,128)(2,1)S(1)}, bf16[128,8192]{1,0:T(8,128)(2,1)}, u32[]{:S(2)}, u32[]{:S(2)}) %collective-permute-start.1) | collective-permute-done | bytes 2097184 | tf_op jit(solution)/shard_map/ppermute | solution.py:16
  234.9 7.2 %fusion.27 = (f32[128]{0:T(128)S(1)}, f32[128,8192]{1,0:T(8,128)}) fusion(bf16[1,1,128,8192]{3,2,1,0:T(8,128)(2,1)S(1)} %copy-done.3, f32[128]{0:T(128)S(1)} %add_rsqrt_fusion, f32[8192]{0:T(1024)S(1)} %bitcast.221, bf16[1,16,8192]{2,1,0:T(8,128)(2,1)S(1)} %copy-done.5, f32[128,8192]{1,0:T(8,128)} %add_multiply_fusion, ...), kind=kOutput, calls=%fused_computation.42 | convolution fusion | flops 75499392 | bytes 13140992 | tf_op jit(solution)/shard_map/dot_general | solution.py:75
  242.2 5.4 fusion.31
  247.6 1.3 collective-permute-start.2
  248.9 44.3 %collective-permute-done.2 = bf16[128,8192]{1,0:T(8,128)(2,1)} collective-permute-done((bf16[128,8192]{1,0:T(8,128)(2,1)S(1)}, bf16[128,8192]{1,0:T(8,128)(2,1)}, u32[]{:S(2)}, u32[]{:S(2)}) %collective-permute-start.2) | collective-permute-done | bytes 2097184 | tf_op jit(solution)/shard_map/ppermute | solution.py:16
  293.2 7.2 %fusion.32 = (f32[128]{0:T(128)S(1)}, f32[128,8192]{1,0:T(8,128)}) fusion(bf16[1,1,128,8192]{3,2,1,0:T(8,128)(2,1)S(1)} %copy-done.3, f32[128]{0:T(128)S(1)} %add_rsqrt_fusion, f32[8192]{0:T(1024)S(1)} %bitcast.222, bf16[1,16,8192]{2,1,0:T(8,128)(2,1)S(1)} %copy-done.5, f32[128,8192]{1,0:T(8,128)} %add_multiply_fusion, ...), kind=kOutput, calls=%fused_computation.47 | convolution fusion | flops 75499392 | bytes 13140992 | tf_op jit(solution)/shard_map/dot_general | solution.py:75
  300.4 5.4 fusion.36
  305.8 1.3 collective-permute-start.3
  307.1 45.3 %collective-permute-done.3 = bf16[128,8192]{1,0:T(8,128)(2,1)} collective-permute-done((bf16[128,8192]{1,0:T(8,128)(2,1)S(1)}, bf16[128,8192]{1,0:T(8,128)(2,1)}, u32[]{:S(2)}, u32[]{:S(2)}) %collective-permute-start.3) | collective-permute-done | bytes 2097184 | tf_op jit(solution)/shard_map/ppermute | solution.py:16
  352.5 7.2 %fusion.37 = (f32[128]{0:T(128)S(1)}, f32[128,8192]{1,0:T(8,128)}) fusion(bf16[1,1,128,8192]{3,2,1,0:T(8,128)(2,1)S(1)} %copy-done.3, f32[128]{0:T(128)S(1)} %add_rsqrt_fusion, f32[8192]{0:T(1024)S(1)} %bitcast.223, bf16[1,16,8192]{2,1,0:T(8,128)(2,1)S(1)} %copy-done.5, f32[128,8192]{1,0:T(8,128)} %add_multiply_fusion, ...), kind=kOutput, calls=%fused_computation.52 | convolution fusion | flops 75499392 | bytes 13140992 | tf_op jit(solution)/shard_map/dot_general | solution.py:75
  359.7 5.4 fusion.41
  365.1 1.5 collective-permute-start.4
  366.6 42.9 %collective-permute-done.4 = bf16[128,8192]{1,0:T(8,128)(2,1)} collective-permute-done((bf16[128,8192]{1,0:T(8,128)(2,1)S(1)}, bf16[128,8192]{1,0:T(8,128)(2,1)}, u32[]{:S(2)}, u32[]{:S(2)}) %collective-permute-start.4) | collective-permute-done | bytes 2097184 | tf_op jit(solution)/shard_map/ppermute | solution.py:16
  409.5 7.2 %fusion.42 = (f32[128]{0:T(128)S(1)}, f32[128,8192]{1,0:T(8,128)}) fusion(bf16[1,1,128,8192]{3,2,1,0:T(8,128)(2,1)S(1)} %copy-done.3, f32[128]{0:T(128)S(1)} %add_rsqrt_fusion, f32[8192]{0:T(1024)S(1)} %bitcast.224, bf16[1,16,8192]{2,1,0:T(8,128)(2,1)S(1)} %copy-done.5, f32[128,8192]{1,0:T(8,128)} %add_multiply_fusion, ...), kind=kOutput, calls=%fused_computation.57 | convolution fusion | flops 75499392 | bytes 13140992 | tf_op jit(solution)/shard_map/dot_general | solution.py:75
  416.7 5.4 fusion.46
  422.1 1.3 collective-permute-start.5
  423.4 42.2 %collective-permute-done.5 = bf16[128,8192]{1,0:T(8,128)(2,1)} collective-permute-done((bf16[128,8192]{1,0:T(8,128)(2,1)S(1)}, bf16[128,8192]{1,0:T(8,128)(2,1)}, u32[]{:S(2)}, u32[]{:S(2)}) %collective-permute-start.5) | collective-permute-done | bytes 2097184 | tf_op jit(solution)/shard_map/ppermute | solution.py:16
  465.6 7.2 %fusion.47 = (f32[128]{0:T(128)S(1)}, f32[128,8192]{1,0:T(8,128)}) fusion(bf16[1,1,128,8192]{3,2,1,0:T(8,128)(2,1)S(1)} %copy-done.3, f32[128]{0:T(128)S(1)} %add_rsqrt_fusion, f32[8192]{0:T(1024)S(1)} %bitcast.225, bf16[1,16,8192]{2,1,0:T(8,128)(2,1)S(1)} %copy-done.5, f32[128,8192]{1,0:T(8,128)} %add_multiply_fusion, ...), kind=kOutput, calls=%fused_computation.62 | convolution fusion | flops 75499392 | bytes 13140992 | tf_op jit(solution)/shard_map/dot_general | solution.py:75
  472.9 5.5 fusion.51
  478.4 1.3 collective-permute-start.6
  479.7 41.3 %collective-permute-done.6 = bf16[128,8192]{1,0:T(8,128)(2,1)} collective-permute-done((bf16[128,8192]{1,0:T(8,128)(2,1)S(1)}, bf16[128,8192]{1,0:T(8,128)(2,1)}, u32[]{:S(2)}, u32[]{:S(2)}) %collective-permute-start.6) | collective-permute-done | bytes 2097184 | tf_op jit(solution)/shard_map/ppermute | solution.py:16
  521.0 3.1 convolution_bitcast_fusion
  524.1 5.8 convolution_bitcast_fusion.1
  529.9 140.4 %all-reduce.4.cloned.1.call-done = (f32[1,16,8192]{2,1,0:T(8,128)}, f32[1,16,8192]{2,1,0:T(8,128)}) async-done(((f32[1,16,8192]{2,1,0:T(8,128)}, f32[1,16,8192]{2,1,0:T(8,128)}), (f32[1,16,8192]{2,1,0:T(8,128)}, f32[1,16,8192]{2,1,0:T(8,128)})) %all-reduce.4.cloned.1.call-update) | async-done | bytes 1048592 | tf_op jit(solution)/shard_map/psum | solution.py:146
  670.3 1.9 copy.18
  672.2 1.9 copy.19
  (27 shorter events, 0.3 us)
Async XLA Ops:
  7.2 1.6 copy-start
  10.8 95.7 %copy-start.3 = (bf16[1,1,128,8192]{3,2,1,0:T(8,128)(2,1)S(1)}, bf16[1,1,128,8192]{3,2,1,0:T(8,128)(2,1)}, u32[]{:S(2)}) copy-start(bf16[1,1,128,8192]{3,2,1,0:T(8,128)(2,1)} %param.8) | copy-start | bytes 6291460
  14.0 92.9 %copy-start.5 = (bf16[1,16,8192]{2,1,0:T(8,128)(2,1)S(1)}, bf16[1,16,8192]{2,1,0:T(8,128)(2,1)}, u32[]{:S(2)}) copy-start(bf16[1,16,8192]{2,1,0:T(8,128)(2,1)} %param.10) | copy-start | bytes 786436
  14.0 92.9 %copy-start.6 = (f32[1,8192]{1,0:T(1,128)S(1)}, f32[1,8192]{1,0:T(1,128)}, u32[]{:S(2)}) copy-start(f32[1,8192]{1,0:T(1,128)} %param.12) | copy-start | bytes 98308
  14.0 93.6 %all-to-all-start = ((bf16[32,128,256]{2,1,0:T(8,128)(2,1)}), bf16[32,128,256]{2,1,0:T(8,128)(2,1)}, u32[]{:S(2)}, u32[]{:S(2)}) async-start(bf16[32,128,256]{2,1,0:T(8,128)(2,1)} %broadcast_select_fusion), calls=%async_computation | async-start | bytes 4194304 | tf_op jit(solution)/shard_map/all_to_all | solution.py:118
  22.8 647.5 %all-reduce.4.cloned.1.call-start = ((), (), s32[]{:S(2)}) async-start(), calls=%async_computation.1 | async-start | bytes 2097152 | tf_op jit(solution)/shard_map/psum | solution.py:146
  109.8 1.0 copy-start.4
  128.9 47.1 %collective-permute-start = (bf16[128,8192]{1,0:T(8,128)(2,1)S(1)}, bf16[128,8192]{1,0:T(8,128)(2,1)}, u32[]{:S(2)}, u32[]{:S(2)}) collective-permute-start(bf16[128,8192]{1,0:T(8,128)(2,1)S(1)} %fusion.21), channel_id=1, source_target_pairs={{32,0},{64,32},{96,64},{128,96},{160,128},{192,160},{224,192},{33,... | collective-permute-start | bytes 6291464 | tf_op jit(solution)/shard_map/ppermute | solution.py:16
  188.6 46.4 %collective-permute-start.1 = (bf16[128,8192]{1,0:T(8,128)(2,1)S(1)}, bf16[128,8192]{1,0:T(8,128)(2,1)}, u32[]{:S(2)}, u32[]{:S(2)}) collective-permute-start(bf16[128,8192]{1,0:T(8,128)(2,1)S(1)} %fusion.26), channel_id=1, source_target_pairs={{32,0},{64,32},{96,64},{128,96},{160,128},{192,160},{224,192},{33,... | collective-permute-start | bytes 6291464 | tf_op jit(solution)/shard_map/ppermute | solution.py:16
  247.6 45.6 %collective-permute-start.2 = (bf16[128,8192]{1,0:T(8,128)(2,1)S(1)}, bf16[128,8192]{1,0:T(8,128)(2,1)}, u32[]{:S(2)}, u32[]{:S(2)}) collective-permute-start(bf16[128,8192]{1,0:T(8,128)(2,1)S(1)} %fusion.31), channel_id=1, source_target_pairs={{32,0},{64,32},{96,64},{128,96},{160,128},{192,160},{224,192},{33,... | collective-permute-start | bytes 6291464 | tf_op jit(solution)/shard_map/ppermute | solution.py:16
  305.8 46.6 %collective-permute-start.3 = (bf16[128,8192]{1,0:T(8,128)(2,1)S(1)}, bf16[128,8192]{1,0:T(8,128)(2,1)}, u32[]{:S(2)}, u32[]{:S(2)}) collective-permute-start(bf16[128,8192]{1,0:T(8,128)(2,1)S(1)} %fusion.36), channel_id=1, source_target_pairs={{32,0},{64,32},{96,64},{128,96},{160,128},{192,160},{224,192},{33,... | collective-permute-start | bytes 6291464 | tf_op jit(solution)/shard_map/ppermute | solution.py:16
  365.1 44.4 %collective-permute-start.4 = (bf16[128,8192]{1,0:T(8,128)(2,1)S(1)}, bf16[128,8192]{1,0:T(8,128)(2,1)}, u32[]{:S(2)}, u32[]{:S(2)}) collective-permute-start(bf16[128,8192]{1,0:T(8,128)(2,1)S(1)} %fusion.41), channel_id=1, source_target_pairs={{32,0},{64,32},{96,64},{128,96},{160,128},{192,160},{224,192},{33,... | collective-permute-start | bytes 6291464 | tf_op jit(solution)/shard_map/ppermute | solution.py:16
  422.1 43.5 %collective-permute-start.5 = (bf16[128,8192]{1,0:T(8,128)(2,1)S(1)}, bf16[128,8192]{1,0:T(8,128)(2,1)}, u32[]{:S(2)}, u32[]{:S(2)}) collective-permute-start(bf16[128,8192]{1,0:T(8,128)(2,1)S(1)} %fusion.46), channel_id=1, source_target_pairs={{32,0},{64,32},{96,64},{128,96},{160,128},{192,160},{224,192},{33,... | collective-permute-start | bytes 6291464 | tf_op jit(solution)/shard_map/ppermute | solution.py:16
  472.9 48.1 %copy-start.2 = (f32[128,8192]{1,0:T(8,128)S(1)}, f32[128,8192]{1,0:T(8,128)}, u32[]{:S(2)}) copy-start(f32[128,8192]{1,0:T(8,128)} %add_multiply_fusion) | copy-start | bytes 12582916
  478.4 42.6 %collective-permute-start.6 = (bf16[128,8192]{1,0:T(8,128)(2,1)S(1)}, bf16[128,8192]{1,0:T(8,128)(2,1)}, u32[]{:S(2)}, u32[]{:S(2)}) collective-permute-start(bf16[128,8192]{1,0:T(8,128)(2,1)S(1)} %fusion.51), channel_id=1, source_target_pairs={{32,0},{64,32},{96,64},{128,96},{160,128},{192,160},{224,192},{33,... | collective-permute-start | bytes 6291464 | tf_op jit(solution)/shard_map/ppermute | solution.py:16
  521.0 153.1 %copy-start.1 = (bf16[1,32,128,256]{3,2,1,0:T(8,128)(2,1)S(1)}, bf16[1,32,128,256]{3,2,1,0:T(8,128)(2,1)}, u32[]{:S(2)}) copy-start(bf16[1,32,128,256]{3,2,1,0:T(8,128)(2,1)} %param.9) | copy-start | bytes 6291460
Sparse Core Ops, SparseCore 0:
  530.0 140.2 all-reduce.3
where the time goes:
time: 682 us; the launch traced here: 681 us
  waiting for transfers between devices  447 us (66%)
  blocking collectives  80.3 us (12%)
  matrix products  61.4 us (9%)
  other arithmetic  50.2 us (7%)
  starting transfers between devices  18.3 us (3%)
  between operations  16.9 us (2%)
    ppermute x7, waiting for transfers between devices, shifted(): return lax.ppermute(value, axis, pairs)  307 us
    psum x1, waiting for transfers between devices, shards(): total_down, total_up = lax.psum((local_down, local_up), 'dp')  140 us
    psum x1, blocking collectives, shards(): lax.psum((jnp.sum(is_valid * is_harm), jnp.sum(is_valid * (1.0 - is_harm)...  80.3 us
    dot_general x7, matrix products, back_input(): jnp.dot(low_grad, down_projection_rows, preferred_element_type=jnp.float32)  49.8 us
    convert_element_type x7, other arithmetic, shards(): incoming = shifted(passed.astype(jnp.bfloat16), 'section', -1)  37.1 us
  transfers between devices with their start and end apart: 9, of which 8 were waited for; matrix products, arithmetic and copies ran while one was open for 0% of the time, Pallas kernels for 0%

commit v1 on v0

v1 whole, which is shorter than its diff:
```python
import functools

import jax
import jax.numpy as jnp
from jax import lax
from jax.experimental import pallas as pl
from jax.experimental.pallas import tpu as pltpu
from jax.sharding import Mesh
from jax.sharding import PartitionSpec as P

norm_eps = 1e-05
stat_eps = 1e-06
coef_reroute = 64.0
coef_retain = 1.0
loss_scale = 2048.0

SEC = "section"
CHIPS = ("y", "x")
DP = ("y", "x", "core")
f32 = jnp.float32
bf16 = jnp.bfloat16


def nt(left, right):
    return lax.dot_general(left, right, (((1,), (1,)), ((), ())), preferred_element_type=f32)


def tn(left, right):
    return lax.dot_general(left, right, (((0,), (0,)), ((), ())), preferred_element_type=f32)


def nn(left, right):
    return lax.dot_general(left, right, (((1,), (0,)), ((), ())), preferred_element_type=f32)


def split2(value):
    hi = value.astype(bf16)
    lo = (value - hi.astype(f32)).astype(bf16)
    return hi, lo


def ring_gather(block, axis):
    n = lax.axis_size(axis)
    up = [(i, (i + 1) % n) for i in range(n)]
    down = [(i, (i - 1) % n) for i in range(n)]
    found = [None] * n
    found[0] = block
    fwd = bwd = block
    for k in range(1, n // 2 + 1):
        fwd = lax.ppermute(fwd, axis, up)
        found[k] = fwd
        if k < n - n // 2:
            bwd = lax.ppermute(bwd, axis, down)
            found[n - k] = bwd
    return found


def total_over_dp(value):
    for axis in ("core", "x", "y"):
        n = lax.axis_size(axis)
        step = 1
        while step < n:
            pairs = [(i, (i + step) % n) for i in range(n)]
            value = value + lax.ppermute(value, axis, pairs)
            step *= 2
    return value


def solve_kernel(layers, rank, width, own_ref, *refs):
    packs = refs[: layers - 1]
    lrt_ref, irms_ref, out_ref, acc = refs[layers - 1 :]
    lanes = own_ref.shape[1]
    rows = layers * rank
    acc[...] = jnp.zeros_like(acc)
    acc[0:rank, :] = own_ref[rows - rank : rows, :]
    for j in range(1, layers):
        low = rank * (layers - 1 - j)
        acc[0 : rank * (j + 1), :] += packs[j - 1][low:rows, 0:lanes].astype(f32)
    for j in range(layers - 1, 0, -1):
        low = rank * (layers - 1 - j)
        grad = acc[rank * j : rank * (j + 1), :].astype(bf16)
        k = layers - j
        lrt = lrt_ref[rank * k : rank * (k + 1), :].astype(f32)
        mean = jnp.sum(grad.astype(f32) * lrt, axis=0, keepdims=True) * (1.0 / width)
        irms = irms_ref[k : k + 1, :]
        w_hi = packs[j - 1][rows : rows + rank, 0:rows][:, low : rows - rank]
        w_lo = packs[j - 1][rows : rows + rank, rows : 2 * rows][:, low : rows - rank]
        term = tn(w_hi, grad) + tn(w_lo, grad)
        scaled_up = packs[j - 1][low : rows - rank, lanes : 2 * lanes].astype(f32)
        acc[0 : rank * j, :] += irms * (term - mean * scaled_up)
    out_ref[...] = acc[0:rank, :]


def solve(width, rank, own, packs, lrt, irms):
    layers = len(packs) + 1
    return pl.pallas_call(
        functools.partial(solve_kernel, layers, rank, width),
        out_shape=jax.ShapeDtypeStruct((rank, own.shape[1]), f32),
        scratch_shapes=[pltpu.VMEM((layers * rank, own.shape[1]), f32)],
        name="solve",
    )(own, *packs, lrt, irms)


def shards(
    layer_input_states,
    frozen_reference_states,
    adapter_down_weight,
    adapter_up_weight,
    layer_norm_gain,
    tile_reference_position,
    tile_harmful_flag,
    tile_valid_count,
):
    stream_bf = layer_input_states[0, 0]
    tokens, width = stream_bf.shape
    down = adapter_down_weight[0]
    up = adapter_up_weight[0]
    gains = layer_norm_gain[0]
    rank = up.shape[0]
    layers = lax.axis_size(SEC)
    core = lax.axis_index("core")
    cores = lax.axis_size("core")
    chips = lax.axis_size("y") * lax.axis_size("x")
    half = width // cores
    swap = [(i, (i + 1) % cores) for i in range(cores)]

    ordered = frozen_reference_states[0].at[tile_reference_position].get(mode="promise_in_bounds", unique_indices=True)
    fetched = lax.all_to_all(ordered, DP, split_axis=0, concat_axis=2, tiled=True)
    refs = fetched.reshape(tokens, width).astype(f32)

    flag = tile_harmful_flag[0].astype(f32)
    valid = tile_valid_count[0].astype(f32)
    lane = lax.broadcasted_iota(jnp.int32, (8, 128), 1)
    counts = jnp.where(lane == 0, flag * valid, jnp.where(lane == 1, (1.0 - flag) * valid, 0.0))
    counts = total_over_dp(counts)
    weight_harm = loss_scale * coef_reroute / counts[0, 0]
    weight_keep = loss_scale * coef_retain / counts[0, 1]

    stream = stream_bf.astype(f32)
    inverse_rms = lax.rsqrt(jnp.mean(stream * stream, axis=-1, keepdims=True) + norm_eps)
    normed = (stream * inverse_rms * gains).astype(bf16)
    lrt_own = nt(down, normed).astype(bf16)
    low_rank = nt(normed, down).astype(bf16)
    output = stream + nn(low_rank, up)
    irms_row = inverse_rms.reshape(1, tokens)
    dg = down.astype(f32) * gains
    dg_hi, dg_lo = split2(dg)

    up_half = lax.dynamic_slice_in_dim(up, core * half, half, axis=1)
    gathered = ring_gather(up_half, SEC)
    up_mine = jnp.concatenate(gathered[::-1], axis=0)
    up_other = lax.ppermute(up_mine, "core", swap)
    up_all = jnp.concatenate(
        [jnp.where(core == 0, up_mine, up_other), jnp.where(core == 0, up_other, up_mine)], axis=1
    )
    side = jnp.concatenate([lrt_own.astype(f32), jnp.broadcast_to(irms_row, (8, tokens))], axis=0)
    sides = ring_gather(side, SEC)
    lrt = jnp.concatenate([s[:rank] for s in sides], axis=0).astype(bf16)
    irms_all = jnp.concatenate([s[rank : rank + 1] for s in sides], axis=0)

    scaled_up = nt(up_all, stream_bf) * irms_row
    w_hi, w_lo = split2(nt(dg_hi, up_all) + nt(dg_lo, up_all))

    difference = output - refs
    out_sq = jnp.sum(output * output, axis=-1, keepdims=True)
    ref_sq = jnp.sum(refs * refs, axis=-1, keepdims=True)
    cross_sum = jnp.sum(output * refs, axis=-1, keepdims=True)
    diff_sq = jnp.sum(difference * difference, axis=-1, keepdims=True)
    out_norm = jnp.sqrt(out_sq + stat_eps)
    ref_norm = jnp.sqrt(ref_sq + stat_eps)
    diff_norm = jnp.sqrt(diff_sq + stat_eps)
    cosine = cross_sum / (out_norm * ref_norm)
    is_valid = lax.broadcasted_iota(jnp.int32, (tokens, 1), 0) < tile_valid_count[0]
    harm = tile_harmful_flag[0] == 1
    on_harm = jnp.where(is_valid & harm & (cosine > 0), weight_harm, 0.0)
    on_keep = jnp.where(is_valid & jnp.logical_not(harm), weight_keep, 0.0)
    coef_ref = on_harm / (out_norm * ref_norm)
    coef_out = -on_harm * cosine / (out_sq + stat_eps)
    coef_diff = on_keep / diff_norm
    own = (coef_ref * refs + coef_out * output + coef_diff * difference).astype(bf16)

    own_up = nt(up_all, own)
    pack = jnp.concatenate(
        [
            jnp.concatenate([own_up.astype(bf16), scaled_up.astype(bf16)], axis=1),
            jnp.concatenate([w_hi, w_lo], axis=1),
        ],
        axis=0,
    )
    packs = [lax.ppermute(pack, SEC, [(t, t - j) for t in range(j, layers)]) for j in range(1, layers)]
    low_grad_t = solve(width, rank, own_up, packs, lrt, irms_all).astype(bf16)

    low_grad_f = low_grad_t.astype(f32)
    mean = jnp.sum(low_grad_f * lrt[:rank].astype(f32), axis=0, keepdims=True) * (1.0 / width)
    below = (lax.broadcasted_iota(jnp.int32, (layers * rank, 1), 0) >= rank).astype(f32)
    lrt_f = lrt.astype(f32) * below
    coef_stream = (lrt_f * (-irms_row * irms_row * mean)).astype(bf16)
    k_hi, k_lo = split2(nt(lrt_f.astype(bf16), (low_grad_f * irms_row).astype(bf16)))
    part_up = (
        nn(lrt, own) + nn(coef_stream, stream_bf) + nn(k_hi, dg_hi) + nn(k_hi, dg_lo) + nn(k_lo, dg_hi)
    )
    part_down = nn(low_grad_t, normed)
    part = jnp.concatenate([part_up, part_down], axis=0)

    lower, upper = part[:, :half], part[:, half:]
    kept = jnp.where(core == 0, lower, upper)
    given = jnp.where(core == 0, upper, lower)
    chip = (kept + lax.ppermute(given, "core", swap)).astype(bf16)
    rows = part.shape[0]
    blocks = chip.reshape(rows, chips, half // chips).transpose(1, 0, 2)
    blocks = lax.all_to_all(blocks, CHIPS, 0, 0, tiled=True)
    summed = jnp.sum(blocks.astype(f32), axis=0)

    grad_up = summed[:rank]
    for k in range(1, layers):
        grad_up = grad_up + lax.ppermute(
            summed[rank * k : rank * (k + 1)], SEC, [(t, t - k) for t in range(k, layers)]
        )
    final = jnp.concatenate([summed[layers * rank :], grad_up], axis=0)

    wide = lax.all_to_all(jnp.broadcast_to(final, (chips,) + final.shape), CHIPS, 0, 0, tiled=True)
    mine = wide.transpose(1, 0, 2).reshape(2 * rank, half)
    other = lax.ppermute(mine, "core", swap)
    full = jnp.concatenate([jnp.where(core == 0, mine, other), jnp.where(core == 0, other, mine)], axis=1)
    return (full[None, :rank], full[None, rank:])


def solution(mesh):
    layers, dp = mesh.devices.shape
    cores = 2
    side = round((dp // cores) ** 0.5)
    mesh4 = Mesh(mesh.devices.reshape(layers, side, side, cores), (SEC,) + DP)
    return jax.shard_map(
        shards,
        mesh=mesh4,
        in_specs=(
            P(SEC, DP, None, None),
            P(SEC, None, None, DP),
            P(SEC, None, None),
            P(SEC, None, None),
            P(SEC, None),
            P(),
            P(DP),
            P(DP),
        ),
        out_specs=(P(SEC, None, None), P(SEC, None, None)),
        check_vma=False,
    )
```

time: 682 us -> 204 us (0.30)
  waiting for transfers between devices: 447 us -> 62.5 us
  matrix products: 61.4 us -> 13.7 us
  starting transfers between devices: 18.3 us -> 63.9 us
  blocking collectives: 80.3 us -> 36.7 us
  other arithmetic: 50.2 us -> 10.7 us
  between operations: 16.9 us -> 4.02 us
    ppermute x7 -> x36, waiting for transfers between devices: 307 us -> 62.5 us  [the longest x5 19.4 us: total_over_dp(): value = value + lax.ppermute(value, axis, pairs)]
    psum x1 -> x0, waiting for transfers between devices: 140 us -> none  [shards(): total_down, total_up = lax.psum((local_down, local_up), 'dp')]
    psum x1 -> x0, blocking collectives: 80.3 us -> none  [shards(): lax.psum((jnp.sum(is_valid * is_harm), jnp.sum(is_valid * (1.0 - is_harm)...]
    dot_general x11 -> x13, matrix products: 61.4 us -> 13.7 us  [the longest x7 7.09 us: nn(): lax.dot_general(left, right, (((1,), (0,)), ((), ())), preferred_element_...]
    ppermute x7 -> x36, starting transfers between devices: 9.45 us -> 56.3 us  [the longest x6 15.4 us: ring_gather(): bwd = lax.ppermute(bwd, axis, down)]
    all_to_all x0 -> x2, blocking collectives: none -> 36.7 us  [the longest x1 24.5 us: shards(): blocks = lax.all_to_all(blocks, CHIPS, 0, 0, tiled=True)]
    convert_element_type x7 -> x4, other arithmetic: 37.1 us -> 1.97 us  [the longest x1 1.51 us: shards(): (coef_ref * refs + coef_out * output + coef_diff * difference).astype(bf16)]
  transfers between devices with their start and end apart: 9 -> 37, of which waited for: 8 -> 19; matrix products, arithmetic and copies ran while one was open for 0% -> 5% of each run, Pallas kernels for 0% -> 0%
where the time goes in v1:
time: 204 us; the launch traced here: 203 us
  starting transfers between devices  63.9 us (31%)
  waiting for transfers between devices  62.5 us (31%)
  blocking collectives  36.7 us (18%)
  matrix products  13.7 us (7%)
  other arithmetic  10.7 us (5%)
  local copies, waits for them, and re-layouts  8.86 us (4%)
  between operations  4.02 us (2%)
  Pallas kernels  2.8 us (1%)
    all_to_all x1, blocking collectives, shards(): blocks = lax.all_to_all(blocks, CHIPS, 0, 0, tiled=True)  24.5 us
    ppermute x5, waiting for transfers between devices, total_over_dp(): value = value + lax.ppermute(value, axis, pairs)  19.4 us
    ppermute x7, waiting for transfers between devices, shards(): lax.ppermute(pack, SEC, [(t, t - j) for t in range(j, layers)])  15.9 us
    ppermute x6, starting transfers between devices, ring_gather(): bwd = lax.ppermute(bwd, axis, down)  15.4 us
    ppermute x8, waiting for transfers between devices, ring_gather(): fwd = lax.ppermute(fwd, axis, up)  15 us
    all_to_all x1, blocking collectives, shards(): lax.all_to_all(jnp.broadcast_to(final, (chips,) + final.shape), CHIPS, 0,...  12.2 us
    ppermute x7, starting transfers between devices, shards(): lax.ppermute(pack, SEC, [(t, t - j) for t in range(j, layers)])  9.27 us
    ppermute x7, starting transfers between devices, shards(): lax.ppermute(summed[rank * k:rank * (k + 1)], SEC, [(t, t - k) for t in r...  9.03 us
  transfers between devices with their start and end apart: 37, of which 19 were waited for; matrix products, arithmetic and copies ran while one was open for 5% of the time, Pallas kernels for 0%

profile of v1, /device:TPU:1, one launch (start us, length us, event | category | flops | bytes accessed | tf_op | source)
XLA Modules:
  0.0 203.3 jit_solution(17853082945260535822)
XLA Ops:
  1.7 6.5 %collective-permute-start.12 = (bf16[16,4096]{1,0:T(8,128)(2,1)S(1)}, bf16[16,4096]{1,0:T(8,128)(2,1)S(1)}, u32[]{:S(2)}, u32[]{:S(2)}) collective-permute-start(bf16[16,4096]{1,0:T(8,128)(2,1)S(1)} %dynamic-slice_bitcast_fusion), channel_id=1, source_target_pairs={{0,224},{32,0},{64,32},{96,64},{128,96},{160,128},{192,160},{224,1... | collective-permute-start | bytes 393224 | tf_op jit(solution)/shard_map/ppermute | solution.py:53
  10.6 2.1 %fusion.2 = f32[128]{0:T(128)S(1)} fusion(bf16[1,1,128,8192]{3,2,1,0:T(8,128)(2,1)} %param.8), kind=kLoop, calls=%fused_computation.13 | loop fusion | flops 3145600 | bytes 2097664 | tf_op jit(solution)/shard_map/reduce_sum | solution.py:140
  12.7 2.3 %constant_dynamic-update-slice_fusion.7 = (bf16[128,128]{1,0:T(8,128)(2,1)S(1)}, bf16[128,16]{0,1:T(8,128)(2,1)S(1)}) fusion(bf16[1,16,8192]{2,1,0:T(8,128)(2,1)} %param.10, bf16[1,1,128,8192]{3,2,1,0:T(8,128)(2,1)} %param.8, f32[8192]{0:T(1024)} %bitcast.107, f32[128]{0:T(128)S(1)} %get-tuple-element.30), kind=kOutput, calls=%fused_computation.80 | convolution fusion | flops 37750784 | bytes 2400768 | tf_op jit(solution)/shard_map/dot_general | solution.py:25
  15.1 3.0 %collective-permute-start.4 = (f32[24,128]{1,0:T(8,128)S(1)}, f32[24,128]{1,0:T(8,128)S(1)}, u32[]{:S(2)}, u32[]{:S(2)}) collective-permute-start(f32[24,128]{1,0:T(8,128)S(1)} %pad_maximum_fusion.4), channel_id=1, source_target_pairs={{0,224},{32,0},{64,32},{96,64},{128,96},{160,128},{192,160},{224,1... | collective-permute-start | bytes 36872 | tf_op jit(solution)/shard_map/ppermute | solution.py:53
  19.5 2.5 %collective-permute-done.8 = f32[8,128]{1,0:T(8,128)S(1)} collective-permute-done((f32[8,128]{1,0:T(8,128)S(1)}, f32[8,128]{1,0:T(8,128)S(1)}, u32[]{:S(2)}, u32[]{:S(2)}) %collective-permute-start.8) | collective-permute-done | bytes 4128 | tf_op jit(solution)/shard_map/ppermute | solution.py:64
  21.9 1.5 collective-permute-start.9
  23.5 2.0 %gather_fusion = bf16[32,128,256]{2,1,0:T(8,128)(2,1)} fusion(bf16[32,128,256]{2,1,0:T(8,128)(2,1)S(1)} %bitcast.99, s32[1024]{0:T(1024)S(1)} %pad_clamp_fusion), kind=kCustom, calls=%fused_computation | custom fusion | bytes 4194432 | tf_op jit(solution)/shard_map/gather | solution.py:127
  25.5 7.6 %all-to-all-start = ((bf16[32,128,256]{2,1,0:T(8,128)(2,1)}), bf16[32,128,256]{2,1,0:T(8,128)(2,1)}, u32[]{:S(2)}, u32[]{:S(2)}) async-start(bf16[32,128,256]{2,1,0:T(8,128)(2,1)} %gather_fusion), calls=%async_computation | async-start | bytes 4194304 | tf_op jit(solution)/shard_map/all_to_all | solution.py:128
  33.1 1.5 collective-permute-start.10
  34.6 16.9 %collective-permute-done.10 = f32[8,128]{1,0:T(8,128)S(1)} collective-permute-done((f32[8,128]{1,0:T(8,128)S(1)}, f32[8,128]{1,0:T(8,128)S(1)}, u32[]{:S(2)}, u32[]{:S(2)}) %collective-permute-start.10) | collective-permute-done | bytes 4128 | tf_op jit(solution)/shard_map/ppermute | solution.py:64
  52.8 1.7 collective-permute-start.13
  54.5 2.5 %collective-permute-done.13 = bf16[16,4096]{1,0:T(8,128)(2,1)S(1)} collective-permute-done((bf16[16,4096]{1,0:T(8,128)(2,1)S(1)}, bf16[16,4096]{1,0:T(8,128)(2,1)S(1)}, u32[]{:S(2)}, u32[]{:S(2)}) %collective-permute-start.13) | collective-permute-done | bytes 131104 | tf_op jit(solution)/shard_map/ppermute | solution.py:53
  57.0 2.9 %collective-permute-start.14 = (bf16[16,4096]{1,0:T(8,128)(2,1)S(1)}, bf16[16,4096]{1,0:T(8,128)(2,1)S(1)}, u32[]{:S(2)}, u32[]{:S(2)}) collective-permute-start(bf16[16,4096]{1,0:T(8,128)(2,1)S(1)} %collective-permute-done.13), channel_id=1, source_target_pairs={{0,224},{32,0},{64,32},{96,64},{128,96},{160,128},{192,160},{224,1... | collective-permute-start | bytes 393224 | tf_op jit(solution)/shard_map/ppermute | solution.py:53
  59.9 5.8 %collective-permute-done.17 = bf16[16,4096]{1,0:T(8,128)(2,1)S(1)} collective-permute-done((bf16[16,4096]{1,0:T(8,128)(2,1)S(1)}, bf16[16,4096]{1,0:T(8,128)(2,1)S(1)}, u32[]{:S(2)}, u32[]{:S(2)}) %collective-permute-start.17) | collective-permute-done | bytes 131104 | tf_op jit(solution)/shard_map/ppermute | solution.py:50
  65.8 5.0 %collective-permute-done.18 = bf16[16,4096]{1,0:T(8,128)(2,1)S(1)} collective-permute-done((bf16[16,4096]{1,0:T(8,128)(2,1)S(1)}, bf16[16,4096]{1,0:T(8,128)(2,1)S(1)}, u32[]{:S(2)}, u32[]{:S(2)}) %collective-permute-start.18) | collective-permute-done | bytes 131104 | tf_op jit(solution)/shard_map/ppermute | solution.py:50
  70.9 9.0 %collective-permute-start.19 = (bf16[128,4096]{1,0:T(8,128)(2,1)S(1)}, bf16[128,4096]{1,0:T(8,128)(2,1)S(1)}, u32[]{:S(2)}, u32[]{:S(2)}) collective-permute-start(bf16[128,4096]{1,0:T(8,128)(2,1)S(1)} %constant_dynamic-update-slice_fusion.8), channel_id=1, source_target_pairs={{0,1},{1,0},{2,3},{3,2},{4,5},{5,4},{6,7},{7,6},{8,9},{9,8},{10,11... | collective-permute-start | bytes 3145736 | tf_op jit(solution)/shard_map/ppermute | solution.py:152
  81.9 1.5 collective-permute-start.2
  83.5 1.3 collective-permute-start.6
  86.4 3.1 %collective-permute-done.3 = f32[24,128]{1,0:T(8,128)S(1)} collective-permute-done((f32[24,128]{1,0:T(8,128)S(1)}, f32[24,128]{1,0:T(8,128)S(1)}, u32[]{:S(2)}, u32[]{:S(2)}) %collective-permute-start.3) | collective-permute-done | bytes 12320 | tf_op jit(solution)/shard_map/ppermute | solution.py:50
  92.8 2.1 %fusion.78 = f32[16,8,32,256]{3,1,0,2:T(8,128)S(1)} fusion(bf16[32,128,256]{2,1,0:T(8,128)(2,1)} %all-to-all-done), kind=kLoop, calls=%fused_computation.143 | loop fusion | flops 1048576 | bytes 6291456
  95.3 2.0 multiply_reduce_fusion.1
  97.3 2.1 %fusion.1 = f32[128]{0:T(128)S(1)} fusion(bf16[32,128,256]{2,1,0:T(8,128)(2,1)} %all-to-all-done), kind=kLoop, calls=%fused_computation.12 | loop fusion | flops 3145600 | bytes 2097664 | tf_op jit(solution)/shard_map/reduce_sum | solution.py:166
  99.5 1.5 add_convert_fusion
  101.0 1.3 copy-done.3
  102.4 1.3 fusion.77
  103.7 1.3 collective-permute-start.20
  105.0 1.3 collective-permute-start.21
  106.3 1.3 collective-permute-start.22
  107.6 1.3 collective-permute-start.23
  110.2 1.3 collective-permute-start.25
  111.6 1.5 collective-permute-start.26
  114.7 2.8 %collective-permute-done.23.refs_3_ = bf16[144,256]{1,0:T(8,128)(2,1)S(1)} collective-permute-done((bf16[144,256]{1,0:T(8,128)(2,1)S(1)}, bf16[144,256]{1,0:T(8,128)(2,1)S(1)}, u32[]{:S(2)}, u32[]{:S(2)}) %collective-permute-start.23) | collective-permute-done | bytes 73760 | tf_op jit(solution)/shard_map/ppermute | solution.py:190
  117.5 1.4 collective-permute-done.24.refs_4_
  118.9 4.1 %collective-permute-done.25.refs_5_ = bf16[144,256]{1,0:T(8,128)(2,1)S(1)} collective-permute-done((bf16[144,256]{1,0:T(8,128)(2,1)S(1)}, bf16[144,256]{1,0:T(8,128)(2,1)S(1)}, u32[]{:S(2)}, u32[]{:S(2)}) %collective-permute-start.25) | collective-permute-done | bytes 73760 | tf_op jit(solution)/shard_map/ppermute | solution.py:190
  123.0 6.7 %collective-permute-done.26.refs_6_ = bf16[144,256]{1,0:T(8,128)(2,1)S(1)} collective-permute-done((bf16[144,256]{1,0:T(8,128)(2,1)S(1)}, bf16[144,256]{1,0:T(8,128)(2,1)S(1)}, u32[]{:S(2)}, u32[]{:S(2)}) %collective-permute-start.26) | collective-permute-done | bytes 73760 | tf_op jit(solution)/shard_map/ppermute | solution.py:190
  130.3 2.8 %solve.1 = f32[16,128]{1,0:T(8,128)} custom-call(f32[128,128]{1,0:T(8,128)} %get-tuple-element.33.own_ref, bf16[144,256]{1,0:T(8,128)(2,1)} %copy-done.14, bf16[144,256]{1,0:T(8,128)(2,1)} %copy-done.15, bf16[144,256]{1,0:T(8,128)(2,1)} %copy-done.16, bf16[144,256]{1,0:T(8,128)(2,1)} %copy-done.17, bf16[144,256]{1,0:T(8,128)(2,1)} %copy-done.18, ...), custom_call_target="tpu_custom_call" | custom-call | tf_op jit(solution)/shard_map/solve/pallas_call | solution.py:96
  133.1 1.4 fusion.9
  141.5 4.2 %collective-permute-done.27 = f32[144,4096]{1,0:T(8,128)S(1)} collective-permute-done((f32[144,4096]{1,0:T(8,128)S(1)}, f32[144,4096]{1,0:T(8,128)S(1)}, u32[]{:S(2)}, u32[]{:S(2)}) %collective-permute-start.27) | collective-permute-done | bytes 2359328 | tf_op jit(solution)/shard_map/ppermute | solution.py:208
  146.3 24.5 %all_to_all.19 = bf16[16,144,256]{2,1,0:T(8,128)(2,1)S(1)} all-to-all(bf16[16,144,256]{2,1,0:T(8,128)(2,1)S(1)} %bitcast.102), channel_id=1, replica_groups=mesh['section'=8,'y'=4,'x'=4,'core'=2] {'y','x'}, dimensions={0} | all-to-all | bytes 2359296 | tf_op jit(solution)/shard_map/all_to_all | solution.py:211
  171.0 1.3 collective-permute-start.34
  172.3 1.3 collective-permute-start.33
  173.6 1.3 collective-permute-start.32
  174.9 1.3 collective-permute-start.31
  176.2 1.3 collective-permute-start.30
  181.0 2.2 %collective-permute-done.31 = f32[16,256]{1,0:T(8,128)S(1)} collective-permute-done((f32[16,256]{1,0:T(8,128)S(1)}, f32[16,256]{1,0:T(8,128)S(1)}, u32[]{:S(2)}, u32[]{:S(2)}) %collective-permute-start.31) | collective-permute-done | bytes 16416 | tf_op jit(solution)/shard_map/ppermute | solution.py:216
  183.7 12.2 %all_to_all.20 = f32[16,32,256]{2,1,0:T(8,128)S(1)} all-to-all(f32[16,32,256]{2,1,0:T(8,128)S(1)} %broadcast_in_dim.49), channel_id=1, replica_groups=mesh['section'=8,'y'=4,'x'=4,'core'=2] {'y','x'}, dimensions={0} | all-to-all | bytes 1048576 | tf_op jit(solution)/shard_map/all_to_all | solution.py:221
  195.9 4.7 %collective-permute-start.35 = (f32[32,4096]{1,0:T(8,128)S(1)}, f32[32,4096]{1,0:T(8,128)S(1)}, u32[]{:S(2)}, u32[]{:S(2)}) collective-permute-start(f32[32,4096]{1,0:T(8,128)S(1)} %bitcast.104), channel_id=1, source_target_pairs={{0,1},{1,0},{2,3},{3,2},{4,5},{5,4},{6,7},{7,6},{8,9},{9,8},{10,11... | collective-permute-start | bytes 1572872 | tf_op jit(solution)/shard_map/ppermute | solution.py:223
  200.6 1.5 collective-permute-done.35
  (152 shorter events, 27.3 us)
Async XLA Ops:
  0.6 22.8 %copy-start = (bf16[1,32,128,256]{3,2,1,0:T(8,128)(2,1)S(1)}, bf16[1,32,128,256]{3,2,1,0:T(8,128)(2,1)}, u32[]{:S(2)}) copy-start(bf16[1,32,128,256]{3,2,1,0:T(8,128)(2,1)} %param.9) | copy-start | bytes 6291460
  0.6 18.8 %copy-start.22 = (s32[32]{0:T(128)S(1)}, s32[32]{0:T(128)}, u32[]{:S(2)}) copy-start(s32[32]{0:T(128)} %param.13) | copy-start | bytes 388
  1.7 51.1 %collective-permute-start.12 = (bf16[16,4096]{1,0:T(8,128)(2,1)S(1)}, bf16[16,4096]{1,0:T(8,128)(2,1)S(1)}, u32[]{:S(2)}, u32[]{:S(2)}) collective-permute-start(bf16[16,4096]{1,0:T(8,128)(2,1)S(1)} %dynamic-slice_bitcast_fusion), channel_id=1, source_target_pairs={{0,224},{32,0},{64,32},{96,64},{128,96},{160,128},{192,160},{224,1... | collective-permute-start | bytes 393224 | tf_op jit(solution)/shard_map/ppermute | solution.py:53
  8.2 46.2 %collective-permute-start.15 = (bf16[16,4096]{1,0:T(8,128)(2,1)S(1)}, bf16[16,4096]{1,0:T(8,128)(2,1)S(1)}, u32[]{:S(2)}, u32[]{:S(2)}) collective-permute-start(bf16[16,4096]{1,0:T(8,128)(2,1)S(1)} %dynamic-slice_bitcast_fusion), channel_id=1, source_target_pairs={{0,32},{32,64},{64,96},{96,128},{128,160},{160,192},{192,224},{224... | collective-permute-start | bytes 393224 | tf_op jit(solution)/shard_map/ppermute | solution.py:50
  9.5 8.6 %collective-permute-start.7 = (f32[8,128]{1,0:T(8,128)S(1)}, f32[8,128]{1,0:T(8,128)S(1)}, u32[]{:S(2)}, u32[]{:S(2)}) collective-permute-start(f32[8,128]{1,0:T(8,128)S(1)} %broadcast_select_fusion.5), channel_id=1, source_target_pairs={{0,1},{1,0},{2,3},{3,2},{4,5},{5,4},{6,7},{7,6},{8,9},{9,8},{10,11... | collective-permute-start | bytes 12296 | tf_op jit(solution)/shard_map/ppermute | solution.py:64
  15.0 19.6 %collective-permute-start = (f32[24,128]{1,0:T(8,128)S(1)}, f32[24,128]{1,0:T(8,128)S(1)}, u32[]{:S(2)}, u32[]{:S(2)}) collective-permute-start(f32[24,128]{1,0:T(8,128)S(1)} %pad_maximum_fusion.4), channel_id=1, source_target_pairs={{0,32},{32,64},{64,96},{96,128},{128,160},{160,192},{192,224},{224... | collective-permute-start | bytes 36872 | tf_op jit(solution)/shard_map/ppermute | solution.py:50
  15.1 64.7 %collective-permute-start.4 = (f32[24,128]{1,0:T(8,128)S(1)}, f32[24,128]{1,0:T(8,128)S(1)}, u32[]{:S(2)}, u32[]{:S(2)}) collective-permute-start(f32[24,128]{1,0:T(8,128)S(1)} %pad_maximum_fusion.4), channel_id=1, source_target_pairs={{0,224},{32,0},{64,32},{96,64},{128,96},{160,128},{192,160},{224,1... | collective-permute-start | bytes 36872 | tf_op jit(solution)/shard_map/ppermute | solution.py:53
  18.2 3.7 %collective-permute-start.8 = (f32[8,128]{1,0:T(8,128)S(1)}, f32[8,128]{1,0:T(8,128)S(1)}, u32[]{:S(2)}, u32[]{:S(2)}) collective-permute-start(f32[8,128]{1,0:T(8,128)S(1)} %fusion.62), channel_id=1, source_target_pairs={{0,2},{2,4},{4,6},{6,0},{1,3},{3,5},{5,7},{7,1},{8,10},{10,12},{12... | collective-permute-start | bytes 12296 | tf_op jit(solution)/shard_map/ppermute | solution.py:64
  21.9 11.2 %collective-permute-start.9 = (f32[8,128]{1,0:T(8,128)S(1)}, f32[8,128]{1,0:T(8,128)S(1)}, u32[]{:S(2)}, u32[]{:S(2)}) collective-permute-start(f32[8,128]{1,0:T(8,128)S(1)} %fusion.83), channel_id=1, source_target_pairs={{0,4},{2,6},{4,0},{6,2},{1,5},{3,7},{5,1},{7,3},{8,12},{10,14},{12... | collective-permute-start | bytes 12296 | tf_op jit(solution)/shard_map/ppermute | solution.py:64
  23.5 47.4 %copy-start.6 = (bf16[1,16,8192]{2,1,0:T(8,128)(2,1)S(1)}, bf16[1,16,8192]{2,1,0:T(8,128)(2,1)}, u32[]{:S(2)}) copy-start(bf16[1,16,8192]{2,1,0:T(8,128)(2,1)} %param.11) | copy-start | bytes 786436
  25.5 67.3 %all-to-all-start = ((bf16[32,128,256]{2,1,0:T(8,128)(2,1)}), bf16[32,128,256]{2,1,0:T(8,128)(2,1)}, u32[]{:S(2)}, u32[]{:S(2)}) async-start(bf16[32,128,256]{2,1,0:T(8,128)(2,1)} %gather_fusion), calls=%async_computation | async-start | bytes 4194304 | tf_op jit(solution)/shard_map/all_to_all | solution.py:128
  33.1 56.7 %copy-start.5 = (bf16[1,16,8192]{2,1,0:T(8,128)(2,1)S(1)}, bf16[1,16,8192]{2,1,0:T(8,128)(2,1)}, u32[]{:S(2)}) copy-start(bf16[1,16,8192]{2,1,0:T(8,128)(2,1)} %param.10) | copy-start | bytes 786436
  33.1 56.7 %copy-start.11 = (f32[1,8192]{1,0:T(1,128)S(1)}, f32[1,8192]{1,0:T(1,128)}, u32[]{:S(2)}) copy-start(f32[1,8192]{1,0:T(1,128)} %param.12) | copy-start | bytes 98308
  33.1 18.4 %collective-permute-start.10 = (f32[8,128]{1,0:T(8,128)S(1)}, f32[8,128]{1,0:T(8,128)S(1)}, u32[]{:S(2)}, u32[]{:S(2)}) collective-permute-start(f32[8,128]{1,0:T(8,128)S(1)} %add.138), channel_id=1, source_target_pairs={{0,8},{8,16},{16,24},{24,0},{1,9},{9,17},{17,25},{25,1},{2,10},{10... | collective-permute-start | bytes 12296 | tf_op jit(solution)/shard_map/ppermute | solution.py:64
  34.6 47.3 %collective-permute-start.1 = (f32[24,128]{1,0:T(8,128)S(1)}, f32[24,128]{1,0:T(8,128)S(1)}, u32[]{:S(2)}, u32[]{:S(2)}) collective-permute-start(f32[24,128]{1,0:T(8,128)S(1)} %collective-permute-done), channel_id=1, source_target_pairs={{0,32},{32,64},{64,96},{96,128},{128,160},{160,192},{192,224},{224... | collective-permute-start | bytes 36872 | tf_op jit(solution)/shard_map/ppermute | solution.py:50
  51.6 28.4 %collective-permute-start.11 = (f32[8,128]{1,0:T(8,128)S(1)}, f32[8,128]{1,0:T(8,128)S(1)}, u32[]{:S(2)}, u32[]{:S(2)}) collective-permute-start(f32[8,128]{1,0:T(8,128)S(1)} %add.139), channel_id=1, source_target_pairs={{0,16},{8,24},{16,0},{24,8},{1,17},{9,25},{17,1},{25,9},{2,18},{10... | collective-permute-start | bytes 12296 | tf_op jit(solution)/shard_map/ppermute | solution.py:64
  52.8 4.2 %collective-permute-start.13 = (bf16[16,4096]{1,0:T(8,128)(2,1)S(1)}, bf16[16,4096]{1,0:T(8,128)(2,1)S(1)}, u32[]{:S(2)}, u32[]{:S(2)}) collective-permute-start(bf16[16,4096]{1,0:T(8,128)(2,1)S(1)} %collective-permute-done.12), channel_id=1, source_target_pairs={{0,224},{32,0},{64,32},{96,64},{128,96},{160,128},{192,160},{224,1... | collective-permute-start | bytes 393224 | tf_op jit(solution)/shard_map/ppermute | solution.py:53
  54.5 5.4 %collective-permute-start.16 = (bf16[16,4096]{1,0:T(8,128)(2,1)S(1)}, bf16[16,4096]{1,0:T(8,128)(2,1)S(1)}, u32[]{:S(2)}, u32[]{:S(2)}) collective-permute-start(bf16[16,4096]{1,0:T(8,128)(2,1)S(1)} %collective-permute-done.15), channel_id=1, source_target_pairs={{0,32},{32,64},{64,96},{96,128},{128,160},{160,192},{192,224},{224... | collective-permute-start | bytes 393224 | tf_op jit(solution)/shard_map/ppermute | solution.py:50
  57.0 8.7 %collective-permute-start.14 = (bf16[16,4096]{1,0:T(8,128)(2,1)S(1)}, bf16[16,4096]{1,0:T(8,128)(2,1)S(1)}, u32[]{:S(2)}, u32[]{:S(2)}) collective-permute-start(bf16[16,4096]{1,0:T(8,128)(2,1)S(1)} %collective-permute-done.13), channel_id=1, source_target_pairs={{0,224},{32,0},{64,32},{96,64},{128,96},{160,128},{192,160},{224,1... | collective-permute-start | bytes 393224 | tf_op jit(solution)/shard_map/ppermute | solution.py:53
  59.9 5.9 %collective-permute-start.17 = (bf16[16,4096]{1,0:T(8,128)(2,1)S(1)}, bf16[16,4096]{1,0:T(8,128)(2,1)S(1)}, u32[]{:S(2)}, u32[]{:S(2)}) collective-permute-start(bf16[16,4096]{1,0:T(8,128)(2,1)S(1)} %collective-permute-done.16), channel_id=1, source_target_pairs={{0,32},{32,64},{64,96},{96,128},{128,160},{160,192},{192,224},{224... | collective-permute-start | bytes 393224 | tf_op jit(solution)/shard_map/ppermute | solution.py:50
  65.7 5.0 %collective-permute-start.18 = (bf16[16,4096]{1,0:T(8,128)(2,1)S(1)}, bf16[16,4096]{1,0:T(8,128)(2,1)S(1)}, u32[]{:S(2)}, u32[]{:S(2)}) collective-permute-start(bf16[16,4096]{1,0:T(8,128)(2,1)S(1)} %collective-permute-done.17), channel_id=1, source_target_pairs={{0,32},{32,64},{64,96},{96,128},{128,160},{160,192},{192,224},{224... | collective-permute-start | bytes 393224 | tf_op jit(solution)/shard_map/ppermute | solution.py:50
  70.9 18.7 %collective-permute-start.19 = (bf16[128,4096]{1,0:T(8,128)(2,1)S(1)}, bf16[128,4096]{1,0:T(8,128)(2,1)S(1)}, u32[]{:S(2)}, u32[]{:S(2)}) collective-permute-start(bf16[128,4096]{1,0:T(8,128)(2,1)S(1)} %constant_dynamic-update-slice_fusion.8), channel_id=1, source_target_pairs={{0,1},{1,0},{2,3},{3,2},{4,5},{5,4},{6,7},{7,6},{8,9},{9,8},{10,11... | collective-permute-start | bytes 3145736 | tf_op jit(solution)/shard_map/ppermute | solution.py:152
  79.9 3.6 %collective-permute-start.5 = (f32[24,128]{1,0:T(8,128)S(1)}, f32[24,128]{1,0:T(8,128)S(1)}, u32[]{:S(2)}, u32[]{:S(2)}) collective-permute-start(f32[24,128]{1,0:T(8,128)S(1)} %collective-permute-done.4), channel_id=1, source_target_pairs={{0,224},{32,0},{64,32},{96,64},{128,96},{160,128},{192,160},{224,1... | collective-permute-start | bytes 36872 | tf_op jit(solution)/shard_map/ppermute | solution.py:53
  81.9 3.8 %collective-permute-start.2 = (f32[24,128]{1,0:T(8,128)S(1)}, f32[24,128]{1,0:T(8,128)S(1)}, u32[]{:S(2)}, u32[]{:S(2)}) collective-permute-start(f32[24,128]{1,0:T(8,128)S(1)} %collective-permute-done.1), channel_id=1, source_target_pairs={{0,32},{32,64},{64,96},{96,128},{128,160},{160,192},{192,224},{224... | collective-permute-start | bytes 36872 | tf_op jit(solution)/shard_map/ppermute | solution.py:50
  83.5 2.9 %collective-permute-start.6 = (f32[24,128]{1,0:T(8,128)S(1)}, f32[24,128]{1,0:T(8,128)S(1)}, u32[]{:S(2)}, u32[]{:S(2)}) collective-permute-start(f32[24,128]{1,0:T(8,128)S(1)} %collective-permute-done.5), channel_id=1, source_target_pairs={{0,224},{32,0},{64,32},{96,64},{128,96},{160,128},{192,160},{224,1... | collective-permute-start | bytes 36872 | tf_op jit(solution)/shard_map/ppermute | solution.py:53
  85.8 3.8 %collective-permute-start.3 = (f32[24,128]{1,0:T(8,128)S(1)}, f32[24,128]{1,0:T(8,128)S(1)}, u32[]{:S(2)}, u32[]{:S(2)}) collective-permute-start(f32[24,128]{1,0:T(8,128)S(1)} %collective-permute-done.2), channel_id=1, source_target_pairs={{0,32},{32,64},{64,96},{96,128},{128,160},{160,192},{192,224},{224... | collective-permute-start | bytes 36872 | tf_op jit(solution)/shard_map/ppermute | solution.py:50
  103.7 6.5 %collective-permute-start.20 = (bf16[144,256]{1,0:T(8,128)(2,1)S(1)}, bf16[144,256]{1,0:T(8,128)(2,1)S(1)}, u32[]{:S(2)}, u32[]{:S(2)}) collective-permute-start(bf16[144,256]{1,0:T(8,128)(2,1)S(1)} %maximum_maximum_fusion), channel_id=1, source_target_pairs={{32,0},{64,32},{96,64},{128,96},{160,128},{192,160},{224,192},{33,... | collective-permute-start | bytes 221192 | tf_op jit(solution)/shard_map/ppermute | solution.py:190
  105.0 6.5 %collective-permute-start.21 = (bf16[144,256]{1,0:T(8,128)(2,1)S(1)}, bf16[144,256]{1,0:T(8,128)(2,1)S(1)}, u32[]{:S(2)}, u32[]{:S(2)}) collective-permute-start(bf16[144,256]{1,0:T(8,128)(2,1)S(1)} %maximum_maximum_fusion), channel_id=1, source_target_pairs={{64,0},{96,32},{128,64},{160,96},{192,128},{224,160},{65,1},{97,33... | collective-permute-start | bytes 221192 | tf_op jit(solution)/shard_map/ppermute | solution.py:190
  106.3 8.4 %collective-permute-start.22 = (bf16[144,256]{1,0:T(8,128)(2,1)S(1)}, bf16[144,256]{1,0:T(8,128)(2,1)S(1)}, u32[]{:S(2)}, u32[]{:S(2)}) collective-permute-start(bf16[144,256]{1,0:T(8,128)(2,1)S(1)} %maximum_maximum_fusion), channel_id=1, source_target_pairs={{96,0},{128,32},{160,64},{192,96},{224,128},{97,1},{129,33},{161,6... | collective-permute-start | bytes 221192 | tf_op jit(solution)/shard_map/ppermute | solution.py:190
  107.6 9.9 %collective-permute-start.23 = (bf16[144,256]{1,0:T(8,128)(2,1)S(1)}, bf16[144,256]{1,0:T(8,128)(2,1)S(1)}, u32[]{:S(2)}, u32[]{:S(2)}) collective-permute-start(bf16[144,256]{1,0:T(8,128)(2,1)S(1)} %maximum_maximum_fusion), channel_id=1, source_target_pairs={{128,0},{160,32},{192,64},{224,96},{129,1},{161,33},{193,65},{225,... | collective-permute-start | bytes 221192 | tf_op jit(solution)/shard_map/ppermute | solution.py:190
  108.9 10.0 %collective-permute-start.24 = (bf16[144,256]{1,0:T(8,128)(2,1)S(1)}, bf16[144,256]{1,0:T(8,128)(2,1)S(1)}, u32[]{:S(2)}, u32[]{:S(2)}) collective-permute-start(bf16[144,256]{1,0:T(8,128)(2,1)S(1)} %maximum_maximum_fusion), channel_id=1, source_target_pairs={{160,0},{192,32},{224,64},{161,1},{193,33},{225,65},{162,2},{194,3... | collective-permute-start | bytes 221192 | tf_op jit(solution)/shard_map/ppermute | solution.py:190
  110.2 19.5 %copy-start.14 = (bf16[144,256]{1,0:T(8,128)(2,1)}, bf16[144,256]{1,0:T(8,128)(2,1)S(1)}, u32[]{:S(2)}) copy-start(bf16[144,256]{1,0:T(8,128)(2,1)S(1)} %collective-permute-done.20.refs_0_) | copy-start | bytes 221188
  110.2 12.8 %collective-permute-start.25 = (bf16[144,256]{1,0:T(8,128)(2,1)S(1)}, bf16[144,256]{1,0:T(8,128)(2,1)S(1)}, u32[]{:S(2)}, u32[]{:S(2)}) collective-permute-start(bf16[144,256]{1,0:T(8,128)(2,1)S(1)} %maximum_maximum_fusion), channel_id=1, source_target_pairs={{192,0},{224,32},{193,1},{225,33},{194,2},{226,34},{195,3},{227,35... | collective-permute-start | bytes 221192 | tf_op jit(solution)/shard_map/ppermute | solution.py:190
  111.5 18.1 %copy-start.15 = (bf16[144,256]{1,0:T(8,128)(2,1)}, bf16[144,256]{1,0:T(8,128)(2,1)S(1)}, u32[]{:S(2)}) copy-start(bf16[144,256]{1,0:T(8,128)(2,1)S(1)} %collective-permute-done.21.refs_1_) | copy-start | bytes 221188
  111.6 18.1 %collective-permute-start.26 = (bf16[144,256]{1,0:T(8,128)(2,1)S(1)}, bf16[144,256]{1,0:T(8,128)(2,1)S(1)}, u32[]{:S(2)}, u32[]{:S(2)}) collective-permute-start(bf16[144,256]{1,0:T(8,128)(2,1)S(1)} %maximum_maximum_fusion), channel_id=1, source_target_pairs={{224,0},{225,1},{226,2},{227,3},{228,4},{229,5},{230,6},{231,7},{2... | collective-permute-start | bytes 221192 | tf_op jit(solution)/shard_map/ppermute | solution.py:190
  113.1 16.6 %copy-start.12 = (bf16[128,128]{1,0:T(8,128)(2,1)}, bf16[128,128]{1,0:T(8,128)(2,1)S(1)}, u32[]{:S(2)}) copy-start(bf16[128,128]{1,0:T(8,128)(2,1)S(1)} %constant_dynamic-update-slice_fusion.refs_7_) | copy-start | bytes 98308
  114.7 15.0 %copy-start.16 = (bf16[144,256]{1,0:T(8,128)(2,1)}, bf16[144,256]{1,0:T(8,128)(2,1)S(1)}, u32[]{:S(2)}) copy-start(bf16[144,256]{1,0:T(8,128)(2,1)S(1)} %collective-permute-done.22.refs_2_) | copy-start | bytes 221188
  117.5 12.2 %copy-start.17 = (bf16[144,256]{1,0:T(8,128)(2,1)}, bf16[144,256]{1,0:T(8,128)(2,1)S(1)}, u32[]{:S(2)}) copy-start(bf16[144,256]{1,0:T(8,128)(2,1)S(1)} %collective-permute-done.23.refs_3_) | copy-start | bytes 221188
  141.0 4.7 %collective-permute-start.27 = (f32[144,4096]{1,0:T(8,128)S(1)}, f32[144,4096]{1,0:T(8,128)S(1)}, u32[]{:S(2)}, u32[]{:S(2)}) collective-permute-start(f32[144,4096]{1,0:T(8,128)S(1)} %broadcast_select_fusion), channel_id=1, source_target_pairs={{0,1},{1,0},{2,3},{3,2},{4,5},{5,4},{6,7},{7,6},{8,9},{9,8},{10,11... | collective-permute-start | bytes 7077896 | tf_op jit(solution)/shard_map/ppermute | solution.py:208
  146.3 57.0 %copy-start.1 = (bf16[1,32,128,256]{3,2,1,0:T(8,128)(2,1)S(1)}, bf16[1,32,128,256]{3,2,1,0:T(8,128)(2,1)}, u32[]{:S(2)}) copy-start(bf16[1,32,128,256]{3,2,1,0:T(8,128)(2,1)} %param.9) | copy-start | bytes 6291460
  171.0 6.5 %collective-permute-start.34 = (f32[16,256]{1,0:T(8,128)S(1)}, f32[16,256]{1,0:T(8,128)S(1)}, u32[]{:S(2)}, u32[]{:S(2)}) collective-permute-start(f32[16,256]{1,0:T(8,128)S(1)} %get-tuple-element.20), channel_id=1, source_target_pairs={{224,0},{225,1},{226,2},{227,3},{228,4},{229,5},{230,6},{231,7},{2... | collective-permute-start | bytes 49160 | tf_op jit(solution)/shard_map/ppermute | solution.py:216
  172.3 6.6 %collective-permute-start.33 = (f32[16,256]{1,0:T(8,128)S(1)}, f32[16,256]{1,0:T(8,128)S(1)}, u32[]{:S(2)}, u32[]{:S(2)}) collective-permute-start(f32[16,256]{1,0:T(8,128)S(1)} %get-tuple-element.21), channel_id=1, source_target_pairs={{192,0},{224,32},{193,1},{225,33},{194,2},{226,34},{195,3},{227,35... | collective-permute-start | bytes 49160 | tf_op jit(solution)/shard_map/ppermute | solution.py:216
  173.6 7.5 %collective-permute-start.32 = (f32[16,256]{1,0:T(8,128)S(1)}, f32[16,256]{1,0:T(8,128)S(1)}, u32[]{:S(2)}, u32[]{:S(2)}) collective-permute-start(f32[16,256]{1,0:T(8,128)S(1)} %get-tuple-element.22), channel_id=1, source_target_pairs={{160,0},{192,32},{224,64},{161,1},{193,33},{225,65},{162,2},{194,3... | collective-permute-start | bytes 49160 | tf_op jit(solution)/shard_map/ppermute | solution.py:216
  174.9 8.4 %collective-permute-start.31 = (f32[16,256]{1,0:T(8,128)S(1)}, f32[16,256]{1,0:T(8,128)S(1)}, u32[]{:S(2)}, u32[]{:S(2)}) collective-permute-start(f32[16,256]{1,0:T(8,128)S(1)} %get-tuple-element.23), channel_id=1, source_target_pairs={{128,0},{160,32},{192,64},{224,96},{129,1},{161,33},{193,65},{225,... | collective-permute-start | bytes 49160 | tf_op jit(solution)/shard_map/ppermute | solution.py:216
  176.2 7.1 %collective-permute-start.30 = (f32[16,256]{1,0:T(8,128)S(1)}, f32[16,256]{1,0:T(8,128)S(1)}, u32[]{:S(2)}, u32[]{:S(2)}) collective-permute-start(f32[16,256]{1,0:T(8,128)S(1)} %get-tuple-element.24), channel_id=1, source_target_pairs={{96,0},{128,32},{160,64},{192,96},{224,128},{97,1},{129,33},{161,6... | collective-permute-start | bytes 49160 | tf_op jit(solution)/shard_map/ppermute | solution.py:216
  177.5 5.8 %collective-permute-start.29 = (f32[16,256]{1,0:T(8,128)S(1)}, f32[16,256]{1,0:T(8,128)S(1)}, u32[]{:S(2)}, u32[]{:S(2)}) collective-permute-start(f32[16,256]{1,0:T(8,128)S(1)} %get-tuple-element.25), channel_id=1, source_target_pairs={{64,0},{96,32},{128,64},{160,96},{192,128},{224,160},{65,1},{97,33... | collective-permute-start | bytes 49160 | tf_op jit(solution)/shard_map/ppermute | solution.py:216
  178.8 4.8 %collective-permute-start.28 = (f32[16,256]{1,0:T(8,128)S(1)}, f32[16,256]{1,0:T(8,128)S(1)}, u32[]{:S(2)}, u32[]{:S(2)}) collective-permute-start(f32[16,256]{1,0:T(8,128)S(1)} %get-tuple-element.26), channel_id=1, source_target_pairs={{32,0},{64,32},{96,64},{128,96},{160,128},{192,160},{224,192},{33,... | collective-permute-start | bytes 49160 | tf_op jit(solution)/shard_map/ppermute | solution.py:216
  195.9 6.2 %collective-permute-start.35 = (f32[32,4096]{1,0:T(8,128)S(1)}, f32[32,4096]{1,0:T(8,128)S(1)}, u32[]{:S(2)}, u32[]{:S(2)}) collective-permute-start(f32[32,4096]{1,0:T(8,128)S(1)} %bitcast.104), channel_id=1, source_target_pairs={{0,1},{1,0},{2,3},{3,2},{4,5},{5,4},{6,7},{7,6},{8,9},{9,8},{10,11... | collective-permute-start | bytes 1572872 | tf_op jit(solution)/shard_map/ppermute | solution.py:223
  (13 other events, 51.3 us)

commit v2 on v1

v2 whole, which is shorter than its diff:
```python
import functools

import jax
import jax.numpy as jnp
from jax import lax
from jax.experimental import pallas as pl
from jax.experimental.pallas import tpu as pltpu
from jax.sharding import Mesh
from jax.sharding import PartitionSpec as P

norm_eps = 1e-05
stat_eps = 1e-06
coef_reroute = 64.0
coef_retain = 1.0
loss_scale = 2048.0

SEC = "section"
CHIPS = ("y", "x")
DP = ("y", "x", "core")
f32 = jnp.float32
bf16 = jnp.bfloat16


def nt(left, right):
    return lax.dot_general(left, right, (((1,), (1,)), ((), ())), preferred_element_type=f32)


def tn(left, right):
    return lax.dot_general(left, right, (((0,), (0,)), ((), ())), preferred_element_type=f32)


def nn(left, right):
    return lax.dot_general(left, right, (((1,), (0,)), ((), ())), preferred_element_type=f32)


def split2(value):
    hi = value.astype(bf16)
    lo = (value - hi.astype(f32)).astype(bf16)
    return hi, lo


def ring_gather(block, axis):
    n = lax.axis_size(axis)
    up = [(i, (i + 1) % n) for i in range(n)]
    down = [(i, (i - 1) % n) for i in range(n)]
    found = [None] * n
    found[0] = block
    fwd = bwd = block
    for k in range(1, n // 2 + 1):
        fwd = lax.ppermute(fwd, axis, up)
        found[k] = fwd
        if k < n - n // 2:
            bwd = lax.ppermute(bwd, axis, down)
            found[n - k] = bwd
    return found

def vmem():
    return pl.BlockSpec(memory_space=pltpu.VMEM)


def smem():
    return pl.BlockSpec(memory_space=pltpu.SMEM)


def hbm():
    return pl.BlockSpec(memory_space=pl.ANY)


def params(mib=48):
    return pltpu.CompilerParams(vmem_limit_bytes=mib << 20)


INFO = 8


def order_kernel(position_ref, info_ref, held_ref, out_ref, tile_sem, info_sem):
    tiles, tokens = held_ref.shape[0], held_ref.shape[1]
    copies = []
    for i in range(tiles):
        copies.append(
            pltpu.make_async_copy(held_ref.at[position_ref[i]], out_ref.at[i, pl.ds(0, tokens)], tile_sem.at[i])
        )
        copies.append(pltpu.make_async_copy(info_ref, out_ref.at[i, pl.ds(tokens, INFO)], info_sem.at[i]))
    for copy in copies:
        copy.start()
    for copy in copies:
        copy.wait()


def order(position, info, held):
    tiles, tokens, width = held.shape
    return pl.pallas_call(
        order_kernel,
        out_shape=jax.ShapeDtypeStruct((tiles, tokens + INFO, width), held.dtype),
        in_specs=[smem(), vmem(), hbm()],
        out_specs=hbm(),
        scratch_shapes=[pltpu.SemaphoreType.DMA((tiles,)), pltpu.SemaphoreType.DMA((tiles,))],
        name="order",
    )(position, info, held)


def fold(value):
    lanes = 128
    total = value[:, :lanes]
    for i in range(1, value.shape[1] // lanes):
        total = total + value[:, i * lanes : (i + 1) * lanes]
    return total


def own_kernel(meta_ref, refs_ref, output_ref, mine_ref, other_ref, own_ref, proj_ref):
    core, flag, valid = meta_ref[0], meta_ref[1], meta_ref[2]
    tiles, padded, chunk = refs_ref.shape
    tokens = padded - INFO
    half = mine_ref.shape[1]
    per_half = half // chunk
    rows = 32

    info = refs_ref[0, tokens:, :128].astype(f32)
    for i in range(1, tiles):
        info = info + refs_ref[i, tokens:, :128].astype(f32)
    weight_harm = (loss_scale * coef_reroute) / info[0:1, 0:1]
    weight_keep = (loss_scale * coef_retain) / info[1:2, 0:1]

    def stats(terms, count):
        found = []
        for low in range(0, tokens, rows):

            def step(i, acc, low=low):
                out = output_ref[low : low + rows, pl.ds(pl.multiple_of(i * chunk, chunk), chunk)]
                ref = refs_ref[i, low : low + rows, :].astype(f32)
                return tuple(a + fold(v) for a, v in zip(acc, terms(out, ref)))

            zero = jnp.zeros((rows, 128), f32)
            acc = lax.fori_loop(0, tiles, step, (zero,) * count, unroll=4)
            found.append([jnp.sum(a, axis=1, keepdims=True) for a in acc])
        return [jnp.concatenate([f[i] for f in found], axis=0) for i in range(count)]

    is_valid = lax.broadcasted_iota(jnp.int32, (tokens, 1), 0) < valid

    def finish(make):
        total = jnp.zeros(proj_ref.shape[1:], f32)
        for base, weights in ((core, mine_ref), (1 - core, other_ref)):

            def step(i, acc, base=base, weights=weights):
                j = base * per_half + i
                columns = pl.ds(pl.multiple_of(j * chunk, chunk), chunk)
                own = make(output_ref[:, columns], refs_ref[j, :tokens, :].astype(f32)).astype(bf16)
                own_ref[:, columns] = own
                return acc + nt(weights[:, pl.ds(pl.multiple_of(i * chunk, chunk), chunk)], own)

            total = lax.fori_loop(0, per_half, step, total, unroll=2)
        total = total.astype(bf16)
        for i in range(proj_ref.shape[0]):
            proj_ref[i] = total

    @pl.when(flag == 1)
    def _():
        out_sq, ref_sq, cross = stats(lambda o, r: (o * o, r * r, o * r), 3)
        out_norm = jnp.sqrt(out_sq + stat_eps)
        ref_norm = jnp.sqrt(ref_sq + stat_eps)
        cosine = cross / (out_norm * ref_norm)
        weight = jnp.where(is_valid & (cosine > 0), weight_harm, 0.0)
        coef_ref = weight / (out_norm * ref_norm)
        coef_out = weight * cosine / (out_sq + stat_eps)
        finish(lambda o, r: coef_ref * r - coef_out * o)

    @pl.when(flag != 1)
    def _():
        (diff_sq,) = stats(lambda o, r: ((o - r) * (o - r),), 1)
        coef = jnp.where(is_valid, weight_keep, 0.0) / jnp.sqrt(diff_sq + stat_eps)
        finish(lambda o, r: coef * (o - r))


def own_gradient(meta, refs, output, mine, other, layers):
    tokens = output.shape[0]
    return pl.pallas_call(
        own_kernel,
        out_shape=(
            jax.ShapeDtypeStruct(output.shape, bf16),
            jax.ShapeDtypeStruct((layers, mine.shape[0], tokens), bf16),
        ),
        in_specs=[smem()] + [vmem()] * 4,
        out_specs=(vmem(), vmem()),
        compiler_params=params(),
        name="own",
    )(meta, refs, output, mine, other)


def solve_kernel(width, rank, me_ref, own_ref, side_ref, low_ref, lrt_ref, coef_ref, k_ref, acc):
    me = me_ref[0]
    layers, rows, _ = own_ref.shape
    acc[...] = jnp.zeros_like(acc)
    for j in range(layers):

        @pl.when(me + j < layers)
        def _(j=j):
            low = rank * (layers - 1 - j)
            acc[0 : rank * (j + 1), :] += own_ref[me + j, low:rows, :].astype(f32)

    def inverse_rms(t):
        return side_ref[t, rows + 3 * rank : rows + 3 * rank + 1, :].astype(f32) + side_ref[
            t, rows + 3 * rank + 1 : rows + 3 * rank + 2, :
        ].astype(f32)

    def mean_of(grad, t):
        lrt = side_ref[t, rows : rows + rank, :].astype(f32)
        return jnp.sum(grad.astype(f32) * lrt, axis=0, keepdims=True) * (1.0 / width)

    for j in range(layers - 1, 0, -1):

        @pl.when(me + j < layers)
        def _(j=j):
            t = me + j
            low = rank * (layers - 1 - j)
            grad = acc[rank * j : rank * (j + 1), :].astype(bf16)
            mean = mean_of(grad, t)
            w_hi = side_ref[t, rows + rank : rows + 2 * rank, :]
            w_lo = side_ref[t, rows + 2 * rank : rows + 3 * rank, :]
            term = tn(w_hi, grad) + tn(w_lo, grad)
            scaled_up = side_ref[t, low : rows - rank, :].astype(f32)
            acc[0 : rank * j, :] += inverse_rms(t) * (term[low : rows - rank, :] - mean * scaled_up)

    grad = acc[0:rank, :].astype(bf16)
    low_ref[...] = grad
    irms = inverse_rms(me)
    mean = mean_of(grad, me)
    lrt = side_ref[:, rows : rows + rank, :].reshape(layers * rank, -1)
    layer = lax.broadcasted_iota(jnp.int32, lrt.shape, 0) // rank
    lrt_f = lrt.astype(f32)
    lrt_ref[...] = jnp.where(layer <= me, lrt_f, 0.0).astype(bf16)
    below = jnp.where(layer < me, lrt_f, 0.0)
    coef_ref[...] = (below * (-irms * irms * mean)).astype(bf16)
    k_hi, k_lo = split2(nt(below.astype(bf16), (grad.astype(f32) * irms).astype(bf16)))
    k_ref[0] = k_hi
    k_ref[1] = k_lo


def solve(width, rank, me, own, side):
    layers, rows, tokens = own.shape
    return pl.pallas_call(
        functools.partial(solve_kernel, width, rank),
        out_shape=(
            jax.ShapeDtypeStruct((rank, tokens), bf16),
            jax.ShapeDtypeStruct((rows, tokens), bf16),
            jax.ShapeDtypeStruct((rows, tokens), bf16),
            jax.ShapeDtypeStruct((2, rows, rank), bf16),
        ),
        in_specs=[smem(), vmem(), vmem()],
        out_specs=(vmem(),) * 4,
        scratch_shapes=[pltpu.VMEM((rows, tokens), f32)],
        compiler_params=params(),
        name="solve",
    )(me, own, side)


def part_kernel(start_ref, low_ref, lrt_ref, coef_ref, k_ref, own_ref, stream_ref, normed_ref, dg_ref, out_ref):
    start = start_ref[0]
    chunks, _, chunk = out_ref.shape
    rows = lrt_ref.shape[0]

    def step(i, carry):
        columns = pl.ds(pl.multiple_of(start + i * chunk, chunk), chunk)
        dg_hi, dg_lo = dg_ref[0, :, columns], dg_ref[1, :, columns]
        out_ref[i, :rows, :] = (
            nn(lrt_ref[...], own_ref[:, columns])
            + nn(coef_ref[...], stream_ref[:, columns])
            + nn(k_ref[0], dg_hi)
            + nn(k_ref[0], dg_lo)
            + nn(k_ref[1], dg_hi)
        )
        out_ref[i, rows:, :] = nn(low_ref[...], normed_ref[:, columns])
        return carry

    lax.fori_loop(0, chunks, step, 0)


def part(start, chunks, chunk, low, lrt, coef, k, own, stream, normed, dg):
    return pl.pallas_call(
        part_kernel,
        out_shape=jax.ShapeDtypeStruct((chunks, lrt.shape[0] + low.shape[0], chunk), f32),
        in_specs=[smem()] + [vmem()] * 8,
        out_specs=vmem(),
        compiler_params=params(),
        name="part",
    )(start, low, lrt, coef, k, own, stream, normed, dg)


def shards(
    layer_input_states,
    frozen_reference_states,
    adapter_down_weight,
    adapter_up_weight,
    layer_norm_gain,
    tile_reference_position,
    tile_harmful_flag,
    tile_valid_count,
):
    tokens, width = layer_input_states.shape[2:]
    rank = adapter_up_weight.shape[1]
    layers = lax.axis_size(SEC)
    me = lax.axis_index(SEC)
    core = lax.axis_index("core")
    cores = lax.axis_size("core")
    chips = lax.axis_size("y") * lax.axis_size("x")
    half = width // cores
    chunk = half // chips
    swap = [(i, (i + 1) % cores) for i in range(cores)]

    flag, valid = tile_harmful_flag[0], tile_valid_count[0]
    row = lax.broadcasted_iota(jnp.int32, (INFO, chunk), 0)
    info = jnp.where((row == 0) & (flag == 1), valid, jnp.where((row == 1) & (flag != 1), valid, 0))
    ordered = order(tile_reference_position, info.astype(bf16), frozen_reference_states[0])
    refs = lax.all_to_all(ordered, DP, split_axis=0, concat_axis=0, tiled=True)
    ordered, stream_bf, down, up, gains = lax.optimization_barrier(
        (ordered, layer_input_states[0, 0], adapter_down_weight[0], adapter_up_weight[0], layer_norm_gain[0])
    )

    up_half = lax.dynamic_slice_in_dim(up, core * half, half, axis=1)
    up_mine = jnp.concatenate(ring_gather(up_half, SEC)[::-1], axis=0)
    up_other = lax.ppermute(up_mine, "core", swap)

    stream = stream_bf.astype(f32)
    inverse_rms = lax.rsqrt(jnp.mean(stream * stream, axis=-1, keepdims=True) + norm_eps)
    normed = (stream * inverse_rms * gains).astype(bf16)
    lrt = nt(down, normed).astype(bf16)
    output = stream + tn(lrt, up)
    irms_row = inverse_rms.reshape(1, tokens)
    dg = jnp.stack(split2(down.astype(f32) * gains))

    def halves(value):
        return (
            lax.dynamic_slice_in_dim(value, core * half, half, axis=1),
            lax.dynamic_slice_in_dim(value, (1 - core) * half, half, axis=1),
        )

    stream_mine, stream_other = halves(stream_bf)
    hi_mine, hi_other = halves(dg[0])
    lo_mine, lo_other = halves(dg[1])
    scaled_up = (nt(up_mine, stream_mine) + nt(up_other, stream_other)) * irms_row
    w = nt(hi_mine, up_mine) + nt(lo_mine, up_mine) + nt(hi_other, up_other) + nt(lo_other, up_other)
    w_hi, w_lo = split2(w)
    irms_hi, irms_lo = split2(irms_row)
    side = jnp.concatenate(
        [scaled_up.astype(bf16), lrt, w_hi, w_lo, irms_hi, irms_lo, jnp.zeros((14, tokens), bf16)], axis=0
    )
    sides = lax.all_to_all(jnp.broadcast_to(side, (layers,) + side.shape), SEC, 0, 0, tiled=True)

    meta = jnp.stack([core, flag, valid]).astype(jnp.int32)
    own, own_up = own_gradient(meta, refs, output, up_mine, up_other, layers)
    own_up = lax.all_to_all(own_up, SEC, 0, 0, tiled=True)
    low, lrt_all, coef, k = solve(width, rank, me[None], own_up, sides)

    given = part(((1 - core) * half)[None], chips, chunk, low, lrt_all, coef, k, own, stream_bf, normed, dg)
    received = lax.ppermute(given, "core", swap)
    kept = part((core * half)[None], chips, chunk, low, lrt_all, coef, k, own, stream_bf, normed, dg)
    blocks = lax.all_to_all((kept + received).astype(bf16), CHIPS, 0, 0, tiled=True)
    summed = jnp.sum(blocks.astype(f32), axis=0)

    by_layer = lax.all_to_all(summed[: layers * rank].reshape(layers, rank, chunk), SEC, 0, 0, tiled=True)
    final = jnp.concatenate([summed[layers * rank :], jnp.sum(by_layer, axis=0)], axis=0)

    wide = lax.all_to_all(jnp.broadcast_to(final, (chips,) + final.shape), CHIPS, 0, 0, tiled=True)
    mine = wide.transpose(1, 0, 2).reshape(2 * rank, half)
    other = lax.ppermute(mine, "core", swap)
    full = jnp.concatenate([jnp.where(core == 0, mine, other), jnp.where(core == 0, other, mine)], axis=1)
    return (full[None, :rank], full[None, rank:])


def solution(mesh):
    layers, dp = mesh.devices.shape
    cores = 2
    side = round((dp // cores) ** 0.5)
    mesh4 = Mesh(mesh.devices.reshape(layers, side, side, cores), (SEC,) + DP)
    return jax.shard_map(
        shards,
        mesh=mesh4,
        in_specs=(
            P(SEC, DP, None, None),
            P(SEC, None, None, DP),
            P(SEC, None, None),
            P(SEC, None, None),
            P(SEC, None),
            P(),
            P(DP),
            P(DP),
        ),
        out_specs=(P(SEC, None, None), P(SEC, None, None)),
        check_vma=False,
    )
```

time: 204 us -> 232 us (1.14)
  Pallas kernels: 2.8 us -> 89.7 us
  waiting for transfers between devices: 62.5 us -> 31.2 us
  starting transfers between devices: 63.9 us -> 44.8 us
  local copies, waits for them, and re-layouts: 8.86 us -> 5.49 us
    pallas_call x1 -> x5, Pallas kernels: 2.8 us -> 89.7 us  [the longest x1 65.9 us: order(): pl.pallas_call(order_kernel, out_shape=jax.ShapeDtypeStruct((tiles, token...]
    ppermute x20 -> x1, waiting for transfers between devices: 43.1 us -> 0.01 us  [shards(): received = lax.ppermute(given, 'core', swap)]
    ppermute x20 -> x1, starting transfers between devices: 25.4 us -> 2.93 us  [shards(): received = lax.ppermute(given, 'core', swap)]
    all_to_all x1 -> x4, waiting for transfers between devices: 0.01 us -> 17.2 us  [the longest x1 8.82 us: shards(): own_up = lax.all_to_all(own_up, SEC, 0, 0, tiled=True)]
    all_to_all x1 -> x4, starting transfers between devices: 7.56 us -> 21.4 us  [the longest x1 8.78 us: shards(): refs = lax.all_to_all(ordered, DP, split_axis=0, concat_axis=0, tiled=True)]
    ppermute x1, starting transfers between devices: 8.96 us -> 4.03 us  [shards(): up_other = lax.ppermute(up_mine, 'core', swap)]
    ppermute x8 -> x4, waiting for transfers between devices: 15 us -> 10.4 us  [ring_gather(): fwd = lax.ppermute(fwd, axis, up)]
    dot_general x7 -> x1, matrix products: 7.09 us -> 3.62 us  [tn(): lax.dot_general(left, right, (((0,), (0,)), ((), ())), preferred_element_...]
  transfers between devices with their start and end apart: 37 -> 14, of which waited for: 19 -> 8; matrix products, arithmetic and copies ran while one was open for 5% -> 7% of each run, Pallas kernels for 0% -> 7%
where the time goes in v2:
time: 232 us; the launch traced here: 231 us
  Pallas kernels  89.7 us (39%)
  starting transfers between devices  44.8 us (19%)
  blocking collectives  36.9 us (16%)
  waiting for transfers between devices  31.2 us (13%)
  matrix products  12.2 us (5%)
  other arithmetic  8.52 us (4%)
  local copies, waits for them, and re-layouts  5.49 us (2%)
    pallas_call x1, Pallas kernels, order(): pl.pallas_call(order_kernel, out_shape=jax.ShapeDtypeStruct((tiles, token...  65.9 us
    all_to_all x1, blocking collectives, shards(): lax.all_to_all((kept + received).astype(bf16), CHIPS, 0, 0, tiled=True)  24.9 us
    pallas_call x2, Pallas kernels, part(): pl.pallas_call(part_kernel, out_shape=jax.ShapeDtypeStruct((chunks, lrt.s...  13.4 us
    ppermute x3, starting transfers between devices, ring_gather(): bwd = lax.ppermute(bwd, axis, down)  12.6 us
    all_to_all x1, blocking collectives, shards(): lax.all_to_all(jnp.broadcast_to(final, (chips,) + final.shape), CHIPS, 0,...  12 us
    ppermute x4, waiting for transfers between devices, ring_gather(): fwd = lax.ppermute(fwd, axis, up)  10.4 us
    all_to_all x1, waiting for transfers between devices, shards(): own_up = lax.all_to_all(own_up, SEC, 0, 0, tiled=True)  8.82 us
    all_to_all x1, starting transfers between devices, shards(): refs = lax.all_to_all(ordered, DP, split_axis=0, concat_axis=0, tiled=True)  8.78 us
  transfers between devices with their start and end apart: 14, of which 8 were waited for; matrix products, arithmetic and copies ran while one was open for 7% of the time, Pallas kernels for 7%

profile of v2, /device:TPU:1, one launch (start us, length us, event | category | flops | bytes accessed | tf_op | source)
XLA Modules:
  0.0 231.0 jit_solution(906791528964982280)
XLA Ops:
  2.0 0.7 select_convert_fusion.info_ref
  2.6 65.9 %order.1 = bf16[32,136,256]{2,1,0:T(8,128)(2,1)} custom-call(s32[32]{0:T(128)} %position_ref.1, bf16[8,256]{1,0:T(8,128)(2,1)} %select_convert_fusion.info_ref, bf16[32,128,256]{2,1,0:T(8,128)(2,1)} %bitcast.53), custom_call_target="tpu_custom_call" | custom-call | tf_op jit(solution)/shard_map/order/pallas_call | solution.py:92
  68.6 8.8 %all-to-all-start = ((bf16[32,136,256]{2,1,0:T(8,128)(2,1)}), bf16[32,136,256]{2,1,0:T(8,128)(2,1)}, u32[]{:S(2)}, u32[]{:S(2)}) async-start(bf16[32,136,256]{2,1,0:T(8,128)(2,1)} %order.1), calls=%async_computation | async-start | bytes 4456448 | tf_op jit(solution)/shard_map/all_to_all | solution.py:313
  77.4 5.7 %collective-permute-start = (bf16[16,4096]{1,0:T(8,128)(2,1)S(1)}, bf16[16,4096]{1,0:T(8,128)(2,1)S(1)}, u32[]{:S(2)}, u32[]{:S(2)}) collective-permute-start(bf16[16,4096]{1,0:T(8,128)(2,1)S(1)} %constant_dynamic-slice_fusion), channel_id=1, source_target_pairs={{0,224},{32,0},{64,32},{96,64},{128,96},{160,128},{192,160},{224,1... | collective-permute-start | bytes 393224 | tf_op jit(solution)/shard_map/ppermute | solution.py:53
  83.1 0.5 fusion
  83.6 2.0 fusion.2.normed_ref
  85.6 0.1 collective-permute-done
  85.7 3.5 %collective-permute-start.1 = (bf16[16,4096]{1,0:T(8,128)(2,1)S(1)}, bf16[16,4096]{1,0:T(8,128)(2,1)S(1)}, u32[]{:S(2)}, u32[]{:S(2)}) collective-permute-start(bf16[16,4096]{1,0:T(8,128)(2,1)S(1)} %collective-permute-done), channel_id=1, source_target_pairs={{0,224},{32,0},{64,32},{96,64},{128,96},{160,128},{192,160},{224,1... | collective-permute-start | bytes 393224 | tf_op jit(solution)/shard_map/ppermute | solution.py:53
  89.2 1.9 collective-permute-done.1
  91.1 3.5 %collective-permute-start.2 = (bf16[16,4096]{1,0:T(8,128)(2,1)S(1)}, bf16[16,4096]{1,0:T(8,128)(2,1)S(1)}, u32[]{:S(2)}, u32[]{:S(2)}) collective-permute-start(bf16[16,4096]{1,0:T(8,128)(2,1)S(1)} %collective-permute-done.1), channel_id=1, source_target_pairs={{0,224},{32,0},{64,32},{96,64},{128,96},{160,128},{192,160},{224,1... | collective-permute-start | bytes 393224 | tf_op jit(solution)/shard_map/ppermute | solution.py:53
  94.6 5.4 %collective-permute-done.5 = bf16[16,4096]{1,0:T(8,128)(2,1)S(1)} collective-permute-done((bf16[16,4096]{1,0:T(8,128)(2,1)S(1)}, bf16[16,4096]{1,0:T(8,128)(2,1)S(1)}, u32[]{:S(2)}, u32[]{:S(2)}) %collective-permute-start.5) | collective-permute-done | bytes 131104 | tf_op jit(solution)/shard_map/ppermute | solution.py:50
  100.1 5.0 %collective-permute-done.6 = bf16[16,4096]{1,0:T(8,128)(2,1)S(1)} collective-permute-done((bf16[16,4096]{1,0:T(8,128)(2,1)S(1)}, bf16[16,4096]{1,0:T(8,128)(2,1)S(1)}, u32[]{:S(2)}, u32[]{:S(2)}) %collective-permute-start.6) | collective-permute-done | bytes 131104 | tf_op jit(solution)/shard_map/ppermute | solution.py:50
  105.2 4.0 %collective-permute-start.7 = (bf16[128,4096]{1,0:T(8,128)(2,1)S(1)}, bf16[128,4096]{1,0:T(8,128)(2,1)}, u32[]{:S(2)}, u32[]{:S(2)}) collective-permute-start(bf16[128,4096]{1,0:T(8,128)(2,1)S(1)} %constant_dynamic-update-slice_fusion.mine_ref), channel_id=1, source_target_pairs={{0,1},{1,0},{2,3},{3,2},{4,5},{5,4},{6,7},{7,6},{8,9},{9,8},{10,11... | collective-permute-start | bytes 3145736 | tf_op jit(solution)/shard_map/ppermute | solution.py:320
  109.2 0.9 fusion.21
  110.1 2.4 %convolution_convert_fusion = bf16[16,128]{1,0:T(8,128)(2,1)S(1)} fusion(bf16[16,8192]{1,0:T(8,128)(2,1)} %bitcast.57, bf16[128,8192]{1,0:T(8,128)(2,1)} %fusion.2.normed_ref), kind=kOutput, calls=%fused_computation.14 | convolution fusion | flops 33556480 | bytes 2363392 | tf_op jit(solution)/shard_map/dot_general | solution.py:25
  112.5 0.4 fusion.18
  112.9 1.6 fusion.14
  114.5 1.6 fusion.16
  116.2 0.4 subtract_convert_fusion.1
  116.5 1.7 fusion.7
  118.2 0.5 fusion.4
  118.7 0.2 concatenate.13
  118.9 0.8 broadcast_in_dim.42
  119.7 3.5 %all-to-all-start.2 = ((bf16[8,192,128]{2,1,0:T(8,128)(2,1)}), bf16[8,192,128]{2,1,0:T(8,128)(2,1)S(1)}, u32[]{:S(2)}, u32[]{:S(2)}) async-start(bf16[8,192,128]{2,1,0:T(8,128)(2,1)} %broadcast_in_dim.42), calls=%async_computation.2 | async-start | bytes 786432 | tf_op jit(solution)/shard_map/all_to_all | solution.py:346
  123.2 0.1 pad_add_fusion.meta_ref
  123.3 3.6 %convolution_add_fusion.output_ref = f32[128,8192]{1,0:T(8,128)} fusion(bf16[16,128]{1,0:T(8,128)(2,1)S(1)} %convolution_convert_fusion, bf16[16,8192]{1,0:T(8,128)(2,1)} %bitcast.54, bf16[128,8192]{1,0:T(8,128)(2,1)S(1)} %bitcast.46), kind=kOutput, calls=%fused_computation | convolution fusion | flops 35651584 | bytes 6557696 | tf_op jit(solution)/shard_map/dot_general | solution.py:29
  126.9 8.6 %own.1 = (bf16[128,8192]{1,0:T(8,128)(2,1)S(1)}, bf16[8,128,128]{2,1,0:T(8,128)(2,1)S(1)}) custom-call(s32[3]{0:T(128)S(1)} %pad_add_fusion.meta_ref, bf16[32,136,256]{2,1,0:T(8,128)(2,1)} %all-to-all-done.refs_ref, f32[128,8192]{1,0:T(8,128)} %convolution_add_fusion.output_ref, bf16[128,4096]{1,0:T(8,128)(2,1)S(1)} %constant_dynamic-update-slice_fusion.mine_ref, ...), custom_call_target="tpu_custom_call" | custom-call | tf_op jit(solution)/shard_map/own/pallas_call | solution.py:176
  135.5 1.3 copy-done.1
  136.8 0.7 copy-done.3
  137.5 0.8 all-to-all-done.2.side_ref
  138.3 5.8 %all-to-all-start.1 = ((bf16[8,128,128]{2,1,0:T(8,128)(2,1)}), bf16[8,128,128]{2,1,0:T(8,128)(2,1)S(1)}, u32[]{:S(2)}, u32[]{:S(2)}) async-start(bf16[8,128,128]{2,1,0:T(8,128)(2,1)} %copy-done.3), calls=%async_computation.1 | async-start | bytes 524288 | tf_op jit(solution)/shard_map/all_to_all | solution.py:350
  144.1 1.1 pad_maximum_fusion.1.dg_ref
  145.2 8.8 %all-to-all-done.1.own_ref = bf16[8,128,128]{2,1,0:T(8,128)(2,1)S(1)} async-done(((bf16[8,128,128]{2,1,0:T(8,128)(2,1)}), bf16[8,128,128]{2,1,0:T(8,128)(2,1)S(1)}, u32[]{:S(2)}, u32[]{:S(2)}) %all-to-all-start.1) | async-done | bytes 262176 | tf_op jit(solution)/shard_map/all_to_all | solution.py:350
  154.0 1.7 solve.1
  155.7 1.6 copy-done.2
  157.3 6.7 %part.3 = f32[16,144,256]{2,1,0:T(8,128)} custom-call(s32[1]{0:T(128)} %bitcast.14.start_ref, bf16[16,128]{1,0:T(8,128)(2,1)S(1)} %get-tuple-element.17.low_ref, bf16[128,128]{1,0:T(8,128)(2,1)S(1)} %get-tuple-element.18.lrt_ref, bf16[128,128]{1,0:T(8,128)(2,1)S(1)} %get-tuple-element.19.coef_ref, bf16[2,128,16]{2,1,0:T(8,128)(2,1)S(1)} %get-tuple-element.20.k_ref, ...), custom_call_target="tpu_custom_call" | custom-call | tf_op jit(solution)/shard_map/part/pallas_call | solution.py:278
  164.0 2.9 %collective-permute-start.8 = (f32[16,144,256]{2,1,0:T(8,128)}, f32[16,144,256]{2,1,0:T(8,128)S(1)}, u32[]{:S(2)}, u32[]{:S(2)}) collective-permute-start(f32[16,144,256]{2,1,0:T(8,128)} %part.3), channel_id=1, source_target_pairs={{0,1},{1,0},{2,3},{3,2},{4,5},{5,4},{6,7},{7,6},{8,9},{9,8},{10,11... | collective-permute-start | bytes 7077896 | tf_op jit(solution)/shard_map/ppermute | solution.py:354
  166.9 6.7 %part.2 = f32[16,144,256]{2,1,0:T(8,128)} custom-call(s32[1]{0:T(128)} %bitcast.start_ref, bf16[16,128]{1,0:T(8,128)(2,1)S(1)} %get-tuple-element.17.low_ref, bf16[128,128]{1,0:T(8,128)(2,1)S(1)} %get-tuple-element.18.lrt_ref, bf16[128,128]{1,0:T(8,128)(2,1)S(1)} %get-tuple-element.19.coef_ref, bf16[2,128,16]{2,1,0:T(8,128)(2,1)S(1)} %get-tuple-element.20.k_ref, ...), custom_call_target="tpu_custom_call" | custom-call | tf_op jit(solution)/shard_map/part/pallas_call | solution.py:278
  173.7 2.0 add_convert_fusion
  175.7 24.9 %all_to_all.30 = bf16[16,144,256]{2,1,0:T(8,128)(2,1)S(1)} all-to-all(bf16[16,144,256]{2,1,0:T(8,128)(2,1)S(1)} %add_convert_fusion), channel_id=1, replica_groups=mesh['section'=8,'y'=4,'x'=4,'core'=2] {'y','x'}, dimensions={0} | all-to-all | bytes 2359296 | tf_op jit(solution)/shard_map/all_to_all | solution.py:356
  200.6 0.2 convert_reduce_fusion
  200.8 0.7 slice.17
  201.5 3.4 %all-to-all-start.4 = ((f32[8,16,256]{2,1,0:T(8,128)}), f32[8,16,256]{2,1,0:T(8,128)S(1)}, u32[]{:S(2)}, u32[]{:S(2)}) async-start(f32[8,16,256]{2,1,0:T(8,128)} %bitcast.15), calls=%async_computation.4 | async-start | bytes 262144 | tf_op jit(solution)/shard_map/all_to_all | solution.py:359
  204.9 7.7 %all-to-all-done.4 = f32[8,16,256]{2,1,0:T(8,128)S(1)} async-done(((f32[8,16,256]{2,1,0:T(8,128)}), f32[8,16,256]{2,1,0:T(8,128)S(1)}, u32[]{:S(2)}, u32[]{:S(2)}) %all-to-all-start.4) | async-done | bytes 131104 | tf_op jit(solution)/shard_map/all_to_all | solution.py:359
  212.6 12.0 %all_to_all.31 = f32[16,32,256]{2,1,0:T(8,128)S(1)} all-to-all(f32[16,32,256]{2,1,0:T(8,128)S(1)} %broadcast_in_dim.44), channel_id=1, replica_groups=mesh['section'=8,'y'=4,'x'=4,'core'=2] {'y','x'}, dimensions={0} | all-to-all | bytes 1048576 | tf_op jit(solution)/shard_map/all_to_all | solution.py:362
  224.6 3.8 %collective-permute-start.9 = (f32[32,4096]{1,0:T(8,128)S(1)}, f32[32,4096]{1,0:T(8,128)S(1)}, u32[]{:S(2)}, u32[]{:S(2)}) collective-permute-start(f32[32,4096]{1,0:T(8,128)S(1)} %bitcast.50), channel_id=1, source_target_pairs={{0,1},{1,0},{2,3},{3,2},{4,5},{5,4},{6,7},{7,6},{8,9},{9,8},{10,11... | collective-permute-start | bytes 1572872 | tf_op jit(solution)/shard_map/ppermute | solution.py:364
  228.4 1.5 collective-permute-done.9
  230.0 1.0 fusion.12
  (45 shorter events, 0.4 us)
Async XLA Ops:
  68.5 8.8 %copy-start.5 = (bf16[1,16,8192]{2,1,0:T(8,128)(2,1)S(1)}, bf16[1,16,8192]{2,1,0:T(8,128)(2,1)}, u32[]{:S(2)}) copy-start(bf16[1,16,8192]{2,1,0:T(8,128)(2,1)} %param.11) | copy-start | bytes 786436
  68.6 14.5 %copy-start = (bf16[1,1,128,8192]{3,2,1,0:T(8,128)(2,1)S(1)}, bf16[1,1,128,8192]{3,2,1,0:T(8,128)(2,1)}, u32[]{:S(2)}) copy-start(bf16[1,1,128,8192]{3,2,1,0:T(8,128)(2,1)} %param.8) | copy-start | bytes 6291460
  68.6 50.3 %all-to-all-start = ((bf16[32,136,256]{2,1,0:T(8,128)(2,1)}), bf16[32,136,256]{2,1,0:T(8,128)(2,1)}, u32[]{:S(2)}, u32[]{:S(2)}) async-start(bf16[32,136,256]{2,1,0:T(8,128)(2,1)} %order.1), calls=%async_computation | async-start | bytes 4456448 | tf_op jit(solution)/shard_map/all_to_all | solution.py:313
  77.4 6.2 %copy-start.8 = (f32[1,8192]{1,0:T(1,128)S(1)}, f32[1,8192]{1,0:T(1,128)}, u32[]{:S(2)}) copy-start(f32[1,8192]{1,0:T(1,128)} %param.12) | copy-start | bytes 98308
  77.4 8.2 %collective-permute-start = (bf16[16,4096]{1,0:T(8,128)(2,1)S(1)}, bf16[16,4096]{1,0:T(8,128)(2,1)S(1)}, u32[]{:S(2)}, u32[]{:S(2)}) collective-permute-start(bf16[16,4096]{1,0:T(8,128)(2,1)S(1)} %constant_dynamic-slice_fusion), channel_id=1, source_target_pairs={{0,224},{32,0},{64,32},{96,64},{128,96},{160,128},{192,160},{224,1... | collective-permute-start | bytes 393224 | tf_op jit(solution)/shard_map/ppermute | solution.py:53
  83.1 6.1 %collective-permute-start.3 = (bf16[16,4096]{1,0:T(8,128)(2,1)S(1)}, bf16[16,4096]{1,0:T(8,128)(2,1)S(1)}, u32[]{:S(2)}, u32[]{:S(2)}) collective-permute-start(bf16[16,4096]{1,0:T(8,128)(2,1)S(1)} %constant_dynamic-slice_fusion), channel_id=1, source_target_pairs={{0,32},{32,64},{64,96},{96,128},{128,160},{160,192},{192,224},{224... | collective-permute-start | bytes 393224 | tf_op jit(solution)/shard_map/ppermute | solution.py:50
  83.6 25.6 %copy-start.6 = (bf16[1,16,8192]{2,1,0:T(8,128)(2,1)S(1)}, bf16[1,16,8192]{2,1,0:T(8,128)(2,1)}, u32[]{:S(2)}) copy-start(bf16[1,16,8192]{2,1,0:T(8,128)(2,1)} %param.10) | copy-start | bytes 786436
  85.7 5.5 %collective-permute-start.1 = (bf16[16,4096]{1,0:T(8,128)(2,1)S(1)}, bf16[16,4096]{1,0:T(8,128)(2,1)S(1)}, u32[]{:S(2)}, u32[]{:S(2)}) collective-permute-start(bf16[16,4096]{1,0:T(8,128)(2,1)S(1)} %collective-permute-done), channel_id=1, source_target_pairs={{0,224},{32,0},{64,32},{96,64},{128,96},{160,128},{192,160},{224,1... | collective-permute-start | bytes 393224 | tf_op jit(solution)/shard_map/ppermute | solution.py:53
  89.2 5.4 %collective-permute-start.4 = (bf16[16,4096]{1,0:T(8,128)(2,1)S(1)}, bf16[16,4096]{1,0:T(8,128)(2,1)S(1)}, u32[]{:S(2)}, u32[]{:S(2)}) collective-permute-start(bf16[16,4096]{1,0:T(8,128)(2,1)S(1)} %collective-permute-done.3), channel_id=1, source_target_pairs={{0,32},{32,64},{64,96},{96,128},{128,160},{160,192},{192,224},{224... | collective-permute-start | bytes 393224 | tf_op jit(solution)/shard_map/ppermute | solution.py:50
  91.1 8.9 %collective-permute-start.2 = (bf16[16,4096]{1,0:T(8,128)(2,1)S(1)}, bf16[16,4096]{1,0:T(8,128)(2,1)S(1)}, u32[]{:S(2)}, u32[]{:S(2)}) collective-permute-start(bf16[16,4096]{1,0:T(8,128)(2,1)S(1)} %collective-permute-done.1), channel_id=1, source_target_pairs={{0,224},{32,0},{64,32},{96,64},{128,96},{160,128},{192,160},{224,1... | collective-permute-start | bytes 393224 | tf_op jit(solution)/shard_map/ppermute | solution.py:53
  94.6 5.4 %collective-permute-start.5 = (bf16[16,4096]{1,0:T(8,128)(2,1)S(1)}, bf16[16,4096]{1,0:T(8,128)(2,1)S(1)}, u32[]{:S(2)}, u32[]{:S(2)}) collective-permute-start(bf16[16,4096]{1,0:T(8,128)(2,1)S(1)} %collective-permute-done.4), channel_id=1, source_target_pairs={{0,32},{32,64},{64,96},{96,128},{128,160},{160,192},{192,224},{224... | collective-permute-start | bytes 393224 | tf_op jit(solution)/shard_map/ppermute | solution.py:50
  100.0 5.0 %collective-permute-start.6 = (bf16[16,4096]{1,0:T(8,128)(2,1)S(1)}, bf16[16,4096]{1,0:T(8,128)(2,1)S(1)}, u32[]{:S(2)}, u32[]{:S(2)}) collective-permute-start(bf16[16,4096]{1,0:T(8,128)(2,1)S(1)} %collective-permute-done.5), channel_id=1, source_target_pairs={{0,32},{32,64},{64,96},{96,128},{128,160},{160,192},{192,224},{224... | collective-permute-start | bytes 393224 | tf_op jit(solution)/shard_map/ppermute | solution.py:50
  105.2 7.8 %collective-permute-start.7 = (bf16[128,4096]{1,0:T(8,128)(2,1)S(1)}, bf16[128,4096]{1,0:T(8,128)(2,1)}, u32[]{:S(2)}, u32[]{:S(2)}) collective-permute-start(bf16[128,4096]{1,0:T(8,128)(2,1)S(1)} %constant_dynamic-update-slice_fusion.mine_ref), channel_id=1, source_target_pairs={{0,1},{1,0},{2,3},{3,2},{4,5},{5,4},{6,7},{7,6},{8,9},{9,8},{10,11... | collective-permute-start | bytes 3145736 | tf_op jit(solution)/shard_map/ppermute | solution.py:320
  110.1 4.5 %copy-start.4 = (bf16[16,8192]{1,0:T(8,128)(2,1)}, bf16[16,8192]{1,0:T(8,128)(2,1)S(1)}, u32[]{:S(2)}) copy-start(bf16[16,8192]{1,0:T(8,128)(2,1)S(1)} %get-tuple-element.29) | copy-start | bytes 786436
  110.1 4.4 %copy-start.7 = (bf16[16,8192]{1,0:T(8,128)(2,1)S(1)}, bf16[16,8192]{1,0:T(8,128)(2,1)}, u32[]{:S(2)}) copy-start(bf16[16,8192]{1,0:T(8,128)(2,1)} %get-tuple-element.30) | copy-start | bytes 786436
  119.7 18.6 %all-to-all-start.2 = ((bf16[8,192,128]{2,1,0:T(8,128)(2,1)}), bf16[8,192,128]{2,1,0:T(8,128)(2,1)S(1)}, u32[]{:S(2)}, u32[]{:S(2)}) async-start(bf16[8,192,128]{2,1,0:T(8,128)(2,1)} %broadcast_in_dim.42), calls=%async_computation.2 | async-start | bytes 786432 | tf_op jit(solution)/shard_map/all_to_all | solution.py:346
  135.5 1.3 copy-start.1
  136.8 0.7 copy-start.3
  138.3 15.7 %all-to-all-start.1 = ((bf16[8,128,128]{2,1,0:T(8,128)(2,1)}), bf16[8,128,128]{2,1,0:T(8,128)(2,1)S(1)}, u32[]{:S(2)}, u32[]{:S(2)}) async-start(bf16[8,128,128]{2,1,0:T(8,128)(2,1)} %copy-done.3), calls=%async_computation.1 | async-start | bytes 524288 | tf_op jit(solution)/shard_map/all_to_all | solution.py:350
  155.7 1.6 copy-start.2
  164.0 9.7 %collective-permute-start.8 = (f32[16,144,256]{2,1,0:T(8,128)}, f32[16,144,256]{2,1,0:T(8,128)S(1)}, u32[]{:S(2)}, u32[]{:S(2)}) collective-permute-start(f32[16,144,256]{2,1,0:T(8,128)} %part.3), channel_id=1, source_target_pairs={{0,1},{1,0},{2,3},{3,2},{4,5},{5,4},{6,7},{7,6},{8,9},{9,8},{10,11... | collective-permute-start | bytes 7077896 | tf_op jit(solution)/shard_map/ppermute | solution.py:354
  201.5 11.0 %all-to-all-start.4 = ((f32[8,16,256]{2,1,0:T(8,128)}), f32[8,16,256]{2,1,0:T(8,128)S(1)}, u32[]{:S(2)}, u32[]{:S(2)}) async-start(f32[8,16,256]{2,1,0:T(8,128)} %bitcast.15), calls=%async_computation.4 | async-start | bytes 262144 | tf_op jit(solution)/shard_map/all_to_all | solution.py:359
  224.6 5.3 %collective-permute-start.9 = (f32[32,4096]{1,0:T(8,128)S(1)}, f32[32,4096]{1,0:T(8,128)S(1)}, u32[]{:S(2)}, u32[]{:S(2)}) collective-permute-start(f32[32,4096]{1,0:T(8,128)S(1)} %bitcast.50), channel_id=1, source_target_pairs={{0,1},{1,0},{2,3},{3,2},{4,5},{5,4},{6,7},{7,6},{8,9},{9,8},{10,11... | collective-permute-start | bytes 1572872 | tf_op jit(solution)/shard_map/ppermute | solution.py:364

commit v3 on v2

v3 whole, which is shorter than its diff:
```python
import functools

import jax
import jax.numpy as jnp
from jax import lax
from jax.experimental import pallas as pl
from jax.experimental.pallas import tpu as pltpu
from jax.sharding import Mesh
from jax.sharding import PartitionSpec as P

norm_eps = 1e-05
stat_eps = 1e-06
coef_reroute = 64.0
coef_retain = 1.0
loss_scale = 2048.0

SEC = "section"
CHIPS = ("y", "x")
DP = ("y", "x", "core")
f32 = jnp.float32
bf16 = jnp.bfloat16


def nt(left, right):
    return lax.dot_general(left, right, (((1,), (1,)), ((), ())), preferred_element_type=f32)


def tn(left, right):
    return lax.dot_general(left, right, (((0,), (0,)), ((), ())), preferred_element_type=f32)


def nn(left, right):
    return lax.dot_general(left, right, (((1,), (0,)), ((), ())), preferred_element_type=f32)


def split2(value):
    hi = value.astype(bf16)
    lo = (value - hi.astype(f32)).astype(bf16)
    return hi, lo


def ring_gather(block, axis, gate):
    n = lax.axis_size(axis)
    up = [(i, (i + 1) % n) for i in range(n)]
    down = [(i, (i - 1) % n) for i in range(n)]
    found = [None] * n
    found[0] = block
    fwd = bwd = block
    for k in range(1, n // 2 + 1):
        fwd = lax.ppermute(fwd, axis, up)
        found[k] = fwd
        if k < n - n // 2:
            bwd = lax.ppermute(bwd, axis, down)
            found[n - k] = bwd
        if k == 1:
            fwd, bwd, _ = lax.optimization_barrier((fwd, bwd, gate))
            found[1], found[n - 1] = fwd, bwd
    return found


def params(mib=63):
    return pltpu.CompilerParams(vmem_limit_bytes=mib << 20)


def smem():
    return pl.BlockSpec(memory_space=pltpu.SMEM)


def in_place():
    return pl.BlockSpec(memory_space=pl.ANY)


def vmem():
    return pl.BlockSpec(memory_space=pltpu.VMEM)


def call(kernel, name, out_shape, scalars, arrays, scratch=()):
    count, total = len(scalars), len(arrays)
    outs = len(out_shape)

    def body(*refs):
        held = refs[count : count + total]
        first = count + total + outs
        buffers, sems = refs[first : first + total], refs[first + total : first + 2 * total]
        kernel(*refs[:count], *zip(held, buffers, sems), *refs[count + total : first], *refs[first + 2 * total :])

    return pl.pallas_call(
        body,
        out_shape=out_shape,
        in_specs=[smem()] * count + [in_place()] * total,
        out_specs=[vmem()] * outs,
        scratch_shapes=[pltpu.VMEM(a.shape, a.dtype) for a in arrays]
        + [pltpu.SemaphoreType.DMA((PIECES,)) for _ in arrays]
        + list(scratch),
        compiler_params=params(),
        name=name,
    )(*scalars, *arrays)


PIECES = 8


def whole(item):
    held, buffer, sem = item
    return pltpu.make_async_copy(held, buffer, sem.at[0])


def columns_piece(item, i, start, width):
    held, buffer, sem = item
    where = (slice(None),) * (len(held.shape) - 1) + (pl.ds(start, width),)
    return pltpu.make_async_copy(held.at[where], buffer.at[where], sem.at[i])


def leading_piece(item, i, start, count):
    held, buffer, sem = item
    return pltpu.make_async_copy(held.at[pl.ds(start, count)], buffer.at[pl.ds(start, count)], sem.at[i])


INFO = 8


def order_kernel(position_ref, meta_ref, held_ref, out_ref, buffer, in_sem, out_sem):
    tiles, tokens, width = held_ref.shape
    loads = [
        pltpu.make_async_copy(held_ref.at[position_ref[i]], buffer.at[i, pl.ds(0, tokens)], in_sem.at[i])
        for i in range(tiles)
    ]
    for load in loads:
        load.start()
    flag, valid = meta_ref[1], meta_ref[2]
    row = lax.broadcasted_iota(jnp.int32, (INFO, width), 0)
    here = ((row == 0) & (flag == 1)) | ((row == 1) & (flag != 1))
    info = jnp.where(here, valid, 0).astype(f32).astype(bf16)
    stores = []
    for i in range(tiles):
        buffer[i, tokens:, :] = info
        loads[i].wait()
        stores.append(pltpu.make_async_copy(buffer.at[i], out_ref.at[i], out_sem.at[i]))
        stores[-1].start()
    for store in stores:
        store.wait()


def order(position, meta, held):
    tiles, tokens, width = held.shape
    shape = (tiles, tokens + INFO, width)
    return pl.pallas_call(
        order_kernel,
        out_shape=jax.ShapeDtypeStruct(shape, held.dtype),
        in_specs=[smem(), smem(), in_place()],
        out_specs=in_place(),
        scratch_shapes=[
            pltpu.VMEM(shape, held.dtype),
            pltpu.SemaphoreType.DMA((tiles,)),
            pltpu.SemaphoreType.DMA((tiles,)),
        ],
        compiler_params=params(),
        name="order",
    )(position, meta, held)


def fold(value):
    lanes = 128
    total = value[:, :lanes]
    for i in range(1, value.shape[1] // lanes):
        total = total + value[:, i * lanes : (i + 1) * lanes]
    return total


def forward_kernel(stream_in, down_in, gain_in, normed_ref, lrt_ref, irms_ref, dg_ref):
    stream_ref, down_ref, gain_ref = stream_in[1], down_in[1], gain_in[1]
    tokens, width = stream_ref.shape
    piece = width // PIECES
    loads = [columns_piece(stream_in, i, i * piece, piece) for i in range(PIECES)]
    for load in loads:
        load.start()
    whole(down_in).start()
    whole(gain_in).start()
    total = jnp.zeros((tokens, 128), f32)
    for i in range(PIECES):
        loads[i].wait()
        for low in range(i * piece, (i + 1) * piece, 256):
            x = stream_ref[:, low : low + 256].astype(f32)
            total = total + fold(x * x)
    irms = lax.rsqrt(jnp.sum(total, axis=1, keepdims=True) * (1.0 / width) + norm_eps)
    irms_ref[...] = jnp.broadcast_to(irms, (tokens, 128)).T[:8, :]
    whole(down_in).wait()
    whole(gain_in).wait()
    chunk = min(512, piece)

    def norm(i, acc):
        columns = pl.ds(pl.multiple_of(i * chunk, chunk), chunk)
        gain = gain_ref[:, columns]
        normed = (stream_ref[:, columns].astype(f32) * irms * gain).astype(bf16)
        normed_ref[:, columns] = normed
        down = down_ref[:, columns]
        hi, lo = split2(down.astype(f32) * gain)
        dg_ref[0, :, columns] = hi
        dg_ref[1, :, columns] = lo
        return acc + nt(down, normed)

    rank = down_ref.shape[0]
    low_rank = lax.fori_loop(0, width // chunk, norm, jnp.zeros((rank, tokens), f32), unroll=2)
    lrt_ref[...] = low_rank.astype(bf16)


def forward(stream, down, gain):
    rank = down.shape[0]
    tokens, width = stream.shape
    return call(
        forward_kernel,
        "forward",
        (
            jax.ShapeDtypeStruct((tokens, width), bf16),
            jax.ShapeDtypeStruct((rank, tokens), bf16),
            jax.ShapeDtypeStruct((8, tokens), f32),
            jax.ShapeDtypeStruct((2, rank, width), bf16),
        ),
        (),
        (stream, down, gain),
    )


def side_kernel(count, meta_ref, stream_in, dg_in, lrt_in, irms_in, *refs):
    mine, other, out_ref = refs[:count], refs[count : 2 * count], refs[2 * count]
    core = meta_ref[0]
    rank, half = mine[0][1].shape
    tokens = stream_in[1].shape[0]
    rows = count * rank
    chunk = min(1024, half)
    for item in (*mine, stream_in, dg_in, *other, lrt_in, irms_in):
        whole(item).start()
    for item in (*mine, stream_in, dg_in):
        whole(item).wait()
    stream_ref, dg_ref = stream_in[1], dg_in[1]
    total = jnp.zeros((rows, tokens + 2 * rank), f32)
    for base, blocks in ((core, mine), (1 - core, other)):
        if blocks is other:
            for item in other:
                whole(item).wait()

        def step(i, acc, base=base, blocks=blocks):
            local = pl.ds(pl.multiple_of(i * chunk, chunk), chunk)
            columns = pl.ds(pl.multiple_of(base * half + i * chunk, chunk), chunk)
            up = jnp.concatenate([b[1][:, local] for b in blocks], axis=0)
            right = jnp.concatenate([stream_ref[:, columns], dg_ref[0, :, columns], dg_ref[1, :, columns]], axis=0)
            return acc + nt(up, right)

        total = lax.fori_loop(0, half // chunk, step, total, unroll=2)
    whole(lrt_in).wait()
    whole(irms_in).wait()
    irms = irms_in[1][0:1, :]
    scaled_up = (total[:, :tokens] * irms).astype(bf16)
    w = total[:, tokens : tokens + rank] + total[:, tokens + rank :]
    w = jnp.concatenate([w, jnp.zeros((rows, 128 - rank), f32)], axis=1).T[:rank, :]
    w_hi, w_lo = split2(w)
    irms_hi = irms.astype(bf16).astype(f32)
    row = lax.broadcasted_iota(jnp.int32, (rank, tokens), 0)
    last = jnp.where(row == 0, irms_hi, jnp.where(row == 1, irms - irms_hi, 0.0)).astype(bf16)
    for i in range(out_ref.shape[0]):
        out_ref[i, :rows, :] = scaled_up
        out_ref[i, rows : rows + rank, :] = lrt_in[1][...]
        out_ref[i, rows + rank : rows + 2 * rank, :] = w_hi
        out_ref[i, rows + 2 * rank : rows + 3 * rank, :] = w_lo
        out_ref[i, rows + 3 * rank :, :] = last


def side_of(meta, stream, dg, lrt, irms, mine, other):
    layers = len(mine)
    rank = lrt.shape[0]
    (side,) = call(
        functools.partial(side_kernel, layers),
        "side",
        (jax.ShapeDtypeStruct((layers, (layers + 4) * rank, stream.shape[0]), bf16),),
        (meta,),
        (stream, dg, lrt, irms, *mine, *other),
    )
    return side


def own_kernel(count, meta_ref, refs_in, stream_in, up_in, lrt_in, *refs):
    mine, other, own_ref, proj_ref, output_ref = (
        refs[:count],
        refs[count : 2 * count],
        refs[2 * count],
        refs[2 * count + 1],
        refs[2 * count + 2],
    )
    core, flag, valid = meta_ref[0], meta_ref[1], meta_ref[2]
    refs_ref, stream_ref, up_ref = refs_in[1], stream_in[1], up_in[1]
    tiles, padded, chunk = refs_ref.shape
    tokens = padded - INFO
    half = mine[0][1].shape[1]
    per_half = half // chunk
    per_piece = tiles // PIECES
    width = per_piece * chunk

    whole(lrt_in).start()
    whole(up_in).start()
    stream_loads = [columns_piece(stream_in, i, i * width, width) for i in range(PIECES)]
    ref_loads = [leading_piece(refs_in, i, i * per_piece, per_piece) for i in range(PIECES)]
    for i in range(PIECES):
        stream_loads[i].start()
        ref_loads[i].start()
    for item in (*mine, *other):
        whole(item).start()
    whole(lrt_in).wait()
    whole(up_in).wait()
    low_rank = lrt_in[1][...].astype(f32).T.astype(bf16)
    is_valid = lax.broadcasted_iota(jnp.int32, (tokens, 1), 0) < valid

    def weight(row):
        info = refs_ref[0, tokens:, :128].astype(f32)
        for i in range(1, tiles):
            info = info + refs_ref[i, tokens:, :128].astype(f32)
        return loss_scale / info[row : row + 1, 0:1]

    def stats(terms, number):
        acc = [jnp.zeros((tokens, 128), f32) for _ in range(number)]
        for i in range(PIECES):
            stream_loads[i].wait()
            ref_loads[i].wait()
            for j in range(i * per_piece, (i + 1) * per_piece):
                columns = slice(j * chunk, (j + 1) * chunk)
                out = stream_ref[:, columns].astype(f32) + nn(low_rank, up_ref[:, columns])
                output_ref[:, columns] = out
                ref = refs_ref[j, :tokens, :].astype(f32)
                acc = [a + fold(v) for a, v in zip(acc, terms(out, ref))]
        return [jnp.sum(a, axis=1, keepdims=True) for a in acc]

    group = min(4, per_half)

    def finish(make):
        for item in (*mine, *other):
            whole(item).wait()
        total = jnp.zeros(proj_ref.shape[1:], f32)
        for base, blocks in ((core, mine), (1 - core, other)):

            def step(i, acc, base=base, blocks=blocks):
                parts = []
                for g in range(group):
                    j = base * per_half + i * group + g
                    columns = pl.ds(pl.multiple_of(j * chunk, chunk), chunk)
                    own = make(output_ref[:, columns], refs_ref[j, :tokens, :].astype(f32)).astype(bf16)
                    own_ref[:, columns] = own
                    parts.append(own)
                local = pl.ds(pl.multiple_of(i * group * chunk, group * chunk), group * chunk)
                up = jnp.concatenate([b[1][:, local] for b in blocks], axis=0)
                return acc + nt(up, jnp.concatenate(parts, axis=1))

            total = lax.fori_loop(0, per_half // group, step, total, unroll=2)
        total = total.astype(bf16)
        for i in range(proj_ref.shape[0]):
            proj_ref[i] = total

    @pl.when(flag == 1)
    def _():
        out_sq, ref_sq, cross = stats(lambda o, r: (o * o, r * r, o * r), 3)
        out_norm = jnp.sqrt(out_sq + stat_eps)
        ref_norm = jnp.sqrt(ref_sq + stat_eps)
        cosine = cross / (out_norm * ref_norm)
        on = jnp.where(is_valid & (cosine > 0), coef_reroute * weight(0), 0.0)
        coef_ref = on / (out_norm * ref_norm)
        coef_out = on * cosine / (out_sq + stat_eps)
        finish(lambda o, r: coef_ref * r - coef_out * o)

    @pl.when(flag != 1)
    def _():
        (diff_sq,) = stats(lambda o, r: ((o - r) * (o - r),), 1)
        coef = jnp.where(is_valid, coef_retain * weight(1), 0.0) / jnp.sqrt(diff_sq + stat_eps)
        finish(lambda o, r: coef * (o - r))


def own_gradient(meta, refs, stream, up, lrt, mine, other):
    layers = len(mine)
    return call(
        functools.partial(own_kernel, layers),
        "own",
        (
            jax.ShapeDtypeStruct(stream.shape, bf16),
            jax.ShapeDtypeStruct((layers, layers * up.shape[0], stream.shape[0]), bf16),
        ),
        (meta,),
        (refs, stream, up, lrt, *mine, *other),
        (pltpu.VMEM(stream.shape, f32),),
    )


def solve_kernel(width, rank, me_ref, own_ref, side_ref, low_ref, lrt_ref, coef_ref, k_ref, acc):
    me = me_ref[0]
    layers, rows, _ = own_ref.shape
    acc[...] = jnp.zeros_like(acc)
    for j in range(layers):

        @pl.when(me + j < layers)
        def _(j=j):
            low = rank * (layers - 1 - j)
            acc[0 : rank * (j + 1), :] += own_ref[me + j, low:rows, :].astype(f32)

    def inverse_rms(t):
        return side_ref[t, rows + 3 * rank : rows + 3 * rank + 1, :].astype(f32) + side_ref[
            t, rows + 3 * rank + 1 : rows + 3 * rank + 2, :
        ].astype(f32)

    def mean_of(grad, t):
        lrt = side_ref[t, rows : rows + rank, :].astype(f32)
        return jnp.sum(grad.astype(f32) * lrt, axis=0, keepdims=True) * (1.0 / width)

    for j in range(layers - 1, 0, -1):

        @pl.when(me + j < layers)
        def _(j=j):
            t = me + j
            low = rank * (layers - 1 - j)
            grad = acc[rank * j : rank * (j + 1), :].astype(bf16)
            mean = mean_of(grad, t)
            w_hi = side_ref[t, rows + rank : rows + 2 * rank, :]
            w_lo = side_ref[t, rows + 2 * rank : rows + 3 * rank, :]
            term = tn(w_hi, grad) + tn(w_lo, grad)
            scaled_up = side_ref[t, low : rows - rank, :].astype(f32)
            acc[0 : rank * j, :] += inverse_rms(t) * (term[low : rows - rank, :] - mean * scaled_up)

    grad = acc[0:rank, :].astype(bf16)
    low_ref[...] = grad
    irms = inverse_rms(me)
    mean = mean_of(grad, me)
    lrt = side_ref[:, rows : rows + rank, :].reshape(layers * rank, -1)
    layer = lax.broadcasted_iota(jnp.int32, lrt.shape, 0) // rank
    lrt_f = lrt.astype(f32)
    lrt_ref[...] = jnp.where(layer <= me, lrt_f, 0.0).astype(bf16)
    below = jnp.where(layer < me, lrt_f, 0.0)
    coef_ref[...] = (below * (-irms * irms * mean)).astype(bf16)
    k_hi, k_lo = split2(nt(below.astype(bf16), (grad.astype(f32) * irms).astype(bf16)))
    k_ref[0] = k_hi
    k_ref[1] = k_lo


def solve(width, rank, me, own, side):
    layers, rows, tokens = own.shape
    return pl.pallas_call(
        functools.partial(solve_kernel, width, rank),
        out_shape=(
            jax.ShapeDtypeStruct((rank, tokens), bf16),
            jax.ShapeDtypeStruct((rows, tokens), bf16),
            jax.ShapeDtypeStruct((rows, tokens), bf16),
            jax.ShapeDtypeStruct((2, rows, rank), bf16),
        ),
        in_specs=[smem(), vmem(), vmem()],
        out_specs=(vmem(),) * 4,
        scratch_shapes=[pltpu.VMEM((rows, tokens), f32)],
        compiler_params=params(8),
        name="solve",
    )(me, own, side)


def part_kernel(start_ref, low_in, lrt_in, coef_in, k_in, own_in, stream_in, normed_in, dg_in, out_ref):
    start = start_ref[0]
    chunks, _, chunk = out_ref.shape
    rows = lrt_in[1].shape[0]
    group = min(4, chunks)
    width = group * chunk
    small = (low_in, lrt_in, coef_in, k_in)
    large = (own_in, stream_in, normed_in, dg_in)
    for item in small:
        whole(item).start()
    loads = [
        [columns_piece(item, i, pl.multiple_of(start + i * width, width), width) for item in large]
        for i in range(chunks // group)
    ]
    for piece in loads:
        for load in piece:
            load.start()
    for item in small:
        whole(item).wait()
    left = jnp.concatenate([lrt_in[1][...], coef_in[1][...]], axis=1)
    k_hi, k_lo = k_in[1][0].astype(f32), k_in[1][1].astype(f32)
    k = jnp.concatenate([k_hi, k_hi, k_lo], axis=1).astype(bf16)
    low = low_in[1][...]
    for i, piece in enumerate(loads):
        for load in piece:
            load.wait()
        columns = pl.ds(pl.multiple_of(start + i * width, width), width)
        right = jnp.concatenate([own_in[1][:, columns], stream_in[1][:, columns]], axis=0)
        dg_hi = dg_in[1][0, :, columns]
        dg = jnp.concatenate([dg_hi, dg_in[1][1, :, columns], dg_hi], axis=0)
        up = nn(left, right) + nn(k, dg)
        down = nn(low, normed_in[1][:, columns])
        for j in range(group):
            out_ref[i * group + j, :rows, :] = up[:, j * chunk : (j + 1) * chunk]
            out_ref[i * group + j, rows:, :] = down[:, j * chunk : (j + 1) * chunk]


def part(start, chunks, chunk, *arrays):
    low, lrt = arrays[:2]
    (found,) = call(
        part_kernel,
        "part",
        (jax.ShapeDtypeStruct((chunks, lrt.shape[0] + low.shape[0], chunk), f32),),
        (start,),
        arrays,
    )
    return found


def shards(
    layer_input_states,
    frozen_reference_states,
    adapter_down_weight,
    adapter_up_weight,
    layer_norm_gain,
    tile_reference_position,
    tile_harmful_flag,
    tile_valid_count,
):
    tokens, width = layer_input_states.shape[2:]
    rank = adapter_up_weight.shape[1]
    layers = lax.axis_size(SEC)
    me = lax.axis_index(SEC)
    core = lax.axis_index("core")
    cores = lax.axis_size("core")
    chips = lax.axis_size("y") * lax.axis_size("x")
    half = width // cores
    chunk = half // chips
    swap = [(i, (i + 1) % cores) for i in range(cores)]

    meta = jnp.stack([core, tile_harmful_flag[0], tile_valid_count[0]]).astype(jnp.int32)
    ordered = order(tile_reference_position, meta, frozen_reference_states[0])
    refs = lax.all_to_all(ordered, DP, split_axis=0, concat_axis=0, tiled=True)
    gate, stream, down, up, gains = lax.optimization_barrier(
        (ordered, layer_input_states[0, 0], adapter_down_weight[0], adapter_up_weight[0], layer_norm_gain)
    )

    up_half = lax.dynamic_slice_in_dim(adapter_up_weight[0], core * half, half, axis=1)
    mine = ring_gather(up_half, SEC, gate)[::-1]
    other = [lax.ppermute(block, "core", swap) for block in mine]

    normed, lrt, irms, dg = forward(stream, down, gains)
    side = side_of(meta, stream, dg, lrt, irms, mine, other)
    sides = lax.all_to_all(side, SEC, 0, 0, tiled=True)

    own, own_up = own_gradient(meta, refs, stream, up, lrt, mine, other)
    own_up = lax.all_to_all(own_up, SEC, 0, 0, tiled=True)
    low, lrt_all, coef, k = solve(width, rank, me[None], own_up, sides)

    given = part(((1 - core) * half)[None], chips, chunk, low, lrt_all, coef, k, own, stream, normed, dg)
    received = lax.ppermute(given, "core", swap)
    kept = part((core * half)[None], chips, chunk, low, lrt_all, coef, k, own, stream, normed, dg)
    blocks = lax.all_to_all((kept + received).astype(bf16), CHIPS, 0, 0, tiled=True)
    summed = jnp.sum(blocks.astype(f32), axis=0)

    by_layer = lax.all_to_all(summed[: layers * rank].reshape(layers, rank, chunk), SEC, 0, 0, tiled=True)
    final = jnp.concatenate([summed[layers * rank :], jnp.sum(by_layer, axis=0)], axis=0)

    wide = lax.all_to_all(jnp.broadcast_to(final, (chips,) + final.shape), CHIPS, 0, 0, tiled=True)
    mine = wide.transpose(1, 0, 2).reshape(2 * rank, half)
    other = lax.ppermute(mine, "core", swap)
    full = jnp.concatenate([jnp.where(core == 0, mine, other), jnp.where(core == 0, other, mine)], axis=1)
    return (full[None, :rank], full[None, rank:])


def solution(mesh):
    layers, dp = mesh.devices.shape
    cores = 2
    side = round((dp // cores) ** 0.5)
    mesh4 = Mesh(mesh.devices.reshape(layers, side, side, cores), (SEC,) + DP)
    return jax.shard_map(
        shards,
        mesh=mesh4,
        in_specs=(
            P(SEC, DP, None, None),
            P(SEC, None, None, DP),
            P(SEC, None, None),
            P(SEC, None, None),
            P(SEC, None),
            P(),
            P(DP),
            P(DP),
        ),
        out_specs=(P(SEC, None, None), P(SEC, None, None)),
        check_vma=False,
    )
```

time: 232 us -> 166 us (0.72)
  Pallas kernels: 89.7 us -> 36.3 us
  matrix products: 12.2 us -> 0 us
  waiting for transfers between devices: 31.2 us -> 36.9 us
  other arithmetic: 8.52 us -> 4.54 us
    pallas_call x4 -> x6, Pallas kernels: 88 us -> 34.6 us  [the longest x5 31.1 us: call(): pl.pallas_call(body, out_shape=out_shape, in_specs=[smem()] * count + [in...]
    dot_general x8 -> x0, matrix products: 12.2 us -> none  [the longest x7 8.55 us: nt(): lax.dot_general(left, right, (((1,), (1,)), ((), ())), preferred_element_...]
    ppermute x1 -> x8, starting transfers between devices: 4.03 us -> 10.1 us  [shards(): other = [lax.ppermute(block, 'core', swap) for block in mine]]
    all_to_all x1, waiting for transfers between devices: 0.75 us -> 5.53 us  [shards(): sides = lax.all_to_all(side, SEC, 0, 0, tiled=True)]
    all_to_all x1, waiting for transfers between devices: 8.82 us -> 12.2 us  [shards(): own_up = lax.all_to_all(own_up, SEC, 0, 0, tiled=True)]
    ppermute x4, waiting for transfers between devices: 10.4 us -> 7.37 us  [ring_gather(): fwd = lax.ppermute(fwd, axis, up)]
    convert_element_type x4 -> x0, other arithmetic: 2.66 us -> none  [the longest x1 1.98 us: shards(): normed = (stream * inverse_rms * gains).astype(bf16)]
    all_to_all x1, starting transfers between devices: 5.82 us -> 3.41 us  [shards(): own_up = lax.all_to_all(own_up, SEC, 0, 0, tiled=True)]
  transfers between devices with their start and end apart: 14 -> 21, of which waited for: 8 -> 8; matrix products, arithmetic and copies ran while one was open for 7% -> 0% of each run, Pallas kernels for 7% -> 16%
where the time goes in v3:
time: 166 us; the launch traced here: 165 us
  starting transfers between devices  44.8 us (27%)
  waiting for transfers between devices  36.9 us (22%)
  blocking collectives  36.9 us (22%)
  Pallas kernels  36.3 us (22%)
  other arithmetic  4.54 us (3%)
  local copies, waits for them, and re-layouts  3.25 us (2%)
  between operations  2.25 us (1%)
    pallas_call x5, Pallas kernels, call(): pl.pallas_call(body, out_shape=out_shape, in_specs=[smem()] * count + [in...  31.1 us
    all_to_all x1, blocking collectives, shards(): lax.all_to_all((kept + received).astype(bf16), CHIPS, 0, 0, tiled=True)  25 us
    all_to_all x1, waiting for transfers between devices, shards(): own_up = lax.all_to_all(own_up, SEC, 0, 0, tiled=True)  12.2 us
    all_to_all x1, blocking collectives, shards(): lax.all_to_all(jnp.broadcast_to(final, (chips,) + final.shape), CHIPS, 0,...  12 us
    ppermute x3, starting transfers between devices, ring_gather(): bwd = lax.ppermute(bwd, axis, down)  11.3 us
    ppermute x8, starting transfers between devices, shards(): other = [lax.ppermute(block, 'core', swap) for block in mine]  10.1 us
    all_to_all x1, starting transfers between devices, shards(): refs = lax.all_to_all(ordered, DP, split_axis=0, concat_axis=0, tiled=True)  8.78 us
    all_to_all x1, waiting for transfers between devices, shards(): lax.all_to_all(summed[:layers * rank].reshape(layers, rank, chunk), SEC,...  7.67 us
  transfers between devices with their start and end apart: 21, of which 8 were waited for; matrix products, arithmetic and copies ran while one was open for 0% of the time, Pallas kernels for 16%

profile of v3, /device:TPU:1, one launch (start us, length us, event | category | flops | bytes accessed | tf_op | source)
XLA Modules:
  0.0 165.0 jit_solution(17113790580731328677)
XLA Ops:
  1.9 0.6 pad_add_fusion.meta_ref.refs_0_
  2.5 3.5 %order.1 = bf16[32,136,256]{2,1,0:T(8,128)(2,1)} custom-call(s32[32]{0:T(128)} %position_ref.1, s32[3]{0:T(128)} %pad_add_fusion.meta_ref.refs_0_, bf16[32,128,256]{2,1,0:T(8,128)(2,1)} %bitcast.23), custom_call_target="tpu_custom_call" | custom-call | tf_op jit(solution)/shard_map/order/pallas_call | solution.py:147
  6.0 0.0 copy-start.5
  6.1 8.8 %all-to-all-start = ((bf16[32,136,256]{2,1,0:T(8,128)(2,1)}), bf16[32,136,256]{2,1,0:T(8,128)(2,1)}, u32[]{:S(2)}, u32[]{:S(2)}) async-start(bf16[32,136,256]{2,1,0:T(8,128)(2,1)} %order.1), calls=%async_computation | async-start | bytes 4456448 | tf_op jit(solution)/shard_map/all_to_all | solution.py:528
  14.9 5.7 %collective-permute-start.1 = (bf16[16,4096]{1,0:T(8,128)(2,1)S(1)}, bf16[16,4096]{1,0:T(8,128)(2,1)S(1)}, u32[]{:S(2)}, u32[]{:S(2)}) collective-permute-start(bf16[16,4096]{1,0:T(8,128)(2,1)S(1)} %dynamic-slice_bitcast_fusion.refs_12_), channel_id=1, source_target_pairs={{0,224},{32,0},{64,32},{96,64},{128,96},{160,128},{192,160},{224,1... | collective-permute-start | bytes 393224 | tf_op jit(solution)/shard_map/ppermute | solution.py:53
  20.5 0.0 collective-permute-start
  20.5 2.6 %collective-permute-done.1.refs_5_ = bf16[16,4096]{1,0:T(8,128)(2,1)S(1)} collective-permute-done((bf16[16,4096]{1,0:T(8,128)(2,1)S(1)}, bf16[16,4096]{1,0:T(8,128)(2,1)S(1)}, u32[]{:S(2)}, u32[]{:S(2)}) %collective-permute-start.1) | collective-permute-done | bytes 131104 | tf_op jit(solution)/shard_map/ppermute | solution.py:53
  23.1 3.2 %collective-permute-done.refs_11_ = bf16[16,4096]{1,0:T(8,128)(2,1)S(1)} collective-permute-done((bf16[16,4096]{1,0:T(8,128)(2,1)S(1)}, bf16[16,4096]{1,0:T(8,128)(2,1)S(1)}, u32[]{:S(2)}, u32[]{:S(2)}) %collective-permute-start) | collective-permute-done | bytes 131104 | tf_op jit(solution)/shard_map/ppermute | solution.py:50
  26.3 0.0 collective-permute-start.4
  26.3 2.7 %collective-permute-start.2 = (bf16[16,4096]{1,0:T(8,128)(2,1)S(1)}, bf16[16,4096]{1,0:T(8,128)(2,1)S(1)}, u32[]{:S(2)}, u32[]{:S(2)}) collective-permute-start(bf16[16,4096]{1,0:T(8,128)(2,1)S(1)} %collective-permute-done.1.refs_5_), channel_id=1, source_target_pairs={{0,224},{32,0},{64,32},{96,64},{128,96},{160,128},{192,160},{224,1... | collective-permute-start | bytes 393224 | tf_op jit(solution)/shard_map/ppermute | solution.py:53
  29.0 2.8 %collective-permute-done.4.refs_10_ = bf16[16,4096]{1,0:T(8,128)(2,1)S(1)} collective-permute-done((bf16[16,4096]{1,0:T(8,128)(2,1)S(1)}, bf16[16,4096]{1,0:T(8,128)(2,1)S(1)}, u32[]{:S(2)}, u32[]{:S(2)}) %collective-permute-start.4) | collective-permute-done | bytes 131104 | tf_op jit(solution)/shard_map/ppermute | solution.py:50
  31.8 2.1 %collective-permute-start.14 = (bf16[16,4096]{1,0:T(8,128)(2,1)S(1)}, bf16[16,4096]{1,0:T(8,128)(2,1)S(1)}, u32[]{:S(2)}, u32[]{:S(2)}) collective-permute-start(bf16[16,4096]{1,0:T(8,128)(2,1)S(1)} %dynamic-slice_bitcast_fusion.refs_12_), channel_id=1, source_target_pairs={{0,1},{1,0},{2,3},{3,2},{4,5},{5,4},{6,7},{7,6},{8,9},{9,8},{10,11... | collective-permute-start | bytes 393224 | tf_op jit(solution)/shard_map/ppermute | solution.py:535
  33.9 0.1 collective-permute-start.7
  33.9 0.4 collective-permute-start.13
  34.4 3.0 %collective-permute-start.3 = (bf16[16,4096]{1,0:T(8,128)(2,1)S(1)}, bf16[16,4096]{1,0:T(8,128)(2,1)}, u32[]{:S(2)}, u32[]{:S(2)}) collective-permute-start(bf16[16,4096]{1,0:T(8,128)(2,1)S(1)} %collective-permute-done.2.refs_6_), channel_id=1, source_target_pairs={{0,224},{32,0},{64,32},{96,64},{128,96},{160,128},{192,160},{224,1... | collective-permute-start | bytes 393224 | tf_op jit(solution)/shard_map/ppermute | solution.py:53
  37.4 2.8 %collective-permute-start.8 = (bf16[16,4096]{1,0:T(8,128)(2,1)S(1)}, bf16[16,4096]{1,0:T(8,128)(2,1)}, u32[]{:S(2)}, u32[]{:S(2)}) collective-permute-start(bf16[16,4096]{1,0:T(8,128)(2,1)S(1)} %collective-permute-done.2.refs_6_), channel_id=1, source_target_pairs={{0,1},{1,0},{2,3},{3,2},{4,5},{5,4},{6,7},{7,6},{8,9},{9,8},{10,11... | collective-permute-start | bytes 393224 | tf_op jit(solution)/shard_map/ppermute | solution.py:535
  40.1 0.1 collective-permute-start.12
  40.3 0.4 collective-permute-start.11
  40.7 0.4 collective-permute-start.9
  41.0 1.4 collective-permute-done.6.refs_8_
  42.5 3.8 %collective-permute-start.10 = (bf16[16,4096]{1,0:T(8,128)(2,1)}, bf16[16,4096]{1,0:T(8,128)(2,1)}, u32[]{:S(2)}, u32[]{:S(2)}) collective-permute-start(bf16[16,4096]{1,0:T(8,128)(2,1)} %collective-permute-done.6.refs_8_), channel_id=1, source_target_pairs={{0,1},{1,0},{2,3},{3,2},{4,5},{5,4},{6,7},{7,6},{8,9},{9,8},{10,11... | collective-permute-start | bytes 393224 | tf_op jit(solution)/shard_map/ppermute | solution.py:535
  46.3 4.9 %forward.1 = (bf16[128,8192]{1,0:T(8,128)(2,1)}, bf16[16,128]{1,0:T(8,128)(2,1)}, f32[8,128]{1,0:T(8,128)}, bf16[2,16,8192]{2,1,0:T(8,128)(2,1)}) custom-call(bf16[128,8192]{1,0:T(8,128)(2,1)} %bitcast.18, bf16[16,8192]{1,0:T(8,128)(2,1)} %bitcast.28, f32[1,8192]{1,0:T(1,128)} %refs_2_), custom_call_target="tpu_custom_call" | custom-call | tf_op jit(solution)/shard_map/forward/pallas_call | solution.py:87
  51.3 6.6 %side.1 = bf16[8,192,128]{2,1,0:T(8,128)(2,1)} custom-call(s32[3]{0:T(128)} %pad_add_fusion.meta_ref.refs_0_, bf16[128,8192]{1,0:T(8,128)(2,1)} %bitcast.19, bf16[2,16,8192]{2,1,0:T(8,128)(2,1)} %get-tuple-element.26.refs_2_.refs_8_, bf16[16,128]{1,0:T(8,128)(2,1)} %get-tuple-element.22.refs_4_.refs_3_, f32[8,128]{1,0:T(8,128)} %get-tuple-element.27.refs_4_, ...), custom_call_target="tpu_custom_call" | custom-call | tf_op jit(solution)/shard_map/side/pallas_call | solution.py:87
  58.0 3.5 %all-to-all-start.2 = ((bf16[8,192,128]{2,1,0:T(8,128)(2,1)}), bf16[8,192,128]{2,1,0:T(8,128)(2,1)S(1)}, u32[]{:S(2)}, u32[]{:S(2)}) async-start(bf16[8,192,128]{2,1,0:T(8,128)(2,1)} %side.1), calls=%async_computation.2 | async-start | bytes 786432 | tf_op jit(solution)/shard_map/all_to_all | solution.py:539
  61.5 9.6 %own.1 = (bf16[128,8192]{1,0:T(8,128)(2,1)}, bf16[8,128,128]{2,1,0:T(8,128)(2,1)}) custom-call(s32[3]{0:T(128)} %pad_add_fusion.meta_ref.refs_0_, bf16[32,136,256]{2,1,0:T(8,128)(2,1)} %all-to-all-done.refs_1_, bf16[128,8192]{1,0:T(8,128)(2,1)} %bitcast.20, bf16[16,8192]{1,0:T(8,128)(2,1)} %bitcast.27, bf16[16,128]{1,0:T(8,128)(2,1)} %get-tuple-element.22.refs_4_.refs_3_, ...), custom_call_target="tpu_custom_call" | custom-call | tf_op jit(solution)/shard_map/own/pallas_call | solution.py:87
  71.1 5.5 %all-to-all-done.2.side_ref = bf16[8,192,128]{2,1,0:T(8,128)(2,1)S(1)} async-done(((bf16[8,192,128]{2,1,0:T(8,128)(2,1)}), bf16[8,192,128]{2,1,0:T(8,128)(2,1)S(1)}, u32[]{:S(2)}, u32[]{:S(2)}) %all-to-all-start.2) | async-done | bytes 393248 | tf_op jit(solution)/shard_map/all_to_all | solution.py:539
  76.6 3.4 %all-to-all-start.1 = ((bf16[8,128,128]{2,1,0:T(8,128)(2,1)}), bf16[8,128,128]{2,1,0:T(8,128)(2,1)S(1)}, u32[]{:S(2)}, u32[]{:S(2)}) async-start(bf16[8,128,128]{2,1,0:T(8,128)(2,1)} %get-tuple-element.25), calls=%async_computation.1 | async-start | bytes 524288 | tf_op jit(solution)/shard_map/all_to_all | solution.py:542
  80.0 12.2 %all-to-all-done.1.own_ref = bf16[8,128,128]{2,1,0:T(8,128)(2,1)S(1)} async-done(((bf16[8,128,128]{2,1,0:T(8,128)(2,1)}), bf16[8,128,128]{2,1,0:T(8,128)(2,1)S(1)}, u32[]{:S(2)}, u32[]{:S(2)}) %all-to-all-start.1) | async-done | bytes 262176 | tf_op jit(solution)/shard_map/all_to_all | solution.py:542
  92.2 1.7 %solve.1 = (bf16[16,128]{1,0:T(8,128)(2,1)S(1)}, bf16[128,128]{1,0:T(8,128)(2,1)S(1)}, bf16[128,128]{1,0:T(8,128)(2,1)S(1)}, bf16[2,128,16]{2,1,0:T(8,128)(2,1)S(1)}) custom-call(s32[1]{0:T(128)} %bitcast.1.me_ref, bf16[8,128,128]{2,1,0:T(8,128)(2,1)S(1)} %all-to-all-done.1.own_ref, bf16[8,192,128]{2,1,0:T(8,128)(2,1)S(1)} %all-to-all-done.2.side_ref), custom_call_target="tpu_custom_call" | custom-call | tf_op jit(solution)/shard_map/solve/pallas_call | solution.py:440
  93.9 0.0 copy-start
  93.9 0.6 copy-done
  94.5 0.6 copy-done.1
  95.1 0.6 copy-done.2
  95.8 0.6 copy-done.3
  96.3 5.0 %part.3 = f32[16,144,256]{2,1,0:T(8,128)} custom-call(s32[1]{0:T(128)} %bitcast.8.refs_0_, bf16[16,128]{1,0:T(8,128)(2,1)} %copy-done.3, bf16[128,128]{1,0:T(8,128)(2,1)} %copy-done.1, bf16[128,128]{1,0:T(8,128)(2,1)} %copy-done.2, bf16[2,128,16]{2,1,0:T(8,128)(2,1)} %copy-done, bf16[128,8192]{1,0:T(8,128)(2,1)} %get-tuple-element.32.refs_5_, ...), custom_call_target="tpu_custom_call" | custom-call | tf_op jit(solution)/shard_map/part/pallas_call | solution.py:87
  101.3 0.6 collective-permute-start.15
  101.9 5.0 %part.2 = f32[16,144,256]{2,1,0:T(8,128)} custom-call(s32[1]{0:T(128)} %bitcast.refs_0_, bf16[16,128]{1,0:T(8,128)(2,1)} %copy-done.3, bf16[128,128]{1,0:T(8,128)(2,1)} %copy-done.1, bf16[128,128]{1,0:T(8,128)(2,1)} %copy-done.2, bf16[2,128,16]{2,1,0:T(8,128)(2,1)} %copy-done, bf16[128,8192]{1,0:T(8,128)(2,1)} %get-tuple-element.32.refs_5_, ...), custom_call_target="tpu_custom_call" | custom-call | tf_op jit(solution)/shard_map/part/pallas_call | solution.py:87
  106.9 2.7 %add_convert_fusion = bf16[16,144,256]{2,1,0:T(8,128)(2,1)S(1)} fusion(f32[16,144,256]{2,1,0:T(8,128)} %part.2, f32[16,144,256]{2,1,0:T(8,128)} %collective-permute-done.15), kind=kLoop, calls=%fused_computation.1 | loop fusion | flops 1179648 | bytes 5898240 | tf_op jit(solution)/shard_map/convert_element_type | solution.py:548
  109.6 25.0 %all_to_all.30 = bf16[16,144,256]{2,1,0:T(8,128)(2,1)S(1)} all-to-all(bf16[16,144,256]{2,1,0:T(8,128)(2,1)S(1)} %add_convert_fusion), channel_id=1, replica_groups=mesh['section'=8,'y'=4,'x'=4,'core'=2] {'y','x'}, dimensions={0} | all-to-all | bytes 2359296 | tf_op jit(solution)/shard_map/all_to_all | solution.py:548
  134.6 0.2 convert_reduce_fusion
  134.7 0.7 slice.17
  135.4 3.4 %all-to-all-start.4 = ((f32[8,16,256]{2,1,0:T(8,128)}), f32[8,16,256]{2,1,0:T(8,128)S(1)}, u32[]{:S(2)}, u32[]{:S(2)}) async-start(f32[8,16,256]{2,1,0:T(8,128)} %bitcast.9), calls=%async_computation.4 | async-start | bytes 262144 | tf_op jit(solution)/shard_map/all_to_all | solution.py:551
  138.8 7.7 %all-to-all-done.4 = f32[8,16,256]{2,1,0:T(8,128)S(1)} async-done(((f32[8,16,256]{2,1,0:T(8,128)}), f32[8,16,256]{2,1,0:T(8,128)S(1)}, u32[]{:S(2)}, u32[]{:S(2)}) %all-to-all-start.4) | async-done | bytes 131104 | tf_op jit(solution)/shard_map/all_to_all | solution.py:551
  146.5 12.0 %all_to_all.31 = f32[16,32,256]{2,1,0:T(8,128)S(1)} all-to-all(f32[16,32,256]{2,1,0:T(8,128)S(1)} %broadcast_in_dim.21), channel_id=1, replica_groups=mesh['section'=8,'y'=4,'x'=4,'core'=2] {'y','x'}, dimensions={0} | all-to-all | bytes 1048576 | tf_op jit(solution)/shard_map/all_to_all | solution.py:554
  158.5 3.8 %collective-permute-start.16 = (f32[32,4096]{1,0:T(8,128)S(1)}, f32[32,4096]{1,0:T(8,128)S(1)}, u32[]{:S(2)}, u32[]{:S(2)}) collective-permute-start(f32[32,4096]{1,0:T(8,128)S(1)} %bitcast.24), channel_id=1, source_target_pairs={{0,1},{1,0},{2,3},{3,2},{4,5},{5,4},{6,7},{7,6},{8,9},{9,8},{10,11... | collective-permute-start | bytes 1572872 | tf_op jit(solution)/shard_map/ppermute | solution.py:556
  162.3 1.5 collective-permute-done.16
  163.9 0.1 broadcast_select_fusion
  163.9 1.0 fusion.2
  (43 shorter events, 0.2 us)
Async XLA Ops:
  6.0 8.8 %copy-start.5 = (bf16[1,16,8192]{2,1,0:T(8,128)(2,1)S(1)}, bf16[1,16,8192]{2,1,0:T(8,128)(2,1)}, u32[]{:S(2)}) copy-start(bf16[1,16,8192]{2,1,0:T(8,128)(2,1)} %param.11) | copy-start | bytes 786436
  6.1 51.9 %all-to-all-start = ((bf16[32,136,256]{2,1,0:T(8,128)(2,1)}), bf16[32,136,256]{2,1,0:T(8,128)(2,1)}, u32[]{:S(2)}, u32[]{:S(2)}) async-start(bf16[32,136,256]{2,1,0:T(8,128)(2,1)} %order.1), calls=%async_computation | async-start | bytes 4456448 | tf_op jit(solution)/shard_map/all_to_all | solution.py:528
  14.9 36.4 %copy-start.4 = (bf16[16,4096]{1,0:T(8,128)(2,1)}, bf16[16,4096]{1,0:T(8,128)(2,1)S(1)}, u32[]{:S(2)}) copy-start(bf16[16,4096]{1,0:T(8,128)(2,1)S(1)} %dynamic-slice_bitcast_fusion.refs_12_) | copy-start | bytes 393220
  14.9 8.2 %collective-permute-start.1 = (bf16[16,4096]{1,0:T(8,128)(2,1)S(1)}, bf16[16,4096]{1,0:T(8,128)(2,1)S(1)}, u32[]{:S(2)}, u32[]{:S(2)}) collective-permute-start(bf16[16,4096]{1,0:T(8,128)(2,1)S(1)} %dynamic-slice_bitcast_fusion.refs_12_), channel_id=1, source_target_pairs={{0,224},{32,0},{64,32},{96,64},{128,96},{160,128},{192,160},{224,1... | collective-permute-start | bytes 393224 | tf_op jit(solution)/shard_map/ppermute | solution.py:53
  20.5 5.8 %collective-permute-start = (bf16[16,4096]{1,0:T(8,128)(2,1)S(1)}, bf16[16,4096]{1,0:T(8,128)(2,1)S(1)}, u32[]{:S(2)}, u32[]{:S(2)}) collective-permute-start(bf16[16,4096]{1,0:T(8,128)(2,1)S(1)} %dynamic-slice_bitcast_fusion.refs_12_), channel_id=1, source_target_pairs={{0,32},{32,64},{64,96},{96,128},{128,160},{160,192},{192,224},{224... | collective-permute-start | bytes 393224 | tf_op jit(solution)/shard_map/ppermute | solution.py:50
  23.1 28.1 %copy-start.6 = (bf16[16,4096]{1,0:T(8,128)(2,1)}, bf16[16,4096]{1,0:T(8,128)(2,1)S(1)}, u32[]{:S(2)}) copy-start(bf16[16,4096]{1,0:T(8,128)(2,1)S(1)} %collective-permute-done.1.refs_5_) | copy-start | bytes 393220
  26.3 25.0 %copy-start.7 = (bf16[16,4096]{1,0:T(8,128)(2,1)}, bf16[16,4096]{1,0:T(8,128)(2,1)S(1)}, u32[]{:S(2)}) copy-start(bf16[16,4096]{1,0:T(8,128)(2,1)S(1)} %collective-permute-done.refs_11_) | copy-start | bytes 393220
  26.3 5.4 %collective-permute-start.4 = (bf16[16,4096]{1,0:T(8,128)(2,1)S(1)}, bf16[16,4096]{1,0:T(8,128)(2,1)S(1)}, u32[]{:S(2)}, u32[]{:S(2)}) collective-permute-start(bf16[16,4096]{1,0:T(8,128)(2,1)S(1)} %collective-permute-done.refs_11_), channel_id=1, source_target_pairs={{0,32},{32,64},{64,96},{96,128},{128,160},{160,192},{192,224},{224... | collective-permute-start | bytes 393224 | tf_op jit(solution)/shard_map/ppermute | solution.py:50
  26.3 8.0 %collective-permute-start.2 = (bf16[16,4096]{1,0:T(8,128)(2,1)S(1)}, bf16[16,4096]{1,0:T(8,128)(2,1)S(1)}, u32[]{:S(2)}, u32[]{:S(2)}) collective-permute-start(bf16[16,4096]{1,0:T(8,128)(2,1)S(1)} %collective-permute-done.1.refs_5_), channel_id=1, source_target_pairs={{0,224},{32,0},{64,32},{96,64},{128,96},{160,128},{192,160},{224,1... | collective-permute-start | bytes 393224 | tf_op jit(solution)/shard_map/ppermute | solution.py:53
  31.8 19.5 %copy-start.8 = (bf16[16,4096]{1,0:T(8,128)(2,1)}, bf16[16,4096]{1,0:T(8,128)(2,1)S(1)}, u32[]{:S(2)}) copy-start(bf16[16,4096]{1,0:T(8,128)(2,1)S(1)} %collective-permute-done.4.refs_10_) | copy-start | bytes 393220
  31.8 5.6 %collective-permute-start.5 = (bf16[16,4096]{1,0:T(8,128)(2,1)S(1)}, bf16[16,4096]{1,0:T(8,128)(2,1)S(1)}, u32[]{:S(2)}, u32[]{:S(2)}) collective-permute-start(bf16[16,4096]{1,0:T(8,128)(2,1)S(1)} %collective-permute-done.4.refs_10_), channel_id=1, source_target_pairs={{0,32},{32,64},{64,96},{96,128},{128,160},{160,192},{192,224},{224... | collective-permute-start | bytes 393224 | tf_op jit(solution)/shard_map/ppermute | solution.py:50
  31.8 5.6 %collective-permute-start.14 = (bf16[16,4096]{1,0:T(8,128)(2,1)S(1)}, bf16[16,4096]{1,0:T(8,128)(2,1)S(1)}, u32[]{:S(2)}, u32[]{:S(2)}) collective-permute-start(bf16[16,4096]{1,0:T(8,128)(2,1)S(1)} %dynamic-slice_bitcast_fusion.refs_12_), channel_id=1, source_target_pairs={{0,1},{1,0},{2,3},{3,2},{4,5},{5,4},{6,7},{7,6},{8,9},{9,8},{10,11... | collective-permute-start | bytes 393224 | tf_op jit(solution)/shard_map/ppermute | solution.py:535
  33.9 6.3 %collective-permute-start.7 = (bf16[16,4096]{1,0:T(8,128)(2,1)S(1)}, bf16[16,4096]{1,0:T(8,128)(2,1)S(1)}, u32[]{:S(2)}, u32[]{:S(2)}) collective-permute-start(bf16[16,4096]{1,0:T(8,128)(2,1)S(1)} %collective-permute-done.1.refs_5_), channel_id=1, source_target_pairs={{0,1},{1,0},{2,3},{3,2},{4,5},{5,4},{6,7},{7,6},{8,9},{9,8},{10,11... | collective-permute-start | bytes 393224 | tf_op jit(solution)/shard_map/ppermute | solution.py:535
  33.9 6.3 %collective-permute-start.13 = (bf16[16,4096]{1,0:T(8,128)(2,1)S(1)}, bf16[16,4096]{1,0:T(8,128)(2,1)S(1)}, u32[]{:S(2)}, u32[]{:S(2)}) collective-permute-start(bf16[16,4096]{1,0:T(8,128)(2,1)S(1)} %collective-permute-done.refs_11_), channel_id=1, source_target_pairs={{0,1},{1,0},{2,3},{3,2},{4,5},{5,4},{6,7},{7,6},{8,9},{9,8},{10,11... | collective-permute-start | bytes 393224 | tf_op jit(solution)/shard_map/ppermute | solution.py:535
  34.4 16.9 %copy-start.9 = (bf16[16,4096]{1,0:T(8,128)(2,1)}, bf16[16,4096]{1,0:T(8,128)(2,1)S(1)}, u32[]{:S(2)}) copy-start(bf16[16,4096]{1,0:T(8,128)(2,1)S(1)} %collective-permute-done.2.refs_6_) | copy-start | bytes 393220
  34.4 6.3 %collective-permute-start.3 = (bf16[16,4096]{1,0:T(8,128)(2,1)S(1)}, bf16[16,4096]{1,0:T(8,128)(2,1)}, u32[]{:S(2)}, u32[]{:S(2)}) collective-permute-start(bf16[16,4096]{1,0:T(8,128)(2,1)S(1)} %collective-permute-done.2.refs_6_), channel_id=1, source_target_pairs={{0,224},{32,0},{64,32},{96,64},{128,96},{160,128},{192,160},{224,1... | collective-permute-start | bytes 393224 | tf_op jit(solution)/shard_map/ppermute | solution.py:53
  37.3 14.0 %copy-start.10 = (bf16[16,4096]{1,0:T(8,128)(2,1)}, bf16[16,4096]{1,0:T(8,128)(2,1)S(1)}, u32[]{:S(2)}) copy-start(bf16[16,4096]{1,0:T(8,128)(2,1)S(1)} %collective-permute-done.5.refs_9_) | copy-start | bytes 393220
  37.3 5.1 %collective-permute-start.6 = (bf16[16,4096]{1,0:T(8,128)(2,1)S(1)}, bf16[16,4096]{1,0:T(8,128)(2,1)}, u32[]{:S(2)}, u32[]{:S(2)}) collective-permute-start(bf16[16,4096]{1,0:T(8,128)(2,1)S(1)} %collective-permute-done.5.refs_9_), channel_id=1, source_target_pairs={{0,32},{32,64},{64,96},{96,128},{128,160},{160,192},{192,224},{224... | collective-permute-start | bytes 393224 | tf_op jit(solution)/shard_map/ppermute | solution.py:50
  37.4 14.0 %copy-start.11 = (bf16[16,4096]{1,0:T(8,128)(2,1)}, bf16[16,4096]{1,0:T(8,128)(2,1)S(1)}, u32[]{:S(2)}) copy-start(bf16[16,4096]{1,0:T(8,128)(2,1)S(1)} %collective-permute-done.14.refs_20_) | copy-start | bytes 393220
  37.4 13.8 %collective-permute-start.8 = (bf16[16,4096]{1,0:T(8,128)(2,1)S(1)}, bf16[16,4096]{1,0:T(8,128)(2,1)}, u32[]{:S(2)}, u32[]{:S(2)}) collective-permute-start(bf16[16,4096]{1,0:T(8,128)(2,1)S(1)} %collective-permute-done.2.refs_6_), channel_id=1, source_target_pairs={{0,1},{1,0},{2,3},{3,2},{4,5},{5,4},{6,7},{7,6},{8,9},{9,8},{10,11... | collective-permute-start | bytes 393224 | tf_op jit(solution)/shard_map/ppermute | solution.py:535
  40.1 2.3 %copy-start.12 = (bf16[16,4096]{1,0:T(8,128)(2,1)}, bf16[16,4096]{1,0:T(8,128)(2,1)S(1)}, u32[]{:S(2)}) copy-start(bf16[16,4096]{1,0:T(8,128)(2,1)S(1)} %collective-permute-done.7.refs_13_) | copy-start | bytes 393220
  40.1 11.1 %collective-permute-start.12 = (bf16[16,4096]{1,0:T(8,128)(2,1)S(1)}, bf16[16,4096]{1,0:T(8,128)(2,1)}, u32[]{:S(2)}, u32[]{:S(2)}) collective-permute-start(bf16[16,4096]{1,0:T(8,128)(2,1)S(1)} %collective-permute-done.4.refs_10_), channel_id=1, source_target_pairs={{0,1},{1,0},{2,3},{3,2},{4,5},{5,4},{6,7},{7,6},{8,9},{9,8},{10,11... | collective-permute-start | bytes 393224 | tf_op jit(solution)/shard_map/ppermute | solution.py:535
  40.3 6.1 %copy-start.13 = (bf16[16,4096]{1,0:T(8,128)(2,1)}, bf16[16,4096]{1,0:T(8,128)(2,1)S(1)}, u32[]{:S(2)}) copy-start(bf16[16,4096]{1,0:T(8,128)(2,1)S(1)} %collective-permute-done.13.refs_19_) | copy-start | bytes 393220
  40.3 11.0 %collective-permute-start.11 = (bf16[16,4096]{1,0:T(8,128)(2,1)S(1)}, bf16[16,4096]{1,0:T(8,128)(2,1)}, u32[]{:S(2)}, u32[]{:S(2)}) collective-permute-start(bf16[16,4096]{1,0:T(8,128)(2,1)S(1)} %collective-permute-done.5.refs_9_), channel_id=1, source_target_pairs={{0,1},{1,0},{2,3},{3,2},{4,5},{5,4},{6,7},{7,6},{8,9},{9,8},{10,11... | collective-permute-start | bytes 393224 | tf_op jit(solution)/shard_map/ppermute | solution.py:535
  40.7 10.6 %collective-permute-start.9 = (bf16[16,4096]{1,0:T(8,128)(2,1)}, bf16[16,4096]{1,0:T(8,128)(2,1)}, u32[]{:S(2)}, u32[]{:S(2)}) collective-permute-start(bf16[16,4096]{1,0:T(8,128)(2,1)} %collective-permute-done.3.refs_7_), channel_id=1, source_target_pairs={{0,1},{1,0},{2,3},{3,2},{4,5},{5,4},{6,7},{7,6},{8,9},{9,8},{10,11... | collective-permute-start | bytes 393224 | tf_op jit(solution)/shard_map/ppermute | solution.py:535
  42.5 8.8 %collective-permute-start.10 = (bf16[16,4096]{1,0:T(8,128)(2,1)}, bf16[16,4096]{1,0:T(8,128)(2,1)}, u32[]{:S(2)}, u32[]{:S(2)}) collective-permute-start(bf16[16,4096]{1,0:T(8,128)(2,1)} %collective-permute-done.6.refs_8_), channel_id=1, source_target_pairs={{0,1},{1,0},{2,3},{3,2},{4,5},{5,4},{6,7},{7,6},{8,9},{9,8},{10,11... | collective-permute-start | bytes 393224 | tf_op jit(solution)/shard_map/ppermute | solution.py:535
  58.0 18.6 %all-to-all-start.2 = ((bf16[8,192,128]{2,1,0:T(8,128)(2,1)}), bf16[8,192,128]{2,1,0:T(8,128)(2,1)S(1)}, u32[]{:S(2)}, u32[]{:S(2)}) async-start(bf16[8,192,128]{2,1,0:T(8,128)(2,1)} %side.1), calls=%async_computation.2 | async-start | bytes 786432 | tf_op jit(solution)/shard_map/all_to_all | solution.py:539
  76.6 15.6 %all-to-all-start.1 = ((bf16[8,128,128]{2,1,0:T(8,128)(2,1)}), bf16[8,128,128]{2,1,0:T(8,128)(2,1)S(1)}, u32[]{:S(2)}, u32[]{:S(2)}) async-start(bf16[8,128,128]{2,1,0:T(8,128)(2,1)} %get-tuple-element.25), calls=%async_computation.1 | async-start | bytes 524288 | tf_op jit(solution)/shard_map/all_to_all | solution.py:542
  93.9 0.6 copy-start
  94.5 0.6 copy-start.1
  95.1 0.6 copy-start.2
  95.8 0.6 copy-start.3
  101.3 5.6 %collective-permute-start.15 = (f32[16,144,256]{2,1,0:T(8,128)}, f32[16,144,256]{2,1,0:T(8,128)}, u32[]{:S(2)}, u32[]{:S(2)}) collective-permute-start(f32[16,144,256]{2,1,0:T(8,128)} %part.3), channel_id=1, source_target_pairs={{0,1},{1,0},{2,3},{3,2},{4,5},{5,4},{6,7},{7,6},{8,9},{9,8},{10,11... | collective-permute-start | bytes 7077896 | tf_op jit(solution)/shard_map/ppermute | solution.py:546
  135.4 11.1 %all-to-all-start.4 = ((f32[8,16,256]{2,1,0:T(8,128)}), f32[8,16,256]{2,1,0:T(8,128)S(1)}, u32[]{:S(2)}, u32[]{:S(2)}) async-start(f32[8,16,256]{2,1,0:T(8,128)} %bitcast.9), calls=%async_computation.4 | async-start | bytes 262144 | tf_op jit(solution)/shard_map/all_to_all | solution.py:551
  158.5 5.3 %collective-permute-start.16 = (f32[32,4096]{1,0:T(8,128)S(1)}, f32[32,4096]{1,0:T(8,128)S(1)}, u32[]{:S(2)}, u32[]{:S(2)}) collective-permute-start(f32[32,4096]{1,0:T(8,128)S(1)} %bitcast.24), channel_id=1, source_target_pairs={{0,1},{1,0},{2,3},{3,2},{4,5},{5,4},{6,7},{7,6},{8,9},{9,8},{10,11... | collective-permute-start | bytes 1572872 | tf_op jit(solution)/shard_map/ppermute | solution.py:556

commit v4 on v3

--- a/solution.py
+++ b/solution.py
@@ -74,7 +74,7 @@
     return pl.BlockSpec(memory_space=pltpu.VMEM)
 
 
-def call(kernel, name, out_shape, scalars, arrays, scratch=()):
+def call(kernel, name, out_shape, scalars, arrays, scratch=(), in_place_outs=0):
     count, total = len(scalars), len(arrays)
     outs = len(out_shape)
 
@@ -88,7 +88,7 @@
         body,
         out_shape=out_shape,
         in_specs=[smem()] * count + [in_place()] * total,
-        out_specs=[vmem()] * outs,
+        out_specs=[in_place()] * in_place_outs + [vmem()] * (outs - in_place_outs),
         scratch_shapes=[pltpu.VMEM(a.shape, a.dtype) for a in arrays]
         + [pltpu.SemaphoreType.DMA((PIECES,)) for _ in arrays]
         + list(scratch),
@@ -98,6 +98,7 @@
 
 
 PIECES = 8
+AHEAD = 2
 
 
 def whole(item):
@@ -299,11 +300,17 @@
     whole(up_in).start()
     stream_loads = [columns_piece(stream_in, i, i * width, width) for i in range(PIECES)]
     ref_loads = [leading_piece(refs_in, i, i * per_piece, per_piece) for i in range(PIECES)]
-    for i in range(PIECES):
-        stream_loads[i].start()
-        ref_loads[i].start()
-    for item in (*mine, *other):
-        whole(item).start()
+
+    def start(i):
+        if i < PIECES:
+            stream_loads[i].start()
+            ref_loads[i].start()
+        else:
+            for item in (*mine, *other)[2 * count * (i - PIECES) // AHEAD : 2 * count * (i - PIECES + 1) // AHEAD]:
+                whole(item).start()
+
+    for i in range(AHEAD):
+        start(i)
     whole(lrt_in).wait()
     whole(up_in).wait()
     low_rank = lrt_in[1][...].astype(f32).T.astype(bf16)
@@ -320,6 +327,7 @@
         for i in range(PIECES):
             stream_loads[i].wait()
             ref_loads[i].wait()
+            start(i + AHEAD)
             for j in range(i * per_piece, (i + 1) * per_piece):
                 columns = slice(j * chunk, (j + 1) * chunk)
                 out = stream_ref[:, columns].astype(f32) + nn(low_rank, up_ref[:, columns])
@@ -386,8 +394,7 @@
     )
 
 
-def solve_kernel(width, rank, me_ref, own_ref, side_ref, low_ref, lrt_ref, coef_ref, k_ref, acc):
-    me = me_ref[0]
+def solve(width, rank, me, own_ref, side_ref, low_ref, lrt_ref, coef_ref, k_ref, acc):
     layers, rows, _ = own_ref.shape
     acc[...] = jnp.zeros_like(acc)
     for j in range(layers):
@@ -435,47 +442,15 @@
     k_ref[1] = k_lo
 
 
-def solve(width, rank, me, own, side):
-    layers, rows, tokens = own.shape
-    return pl.pallas_call(
-        functools.partial(solve_kernel, width, rank),
-        out_shape=(
-            jax.ShapeDtypeStruct((rank, tokens), bf16),
-            jax.ShapeDtypeStruct((rows, tokens), bf16),
-            jax.ShapeDtypeStruct((rows, tokens), bf16),
-            jax.ShapeDtypeStruct((2, rows, rank), bf16),
-        ),
-        in_specs=[smem(), vmem(), vmem()],
-        out_specs=(vmem(),) * 4,
-        scratch_shapes=[pltpu.VMEM((rows, tokens), f32)],
-        compiler_params=params(8),
-        name="solve",
-    )(me, own, side)
-
-
-def part_kernel(start_ref, low_in, lrt_in, coef_in, k_in, own_in, stream_in, normed_in, dg_in, out_ref):
-    start = start_ref[0]
-    chunks, _, chunk = out_ref.shape
-    rows = lrt_in[1].shape[0]
-    group = min(4, chunks)
+def part(start, loads, low, lrt, coef, k, own_in, stream_in, normed_in, dg_in, out_ref, buffer, out_sem):
+    chunks, _, chunk = buffer.shape
+    rows = lrt.shape[0]
+    group = chunks // len(loads)
     width = group * chunk
-    small = (low_in, lrt_in, coef_in, k_in)
-    large = (own_in, stream_in, normed_in, dg_in)
-    for item in small:
-        whole(item).start()
-    loads = [
-        [columns_piece(item, i, pl.multiple_of(start + i * width, width), width) for item in large]
-        for i in range(chunks // group)
-    ]
-    for piece in loads:
-        for load in piece:
-            load.start()
-    for item in small:
-        whole(item).wait()
-    left = jnp.concatenate([lrt_in[1][...], coef_in[1][...]], axis=1)
-    k_hi, k_lo = k_in[1][0].astype(f32), k_in[1][1].astype(f32)
+    left = jnp.concatenate([lrt, coef], axis=1)
+    k_hi, k_lo = k[0].astype(f32), k[1].astype(f32)
     k = jnp.concatenate([k_hi, k_hi, k_lo], axis=1).astype(bf16)
-    low = low_in[1][...]
+    stores = []
     for i, piece in enumerate(loads):
         for load in piece:
             load.wait()
@@ -486,19 +461,81 @@
         up = nn(left, right) + nn(k, dg)
         down = nn(low, normed_in[1][:, columns])
         for j in range(group):
-            out_ref[i * group + j, :rows, :] = up[:, j * chunk : (j + 1) * chunk]
-            out_ref[i * group + j, rows:, :] = down[:, j * chunk : (j + 1) * chunk]
-
-
-def part(start, chunks, chunk, *arrays):
-    low, lrt = arrays[:2]
-    (found,) = call(
-        part_kernel,
-        "part",
-        (jax.ShapeDtypeStruct((chunks, lrt.shape[0] + low.shape[0], chunk), f32),),
-        (start,),
-        arrays,
+            buffer[i * group + j, :rows, :] = up[:, j * chunk : (j + 1) * chunk]
+            buffer[i * group + j, rows:, :] = down[:, j * chunk : (j + 1) * chunk]
+        here = pl.ds(i * group, group)
+        stores.append(pltpu.make_async_copy(buffer.at[here], out_ref.at[here], out_sem.at[i]))
+        stores[-1].start()
+    for store in stores:
+        store.wait()
+
+
+def part_loads(start, large, chunks, chunk):
+    pieces = min(4, chunks)
+    width = chunks // pieces * chunk
+    return [
+        [columns_piece(item, i, pl.multiple_of(start + i * width, width), width) for item in large]
+        for i in range(pieces)
+    ]
+
+
+def given_kernel(rank, meta_ref, own_up_in, side_in, *refs):
+    large, (out_ref, low_ref, lrt_ref, coef_ref, k_ref, acc, buffer, out_sem) = refs[:4], refs[4:]
+    start, me = meta_ref[0], meta_ref[1]
+    loads = part_loads(start, large, buffer.shape[0], buffer.shape[2])
+    whole(own_up_in).start()
+    whole(side_in).start()
+    for load in loads:
+        for item in load:
+            item.start()
+    whole(own_up_in).wait()
+    whole(side_in).wait()
+    solve(large[0][0].shape[1], rank, me, own_up_in[1], side_in[1], low_ref, lrt_ref, coef_ref, k_ref, acc)
+    part(start, loads, low_ref[...], lrt_ref[...], coef_ref[...], k_ref, *large, out_ref, buffer, out_sem)
+
+
+def kept_kernel(meta_ref, low_in, lrt_in, coef_in, k_in, *refs):
+    large, (out_ref, buffer, out_sem) = refs[:4], refs[4:]
+    start = meta_ref[0]
+    loads = part_loads(start, large, buffer.shape[0], buffer.shape[2])
+    for item in (low_in, lrt_in, coef_in, k_in):
+        whole(item).start()
+    for load in loads:
+        for item in load:
+            item.start()
+    for item in (low_in, lrt_in, coef_in, k_in):
+        whole(item).wait()
+    part(start, loads, low_in[1][...], lrt_in[1][...], coef_in[1][...], k_in[1], *large, out_ref, buffer, out_sem)
+
+
+def part_shapes(chunks, chunk, rows, rank):
+    shape = (chunks, rows + rank, chunk)
+    return jax.ShapeDtypeStruct(shape, f32), (pltpu.VMEM(shape, f32), pltpu.SemaphoreType.DMA((PIECES,)))
+
+
+def given_part(meta, chunks, chunk, rank, own_up, side, *large):
+    _, rows, tokens = own_up.shape
+    shape, scratch = part_shapes(chunks, chunk, rows, rank)
+    return call(
+        functools.partial(given_kernel, rank),
+        "given",
+        (
+            shape,
+            jax.ShapeDtypeStruct((rank, tokens), bf16),
+            jax.ShapeDtypeStruct((rows, tokens), bf16),
+            jax.ShapeDtypeStruct((rows, tokens), bf16),
+            jax.ShapeDtypeStruct((2, rows, rank), bf16),
+        ),
+        (meta,),
+        (own_up, side, *large),
+        (pltpu.VMEM((rows, tokens), f32),) + scratch,
+        in_place_outs=1,
     )
+
+
+def kept_part(meta, chunks, chunk, low, lrt, coef, k, *large):
+    shape, scratch = part_shapes(chunks, chunk, lrt.shape[0], low.shape[0])
+    (found,) = call(kept_kernel, "kept", (shape,), (meta,), (low, lrt, coef, k, *large), scratch, in_place_outs=1)
     return found
 
 
@@ -526,31 +563,33 @@
     meta = jnp.stack([core, tile_harmful_flag[0], tile_valid_count[0]]).astype(jnp.int32)
     ordered = order(tile_reference_position, meta, frozen_reference_states[0])
     refs = lax.all_to_all(ordered, DP, split_axis=0, concat_axis=0, tiled=True)
-    gate, stream, down, up, gains = lax.optimization_barrier(
+    _, stream, down, up, gains = lax.optimization_barrier(
         (ordered, layer_input_states[0, 0], adapter_down_weight[0], adapter_up_weight[0], layer_norm_gain)
     )
 
     up_half = lax.dynamic_slice_in_dim(adapter_up_weight[0], core * half, half, axis=1)
-    mine = ring_gather(up_half, SEC, gate)[::-1]
+    normed, lrt, irms, dg = forward(stream, down, gains)
+    mine = ring_gather(up_half, SEC, lrt)[::-1]
     other = [lax.ppermute(block, "core", swap) for block in mine]
 
-    normed, lrt, irms, dg = forward(stream, down, gains)
     side = side_of(meta, stream, dg, lrt, irms, mine, other)
     sides = lax.all_to_all(side, SEC, 0, 0, tiled=True)
 
     own, own_up = own_gradient(meta, refs, stream, up, lrt, mine, other)
     own_up = lax.all_to_all(own_up, SEC, 0, 0, tiled=True)
-    low, lrt_all, coef, k = solve(width, rank, me[None], own_up, sides)
-
-    given = part(((1 - core) * half)[None], chips, chunk, low, lrt_all, coef, k, own, stream, normed, dg)
+
+    large = (own, stream, normed, dg)
+    away = jnp.stack([(1 - core) * half, me]).astype(jnp.int32)
+    here = (core * half)[None].astype(jnp.int32)
+    given, *coefs = given_part(away, chips, chunk, rank, own_up, sides, *large)
     received = lax.ppermute(given, "core", swap)
-    kept = part((core * half)[None], chips, chunk, low, lrt_all, coef, k, own, stream, normed, dg)
+    kept = kept_part(here, chips, chunk, *coefs, *large)
     blocks = lax.all_to_all((kept + received).astype(bf16), CHIPS, 0, 0, tiled=True)
-    summed = jnp.sum(blocks.astype(f32), axis=0)
-
-    by_layer = lax.all_to_all(summed[: layers * rank].reshape(layers, rank, chunk), SEC, 0, 0, tiled=True)
-    final = jnp.concatenate([summed[layers * rank :], jnp.sum(by_layer, axis=0)], axis=0)
-
+    grad_up = jnp.sum(blocks[:, : layers * rank].astype(f32), axis=0)
+    grad_down = jnp.sum(blocks[:, layers * rank :].astype(f32), axis=0)
+
+    by_layer = lax.all_to_all(grad_up.reshape(layers, rank, chunk), SEC, 0, 0, tiled=True)
+    final = jnp.concatenate([grad_down, jnp.sum(by_layer, axis=0)], axis=0)
     wide = lax.all_to_all(jnp.broadcast_to(final, (chips,) + final.shape), CHIPS, 0, 0, tiled=True)
     mine = wide.transpose(1, 0, 2).reshape(2 * rank, half)
     other = lax.ppermute(mine, "core", swap)

time: 166 us -> 161 us (0.970)
  waiting for transfers between devices: 36.9 us -> 29 us
  Pallas kernels: 36.3 us -> 38.5 us
  local copies, waits for them, and re-layouts: 3.25 us -> 1.48 us
    pallas_call x5, Pallas kernels: 31.1 us -> 34.9 us  [call(): pl.pallas_call(body, out_shape=out_shape, in_specs=[smem()] * count + [in...]
    ppermute x3, waiting for transfers between devices: 2.59 us -> 0.01 us  [ring_gather(): bwd = lax.ppermute(bwd, axis, down)]
    ppermute x4, waiting for transfers between devices: 7.37 us -> 4.94 us  [ring_gather(): fwd = lax.ppermute(fwd, axis, up)]
    all_to_all x1, waiting for transfers between devices: 12.2 us -> 10.1 us  [shards(): own_up = lax.all_to_all(own_up, SEC, 0, 0, tiled=True)]
    all_to_all x1, waiting for transfers between devices: 5.53 us -> 3.55 us  [shards(): sides = lax.all_to_all(side, SEC, 0, 0, tiled=True)]
    pallas_call x1 -> x0, Pallas kernels: 1.69 us -> none  [solve(): pl.pallas_call(functools.partial(solve_kernel, width, rank), out_shape=(j...]
  transfers between devices with their start and end apart: 21 -> 21, of which waited for: 8 -> 9; matrix products, arithmetic and copies ran while one was open for 0% -> 0% of each run, Pallas kernels for 16% -> 17%
where the time goes in v4:
time: 161 us; the launch traced here: 160 us
  starting transfers between devices  46.4 us (29%)
  Pallas kernels  38.5 us (24%)
  blocking collectives  36.6 us (23%)
  waiting for transfers between devices  29 us (18%)
  other arithmetic  5.83 us (4%)
  between operations  2.27 us (1%)
    pallas_call x5, Pallas kernels, call(): pl.pallas_call(body, out_shape=out_shape, in_specs=[smem()] * count + [in...  34.9 us
    all_to_all x1, blocking collectives, shards(): lax.all_to_all((kept + received).astype(bf16), CHIPS, 0, 0, tiled=True)  24.5 us
    all_to_all x1, blocking collectives, shards(): lax.all_to_all(jnp.broadcast_to(final, (chips,) + final.shape), CHIPS, 0,...  12.1 us
    ppermute x3, starting transfers between devices, ring_gather(): bwd = lax.ppermute(bwd, axis, down)  11.3 us
    all_to_all x1, waiting for transfers between devices, shards(): own_up = lax.all_to_all(own_up, SEC, 0, 0, tiled=True)  10.1 us
    ppermute x8, starting transfers between devices, shards(): other = [lax.ppermute(block, 'core', swap) for block in mine]  10.1 us
    all_to_all x1, starting transfers between devices, shards(): refs = lax.all_to_all(ordered, DP, split_axis=0, concat_axis=0, tiled=True)  8.78 us
    all_to_all x1, waiting for transfers between devices, shards(): lax.all_to_all(grad_up.reshape(layers, rank, chunk), SEC, 0, 0, tiled=True)  7.84 us
  transfers between devices with their start and end apart: 21, of which 9 were waited for; matrix products, arithmetic and copies ran while one was open for 0% of the time, Pallas kernels for 17%

profile of v4, /device:TPU:1, one launch (start us, length us, event | category | flops | bytes accessed | tf_op | source)
XLA Modules:
  0.0 160.0 jit_solution(10046854773681766194)
XLA Ops:
  1.9 0.6 pad_add_fusion.1.meta_ref.refs_0_
  2.5 3.5 %order.1 = bf16[32,136,256]{2,1,0:T(8,128)(2,1)} custom-call(s32[32]{0:T(128)} %position_ref.1, s32[3]{0:T(128)} %pad_add_fusion.1.meta_ref.refs_0_, bf16[32,128,256]{2,1,0:T(8,128)(2,1)} %bitcast.23), custom_call_target="tpu_custom_call" | custom-call | tf_op jit(solution)/shard_map/order/pallas_call | solution.py:148
  6.1 0.0 copy-start.3
  6.1 8.8 %all-to-all-start = ((bf16[32,136,256]{2,1,0:T(8,128)(2,1)}), bf16[32,136,256]{2,1,0:T(8,128)(2,1)}, u32[]{:S(2)}, u32[]{:S(2)}) async-start(bf16[32,136,256]{2,1,0:T(8,128)(2,1)} %order.1), calls=%async_computation | async-start | bytes 4456448 | tf_op jit(solution)/shard_map/all_to_all | solution.py:565
  14.9 5.7 %collective-permute-start.1 = (bf16[16,4096]{1,0:T(8,128)(2,1)S(1)}, bf16[16,4096]{1,0:T(8,128)(2,1)S(1)}, u32[]{:S(2)}, u32[]{:S(2)}) collective-permute-start(bf16[16,4096]{1,0:T(8,128)(2,1)S(1)} %dynamic-slice_bitcast_fusion.refs_12_), channel_id=1, source_target_pairs={{0,224},{32,0},{64,32},{96,64},{128,96},{160,128},{192,160},{224,1... | collective-permute-start | bytes 393224 | tf_op jit(solution)/shard_map/ppermute | solution.py:53
  20.6 0.0 collective-permute-start
  20.6 4.9 %forward.1 = (bf16[128,8192]{1,0:T(8,128)(2,1)}, bf16[16,128]{1,0:T(8,128)(2,1)}, f32[8,128]{1,0:T(8,128)}, bf16[2,16,8192]{2,1,0:T(8,128)(2,1)}) custom-call(bf16[128,8192]{1,0:T(8,128)(2,1)} %bitcast.18, bf16[16,8192]{1,0:T(8,128)(2,1)} %bitcast.28, f32[1,8192]{1,0:T(1,128)} %refs_2_), custom_call_target="tpu_custom_call" | custom-call | tf_op jit(solution)/shard_map/forward/pallas_call | solution.py:87
  25.5 0.0 collective-permute-done.1.refs_5_
  25.5 0.9 collective-permute-done.refs_11_
  26.4 0.0 collective-permute-start.4
  26.4 2.7 %collective-permute-start.2 = (bf16[16,4096]{1,0:T(8,128)(2,1)S(1)}, bf16[16,4096]{1,0:T(8,128)(2,1)S(1)}, u32[]{:S(2)}, u32[]{:S(2)}) collective-permute-start(bf16[16,4096]{1,0:T(8,128)(2,1)S(1)} %collective-permute-done.1.refs_5_), channel_id=1, source_target_pairs={{0,224},{32,0},{64,32},{96,64},{128,96},{160,128},{192,160},{224,1... | collective-permute-start | bytes 393224 | tf_op jit(solution)/shard_map/ppermute | solution.py:53
  29.0 2.8 %collective-permute-done.4.refs_10_ = bf16[16,4096]{1,0:T(8,128)(2,1)S(1)} collective-permute-done((bf16[16,4096]{1,0:T(8,128)(2,1)S(1)}, bf16[16,4096]{1,0:T(8,128)(2,1)S(1)}, u32[]{:S(2)}, u32[]{:S(2)}) %collective-permute-start.4) | collective-permute-done | bytes 131104 | tf_op jit(solution)/shard_map/ppermute | solution.py:50
  31.8 0.0 collective-permute-start.5
  31.8 2.1 %collective-permute-start.14 = (bf16[16,4096]{1,0:T(8,128)(2,1)S(1)}, bf16[16,4096]{1,0:T(8,128)(2,1)S(1)}, u32[]{:S(2)}, u32[]{:S(2)}) collective-permute-start(bf16[16,4096]{1,0:T(8,128)(2,1)S(1)} %dynamic-slice_bitcast_fusion.refs_12_), channel_id=1, source_target_pairs={{0,1},{1,0},{2,3},{3,2},{4,5},{5,4},{6,7},{7,6},{8,9},{9,8},{10,11... | collective-permute-start | bytes 393224 | tf_op jit(solution)/shard_map/ppermute | solution.py:573
  33.9 0.1 collective-permute-start.7
  34.0 0.4 collective-permute-start.13
  34.4 0.0 collective-permute-done.2.refs_6_
  34.4 3.0 %collective-permute-start.3 = (bf16[16,4096]{1,0:T(8,128)(2,1)S(1)}, bf16[16,4096]{1,0:T(8,128)(2,1)S(1)}, u32[]{:S(2)}, u32[]{:S(2)}) collective-permute-start(bf16[16,4096]{1,0:T(8,128)(2,1)S(1)} %collective-permute-done.2.refs_6_), channel_id=1, source_target_pairs={{0,224},{32,0},{64,32},{96,64},{128,96},{160,128},{192,160},{224,1... | collective-permute-start | bytes 393224 | tf_op jit(solution)/shard_map/ppermute | solution.py:53
  37.4 2.8 %collective-permute-start.8 = (bf16[16,4096]{1,0:T(8,128)(2,1)S(1)}, bf16[16,4096]{1,0:T(8,128)(2,1)S(1)}, u32[]{:S(2)}, u32[]{:S(2)}) collective-permute-start(bf16[16,4096]{1,0:T(8,128)(2,1)S(1)} %collective-permute-done.2.refs_6_), channel_id=1, source_target_pairs={{0,1},{1,0},{2,3},{3,2},{4,5},{5,4},{6,7},{7,6},{8,9},{9,8},{10,11... | collective-permute-start | bytes 393224 | tf_op jit(solution)/shard_map/ppermute | solution.py:573
  40.2 0.1 collective-permute-start.12
  40.3 0.4 collective-permute-start.11
  40.7 0.4 collective-permute-start.9
  41.1 1.3 collective-permute-done.6.refs_8_
  42.4 3.8 %collective-permute-start.10 = (bf16[16,4096]{1,0:T(8,128)(2,1)S(1)}, bf16[16,4096]{1,0:T(8,128)(2,1)S(1)}, u32[]{:S(2)}, u32[]{:S(2)}) collective-permute-start(bf16[16,4096]{1,0:T(8,128)(2,1)S(1)} %collective-permute-done.6.refs_8_), channel_id=1, source_target_pairs={{0,1},{1,0},{2,3},{3,2},{4,5},{5,4},{6,7},{7,6},{8,9},{9,8},{10,11... | collective-permute-start | bytes 393224 | tf_op jit(solution)/shard_map/ppermute | solution.py:573
  46.3 0.9 collective-permute-done.10.refs_16_
  47.3 0.6 copy-done.18
  47.9 6.6 %side.1 = bf16[8,192,128]{2,1,0:T(8,128)(2,1)} custom-call(s32[3]{0:T(128)} %pad_add_fusion.1.meta_ref.refs_0_, bf16[128,8192]{1,0:T(8,128)(2,1)} %bitcast.19, bf16[2,16,8192]{2,1,0:T(8,128)(2,1)} %get-tuple-element.27.refs_2_.refs_6_.refs_8_, bf16[16,128]{1,0:T(8,128)(2,1)} %get-tuple-element.23.refs_4_.refs_3_, f32[8,128]{1,0:T(8,128)} %get-tuple-element.28.refs_4_, ...), custom_call_target="tpu_custom_call" | custom-call | tf_op jit(solution)/shard_map/side/pallas_call | solution.py:87
  54.6 3.5 %all-to-all-start.2 = ((bf16[8,192,128]{2,1,0:T(8,128)(2,1)}), bf16[8,192,128]{2,1,0:T(8,128)(2,1)S(1)}, u32[]{:S(2)}, u32[]{:S(2)}) async-start(bf16[8,192,128]{2,1,0:T(8,128)(2,1)} %side.1), calls=%async_computation.2 | async-start | bytes 786432 | tf_op jit(solution)/shard_map/all_to_all | solution.py:576
  58.0 11.5 %own.1 = (bf16[128,8192]{1,0:T(8,128)(2,1)}, bf16[8,128,128]{2,1,0:T(8,128)(2,1)}) custom-call(s32[3]{0:T(128)} %pad_add_fusion.1.meta_ref.refs_0_, bf16[32,136,256]{2,1,0:T(8,128)(2,1)} %all-to-all-done.refs_1_, bf16[128,8192]{1,0:T(8,128)(2,1)} %bitcast.20, bf16[16,8192]{1,0:T(8,128)(2,1)} %bitcast.27, bf16[16,128]{1,0:T(8,128)(2,1)} %get-tuple-element.23.refs_4_.refs_3_, ...), custom_call_target="tpu_custom_call" | custom-call | tf_op jit(solution)/shard_map/own/pallas_call | solution.py:87
  69.6 3.6 %all-to-all-done.2.refs_2_ = bf16[8,192,128]{2,1,0:T(8,128)(2,1)S(1)} async-done(((bf16[8,192,128]{2,1,0:T(8,128)(2,1)}), bf16[8,192,128]{2,1,0:T(8,128)(2,1)S(1)}, u32[]{:S(2)}, u32[]{:S(2)}) %all-to-all-start.2) | async-done | bytes 393248 | tf_op jit(solution)/shard_map/all_to_all | solution.py:576
  73.1 3.4 %all-to-all-start.1 = ((bf16[8,128,128]{2,1,0:T(8,128)(2,1)}), bf16[8,128,128]{2,1,0:T(8,128)(2,1)S(1)}, u32[]{:S(2)}, u32[]{:S(2)}) async-start(bf16[8,128,128]{2,1,0:T(8,128)(2,1)} %get-tuple-element.26), calls=%async_computation.1 | async-start | bytes 524288 | tf_op jit(solution)/shard_map/all_to_all | solution.py:579
  76.5 0.6 pad_add_fusion.refs_0_
  77.2 10.1 %all-to-all-done.1.refs_1_ = bf16[8,128,128]{2,1,0:T(8,128)(2,1)S(1)} async-done(((bf16[8,128,128]{2,1,0:T(8,128)(2,1)}), bf16[8,128,128]{2,1,0:T(8,128)(2,1)S(1)}, u32[]{:S(2)}, u32[]{:S(2)}) %all-to-all-start.1) | async-done | bytes 262176 | tf_op jit(solution)/shard_map/all_to_all | solution.py:579
  87.3 0.7 copy-done.2
  88.0 7.5 %given.1 = (f32[16,144,256]{2,1,0:T(8,128)}, bf16[16,128]{1,0:T(8,128)(2,1)}, bf16[128,128]{1,0:T(8,128)(2,1)}, bf16[128,128]{1,0:T(8,128)(2,1)}, bf16[2,128,16]{2,1,0:T(8,128)(2,1)}) custom-call(s32[2]{0:T(128)} %pad_add_fusion.refs_0_, bf16[8,128,128]{2,1,0:T(8,128)(2,1)} %copy-done.2, bf16[8,192,128]{2,1,0:T(8,128)(2,1)} %copy-done, ...), custom_call_target="tpu_custom_call" | custom-call | tf_op jit(solution)/shard_map/given/pallas_call | solution.py:87
  95.5 2.1 %collective-permute-start.15 = (f32[16,144,256]{2,1,0:T(8,128)}, f32[16,144,256]{2,1,0:T(8,128)}, u32[]{:S(2)}, u32[]{:S(2)}) collective-permute-start(f32[16,144,256]{2,1,0:T(8,128)} %get-tuple-element.35), channel_id=1, source_target_pairs={{0,1},{1,0},{2,3},{3,2},{4,5},{5,4},{6,7},{7,6},{8,9},{9,8},{10,11... | collective-permute-start | bytes 7077896 | tf_op jit(solution)/shard_map/ppermute | solution.py:585
  97.6 4.4 %kept.1 = f32[16,144,256]{2,1,0:T(8,128)} custom-call(s32[1]{0:T(128)} %bitcast.refs_0_, bf16[16,128]{1,0:T(8,128)(2,1)} %get-tuple-element.31.refs_1_, bf16[128,128]{1,0:T(8,128)(2,1)} %get-tuple-element.32.refs_2_, bf16[128,128]{1,0:T(8,128)(2,1)} %get-tuple-element.33.refs_3_, bf16[2,128,16]{2,1,0:T(8,128)(2,1)} %get-tuple-element.34.refs_4_, ...), custom_call_target="tpu_custom_call" | custom-call | tf_op jit(solution)/shard_map/kept/pallas_call | solution.py:87
  102.0 0.1 collective-permute-done.15
  102.1 2.7 %add_convert_fusion = bf16[16,144,256]{2,1,0:T(8,128)(2,1)S(1)} fusion(f32[16,144,256]{2,1,0:T(8,128)} %kept.1, f32[16,144,256]{2,1,0:T(8,128)} %collective-permute-done.15), kind=kLoop, calls=%fused_computation | loop fusion | flops 1179648 | bytes 5898240 | tf_op jit(solution)/shard_map/convert_element_type | solution.py:587
  104.8 24.5 %all_to_all.30 = bf16[16,144,256]{2,1,0:T(8,128)(2,1)S(1)} all-to-all(bf16[16,144,256]{2,1,0:T(8,128)(2,1)S(1)} %add_convert_fusion), channel_id=1, replica_groups=mesh['section'=8,'y'=4,'x'=4,'core'=2] {'y','x'}, dimensions={0} | all-to-all | bytes 2359296 | tf_op jit(solution)/shard_map/all_to_all | solution.py:587
  129.3 0.8 convert_reduce_fusion
  130.1 3.4 %all-to-all-start.4 = ((f32[8,16,256]{2,1,0:T(8,128)}), f32[8,16,256]{2,1,0:T(8,128)S(1)}, u32[]{:S(2)}, u32[]{:S(2)}) async-start(f32[8,16,256]{2,1,0:T(8,128)} %bitcast.9), calls=%async_computation.4 | async-start | bytes 262144 | tf_op jit(solution)/shard_map/all_to_all | solution.py:591
  133.5 7.8 %all-to-all-done.4 = f32[8,16,256]{2,1,0:T(8,128)S(1)} async-done(((f32[8,16,256]{2,1,0:T(8,128)}), f32[8,16,256]{2,1,0:T(8,128)S(1)}, u32[]{:S(2)}, u32[]{:S(2)}) %all-to-all-start.4) | async-done | bytes 131104 | tf_op jit(solution)/shard_map/all_to_all | solution.py:591
  141.4 12.1 %all_to_all.31 = f32[16,32,256]{2,1,0:T(8,128)S(1)} all-to-all(f32[16,32,256]{2,1,0:T(8,128)S(1)} %broadcast_in_dim.13), channel_id=1, replica_groups=mesh['section'=8,'y'=4,'x'=4,'core'=2] {'y','x'}, dimensions={0} | all-to-all | bytes 1048576 | tf_op jit(solution)/shard_map/all_to_all | solution.py:593
  153.5 3.8 %collective-permute-start.16 = (f32[32,4096]{1,0:T(8,128)S(1)}, f32[32,4096]{1,0:T(8,128)S(1)}, u32[]{:S(2)}, u32[]{:S(2)}) collective-permute-start(f32[32,4096]{1,0:T(8,128)S(1)} %bitcast.24), channel_id=1, source_target_pairs={{0,1},{1,0},{2,3},{3,2},{4,5},{5,4},{6,7},{7,6},{8,9},{9,8},{10,11... | collective-permute-start | bytes 1572872 | tf_op jit(solution)/shard_map/ppermute | solution.py:595
  157.3 1.5 collective-permute-done.16
  158.9 0.1 broadcast_select_fusion
  159.0 1.0 fusion.2
  (52 shorter events, 0.2 us)
Async XLA Ops:
  6.1 8.8 %copy-start.3 = (bf16[1,16,8192]{2,1,0:T(8,128)(2,1)S(1)}, bf16[1,16,8192]{2,1,0:T(8,128)(2,1)}, u32[]{:S(2)}) copy-start(bf16[1,16,8192]{2,1,0:T(8,128)(2,1)} %param.11) | copy-start | bytes 786436
  6.1 48.5 %all-to-all-start = ((bf16[32,136,256]{2,1,0:T(8,128)(2,1)}), bf16[32,136,256]{2,1,0:T(8,128)(2,1)}, u32[]{:S(2)}, u32[]{:S(2)}) async-start(bf16[32,136,256]{2,1,0:T(8,128)(2,1)} %order.1), calls=%async_computation | async-start | bytes 4456448 | tf_op jit(solution)/shard_map/all_to_all | solution.py:565
  14.9 33.0 %copy-start.1 = (bf16[16,4096]{1,0:T(8,128)(2,1)}, bf16[16,4096]{1,0:T(8,128)(2,1)S(1)}, u32[]{:S(2)}) copy-start(bf16[16,4096]{1,0:T(8,128)(2,1)S(1)} %dynamic-slice_bitcast_fusion.refs_12_) | copy-start | bytes 393220
  14.9 10.6 %collective-permute-start.1 = (bf16[16,4096]{1,0:T(8,128)(2,1)S(1)}, bf16[16,4096]{1,0:T(8,128)(2,1)S(1)}, u32[]{:S(2)}, u32[]{:S(2)}) collective-permute-start(bf16[16,4096]{1,0:T(8,128)(2,1)S(1)} %dynamic-slice_bitcast_fusion.refs_12_), channel_id=1, source_target_pairs={{0,224},{32,0},{64,32},{96,64},{128,96},{160,128},{192,160},{224,1... | collective-permute-start | bytes 393224 | tf_op jit(solution)/shard_map/ppermute | solution.py:53
  20.6 5.8 %collective-permute-start = (bf16[16,4096]{1,0:T(8,128)(2,1)S(1)}, bf16[16,4096]{1,0:T(8,128)(2,1)S(1)}, u32[]{:S(2)}, u32[]{:S(2)}) collective-permute-start(bf16[16,4096]{1,0:T(8,128)(2,1)S(1)} %dynamic-slice_bitcast_fusion.refs_12_), channel_id=1, source_target_pairs={{0,32},{32,64},{64,96},{96,128},{128,160},{160,192},{192,224},{224... | collective-permute-start | bytes 393224 | tf_op jit(solution)/shard_map/ppermute | solution.py:50
  25.5 22.4 %copy-start.4 = (bf16[16,4096]{1,0:T(8,128)(2,1)}, bf16[16,4096]{1,0:T(8,128)(2,1)S(1)}, u32[]{:S(2)}) copy-start(bf16[16,4096]{1,0:T(8,128)(2,1)S(1)} %collective-permute-done.1.refs_5_) | copy-start | bytes 393220
  26.4 21.5 %copy-start.5 = (bf16[16,4096]{1,0:T(8,128)(2,1)}, bf16[16,4096]{1,0:T(8,128)(2,1)S(1)}, u32[]{:S(2)}) copy-start(bf16[16,4096]{1,0:T(8,128)(2,1)S(1)} %collective-permute-done.refs_11_) | copy-start | bytes 393220
  26.4 5.4 %collective-permute-start.4 = (bf16[16,4096]{1,0:T(8,128)(2,1)S(1)}, bf16[16,4096]{1,0:T(8,128)(2,1)S(1)}, u32[]{:S(2)}, u32[]{:S(2)}) collective-permute-start(bf16[16,4096]{1,0:T(8,128)(2,1)S(1)} %collective-permute-done.refs_11_), channel_id=1, source_target_pairs={{0,32},{32,64},{64,96},{96,128},{128,160},{160,192},{192,224},{224... | collective-permute-start | bytes 393224 | tf_op jit(solution)/shard_map/ppermute | solution.py:50
  26.4 8.0 %collective-permute-start.2 = (bf16[16,4096]{1,0:T(8,128)(2,1)S(1)}, bf16[16,4096]{1,0:T(8,128)(2,1)S(1)}, u32[]{:S(2)}, u32[]{:S(2)}) collective-permute-start(bf16[16,4096]{1,0:T(8,128)(2,1)S(1)} %collective-permute-done.1.refs_5_), channel_id=1, source_target_pairs={{0,224},{32,0},{64,32},{96,64},{128,96},{160,128},{192,160},{224,1... | collective-permute-start | bytes 393224 | tf_op jit(solution)/shard_map/ppermute | solution.py:53
  31.8 16.1 %copy-start.6 = (bf16[16,4096]{1,0:T(8,128)(2,1)}, bf16[16,4096]{1,0:T(8,128)(2,1)S(1)}, u32[]{:S(2)}) copy-start(bf16[16,4096]{1,0:T(8,128)(2,1)S(1)} %collective-permute-done.4.refs_10_) | copy-start | bytes 393220
  31.8 5.6 %collective-permute-start.5 = (bf16[16,4096]{1,0:T(8,128)(2,1)S(1)}, bf16[16,4096]{1,0:T(8,128)(2,1)S(1)}, u32[]{:S(2)}, u32[]{:S(2)}) collective-permute-start(bf16[16,4096]{1,0:T(8,128)(2,1)S(1)} %collective-permute-done.4.refs_10_), channel_id=1, source_target_pairs={{0,32},{32,64},{64,96},{96,128},{128,160},{160,192},{192,224},{224... | collective-permute-start | bytes 393224 | tf_op jit(solution)/shard_map/ppermute | solution.py:50
  31.8 5.6 %collective-permute-start.14 = (bf16[16,4096]{1,0:T(8,128)(2,1)S(1)}, bf16[16,4096]{1,0:T(8,128)(2,1)S(1)}, u32[]{:S(2)}, u32[]{:S(2)}) collective-permute-start(bf16[16,4096]{1,0:T(8,128)(2,1)S(1)} %dynamic-slice_bitcast_fusion.refs_12_), channel_id=1, source_target_pairs={{0,1},{1,0},{2,3},{3,2},{4,5},{5,4},{6,7},{7,6},{8,9},{9,8},{10,11... | collective-permute-start | bytes 393224 | tf_op jit(solution)/shard_map/ppermute | solution.py:573
  33.9 6.3 %collective-permute-start.7 = (bf16[16,4096]{1,0:T(8,128)(2,1)S(1)}, bf16[16,4096]{1,0:T(8,128)(2,1)S(1)}, u32[]{:S(2)}, u32[]{:S(2)}) collective-permute-start(bf16[16,4096]{1,0:T(8,128)(2,1)S(1)} %collective-permute-done.1.refs_5_), channel_id=1, source_target_pairs={{0,1},{1,0},{2,3},{3,2},{4,5},{5,4},{6,7},{7,6},{8,9},{9,8},{10,11... | collective-permute-start | bytes 393224 | tf_op jit(solution)/shard_map/ppermute | solution.py:573
  34.0 6.3 %collective-permute-start.13 = (bf16[16,4096]{1,0:T(8,128)(2,1)S(1)}, bf16[16,4096]{1,0:T(8,128)(2,1)S(1)}, u32[]{:S(2)}, u32[]{:S(2)}) collective-permute-start(bf16[16,4096]{1,0:T(8,128)(2,1)S(1)} %collective-permute-done.refs_11_), channel_id=1, source_target_pairs={{0,1},{1,0},{2,3},{3,2},{4,5},{5,4},{6,7},{7,6},{8,9},{9,8},{10,11... | collective-permute-start | bytes 393224 | tf_op jit(solution)/shard_map/ppermute | solution.py:573
  34.4 13.5 %copy-start.7 = (bf16[16,4096]{1,0:T(8,128)(2,1)}, bf16[16,4096]{1,0:T(8,128)(2,1)S(1)}, u32[]{:S(2)}) copy-start(bf16[16,4096]{1,0:T(8,128)(2,1)S(1)} %collective-permute-done.2.refs_6_) | copy-start | bytes 393220
  34.4 6.3 %collective-permute-start.3 = (bf16[16,4096]{1,0:T(8,128)(2,1)S(1)}, bf16[16,4096]{1,0:T(8,128)(2,1)S(1)}, u32[]{:S(2)}, u32[]{:S(2)}) collective-permute-start(bf16[16,4096]{1,0:T(8,128)(2,1)S(1)} %collective-permute-done.2.refs_6_), channel_id=1, source_target_pairs={{0,224},{32,0},{64,32},{96,64},{128,96},{160,128},{192,160},{224,1... | collective-permute-start | bytes 393224 | tf_op jit(solution)/shard_map/ppermute | solution.py:53
  37.4 10.5 %copy-start.8 = (bf16[16,4096]{1,0:T(8,128)(2,1)}, bf16[16,4096]{1,0:T(8,128)(2,1)S(1)}, u32[]{:S(2)}) copy-start(bf16[16,4096]{1,0:T(8,128)(2,1)S(1)} %collective-permute-done.5.refs_9_) | copy-start | bytes 393220
  37.4 5.0 %collective-permute-start.6 = (bf16[16,4096]{1,0:T(8,128)(2,1)S(1)}, bf16[16,4096]{1,0:T(8,128)(2,1)S(1)}, u32[]{:S(2)}, u32[]{:S(2)}) collective-permute-start(bf16[16,4096]{1,0:T(8,128)(2,1)S(1)} %collective-permute-done.5.refs_9_), channel_id=1, source_target_pairs={{0,32},{32,64},{64,96},{96,128},{128,160},{160,192},{192,224},{224... | collective-permute-start | bytes 393224 | tf_op jit(solution)/shard_map/ppermute | solution.py:50
  37.4 10.5 %copy-start.9 = (bf16[16,4096]{1,0:T(8,128)(2,1)}, bf16[16,4096]{1,0:T(8,128)(2,1)S(1)}, u32[]{:S(2)}) copy-start(bf16[16,4096]{1,0:T(8,128)(2,1)S(1)} %collective-permute-done.14.refs_20_) | copy-start | bytes 393220
  37.4 8.8 %collective-permute-start.8 = (bf16[16,4096]{1,0:T(8,128)(2,1)S(1)}, bf16[16,4096]{1,0:T(8,128)(2,1)S(1)}, u32[]{:S(2)}, u32[]{:S(2)}) collective-permute-start(bf16[16,4096]{1,0:T(8,128)(2,1)S(1)} %collective-permute-done.2.refs_6_), channel_id=1, source_target_pairs={{0,1},{1,0},{2,3},{3,2},{4,5},{5,4},{6,7},{7,6},{8,9},{9,8},{10,11... | collective-permute-start | bytes 393224 | tf_op jit(solution)/shard_map/ppermute | solution.py:573
  40.2 6.1 %copy-start.10 = (bf16[16,4096]{1,0:T(8,128)(2,1)}, bf16[16,4096]{1,0:T(8,128)(2,1)S(1)}, u32[]{:S(2)}) copy-start(bf16[16,4096]{1,0:T(8,128)(2,1)S(1)} %collective-permute-done.7.refs_13_) | copy-start | bytes 393220
  40.2 6.1 %collective-permute-start.12 = (bf16[16,4096]{1,0:T(8,128)(2,1)S(1)}, bf16[16,4096]{1,0:T(8,128)(2,1)S(1)}, u32[]{:S(2)}, u32[]{:S(2)}) collective-permute-start(bf16[16,4096]{1,0:T(8,128)(2,1)S(1)} %collective-permute-done.4.refs_10_), channel_id=1, source_target_pairs={{0,1},{1,0},{2,3},{3,2},{4,5},{5,4},{6,7},{7,6},{8,9},{9,8},{10,11... | collective-permute-start | bytes 393224 | tf_op jit(solution)/shard_map/ppermute | solution.py:573
  40.3 6.9 %copy-start.11 = (bf16[16,4096]{1,0:T(8,128)(2,1)}, bf16[16,4096]{1,0:T(8,128)(2,1)S(1)}, u32[]{:S(2)}) copy-start(bf16[16,4096]{1,0:T(8,128)(2,1)S(1)} %collective-permute-done.13.refs_19_) | copy-start | bytes 393220
  40.3 6.0 %collective-permute-start.11 = (bf16[16,4096]{1,0:T(8,128)(2,1)S(1)}, bf16[16,4096]{1,0:T(8,128)(2,1)S(1)}, u32[]{:S(2)}, u32[]{:S(2)}) collective-permute-start(bf16[16,4096]{1,0:T(8,128)(2,1)S(1)} %collective-permute-done.5.refs_9_), channel_id=1, source_target_pairs={{0,1},{1,0},{2,3},{3,2},{4,5},{5,4},{6,7},{7,6},{8,9},{9,8},{10,11... | collective-permute-start | bytes 393224 | tf_op jit(solution)/shard_map/ppermute | solution.py:573
  40.7 6.5 %copy-start.12 = (bf16[16,4096]{1,0:T(8,128)(2,1)}, bf16[16,4096]{1,0:T(8,128)(2,1)S(1)}, u32[]{:S(2)}) copy-start(bf16[16,4096]{1,0:T(8,128)(2,1)S(1)} %collective-permute-done.3.refs_7_) | copy-start | bytes 393220
  40.7 5.6 %collective-permute-start.9 = (bf16[16,4096]{1,0:T(8,128)(2,1)S(1)}, bf16[16,4096]{1,0:T(8,128)(2,1)S(1)}, u32[]{:S(2)}, u32[]{:S(2)}) collective-permute-start(bf16[16,4096]{1,0:T(8,128)(2,1)S(1)} %collective-permute-done.3.refs_7_), channel_id=1, source_target_pairs={{0,1},{1,0},{2,3},{3,2},{4,5},{5,4},{6,7},{7,6},{8,9},{9,8},{10,11... | collective-permute-start | bytes 393224 | tf_op jit(solution)/shard_map/ppermute | solution.py:573
  42.4 4.8 %copy-start.13 = (bf16[16,4096]{1,0:T(8,128)(2,1)}, bf16[16,4096]{1,0:T(8,128)(2,1)S(1)}, u32[]{:S(2)}) copy-start(bf16[16,4096]{1,0:T(8,128)(2,1)S(1)} %collective-permute-done.6.refs_8_) | copy-start | bytes 393220
  42.4 4.8 %collective-permute-start.10 = (bf16[16,4096]{1,0:T(8,128)(2,1)S(1)}, bf16[16,4096]{1,0:T(8,128)(2,1)S(1)}, u32[]{:S(2)}, u32[]{:S(2)}) collective-permute-start(bf16[16,4096]{1,0:T(8,128)(2,1)S(1)} %collective-permute-done.6.refs_8_), channel_id=1, source_target_pairs={{0,1},{1,0},{2,3},{3,2},{4,5},{5,4},{6,7},{7,6},{8,9},{9,8},{10,11... | collective-permute-start | bytes 393224 | tf_op jit(solution)/shard_map/ppermute | solution.py:573
  46.2 1.0 copy-start.14
  46.3 1.0 copy-start.15
  46.3 1.0 copy-start.17
  46.3 1.0 copy-start.16
  47.2 0.7 copy-start.18
  54.6 18.5 %all-to-all-start.2 = ((bf16[8,192,128]{2,1,0:T(8,128)(2,1)}), bf16[8,192,128]{2,1,0:T(8,128)(2,1)S(1)}, u32[]{:S(2)}, u32[]{:S(2)}) async-start(bf16[8,192,128]{2,1,0:T(8,128)(2,1)} %side.1), calls=%async_computation.2 | async-start | bytes 786432 | tf_op jit(solution)/shard_map/all_to_all | solution.py:576
  73.1 14.2 %copy-start = (bf16[8,192,128]{2,1,0:T(8,128)(2,1)}, bf16[8,192,128]{2,1,0:T(8,128)(2,1)S(1)}, u32[]{:S(2)}) copy-start(bf16[8,192,128]{2,1,0:T(8,128)(2,1)S(1)} %all-to-all-done.2.refs_2_) | copy-start | bytes 1179652
  73.1 14.2 %all-to-all-start.1 = ((bf16[8,128,128]{2,1,0:T(8,128)(2,1)}), bf16[8,128,128]{2,1,0:T(8,128)(2,1)S(1)}, u32[]{:S(2)}, u32[]{:S(2)}) async-start(bf16[8,128,128]{2,1,0:T(8,128)(2,1)} %get-tuple-element.26), calls=%async_computation.1 | async-start | bytes 524288 | tf_op jit(solution)/shard_map/all_to_all | solution.py:579
  87.3 0.7 copy-start.2
  95.5 6.6 %collective-permute-start.15 = (f32[16,144,256]{2,1,0:T(8,128)}, f32[16,144,256]{2,1,0:T(8,128)}, u32[]{:S(2)}, u32[]{:S(2)}) collective-permute-start(f32[16,144,256]{2,1,0:T(8,128)} %get-tuple-element.35), channel_id=1, source_target_pairs={{0,1},{1,0},{2,3},{3,2},{4,5},{5,4},{6,7},{7,6},{8,9},{9,8},{10,11... | collective-permute-start | bytes 7077896 | tf_op jit(solution)/shard_map/ppermute | solution.py:585
  130.1 11.2 %all-to-all-start.4 = ((f32[8,16,256]{2,1,0:T(8,128)}), f32[8,16,256]{2,1,0:T(8,128)S(1)}, u32[]{:S(2)}, u32[]{:S(2)}) async-start(f32[8,16,256]{2,1,0:T(8,128)} %bitcast.9), calls=%async_computation.4 | async-start | bytes 262144 | tf_op jit(solution)/shard_map/all_to_all | solution.py:591
  153.5 5.4 %collective-permute-start.16 = (f32[32,4096]{1,0:T(8,128)S(1)}, f32[32,4096]{1,0:T(8,128)S(1)}, u32[]{:S(2)}, u32[]{:S(2)}) collective-permute-start(f32[32,4096]{1,0:T(8,128)S(1)} %bitcast.24), channel_id=1, source_target_pairs={{0,1},{1,0},{2,3},{3,2},{4,5},{5,4},{6,7},{7,6},{8,9},{9,8},{10,11... | collective-permute-start | bytes 1572872 | tf_op jit(solution)/shard_map/ppermute | solution.py:595

commit v5 on v4

--- a/solution.py
+++ b/solution.py
@@ -74,31 +74,42 @@
     return pl.BlockSpec(memory_space=pltpu.VMEM)
 
 
-def call(kernel, name, out_shape, scalars, arrays, scratch=(), in_place_outs=0):
+def call(kernel, name, out_shape, scalars, arrays, pieces, scratch=(), in_place_outs=0):
     count, total = len(scalars), len(arrays)
     outs = len(out_shape)
+    buffered = [(a, n) for a, n in zip(arrays, pieces, strict=True) if n]
 
     def body(*refs):
         held = refs[count : count + total]
         first = count + total + outs
-        buffers, sems = refs[first : first + total], refs[first + total : first + 2 * total]
-        kernel(*refs[:count], *zip(held, buffers, sems), *refs[count + total : first], *refs[first + 2 * total :])
+        buffers = iter(refs[first : first + len(buffered)])
+        sems = iter(refs[first + len(buffered) : first + 2 * len(buffered)])
+        inputs = [(h, next(buffers), next(sems)) if n else h for h, n in zip(held, pieces)]
+        kernel(*refs[:count], *inputs, *refs[count + total : first], *refs[first + 2 * len(buffered) :])
 
     return pl.pallas_call(
         body,
         out_shape=out_shape,
         in_specs=[smem()] * count + [in_place()] * total,
         out_specs=[in_place()] * in_place_outs + [vmem()] * (outs - in_place_outs),
-        scratch_shapes=[pltpu.VMEM(a.shape, a.dtype) for a in arrays]
-        + [pltpu.SemaphoreType.DMA((PIECES,)) for _ in arrays]
+        scratch_shapes=[pltpu.VMEM(a.shape, a.dtype) for a, _ in buffered]
+        + [pltpu.SemaphoreType.DMA((n,)) for _, n in buffered]
         + list(scratch),
         compiler_params=params(),
+        cost_estimate=pl.CostEstimate(flops=COST[name] * 10**9, bytes_accessed=COST[name] * 3 * 10**6, transcendentals=0),
         name=name,
     )(*scalars, *arrays)
 
 
 PIECES = 8
-AHEAD = 2
+COST = dict(forward=4, side=5, own=8, given=5, kept=4)
+
+
+def gather_into(blocks, buffer, sem):
+    rows = blocks[0].shape[0]
+    for i, block in enumerate(blocks):
+        pltpu.make_async_copy(block, buffer.at[pl.ds(i * rows, rows)], sem).start()
+    return pltpu.make_async_copy(buffer, buffer, sem)
 
 
 def whole(item):
@@ -122,21 +133,24 @@
 
 def order_kernel(position_ref, meta_ref, held_ref, out_ref, buffer, in_sem, out_sem):
     tiles, tokens, width = held_ref.shape
-    loads = [
-        pltpu.make_async_copy(held_ref.at[position_ref[i]], buffer.at[i, pl.ds(0, tokens)], in_sem.at[i])
-        for i in range(tiles)
-    ]
-    for load in loads:
-        load.start()
+    groups = in_sem.shape[0]
+    group = tiles // groups
+    for i in range(tiles):
+        pltpu.make_async_copy(
+            held_ref.at[position_ref[i]], buffer.at[i, pl.ds(0, tokens)], in_sem.at[i // group]
+        ).start()
     flag, valid = meta_ref[1], meta_ref[2]
     row = lax.broadcasted_iota(jnp.int32, (INFO, width), 0)
     here = ((row == 0) & (flag == 1)) | ((row == 1) & (flag != 1))
     info = jnp.where(here, valid, 0).astype(f32).astype(bf16)
-    stores = []
     for i in range(tiles):
         buffer[i, tokens:, :] = info
-        loads[i].wait()
-        stores.append(pltpu.make_async_copy(buffer.at[i], out_ref.at[i], out_sem.at[i]))
+    stores = []
+    for i in range(groups):
+        part = pl.ds(i * group, group)
+        landed = buffer.at[part, pl.ds(0, tokens)]
+        pltpu.make_async_copy(landed, landed, in_sem.at[i]).wait()
+        stores.append(pltpu.make_async_copy(buffer.at[part], out_ref.at[part], out_sem.at[i]))
         stores[-1].start()
     for store in stores:
         store.wait()
@@ -152,8 +166,8 @@
         out_specs=in_place(),
         scratch_shapes=[
             pltpu.VMEM(shape, held.dtype),
-            pltpu.SemaphoreType.DMA((tiles,)),
-            pltpu.SemaphoreType.DMA((tiles,)),
+            pltpu.SemaphoreType.DMA((4,)),
+            pltpu.SemaphoreType.DMA((4,)),
         ],
         compiler_params=params(),
         name="order",
@@ -219,51 +233,56 @@
         ),
         (),
         (stream, down, gain),
+        (PIECES, 1, 1),
     )
 
 
 def side_kernel(count, meta_ref, stream_in, dg_in, lrt_in, irms_in, *refs):
-    mine, other, out_ref = refs[:count], refs[count : 2 * count], refs[2 * count]
+    mine, other, (out_ref, up_ref, up_sem) = refs[:count], refs[count : 2 * count], refs[2 * count :]
     core = meta_ref[0]
-    rank, half = mine[0][1].shape
+    rank, half = mine[0].shape
     tokens = stream_in[1].shape[0]
     rows = count * rank
     chunk = min(1024, half)
-    for item in (*mine, stream_in, dg_in, *other, lrt_in, irms_in):
+    ready = [gather_into(mine, up_ref.at[0], up_sem.at[0])]
+    for item in (stream_in, dg_in):
         whole(item).start()
-    for item in (*mine, stream_in, dg_in):
+    ready.append(gather_into(other, up_ref.at[1], up_sem.at[1]))
+    for item in (lrt_in, irms_in):
+        whole(item).start()
+    for item in (stream_in, dg_in):
         whole(item).wait()
     stream_ref, dg_ref = stream_in[1], dg_in[1]
     total = jnp.zeros((rows, tokens + 2 * rank), f32)
-    for base, blocks in ((core, mine), (1 - core, other)):
-        if blocks is other:
-            for item in other:
-                whole(item).wait()
-
-        def step(i, acc, base=base, blocks=blocks):
+    for which, base in enumerate((core, 1 - core)):
+        ready[which].wait()
+
+        def step(i, acc, which=which, base=base):
             local = pl.ds(pl.multiple_of(i * chunk, chunk), chunk)
             columns = pl.ds(pl.multiple_of(base * half + i * chunk, chunk), chunk)
-            up = jnp.concatenate([b[1][:, local] for b in blocks], axis=0)
             right = jnp.concatenate([stream_ref[:, columns], dg_ref[0, :, columns], dg_ref[1, :, columns]], axis=0)
-            return acc + nt(up, right)
+            return acc + nt(up_ref[which, :, local], right)
 
         total = lax.fori_loop(0, half // chunk, step, total, unroll=2)
     whole(lrt_in).wait()
     whole(irms_in).wait()
     irms = irms_in[1][0:1, :]
-    scaled_up = (total[:, :tokens] * irms).astype(bf16)
     w = total[:, tokens : tokens + rank] + total[:, tokens + rank :]
     w = jnp.concatenate([w, jnp.zeros((rows, 128 - rank), f32)], axis=1).T[:rank, :]
     w_hi, w_lo = split2(w)
     irms_hi = irms.astype(bf16).astype(f32)
     row = lax.broadcasted_iota(jnp.int32, (rank, tokens), 0)
     last = jnp.where(row == 0, irms_hi, jnp.where(row == 1, irms - irms_hi, 0.0)).astype(bf16)
-    for i in range(out_ref.shape[0]):
-        out_ref[i, :rows, :] = scaled_up
-        out_ref[i, rows : rows + rank, :] = lrt_in[1][...]
-        out_ref[i, rows + rank : rows + 2 * rank, :] = w_hi
-        out_ref[i, rows + 2 * rank : rows + 3 * rank, :] = w_lo
-        out_ref[i, rows + 3 * rank :, :] = last
+    out_ref[:rows, :] = (total[:, :tokens] * irms).astype(bf16)
+    out_ref[rows : rows + rank, :] = lrt_in[1][...]
+    out_ref[rows + rank : rows + 2 * rank, :] = w_hi
+    out_ref[rows + 2 * rank : rows + 3 * rank, :] = w_lo
+    out_ref[rows + 3 * rank :, :] = last
+
+
+def up_scratch(mine):
+    rank, half = mine[0].shape
+    return (pltpu.VMEM((2, len(mine) * rank, half), bf16), pltpu.SemaphoreType.DMA((2,)))
 
 
 def side_of(meta, stream, dg, lrt, irms, mine, other):
@@ -272,26 +291,23 @@
     (side,) = call(
         functools.partial(side_kernel, layers),
         "side",
-        (jax.ShapeDtypeStruct((layers, (layers + 4) * rank, stream.shape[0]), bf16),),
+        (jax.ShapeDtypeStruct(((layers + 4) * rank, stream.shape[0]), bf16),),
         (meta,),
         (stream, dg, lrt, irms, *mine, *other),
+        (1, 1, 1, 1) + (0,) * (2 * layers),
+        up_scratch(mine),
     )
     return side
 
 
 def own_kernel(count, meta_ref, refs_in, stream_in, up_in, lrt_in, *refs):
-    mine, other, own_ref, proj_ref, output_ref = (
-        refs[:count],
-        refs[count : 2 * count],
-        refs[2 * count],
-        refs[2 * count + 1],
-        refs[2 * count + 2],
-    )
+    mine, other = refs[:count], refs[count : 2 * count]
+    own_ref, proj_ref, output_ref, ups_ref, up_sem = refs[2 * count :]
     core, flag, valid = meta_ref[0], meta_ref[1], meta_ref[2]
     refs_ref, stream_ref, up_ref = refs_in[1], stream_in[1], up_in[1]
     tiles, padded, chunk = refs_ref.shape
     tokens = padded - INFO
-    half = mine[0][1].shape[1]
+    half = mine[0].shape[1]
     per_half = half // chunk
     per_piece = tiles // PIECES
     width = per_piece * chunk
@@ -300,17 +316,10 @@
     whole(up_in).start()
     stream_loads = [columns_piece(stream_in, i, i * width, width) for i in range(PIECES)]
     ref_loads = [leading_piece(refs_in, i, i * per_piece, per_piece) for i in range(PIECES)]
-
-    def start(i):
-        if i < PIECES:
-            stream_loads[i].start()
-            ref_loads[i].start()
-        else:
-            for item in (*mine, *other)[2 * count * (i - PIECES) // AHEAD : 2 * count * (i - PIECES + 1) // AHEAD]:
-                whole(item).start()
-
-    for i in range(AHEAD):
-        start(i)
+    for i in range(PIECES):
+        stream_loads[i].start()
+        ref_loads[i].start()
+    ready = [gather_into(blocks, ups_ref.at[i], up_sem.at[i]) for i, blocks in enumerate((mine, other))]
     whole(lrt_in).wait()
     whole(up_in).wait()
     low_rank = lrt_in[1][...].astype(f32).T.astype(bf16)
@@ -327,7 +336,6 @@
         for i in range(PIECES):
             stream_loads[i].wait()
             ref_loads[i].wait()
-            start(i + AHEAD)
             for j in range(i * per_piece, (i + 1) * per_piece):
                 columns = slice(j * chunk, (j + 1) * chunk)
                 out = stream_ref[:, columns].astype(f32) + nn(low_rank, up_ref[:, columns])
@@ -339,12 +347,12 @@
     group = min(4, per_half)
 
     def finish(make):
-        for item in (*mine, *other):
-            whole(item).wait()
+        for wait in ready:
+            wait.wait()
         total = jnp.zeros(proj_ref.shape[1:], f32)
-        for base, blocks in ((core, mine), (1 - core, other)):
-
-            def step(i, acc, base=base, blocks=blocks):
+        for which, base in enumerate((core, 1 - core)):
+
+            def step(i, acc, which=which, base=base):
                 parts = []
                 for g in range(group):
                     j = base * per_half + i * group + g
@@ -353,8 +361,7 @@
                     own_ref[:, columns] = own
                     parts.append(own)
                 local = pl.ds(pl.multiple_of(i * group * chunk, group * chunk), group * chunk)
-                up = jnp.concatenate([b[1][:, local] for b in blocks], axis=0)
-                return acc + nt(up, jnp.concatenate(parts, axis=1))
+                return acc + nt(ups_ref[which, :, local], jnp.concatenate(parts, axis=1))
 
             total = lax.fori_loop(0, per_half // group, step, total, unroll=2)
         total = total.astype(bf16)
@@ -390,11 +397,12 @@
         ),
         (meta,),
         (refs, stream, up, lrt, *mine, *other),
-        (pltpu.VMEM(stream.shape, f32),),
+        (PIECES, PIECES, 1, 1) + (0,) * (2 * layers),
+        (pltpu.VMEM(stream.shape, f32),) + up_scratch(mine),
     )
 
 
-def solve(width, rank, me, own_ref, side_ref, low_ref, lrt_ref, coef_ref, k_ref, acc):
+def solve(width, rank, me, own_ref, side_ref, low_ref, lrt_ref, coef_ref, k_ref, acc, lrt_all):
     layers, rows, _ = own_ref.shape
     acc[...] = jnp.zeros_like(acc)
     for j in range(layers):
@@ -404,36 +412,36 @@
             low = rank * (layers - 1 - j)
             acc[0 : rank * (j + 1), :] += own_ref[me + j, low:rows, :].astype(f32)
 
-    def inverse_rms(t):
-        return side_ref[t, rows + 3 * rank : rows + 3 * rank + 1, :].astype(f32) + side_ref[
-            t, rows + 3 * rank + 1 : rows + 3 * rank + 2, :
-        ].astype(f32)
-
-    def mean_of(grad, t):
-        lrt = side_ref[t, rows : rows + rank, :].astype(f32)
+    def inverse_rms(j):
+        hi = side_ref[j, rows + 3 * rank : rows + 3 * rank + 1, :].astype(f32)
+        return hi + side_ref[j, rows + 3 * rank + 1 : rows + 3 * rank + 2, :].astype(f32)
+
+    def mean_of(grad, j):
+        lrt = side_ref[j, rows : rows + rank, :].astype(f32)
         return jnp.sum(grad.astype(f32) * lrt, axis=0, keepdims=True) * (1.0 / width)
 
     for j in range(layers - 1, 0, -1):
 
         @pl.when(me + j < layers)
         def _(j=j):
-            t = me + j
             low = rank * (layers - 1 - j)
             grad = acc[rank * j : rank * (j + 1), :].astype(bf16)
-            mean = mean_of(grad, t)
-            w_hi = side_ref[t, rows + rank : rows + 2 * rank, :]
-            w_lo = side_ref[t, rows + 2 * rank : rows + 3 * rank, :]
+            mean = mean_of(grad, j)
+            w_hi = side_ref[j, rows + rank : rows + 2 * rank, :]
+            w_lo = side_ref[j, rows + 2 * rank : rows + 3 * rank, :]
             term = tn(w_hi, grad) + tn(w_lo, grad)
-            scaled_up = side_ref[t, low : rows - rank, :].astype(f32)
-            acc[0 : rank * j, :] += inverse_rms(t) * (term[low : rows - rank, :] - mean * scaled_up)
+            scaled_up = side_ref[j, low : rows - rank, :].astype(f32)
+            acc[0 : rank * j, :] += inverse_rms(j) * (term[low : rows - rank, :] - mean * scaled_up)
 
     grad = acc[0:rank, :].astype(bf16)
     low_ref[...] = grad
-    irms = inverse_rms(me)
-    mean = mean_of(grad, me)
-    lrt = side_ref[:, rows : rows + rank, :].reshape(layers * rank, -1)
-    layer = lax.broadcasted_iota(jnp.int32, lrt.shape, 0) // rank
-    lrt_f = lrt.astype(f32)
+    irms = inverse_rms(0)
+    mean = mean_of(grad, 0)
+    for j in range(layers):
+        where = lax.rem(me + j, layers) * rank
+        lrt_all[pl.ds(pl.multiple_of(where, rank), rank), :] = side_ref[j, rows : rows + rank, :]
+    lrt_f = lrt_all[...].astype(f32)
+    layer = lax.broadcasted_iota(jnp.int32, lrt_f.shape, 0) // rank
     lrt_ref[...] = jnp.where(layer <= me, lrt_f, 0.0).astype(bf16)
     below = jnp.where(layer < me, lrt_f, 0.0)
     coef_ref[...] = (below * (-irms * irms * mean)).astype(bf16)
@@ -479,18 +487,20 @@
     ]
 
 
-def given_kernel(rank, meta_ref, own_up_in, side_in, *refs):
-    large, (out_ref, low_ref, lrt_ref, coef_ref, k_ref, acc, buffer, out_sem) = refs[:4], refs[4:]
+def given_kernel(rank, count, meta_ref, own_up_in, *refs):
+    sides, large = refs[:count], refs[count : count + 4]
+    out_ref, low_ref, lrt_ref, coef_ref, k_ref, acc, lrt_all, side_ref, side_sem, buffer, out_sem = refs[count + 4 :]
     start, me = meta_ref[0], meta_ref[1]
     loads = part_loads(start, large, buffer.shape[0], buffer.shape[2])
     whole(own_up_in).start()
-    whole(side_in).start()
+    for i, side in enumerate(sides):
+        pltpu.make_async_copy(side, side_ref.at[i], side_sem).start()
     for load in loads:
         for item in load:
             item.start()
     whole(own_up_in).wait()
-    whole(side_in).wait()
-    solve(large[0][0].shape[1], rank, me, own_up_in[1], side_in[1], low_ref, lrt_ref, coef_ref, k_ref, acc)
+    pltpu.make_async_copy(side_ref, side_ref, side_sem).wait()
+    solve(large[0][0].shape[1], rank, me, own_up_in[1], side_ref, low_ref, lrt_ref, coef_ref, k_ref, acc, lrt_all)
     part(start, loads, low_ref[...], lrt_ref[...], coef_ref[...], k_ref, *large, out_ref, buffer, out_sem)
 
 
@@ -510,14 +520,14 @@
 
 def part_shapes(chunks, chunk, rows, rank):
     shape = (chunks, rows + rank, chunk)
-    return jax.ShapeDtypeStruct(shape, f32), (pltpu.VMEM(shape, f32), pltpu.SemaphoreType.DMA((PIECES,)))
-
-
-def given_part(meta, chunks, chunk, rank, own_up, side, *large):
-    _, rows, tokens = own_up.shape
+    return jax.ShapeDtypeStruct(shape, f32), (pltpu.VMEM(shape, f32), pltpu.SemaphoreType.DMA((4,)))
+
+
+def given_part(meta, chunks, chunk, rank, own_up, sides, *large):
+    layers, rows, tokens = own_up.shape
     shape, scratch = part_shapes(chunks, chunk, rows, rank)
     return call(
-        functools.partial(given_kernel, rank),
+        functools.partial(given_kernel, rank, layers),
         "given",
         (
             shape,
@@ -527,15 +537,31 @@
             jax.ShapeDtypeStruct((2, rows, rank), bf16),
         ),
         (meta,),
-        (own_up, side, *large),
-        (pltpu.VMEM((rows, tokens), f32),) + scratch,
+        (own_up, *sides, *large),
+        (1,) + (0,) * layers + (4,) * 4,
+        (
+            pltpu.VMEM((rows, tokens), f32),
+            pltpu.VMEM((rows, tokens), bf16),
+            pltpu.VMEM((layers,) + sides[0].shape, bf16),
+            pltpu.SemaphoreType.DMA,
+        )
+        + scratch,
         in_place_outs=1,
     )
 
 
 def kept_part(meta, chunks, chunk, low, lrt, coef, k, *large):
     shape, scratch = part_shapes(chunks, chunk, lrt.shape[0], low.shape[0])
-    (found,) = call(kept_kernel, "kept", (shape,), (meta,), (low, lrt, coef, k, *large), scratch, in_place_outs=1)
+    (found,) = call(
+        kept_kernel,
+        "kept",
+        (shape,),
+        (meta,),
+        (low, lrt, coef, k, *large),
+        (1,) * 4 + (4,) * 4,
+        scratch,
+        in_place_outs=1,
+    )
     return found
 
 
@@ -561,19 +587,24 @@
     swap = [(i, (i + 1) % cores) for i in range(cores)]
 
     meta = jnp.stack([core, tile_harmful_flag[0], tile_valid_count[0]]).astype(jnp.int32)
-    ordered = order(tile_reference_position, meta, frozen_reference_states[0])
+    up_half = lax.dynamic_slice_in_dim(adapter_up_weight[0], core * half, half, axis=1)
+    up_half, position = lax.optimization_barrier((up_half, tile_reference_position))
+    ordered = order(position, meta, frozen_reference_states[0])
     refs = lax.all_to_all(ordered, DP, split_axis=0, concat_axis=0, tiled=True)
     _, stream, down, up, gains = lax.optimization_barrier(
         (ordered, layer_input_states[0, 0], adapter_down_weight[0], adapter_up_weight[0], layer_norm_gain)
     )
 
-    up_half = lax.dynamic_slice_in_dim(adapter_up_weight[0], core * half, half, axis=1)
     normed, lrt, irms, dg = forward(stream, down, gains)
     mine = ring_gather(up_half, SEC, lrt)[::-1]
     other = [lax.ppermute(block, "core", swap) for block in mine]
 
     side = side_of(meta, stream, dg, lrt, irms, mine, other)
-    sides = lax.all_to_all(side, SEC, 0, 0, tiled=True)
+    sides = [side]
+    for j in range(1, layers):
+        sides.append(lax.ppermute(side, SEC, [(t, (t - j) % layers) for t in range(layers)]))
+
+    refs, _ = lax.optimization_barrier((refs, side))
 
     own, own_up = own_gradient(meta, refs, stream, up, lrt, mine, other)
     own_up = lax.all_to_all(own_up, SEC, 0, 0, tiled=True)

time: 161 us -> 158 us (0.981)
  starting transfers between devices: 46.4 us -> 56.8 us
  waiting for transfers between devices: 29 us -> 20.2 us
  Pallas kernels: 38.5 us -> 33.7 us
    ppermute x0 -> x7, starting transfers between devices: none -> 14.8 us  [shards(): lax.ppermute(side, SEC, [(t, (t - j) % layers) for t in range(layers)])]
    all_to_all x1, waiting for transfers between devices: 10.1 us -> 0.01 us  [shards(): own_up = lax.all_to_all(own_up, SEC, 0, 0, tiled=True)]
    pallas_call x5, Pallas kernels: 34.9 us -> 30.5 us  [call(): pl.pallas_call(body, out_shape=out_shape, in_specs=[smem()] * count + [in...]
    ppermute x0 -> x7, waiting for transfers between devices: none -> 4.33 us  [shards(): lax.ppermute(side, SEC, [(t, (t - j) % layers) for t in range(layers)])]
    all_to_all x1 -> x0, waiting for transfers between devices: 3.55 us -> none  [shards(): sides = lax.all_to_all(side, SEC, 0, 0, tiled=True)]
    all_to_all x1 -> x0, starting transfers between devices: 3.47 us -> none  [shards(): sides = lax.all_to_all(side, SEC, 0, 0, tiled=True)]
  transfers between devices with their start and end apart: 21 -> 27, of which waited for: 9 -> 9; matrix products, arithmetic and copies ran while one was open for 0% -> 0% of each run, Pallas kernels for 17% -> 9%
where the time goes in v5:
time: 158 us
  starting transfers between devices  56.8 us (36%)
  blocking collectives  36.7 us (23%)
  Pallas kernels  33.7 us (21%)
  waiting for transfers between devices  20.2 us (13%)
  other arithmetic  5.86 us (4%)
  local copies, waits for them, and re-layouts  2.35 us (1%)
  between operations  2.3 us (1%)
    pallas_call x5, Pallas kernels, call(): pl.pallas_call(body, out_shape=out_shape, in_specs=[smem()] * count + [in...  30.5 us
    all_to_all x1, blocking collectives, shards(): lax.all_to_all((kept + received).astype(bf16), CHIPS, 0, 0, tiled=True)  24.6 us
    ppermute x7, starting transfers between devices, shards(): lax.ppermute(side, SEC, [(t, (t - j) % layers) for t in range(layers)])  14.8 us
    all_to_all x1, blocking collectives, shards(): lax.all_to_all(jnp.broadcast_to(final, (chips,) + final.shape), CHIPS, 0,...  12.1 us
    ppermute x3, starting transfers between devices, ring_gather(): bwd = lax.ppermute(bwd, axis, down)  11.2 us
    ppermute x8, starting transfers between devices, shards(): other = [lax.ppermute(block, 'core', swap) for block in mine]  10.2 us
    all_to_all x1, starting transfers between devices, shards(): refs = lax.all_to_all(ordered, DP, split_axis=0, concat_axis=0, tiled=True)  8.65 us
    all_to_all x1, waiting for transfers between devices, shards(): lax.all_to_all(grad_up.reshape(layers, rank, chunk), SEC, 0, 0, tiled=True)  7.84 us
  transfers between devices with their start and end apart: 27, of which 9 were waited for; matrix products, arithmetic and copies ran while one was open for 0% of the time, Pallas kernels for 9%

profile of v5, /device:TPU:1, one launch (start us, length us, event | category | flops | bytes accessed | tf_op | source)
XLA Modules:
  0.0 157.8 jit_solution(14700310084925603337)
XLA Ops:
  1.9 0.9 dynamic-slice_bitcast_fusion.refs_12_
  2.9 0.6 pad_add_fusion.1.meta_ref.refs_0_
  3.4 3.2 %order.1 = bf16[32,136,256]{2,1,0:T(8,128)(2,1)} custom-call(s32[32]{0:T(128)} %position_ref, s32[3]{0:T(128)} %pad_add_fusion.1.meta_ref.refs_0_, bf16[32,128,256]{2,1,0:T(8,128)(2,1)} %bitcast.18), custom_call_target="tpu_custom_call" | custom-call | tf_op jit(solution)/shard_map/order/pallas_call | solution.py:162
  6.7 8.6 %all-to-all-start = ((bf16[32,136,256]{2,1,0:T(8,128)(2,1)}), bf16[32,136,256]{2,1,0:T(8,128)(2,1)}, u32[]{:S(2)}, u32[]{:S(2)}) async-start(bf16[32,136,256]{2,1,0:T(8,128)(2,1)} %order.1), calls=%async_computation | async-start | bytes 4456448 | tf_op jit(solution)/shard_map/all_to_all | solution.py:593
  15.3 5.7 %collective-permute-start.1 = (bf16[16,4096]{1,0:T(8,128)(2,1)S(1)}, bf16[16,4096]{1,0:T(8,128)(2,1)S(1)}, u32[]{:S(2)}, u32[]{:S(2)}) collective-permute-start(bf16[16,4096]{1,0:T(8,128)(2,1)S(1)} %dynamic-slice_bitcast_fusion.refs_12_), channel_id=1, source_target_pairs={{0,224},{32,0},{64,32},{96,64},{128,96},{160,128},{192,160},{224,1... | collective-permute-start | bytes 393224 | tf_op jit(solution)/shard_map/ppermute | solution.py:53
  21.0 4.8 %forward.1 = (bf16[128,8192]{1,0:T(8,128)(2,1)}, bf16[16,128]{1,0:T(8,128)(2,1)}, f32[8,128]{1,0:T(8,128)}, bf16[2,16,8192]{2,1,0:T(8,128)(2,1)}) custom-call(bf16[128,8192]{1,0:T(8,128)(2,1)} %bitcast.23, bf16[16,8192]{1,0:T(8,128)(2,1)} %bitcast.28, f32[1,8192]{1,0:T(1,128)} %refs_2_), custom_call_target="tpu_custom_call" | custom-call | flops 4000000000 | bytes 12000000 | tf_op jit(solution)/shard_map/forward/pallas_call | solution.py:90
  25.8 1.0 collective-permute-done.refs_11_
  26.8 2.7 %collective-permute-start.2 = (bf16[16,4096]{1,0:T(8,128)(2,1)S(1)}, bf16[16,4096]{1,0:T(8,128)(2,1)S(1)}, u32[]{:S(2)}, u32[]{:S(2)}) collective-permute-start(bf16[16,4096]{1,0:T(8,128)(2,1)S(1)} %collective-permute-done.1.refs_5_), channel_id=1, source_target_pairs={{0,224},{32,0},{64,32},{96,64},{128,96},{160,128},{192,160},{224,1... | collective-permute-start | bytes 393224 | tf_op jit(solution)/shard_map/ppermute | solution.py:53
  29.4 2.8 %collective-permute-done.4.refs_10_ = bf16[16,4096]{1,0:T(8,128)(2,1)S(1)} collective-permute-done((bf16[16,4096]{1,0:T(8,128)(2,1)S(1)}, bf16[16,4096]{1,0:T(8,128)(2,1)S(1)}, u32[]{:S(2)}, u32[]{:S(2)}) %collective-permute-start.4) | collective-permute-done | bytes 131104 | tf_op jit(solution)/shard_map/ppermute | solution.py:50
  32.2 2.2 %collective-permute-start.14 = (bf16[16,4096]{1,0:T(8,128)(2,1)S(1)}, bf16[16,4096]{1,0:T(8,128)(2,1)S(1)}, u32[]{:S(2)}, u32[]{:S(2)}) collective-permute-start(bf16[16,4096]{1,0:T(8,128)(2,1)S(1)} %dynamic-slice_bitcast_fusion.refs_12_), channel_id=1, source_target_pairs={{0,1},{1,0},{2,3},{3,2},{4,5},{5,4},{6,7},{7,6},{8,9},{9,8},{10,11... | collective-permute-start | bytes 393224 | tf_op jit(solution)/shard_map/ppermute | solution.py:600
  34.5 0.4 collective-permute-start.13
  34.9 2.9 %collective-permute-start.3 = (bf16[16,4096]{1,0:T(8,128)(2,1)S(1)}, bf16[16,4096]{1,0:T(8,128)(2,1)S(1)}, u32[]{:S(2)}, u32[]{:S(2)}) collective-permute-start(bf16[16,4096]{1,0:T(8,128)(2,1)S(1)} %collective-permute-done.2.refs_6_), channel_id=1, source_target_pairs={{0,224},{32,0},{64,32},{96,64},{128,96},{160,128},{192,160},{224,1... | collective-permute-start | bytes 393224 | tf_op jit(solution)/shard_map/ppermute | solution.py:53
  37.8 2.8 %collective-permute-start.8 = (bf16[16,4096]{1,0:T(8,128)(2,1)S(1)}, bf16[16,4096]{1,0:T(8,128)(2,1)S(1)}, u32[]{:S(2)}, u32[]{:S(2)}) collective-permute-start(bf16[16,4096]{1,0:T(8,128)(2,1)S(1)} %collective-permute-done.2.refs_6_), channel_id=1, source_target_pairs={{0,1},{1,0},{2,3},{3,2},{4,5},{5,4},{6,7},{7,6},{8,9},{9,8},{10,11... | collective-permute-start | bytes 393224 | tf_op jit(solution)/shard_map/ppermute | solution.py:600
  40.6 0.1 collective-permute-start.12
  40.7 0.4 collective-permute-start.11
  41.1 0.4 collective-permute-start.9
  41.5 1.3 collective-permute-done.6.refs_8_
  42.8 3.8 %collective-permute-start.10 = (bf16[16,4096]{1,0:T(8,128)(2,1)S(1)}, bf16[16,4096]{1,0:T(8,128)(2,1)S(1)}, u32[]{:S(2)}, u32[]{:S(2)}) collective-permute-start(bf16[16,4096]{1,0:T(8,128)(2,1)S(1)} %collective-permute-done.6.refs_8_), channel_id=1, source_target_pairs={{0,1},{1,0},{2,3},{3,2},{4,5},{5,4},{6,7},{7,6},{8,9},{9,8},{10,11... | collective-permute-start | bytes 393224 | tf_op jit(solution)/shard_map/ppermute | solution.py:600
  46.7 0.9 collective-permute-done.10.refs_16_
  47.7 0.6 copy-done.16
  48.3 5.3 %side.1.refs_2_ = bf16[192,128]{1,0:T(8,128)(2,1)} custom-call(s32[3]{0:T(128)} %pad_add_fusion.1.meta_ref.refs_0_, bf16[128,8192]{1,0:T(8,128)(2,1)} %bitcast.24, bf16[2,16,8192]{2,1,0:T(8,128)(2,1)} %get-tuple-element.26.refs_2_.refs_13_.refs_8_, bf16[16,128]{1,0:T(8,128)(2,1)} %get-tuple-element.27.refs_3_.refs_4_, f32[8,128]{1,0:T(8,128)} %get-tuple-element.28.refs_4_, ...), custom_call_target="tpu_custom_call" | custom-call | flops 5000000000 | bytes 15000000 | tf_op jit(solution)/shard_map/side/pallas_call | solution.py:90
  53.7 9.1 %own.1 = (bf16[128,8192]{1,0:T(8,128)(2,1)}, bf16[8,128,128]{2,1,0:T(8,128)(2,1)}) custom-call(s32[3]{0:T(128)} %pad_add_fusion.1.meta_ref.refs_0_, bf16[32,136,256]{2,1,0:T(8,128)(2,1)} %all-to-all-done.refs_1_, bf16[128,8192]{1,0:T(8,128)(2,1)} %bitcast.25, bf16[16,8192]{1,0:T(8,128)(2,1)} %bitcast.22, bf16[16,128]{1,0:T(8,128)(2,1)} %get-tuple-element.27.refs_3_.refs_4_, ...), custom_call_target="tpu_custom_call" | custom-call | flops 8000000000 | bytes 24000000 | tf_op jit(solution)/shard_map/own/pallas_call | solution.py:90
  62.8 3.4 %all-to-all-start.1 = ((bf16[8,128,128]{2,1,0:T(8,128)(2,1)}), bf16[8,128,128]{2,1,0:T(8,128)(2,1)S(1)}, u32[]{:S(2)}, u32[]{:S(2)}) async-start(bf16[8,128,128]{2,1,0:T(8,128)(2,1)} %get-tuple-element.34), calls=%async_computation.1 | async-start | bytes 524288 | tf_op jit(solution)/shard_map/all_to_all | solution.py:610
  66.3 1.4 collective-permute-start.21
  67.6 2.1 %collective-permute-start.20 = (bf16[192,128]{1,0:T(8,128)(2,1)S(1)}, bf16[192,128]{1,0:T(8,128)(2,1)S(1)}, u32[]{:S(2)}, u32[]{:S(2)}) collective-permute-start(bf16[192,128]{1,0:T(8,128)(2,1)S(1)} %copy-done.17), channel_id=1, source_target_pairs={{0,64},{32,96},{64,128},{96,160},{128,192},{160,224},{192,0},{224,... | collective-permute-start | bytes 147464 | tf_op jit(solution)/shard_map/ppermute | solution.py:605
  69.7 2.4 %collective-permute-start.19 = (bf16[192,128]{1,0:T(8,128)(2,1)S(1)}, bf16[192,128]{1,0:T(8,128)(2,1)S(1)}, u32[]{:S(2)}, u32[]{:S(2)}) collective-permute-start(bf16[192,128]{1,0:T(8,128)(2,1)S(1)} %copy-done.17), channel_id=1, source_target_pairs={{0,96},{32,128},{64,160},{96,192},{128,224},{160,0},{192,32},{224,... | collective-permute-start | bytes 147464 | tf_op jit(solution)/shard_map/ppermute | solution.py:605
  72.1 2.1 %collective-permute-start.18 = (bf16[192,128]{1,0:T(8,128)(2,1)S(1)}, bf16[192,128]{1,0:T(8,128)(2,1)S(1)}, u32[]{:S(2)}, u32[]{:S(2)}) collective-permute-start(bf16[192,128]{1,0:T(8,128)(2,1)S(1)} %copy-done.17), channel_id=1, source_target_pairs={{0,128},{32,160},{64,192},{96,224},{128,0},{160,32},{192,64},{224,... | collective-permute-start | bytes 147464 | tf_op jit(solution)/shard_map/ppermute | solution.py:605
  74.2 2.4 %collective-permute-start.17 = (bf16[192,128]{1,0:T(8,128)(2,1)S(1)}, bf16[192,128]{1,0:T(8,128)(2,1)S(1)}, u32[]{:S(2)}, u32[]{:S(2)}) collective-permute-start(bf16[192,128]{1,0:T(8,128)(2,1)S(1)} %copy-done.17), channel_id=1, source_target_pairs={{0,160},{32,192},{64,224},{96,0},{128,32},{160,64},{192,96},{224,1... | collective-permute-start | bytes 147464 | tf_op jit(solution)/shard_map/ppermute | solution.py:605
  76.6 3.3 %collective-permute-start.16 = (bf16[192,128]{1,0:T(8,128)(2,1)S(1)}, bf16[192,128]{1,0:T(8,128)(2,1)S(1)}, u32[]{:S(2)}, u32[]{:S(2)}) collective-permute-start(bf16[192,128]{1,0:T(8,128)(2,1)S(1)} %copy-done.17), channel_id=1, source_target_pairs={{0,192},{32,224},{64,0},{96,32},{128,64},{160,96},{192,128},{224,1... | collective-permute-start | bytes 147464 | tf_op jit(solution)/shard_map/ppermute | solution.py:605
  79.9 1.2 collective-permute-start.15
  81.1 0.7 pad_add_fusion.refs_0_
  81.7 3.0 %collective-permute-done.18.refs_6_ = bf16[192,128]{1,0:T(8,128)(2,1)S(1)} collective-permute-done((bf16[192,128]{1,0:T(8,128)(2,1)S(1)}, bf16[192,128]{1,0:T(8,128)(2,1)S(1)}, u32[]{:S(2)}, u32[]{:S(2)}) %collective-permute-start.18) | collective-permute-done | bytes 49184 | tf_op jit(solution)/shard_map/ppermute | solution.py:605
  84.8 1.3 collective-permute-done.16.refs_4_
  86.1 0.5 copy-done.23
  86.7 0.1 copy-done
  86.8 7.2 %given.1 = (f32[16,144,256]{2,1,0:T(8,128)}, bf16[16,128]{1,0:T(8,128)(2,1)}, bf16[128,128]{1,0:T(8,128)(2,1)}, bf16[128,128]{1,0:T(8,128)(2,1)}, bf16[2,128,16]{2,1,0:T(8,128)(2,1)}) custom-call(s32[2]{0:T(128)} %pad_add_fusion.refs_0_, bf16[8,128,128]{2,1,0:T(8,128)(2,1)} %copy-done, bf16[192,128]{1,0:T(8,128)(2,1)} %side.1.refs_2_, ...), custom_call_target="tpu_custom_call" | custom-call | flops 5000000000 | bytes 15000000 | tf_op jit(solution)/shard_map/given/pallas_call | solution.py:90
  94.1 1.3 collective-permute-start.22
  95.4 4.0 %kept.1 = f32[16,144,256]{2,1,0:T(8,128)} custom-call(s32[1]{0:T(128)} %bitcast.refs_0_, bf16[16,128]{1,0:T(8,128)(2,1)} %get-tuple-element.37.refs_1_, bf16[128,128]{1,0:T(8,128)(2,1)} %get-tuple-element.38.refs_2_, bf16[128,128]{1,0:T(8,128)(2,1)} %get-tuple-element.39.refs_3_, bf16[2,128,16]{2,1,0:T(8,128)(2,1)} %get-tuple-element.40.refs_4_, ...), custom_call_target="tpu_custom_call" | custom-call | flops 4000000000 | bytes 12000000 | tf_op jit(solution)/shard_map/kept/pallas_call | solution.py:90
  99.4 0.5 collective-permute-done.22
  99.9 2.7 %add_convert_fusion = bf16[16,144,256]{2,1,0:T(8,128)(2,1)S(1)} fusion(f32[16,144,256]{2,1,0:T(8,128)} %kept.1, f32[16,144,256]{2,1,0:T(8,128)} %collective-permute-done.22), kind=kLoop, calls=%fused_computation | loop fusion | flops 1179648 | bytes 5898240 | tf_op jit(solution)/shard_map/convert_element_type | solution.py:618
  102.5 24.6 %all_to_all.25 = bf16[16,144,256]{2,1,0:T(8,128)(2,1)S(1)} all-to-all(bf16[16,144,256]{2,1,0:T(8,128)(2,1)S(1)} %add_convert_fusion), channel_id=1, replica_groups=mesh['section'=8,'y'=4,'x'=4,'core'=2] {'y','x'}, dimensions={0} | all-to-all | bytes 2359296 | tf_op jit(solution)/shard_map/all_to_all | solution.py:618
  127.1 0.8 convert_reduce_fusion
  127.9 3.4 %all-to-all-start.3 = ((f32[8,16,256]{2,1,0:T(8,128)}), f32[8,16,256]{2,1,0:T(8,128)S(1)}, u32[]{:S(2)}, u32[]{:S(2)}) async-start(f32[8,16,256]{2,1,0:T(8,128)} %bitcast.9), calls=%async_computation.3 | async-start | bytes 262144 | tf_op jit(solution)/shard_map/all_to_all | solution.py:622
  131.3 7.8 %all-to-all-done.3 = f32[8,16,256]{2,1,0:T(8,128)S(1)} async-done(((f32[8,16,256]{2,1,0:T(8,128)}), f32[8,16,256]{2,1,0:T(8,128)S(1)}, u32[]{:S(2)}, u32[]{:S(2)}) %all-to-all-start.3) | async-done | bytes 131104 | tf_op jit(solution)/shard_map/all_to_all | solution.py:622
  139.2 12.1 %all_to_all.26 = f32[16,32,256]{2,1,0:T(8,128)S(1)} all-to-all(f32[16,32,256]{2,1,0:T(8,128)S(1)} %broadcast_in_dim.13), channel_id=1, replica_groups=mesh['section'=8,'y'=4,'x'=4,'core'=2] {'y','x'}, dimensions={0} | all-to-all | bytes 1048576 | tf_op jit(solution)/shard_map/all_to_all | solution.py:624
  151.3 3.8 %collective-permute-start.23 = (f32[32,4096]{1,0:T(8,128)S(1)}, f32[32,4096]{1,0:T(8,128)S(1)}, u32[]{:S(2)}, u32[]{:S(2)}) collective-permute-start(f32[32,4096]{1,0:T(8,128)S(1)} %bitcast.19), channel_id=1, source_target_pairs={{0,1},{1,0},{2,3},{3,2},{4,5},{5,4},{6,7},{7,6},{8,9},{9,8},{10,11... | collective-permute-start | bytes 1572872 | tf_op jit(solution)/shard_map/ppermute | solution.py:626
  155.2 1.5 collective-permute-done.23
  156.8 1.0 fusion.2
  (76 shorter events, 0.5 us)
Async XLA Ops:
  2.9 29.3 %copy-start.1 = (bf16[16,4096]{1,0:T(8,128)(2,1)}, bf16[16,4096]{1,0:T(8,128)(2,1)S(1)}, u32[]{:S(2)}) copy-start(bf16[16,4096]{1,0:T(8,128)(2,1)S(1)} %dynamic-slice_bitcast_fusion.refs_12_) | copy-start | bytes 393220
  6.7 47.0 %all-to-all-start = ((bf16[32,136,256]{2,1,0:T(8,128)(2,1)}), bf16[32,136,256]{2,1,0:T(8,128)(2,1)}, u32[]{:S(2)}, u32[]{:S(2)}) async-start(bf16[32,136,256]{2,1,0:T(8,128)(2,1)} %order.1), calls=%async_computation | async-start | bytes 4456448 | tf_op jit(solution)/shard_map/all_to_all | solution.py:593
  15.3 10.4 %collective-permute-start.1 = (bf16[16,4096]{1,0:T(8,128)(2,1)S(1)}, bf16[16,4096]{1,0:T(8,128)(2,1)S(1)}, u32[]{:S(2)}, u32[]{:S(2)}) collective-permute-start(bf16[16,4096]{1,0:T(8,128)(2,1)S(1)} %dynamic-slice_bitcast_fusion.refs_12_), channel_id=1, source_target_pairs={{0,224},{32,0},{64,32},{96,64},{128,96},{160,128},{192,160},{224,1... | collective-permute-start | bytes 393224 | tf_op jit(solution)/shard_map/ppermute | solution.py:53
  21.0 5.8 %collective-permute-start = (bf16[16,4096]{1,0:T(8,128)(2,1)S(1)}, bf16[16,4096]{1,0:T(8,128)(2,1)S(1)}, u32[]{:S(2)}, u32[]{:S(2)}) collective-permute-start(bf16[16,4096]{1,0:T(8,128)(2,1)S(1)} %dynamic-slice_bitcast_fusion.refs_12_), channel_id=1, source_target_pairs={{0,32},{32,64},{64,96},{96,128},{128,160},{160,192},{192,224},{224... | collective-permute-start | bytes 393224 | tf_op jit(solution)/shard_map/ppermute | solution.py:50
  25.7 22.5 %copy-start.2 = (bf16[16,4096]{1,0:T(8,128)(2,1)}, bf16[16,4096]{1,0:T(8,128)(2,1)S(1)}, u32[]{:S(2)}) copy-start(bf16[16,4096]{1,0:T(8,128)(2,1)S(1)} %collective-permute-done.1.refs_5_) | copy-start | bytes 393220
  26.7 21.5 %copy-start.3 = (bf16[16,4096]{1,0:T(8,128)(2,1)}, bf16[16,4096]{1,0:T(8,128)(2,1)S(1)}, u32[]{:S(2)}) copy-start(bf16[16,4096]{1,0:T(8,128)(2,1)S(1)} %collective-permute-done.refs_11_) | copy-start | bytes 393220
  26.7 5.4 %collective-permute-start.4 = (bf16[16,4096]{1,0:T(8,128)(2,1)S(1)}, bf16[16,4096]{1,0:T(8,128)(2,1)S(1)}, u32[]{:S(2)}, u32[]{:S(2)}) collective-permute-start(bf16[16,4096]{1,0:T(8,128)(2,1)S(1)} %collective-permute-done.refs_11_), channel_id=1, source_target_pairs={{0,32},{32,64},{64,96},{96,128},{128,160},{160,192},{192,224},{224... | collective-permute-start | bytes 393224 | tf_op jit(solution)/shard_map/ppermute | solution.py:50
  26.8 8.1 %collective-permute-start.2 = (bf16[16,4096]{1,0:T(8,128)(2,1)S(1)}, bf16[16,4096]{1,0:T(8,128)(2,1)S(1)}, u32[]{:S(2)}, u32[]{:S(2)}) collective-permute-start(bf16[16,4096]{1,0:T(8,128)(2,1)S(1)} %collective-permute-done.1.refs_5_), channel_id=1, source_target_pairs={{0,224},{32,0},{64,32},{96,64},{128,96},{160,128},{192,160},{224,1... | collective-permute-start | bytes 393224 | tf_op jit(solution)/shard_map/ppermute | solution.py:53
  32.2 16.1 %copy-start.4 = (bf16[16,4096]{1,0:T(8,128)(2,1)}, bf16[16,4096]{1,0:T(8,128)(2,1)S(1)}, u32[]{:S(2)}) copy-start(bf16[16,4096]{1,0:T(8,128)(2,1)S(1)} %collective-permute-done.4.refs_10_) | copy-start | bytes 393220
  32.2 5.6 %collective-permute-start.5 = (bf16[16,4096]{1,0:T(8,128)(2,1)S(1)}, bf16[16,4096]{1,0:T(8,128)(2,1)S(1)}, u32[]{:S(2)}, u32[]{:S(2)}) collective-permute-start(bf16[16,4096]{1,0:T(8,128)(2,1)S(1)} %collective-permute-done.4.refs_10_), channel_id=1, source_target_pairs={{0,32},{32,64},{64,96},{96,128},{128,160},{160,192},{192,224},{224... | collective-permute-start | bytes 393224 | tf_op jit(solution)/shard_map/ppermute | solution.py:50
  32.2 5.6 %collective-permute-start.14 = (bf16[16,4096]{1,0:T(8,128)(2,1)S(1)}, bf16[16,4096]{1,0:T(8,128)(2,1)S(1)}, u32[]{:S(2)}, u32[]{:S(2)}) collective-permute-start(bf16[16,4096]{1,0:T(8,128)(2,1)S(1)} %dynamic-slice_bitcast_fusion.refs_12_), channel_id=1, source_target_pairs={{0,1},{1,0},{2,3},{3,2},{4,5},{5,4},{6,7},{7,6},{8,9},{9,8},{10,11... | collective-permute-start | bytes 393224 | tf_op jit(solution)/shard_map/ppermute | solution.py:600
  34.4 6.2 %collective-permute-start.7 = (bf16[16,4096]{1,0:T(8,128)(2,1)S(1)}, bf16[16,4096]{1,0:T(8,128)(2,1)S(1)}, u32[]{:S(2)}, u32[]{:S(2)}) collective-permute-start(bf16[16,4096]{1,0:T(8,128)(2,1)S(1)} %collective-permute-done.1.refs_5_), channel_id=1, source_target_pairs={{0,1},{1,0},{2,3},{3,2},{4,5},{5,4},{6,7},{7,6},{8,9},{9,8},{10,11... | collective-permute-start | bytes 393224 | tf_op jit(solution)/shard_map/ppermute | solution.py:600
  34.5 6.2 %collective-permute-start.13 = (bf16[16,4096]{1,0:T(8,128)(2,1)S(1)}, bf16[16,4096]{1,0:T(8,128)(2,1)S(1)}, u32[]{:S(2)}, u32[]{:S(2)}) collective-permute-start(bf16[16,4096]{1,0:T(8,128)(2,1)S(1)} %collective-permute-done.refs_11_), channel_id=1, source_target_pairs={{0,1},{1,0},{2,3},{3,2},{4,5},{5,4},{6,7},{7,6},{8,9},{9,8},{10,11... | collective-permute-start | bytes 393224 | tf_op jit(solution)/shard_map/ppermute | solution.py:600
  34.9 13.4 %copy-start.5 = (bf16[16,4096]{1,0:T(8,128)(2,1)}, bf16[16,4096]{1,0:T(8,128)(2,1)S(1)}, u32[]{:S(2)}) copy-start(bf16[16,4096]{1,0:T(8,128)(2,1)S(1)} %collective-permute-done.2.refs_6_) | copy-start | bytes 393220
  34.9 6.2 %collective-permute-start.3 = (bf16[16,4096]{1,0:T(8,128)(2,1)S(1)}, bf16[16,4096]{1,0:T(8,128)(2,1)S(1)}, u32[]{:S(2)}, u32[]{:S(2)}) collective-permute-start(bf16[16,4096]{1,0:T(8,128)(2,1)S(1)} %collective-permute-done.2.refs_6_), channel_id=1, source_target_pairs={{0,224},{32,0},{64,32},{96,64},{128,96},{160,128},{192,160},{224,1... | collective-permute-start | bytes 393224 | tf_op jit(solution)/shard_map/ppermute | solution.py:53
  37.8 10.5 %copy-start.6 = (bf16[16,4096]{1,0:T(8,128)(2,1)}, bf16[16,4096]{1,0:T(8,128)(2,1)S(1)}, u32[]{:S(2)}) copy-start(bf16[16,4096]{1,0:T(8,128)(2,1)S(1)} %collective-permute-done.5.refs_9_) | copy-start | bytes 393220
  37.8 5.0 %collective-permute-start.6 = (bf16[16,4096]{1,0:T(8,128)(2,1)S(1)}, bf16[16,4096]{1,0:T(8,128)(2,1)S(1)}, u32[]{:S(2)}, u32[]{:S(2)}) collective-permute-start(bf16[16,4096]{1,0:T(8,128)(2,1)S(1)} %collective-permute-done.5.refs_9_), channel_id=1, source_target_pairs={{0,32},{32,64},{64,96},{96,128},{128,160},{160,192},{192,224},{224... | collective-permute-start | bytes 393224 | tf_op jit(solution)/shard_map/ppermute | solution.py:50
  37.8 10.5 %copy-start.7 = (bf16[16,4096]{1,0:T(8,128)(2,1)}, bf16[16,4096]{1,0:T(8,128)(2,1)S(1)}, u32[]{:S(2)}) copy-start(bf16[16,4096]{1,0:T(8,128)(2,1)S(1)} %collective-permute-done.14.refs_20_) | copy-start | bytes 393220
  37.8 8.8 %collective-permute-start.8 = (bf16[16,4096]{1,0:T(8,128)(2,1)S(1)}, bf16[16,4096]{1,0:T(8,128)(2,1)S(1)}, u32[]{:S(2)}, u32[]{:S(2)}) collective-permute-start(bf16[16,4096]{1,0:T(8,128)(2,1)S(1)} %collective-permute-done.2.refs_6_), channel_id=1, source_target_pairs={{0,1},{1,0},{2,3},{3,2},{4,5},{5,4},{6,7},{7,6},{8,9},{9,8},{10,11... | collective-permute-start | bytes 393224 | tf_op jit(solution)/shard_map/ppermute | solution.py:600
  40.6 6.1 %copy-start.8 = (bf16[16,4096]{1,0:T(8,128)(2,1)}, bf16[16,4096]{1,0:T(8,128)(2,1)S(1)}, u32[]{:S(2)}) copy-start(bf16[16,4096]{1,0:T(8,128)(2,1)S(1)} %collective-permute-done.7.refs_13_) | copy-start | bytes 393220
  40.6 6.1 %collective-permute-start.12 = (bf16[16,4096]{1,0:T(8,128)(2,1)S(1)}, bf16[16,4096]{1,0:T(8,128)(2,1)S(1)}, u32[]{:S(2)}, u32[]{:S(2)}) collective-permute-start(bf16[16,4096]{1,0:T(8,128)(2,1)S(1)} %collective-permute-done.4.refs_10_), channel_id=1, source_target_pairs={{0,1},{1,0},{2,3},{3,2},{4,5},{5,4},{6,7},{7,6},{8,9},{9,8},{10,11... | collective-permute-start | bytes 393224 | tf_op jit(solution)/shard_map/ppermute | solution.py:600
  40.7 6.9 %copy-start.9 = (bf16[16,4096]{1,0:T(8,128)(2,1)}, bf16[16,4096]{1,0:T(8,128)(2,1)S(1)}, u32[]{:S(2)}) copy-start(bf16[16,4096]{1,0:T(8,128)(2,1)S(1)} %collective-permute-done.13.refs_19_) | copy-start | bytes 393220
  40.7 6.0 %collective-permute-start.11 = (bf16[16,4096]{1,0:T(8,128)(2,1)S(1)}, bf16[16,4096]{1,0:T(8,128)(2,1)S(1)}, u32[]{:S(2)}, u32[]{:S(2)}) collective-permute-start(bf16[16,4096]{1,0:T(8,128)(2,1)S(1)} %collective-permute-done.5.refs_9_), channel_id=1, source_target_pairs={{0,1},{1,0},{2,3},{3,2},{4,5},{5,4},{6,7},{7,6},{8,9},{9,8},{10,11... | collective-permute-start | bytes 393224 | tf_op jit(solution)/shard_map/ppermute | solution.py:600
  41.1 6.5 %copy-start.10 = (bf16[16,4096]{1,0:T(8,128)(2,1)}, bf16[16,4096]{1,0:T(8,128)(2,1)S(1)}, u32[]{:S(2)}) copy-start(bf16[16,4096]{1,0:T(8,128)(2,1)S(1)} %collective-permute-done.3.refs_7_) | copy-start | bytes 393220
  41.1 5.6 %collective-permute-start.9 = (bf16[16,4096]{1,0:T(8,128)(2,1)S(1)}, bf16[16,4096]{1,0:T(8,128)(2,1)S(1)}, u32[]{:S(2)}, u32[]{:S(2)}) collective-permute-start(bf16[16,4096]{1,0:T(8,128)(2,1)S(1)} %collective-permute-done.3.refs_7_), channel_id=1, source_target_pairs={{0,1},{1,0},{2,3},{3,2},{4,5},{5,4},{6,7},{7,6},{8,9},{9,8},{10,11... | collective-permute-start | bytes 393224 | tf_op jit(solution)/shard_map/ppermute | solution.py:600
  42.8 4.8 %copy-start.11 = (bf16[16,4096]{1,0:T(8,128)(2,1)}, bf16[16,4096]{1,0:T(8,128)(2,1)S(1)}, u32[]{:S(2)}) copy-start(bf16[16,4096]{1,0:T(8,128)(2,1)S(1)} %collective-permute-done.6.refs_8_) | copy-start | bytes 393220
  42.8 4.8 %collective-permute-start.10 = (bf16[16,4096]{1,0:T(8,128)(2,1)S(1)}, bf16[16,4096]{1,0:T(8,128)(2,1)S(1)}, u32[]{:S(2)}, u32[]{:S(2)}) collective-permute-start(bf16[16,4096]{1,0:T(8,128)(2,1)S(1)} %collective-permute-done.6.refs_8_), channel_id=1, source_target_pairs={{0,1},{1,0},{2,3},{3,2},{4,5},{5,4},{6,7},{7,6},{8,9},{9,8},{10,11... | collective-permute-start | bytes 393224 | tf_op jit(solution)/shard_map/ppermute | solution.py:600
  46.6 1.7 %copy-start.12 = (bf16[16,4096]{1,0:T(8,128)(2,1)}, bf16[16,4096]{1,0:T(8,128)(2,1)S(1)}, u32[]{:S(2)}) copy-start(bf16[16,4096]{1,0:T(8,128)(2,1)S(1)} %collective-permute-done.8.refs_14_) | copy-start | bytes 393220
  46.6 1.0 copy-start.13
  46.7 1.0 copy-start.15
  46.7 1.0 copy-start.14
  53.7 12.6 %copy-start.17 = (bf16[192,128]{1,0:T(8,128)(2,1)S(1)}, bf16[192,128]{1,0:T(8,128)(2,1)}, u32[]{:S(2)}) copy-start(bf16[192,128]{1,0:T(8,128)(2,1)} %side.1.refs_2_) | copy-start | bytes 147460
  62.8 23.2 %all-to-all-start.1 = ((bf16[8,128,128]{2,1,0:T(8,128)(2,1)}), bf16[8,128,128]{2,1,0:T(8,128)(2,1)S(1)}, u32[]{:S(2)}, u32[]{:S(2)}) async-start(bf16[8,128,128]{2,1,0:T(8,128)(2,1)} %get-tuple-element.34), calls=%async_computation.1 | async-start | bytes 524288 | tf_op jit(solution)/shard_map/all_to_all | solution.py:610
  66.3 10.3 %collective-permute-start.21 = (bf16[192,128]{1,0:T(8,128)(2,1)S(1)}, bf16[192,128]{1,0:T(8,128)(2,1)S(1)}, u32[]{:S(2)}, u32[]{:S(2)}) collective-permute-start(bf16[192,128]{1,0:T(8,128)(2,1)S(1)} %copy-done.17), channel_id=1, source_target_pairs={{0,32},{32,64},{64,96},{96,128},{128,160},{160,192},{192,224},{224... | collective-permute-start | bytes 147464 | tf_op jit(solution)/shard_map/ppermute | solution.py:605
  67.6 12.3 %collective-permute-start.20 = (bf16[192,128]{1,0:T(8,128)(2,1)S(1)}, bf16[192,128]{1,0:T(8,128)(2,1)S(1)}, u32[]{:S(2)}, u32[]{:S(2)}) collective-permute-start(bf16[192,128]{1,0:T(8,128)(2,1)S(1)} %copy-done.17), channel_id=1, source_target_pairs={{0,64},{32,96},{64,128},{96,160},{128,192},{160,224},{192,0},{224,... | collective-permute-start | bytes 147464 | tf_op jit(solution)/shard_map/ppermute | solution.py:605
  69.7 12.0 %collective-permute-start.19 = (bf16[192,128]{1,0:T(8,128)(2,1)S(1)}, bf16[192,128]{1,0:T(8,128)(2,1)S(1)}, u32[]{:S(2)}, u32[]{:S(2)}) collective-permute-start(bf16[192,128]{1,0:T(8,128)(2,1)S(1)} %copy-done.17), channel_id=1, source_target_pairs={{0,96},{32,128},{64,160},{96,192},{128,224},{160,0},{192,32},{224,... | collective-permute-start | bytes 147464 | tf_op jit(solution)/shard_map/ppermute | solution.py:605
  72.1 12.6 %collective-permute-start.18 = (bf16[192,128]{1,0:T(8,128)(2,1)S(1)}, bf16[192,128]{1,0:T(8,128)(2,1)S(1)}, u32[]{:S(2)}, u32[]{:S(2)}) collective-permute-start(bf16[192,128]{1,0:T(8,128)(2,1)S(1)} %copy-done.17), channel_id=1, source_target_pairs={{0,128},{32,160},{64,192},{96,224},{128,0},{160,32},{192,64},{224,... | collective-permute-start | bytes 147464 | tf_op jit(solution)/shard_map/ppermute | solution.py:605
  74.2 10.6 %collective-permute-start.17 = (bf16[192,128]{1,0:T(8,128)(2,1)S(1)}, bf16[192,128]{1,0:T(8,128)(2,1)S(1)}, u32[]{:S(2)}, u32[]{:S(2)}) collective-permute-start(bf16[192,128]{1,0:T(8,128)(2,1)S(1)} %copy-done.17), channel_id=1, source_target_pairs={{0,160},{32,192},{64,224},{96,0},{128,32},{160,64},{192,96},{224,1... | collective-permute-start | bytes 147464 | tf_op jit(solution)/shard_map/ppermute | solution.py:605
  76.6 9.5 %copy-start.18 = (bf16[192,128]{1,0:T(8,128)(2,1)}, bf16[192,128]{1,0:T(8,128)(2,1)S(1)}, u32[]{:S(2)}) copy-start(bf16[192,128]{1,0:T(8,128)(2,1)S(1)} %collective-permute-done.21.refs_9_) | copy-start | bytes 147460
  76.6 9.4 %collective-permute-start.16 = (bf16[192,128]{1,0:T(8,128)(2,1)S(1)}, bf16[192,128]{1,0:T(8,128)(2,1)S(1)}, u32[]{:S(2)}, u32[]{:S(2)}) collective-permute-start(bf16[192,128]{1,0:T(8,128)(2,1)S(1)} %copy-done.17), channel_id=1, source_target_pairs={{0,192},{32,224},{64,0},{96,32},{128,64},{160,96},{192,128},{224,1... | collective-permute-start | bytes 147464 | tf_op jit(solution)/shard_map/ppermute | solution.py:605
  79.9 6.2 %copy-start.19 = (bf16[192,128]{1,0:T(8,128)(2,1)}, bf16[192,128]{1,0:T(8,128)(2,1)S(1)}, u32[]{:S(2)}) copy-start(bf16[192,128]{1,0:T(8,128)(2,1)S(1)} %collective-permute-done.20.refs_8_) | copy-start | bytes 147460
  79.9 6.2 %collective-permute-start.15 = (bf16[192,128]{1,0:T(8,128)(2,1)S(1)}, bf16[192,128]{1,0:T(8,128)(2,1)S(1)}, u32[]{:S(2)}, u32[]{:S(2)}) collective-permute-start(bf16[192,128]{1,0:T(8,128)(2,1)S(1)} %copy-done.17), channel_id=1, source_target_pairs={{0,224},{32,0},{64,32},{96,64},{128,96},{160,128},{192,160},{224,1... | collective-permute-start | bytes 147464 | tf_op jit(solution)/shard_map/ppermute | solution.py:605
  81.7 4.4 %copy-start.20 = (bf16[192,128]{1,0:T(8,128)(2,1)}, bf16[192,128]{1,0:T(8,128)(2,1)S(1)}, u32[]{:S(2)}) copy-start(bf16[192,128]{1,0:T(8,128)(2,1)S(1)} %collective-permute-done.19.refs_7_) | copy-start | bytes 147460
  84.8 1.4 copy-start.21
  84.8 1.4 copy-start.22
  94.1 5.8 %collective-permute-start.22 = (f32[16,144,256]{2,1,0:T(8,128)}, f32[16,144,256]{2,1,0:T(8,128)}, u32[]{:S(2)}, u32[]{:S(2)}) collective-permute-start(f32[16,144,256]{2,1,0:T(8,128)} %get-tuple-element.41), channel_id=1, source_target_pairs={{0,1},{1,0},{2,3},{3,2},{4,5},{5,4},{6,7},{7,6},{8,9},{9,8},{10,11... | collective-permute-start | bytes 7077896 | tf_op jit(solution)/shard_map/ppermute | solution.py:616
  127.9 11.2 %all-to-all-start.3 = ((f32[8,16,256]{2,1,0:T(8,128)}), f32[8,16,256]{2,1,0:T(8,128)S(1)}, u32[]{:S(2)}, u32[]{:S(2)}) async-start(f32[8,16,256]{2,1,0:T(8,128)} %bitcast.9), calls=%async_computation.3 | async-start | bytes 262144 | tf_op jit(solution)/shard_map/all_to_all | solution.py:622
  151.3 5.4 %collective-permute-start.23 = (f32[32,4096]{1,0:T(8,128)S(1)}, f32[32,4096]{1,0:T(8,128)S(1)}, u32[]{:S(2)}, u32[]{:S(2)}) collective-permute-start(f32[32,4096]{1,0:T(8,128)S(1)} %bitcast.19), channel_id=1, source_target_pairs={{0,1},{1,0},{2,3},{3,2},{4,5},{5,4},{6,7},{7,6},{8,9},{9,8},{10,11... | collective-permute-start | bytes 1572872 | tf_op jit(solution)/shard_map/ppermute | solution.py:626
  (4 other events, 2.6 us)

commit v6 on v5

--- a/solution.py
+++ b/solution.py
@@ -39,22 +39,28 @@
     return hi, lo
 
 
-def ring_gather(block, axis, gate):
+def ring_first(block, axis):
+    n = lax.axis_size(axis)
+    up = [(i, (i + 1) % n) for i in range(n)]
+    down = [(i, (i - 1) % n) for i in range(n)]
+    return lax.ppermute(block, axis, up), lax.ppermute(block, axis, down)
+
+
+def ring_gather(block, fwd, bwd, axis, gate):
     n = lax.axis_size(axis)
     up = [(i, (i + 1) % n) for i in range(n)]
     down = [(i, (i - 1) % n) for i in range(n)]
     found = [None] * n
-    found[0] = block
-    fwd = bwd = block
-    for k in range(1, n // 2 + 1):
+    found[0], found[1], found[n - 1] = block, fwd, bwd
+    for k in range(2, n // 2 + 1):
         fwd = lax.ppermute(fwd, axis, up)
         found[k] = fwd
         if k < n - n // 2:
             bwd = lax.ppermute(bwd, axis, down)
             found[n - k] = bwd
-        if k == 1:
+        if k == 2:
             fwd, bwd, _ = lax.optimization_barrier((fwd, bwd, gate))
-            found[1], found[n - 1] = fwd, bwd
+            found[2], found[n - 2] = fwd, bwd
     return found
 
 
@@ -589,14 +595,16 @@
     meta = jnp.stack([core, tile_harmful_flag[0], tile_valid_count[0]]).astype(jnp.int32)
     up_half = lax.dynamic_slice_in_dim(adapter_up_weight[0], core * half, half, axis=1)
     up_half, position = lax.optimization_barrier((up_half, tile_reference_position))
+    fwd, bwd = ring_first(up_half, SEC)
     ordered = order(position, meta, frozen_reference_states[0])
+    ordered, fwd, bwd = lax.optimization_barrier((ordered, fwd, bwd))
     refs = lax.all_to_all(ordered, DP, split_axis=0, concat_axis=0, tiled=True)
     _, stream, down, up, gains = lax.optimization_barrier(
         (ordered, layer_input_states[0, 0], adapter_down_weight[0], adapter_up_weight[0], layer_norm_gain)
     )
 
     normed, lrt, irms, dg = forward(stream, down, gains)
-    mine = ring_gather(up_half, SEC, lrt)[::-1]
+    mine = ring_gather(up_half, fwd, bwd, SEC, lrt)[::-1]
     other = [lax.ppermute(block, "core", swap) for block in mine]
 
     side = side_of(meta, stream, dg, lrt, irms, mine, other)
@@ -604,7 +612,7 @@
     for j in range(1, layers):
         sides.append(lax.ppermute(side, SEC, [(t, (t - j) % layers) for t in range(layers)]))
 
-    refs, _ = lax.optimization_barrier((refs, side))
+    refs, *sides = lax.optimization_barrier((refs, *sides))
 
     own, own_up = own_gradient(meta, refs, stream, up, lrt, mine, other)
     own_up = lax.all_to_all(own_up, SEC, 0, 0, tiled=True)

time: 158 us -> 166 us (1.051)
  waiting for transfers between devices: 20.2 us -> 30.4 us
  starting transfers between devices: 56.8 us -> 54 us
    all_to_all x1, waiting for transfers between devices: 0.01 us -> 9.49 us  [shards(): own_up = lax.all_to_all(own_up, SEC, 0, 0, tiled=True)]
    ppermute x0 -> x2, starting transfers between devices: none -> 6.48 us  [ring_first(): return (lax.ppermute(block, axis, up), lax.ppermute(block, axis, down))]
    ppermute x3 -> x2, starting transfers between devices: 11.2 us -> 4.95 us  [ring_gather(): bwd = lax.ppermute(bwd, axis, down)]
    ppermute x7, starting transfers between devices: 14.8 us -> 10.9 us  [shards(): lax.ppermute(side, SEC, [(t, (t - j) % layers) for t in range(layers)])]
    ppermute x8, starting transfers between devices: 10.2 us -> 7.84 us  [shards(): other = [lax.ppermute(block, 'core', swap) for block in mine]]
    ppermute x7, waiting for transfers between devices: 4.33 us -> 6.19 us  [shards(): lax.ppermute(side, SEC, [(t, (t - j) % layers) for t in range(layers)])]
    ppermute x1, starting transfers between devices: 1.3 us -> 2.99 us  [shards(): received = lax.ppermute(given, 'core', swap)]
    ppermute x4 -> x3, waiting for transfers between devices: 5.07 us -> 3.91 us  [ring_gather(): fwd = lax.ppermute(fwd, axis, up)]
  transfers between devices with their start and end apart: 27 -> 27, of which waited for: 9 -> 11; matrix products, arithmetic and copies ran while one was open for 0% -> 1% of each run, Pallas kernels for 9% -> 10%
where the time goes in v6:
time: 166 us
  starting transfers between devices  54 us (33%)
  blocking collectives  37 us (22%)
  Pallas kernels  33.5 us (20%)
  waiting for transfers between devices  30.4 us (18%)
  other arithmetic  5.92 us (4%)
  local copies, waits for them, and re-layouts  2.42 us (1%)
  between operations  2.31 us (1%)
    pallas_call x5, Pallas kernels, call(): pl.pallas_call(body, out_shape=out_shape, in_specs=[smem()] * count + [in...  30.3 us
    all_to_all x1, blocking collectives, shards(): lax.all_to_all((kept + received).astype(bf16), CHIPS, 0, 0, tiled=True)  24.9 us
    all_to_all x1, blocking collectives, shards(): lax.all_to_all(jnp.broadcast_to(final, (chips,) + final.shape), CHIPS, 0,...  12.1 us
    ppermute x7, starting transfers between devices, shards(): lax.ppermute(side, SEC, [(t, (t - j) % layers) for t in range(layers)])  10.9 us
    all_to_all x1, waiting for transfers between devices, shards(): own_up = lax.all_to_all(own_up, SEC, 0, 0, tiled=True)  9.49 us
    all_to_all x1, starting transfers between devices, shards(): refs = lax.all_to_all(ordered, DP, split_axis=0, concat_axis=0, tiled=True)  9.06 us
    ppermute x8, starting transfers between devices, shards(): other = [lax.ppermute(block, 'core', swap) for block in mine]  7.84 us
    all_to_all x1, waiting for transfers between devices, shards(): lax.all_to_all(grad_up.reshape(layers, rank, chunk), SEC, 0, 0, tiled=True)  7.84 us
  transfers between devices with their start and end apart: 27, of which 11 were waited for; matrix products, arithmetic and copies ran while one was open for 1% of the time, Pallas kernels for 10%

profile of v6, /device:TPU:1, one launch (start us, length us, event | category | flops | bytes accessed | tf_op | source)
XLA Modules:
  0.0 165.6 jit_solution(684037019933562884)
XLA Ops:
  0.6 0.9 dynamic-slice_bitcast_fusion.refs_12_
  1.6 6.5 %collective-permute-start.1 = (bf16[16,4096]{1,0:T(8,128)(2,1)S(1)}, bf16[16,4096]{1,0:T(8,128)(2,1)S(1)}, u32[]{:S(2)}, u32[]{:S(2)}) collective-permute-start(bf16[16,4096]{1,0:T(8,128)(2,1)S(1)} %dynamic-slice_bitcast_fusion.refs_12_), channel_id=1, source_target_pairs={{0,224},{32,0},{64,32},{96,64},{128,96},{160,128},{192,160},{224,1... | collective-permute-start | bytes 393224 | tf_op jit(solution)/shard_map/ppermute | solution.py:46
  9.3 0.7 pad_add_fusion.1.meta_ref.refs_0_
  10.0 3.2 %order.1 = bf16[32,136,256]{2,1,0:T(8,128)(2,1)} custom-call(s32[32]{0:T(128)} %position_ref, s32[3]{0:T(128)} %pad_add_fusion.1.meta_ref.refs_0_, bf16[32,128,256]{2,1,0:T(8,128)(2,1)} %bitcast.18), custom_call_target="tpu_custom_call" | custom-call | tf_op jit(solution)/shard_map/order/pallas_call | solution.py:168
  13.3 9.1 %all-to-all-start = ((bf16[32,136,256]{2,1,0:T(8,128)(2,1)}), bf16[32,136,256]{2,1,0:T(8,128)(2,1)}, u32[]{:S(2)}, u32[]{:S(2)}) async-start(bf16[32,136,256]{2,1,0:T(8,128)(2,1)} %order.1), calls=%async_computation | async-start | bytes 4456448 | tf_op jit(solution)/shard_map/all_to_all | solution.py:601
  22.3 2.1 %collective-permute-start.3 = (bf16[16,4096]{1,0:T(8,128)(2,1)S(1)}, bf16[16,4096]{1,0:T(8,128)(2,1)S(1)}, u32[]{:S(2)}, u32[]{:S(2)}) collective-permute-start(bf16[16,4096]{1,0:T(8,128)(2,1)S(1)} %collective-permute-done.1.refs_5_), channel_id=1, source_target_pairs={{0,224},{32,0},{64,32},{96,64},{128,96},{160,128},{192,160},{224,1... | collective-permute-start | bytes 393224 | tf_op jit(solution)/shard_map/ppermute | solution.py:59
  24.4 4.8 %forward.1 = (bf16[128,8192]{1,0:T(8,128)(2,1)}, bf16[16,128]{1,0:T(8,128)(2,1)}, f32[8,128]{1,0:T(8,128)}, bf16[2,16,8192]{2,1,0:T(8,128)(2,1)}) custom-call(bf16[128,8192]{1,0:T(8,128)(2,1)} %bitcast.23, bf16[16,8192]{1,0:T(8,128)(2,1)} %bitcast.28, f32[1,8192]{1,0:T(1,128)} %refs_2_), custom_call_target="tpu_custom_call" | custom-call | flops 4000000000 | bytes 12000000 | tf_op jit(solution)/shard_map/forward/pallas_call | solution.py:96
  29.2 1.0 collective-permute-done.2.refs_10_
  30.2 1.4 collective-permute-start.14
  31.7 0.4 collective-permute-start.13
  32.1 2.9 %collective-permute-start.4 = (bf16[16,4096]{1,0:T(8,128)(2,1)S(1)}, bf16[16,4096]{1,0:T(8,128)(2,1)S(1)}, u32[]{:S(2)}, u32[]{:S(2)}) collective-permute-start(bf16[16,4096]{1,0:T(8,128)(2,1)S(1)} %collective-permute-done.3.refs_6_), channel_id=1, source_target_pairs={{0,224},{32,0},{64,32},{96,64},{128,96},{160,128},{192,160},{224,1... | collective-permute-start | bytes 393224 | tf_op jit(solution)/shard_map/ppermute | solution.py:59
  35.0 0.6 collective-permute-done.5.refs_9_
  35.6 2.2 %collective-permute-start.8 = (bf16[16,4096]{1,0:T(8,128)(2,1)S(1)}, bf16[16,4096]{1,0:T(8,128)(2,1)S(1)}, u32[]{:S(2)}, u32[]{:S(2)}) collective-permute-start(bf16[16,4096]{1,0:T(8,128)(2,1)S(1)} %collective-permute-done.3.refs_6_), channel_id=1, source_target_pairs={{0,1},{1,0},{2,3},{3,2},{4,5},{5,4},{6,7},{7,6},{8,9},{9,8},{10,11... | collective-permute-start | bytes 393224 | tf_op jit(solution)/shard_map/ppermute | solution.py:608
  37.8 0.1 collective-permute-start.12
  37.9 0.4 collective-permute-start.11
  38.3 0.4 collective-permute-start.9
  38.7 2.3 %collective-permute-done.6.refs_8_ = bf16[16,4096]{1,0:T(8,128)(2,1)S(1)} collective-permute-done((bf16[16,4096]{1,0:T(8,128)(2,1)S(1)}, bf16[16,4096]{1,0:T(8,128)(2,1)S(1)}, u32[]{:S(2)}, u32[]{:S(2)}) %collective-permute-start.6) | collective-permute-done | bytes 131104 | tf_op jit(solution)/shard_map/ppermute | solution.py:56
  41.0 2.8 %collective-permute-start.10 = (bf16[16,4096]{1,0:T(8,128)(2,1)S(1)}, bf16[16,4096]{1,0:T(8,128)(2,1)S(1)}, u32[]{:S(2)}, u32[]{:S(2)}) collective-permute-start(bf16[16,4096]{1,0:T(8,128)(2,1)S(1)} %collective-permute-done.6.refs_8_), channel_id=1, source_target_pairs={{0,1},{1,0},{2,3},{3,2},{4,5},{5,4},{6,7},{7,6},{8,9},{9,8},{10,11... | collective-permute-start | bytes 393224 | tf_op jit(solution)/shard_map/ppermute | solution.py:608
  44.0 0.9 collective-permute-done.10.refs_16_
  44.9 0.6 copy-done.16
  45.6 5.3 %side.1.refs_2_ = bf16[192,128]{1,0:T(8,128)(2,1)} custom-call(s32[3]{0:T(128)} %pad_add_fusion.1.meta_ref.refs_0_, bf16[128,8192]{1,0:T(8,128)(2,1)} %bitcast.24, bf16[2,16,8192]{2,1,0:T(8,128)(2,1)} %get-tuple-element.39.refs_2_.refs_13_.refs_8_, bf16[16,128]{1,0:T(8,128)(2,1)} %get-tuple-element.40.refs_3_.refs_4_, f32[8,128]{1,0:T(8,128)} %get-tuple-element.41.refs_4_, ...), custom_call_target="tpu_custom_call" | custom-call | flops 5000000000 | bytes 15000000 | tf_op jit(solution)/shard_map/side/pallas_call | solution.py:96
  50.9 0.3 collective-permute-start.21
  51.3 1.3 collective-permute-start.19
  52.6 4.2 %collective-permute-start.18 = (bf16[192,128]{1,0:T(8,128)(2,1)}, bf16[192,128]{1,0:T(8,128)(2,1)S(1)}, u32[]{:S(2)}, u32[]{:S(2)}) collective-permute-start(bf16[192,128]{1,0:T(8,128)(2,1)} %side.1.refs_2_), channel_id=1, source_target_pairs={{0,128},{32,160},{64,192},{96,224},{128,0},{160,32},{192,64},{224,... | collective-permute-start | bytes 147464 | tf_op jit(solution)/shard_map/ppermute | solution.py:613
  56.8 1.4 collective-permute-start.17
  58.2 2.3 %collective-permute-start.16 = (bf16[192,128]{1,0:T(8,128)(2,1)}, bf16[192,128]{1,0:T(8,128)(2,1)S(1)}, u32[]{:S(2)}, u32[]{:S(2)}) collective-permute-start(bf16[192,128]{1,0:T(8,128)(2,1)} %side.1.refs_2_), channel_id=1, source_target_pairs={{0,192},{32,224},{64,0},{96,32},{128,64},{160,96},{192,128},{224,1... | collective-permute-start | bytes 147464 | tf_op jit(solution)/shard_map/ppermute | solution.py:613
  60.5 1.4 collective-permute-start.15
  61.9 0.3 collective-permute-done.17.refs_5_
  62.2 3.9 %collective-permute-done.16.refs_4_ = bf16[192,128]{1,0:T(8,128)(2,1)S(1)} collective-permute-done((bf16[192,128]{1,0:T(8,128)(2,1)}, bf16[192,128]{1,0:T(8,128)(2,1)S(1)}, u32[]{:S(2)}, u32[]{:S(2)}) %collective-permute-start.16) | collective-permute-done | bytes 49184 | tf_op jit(solution)/shard_map/ppermute | solution.py:613
  66.0 2.1 %collective-permute-done.15.refs_3_ = bf16[192,128]{1,0:T(8,128)(2,1)S(1)} collective-permute-done((bf16[192,128]{1,0:T(8,128)(2,1)}, bf16[192,128]{1,0:T(8,128)(2,1)S(1)}, u32[]{:S(2)}, u32[]{:S(2)}) %collective-permute-start.15) | collective-permute-done | bytes 49184 | tf_op jit(solution)/shard_map/ppermute | solution.py:613
  68.1 9.0 %own.1 = (bf16[128,8192]{1,0:T(8,128)(2,1)}, bf16[8,128,128]{2,1,0:T(8,128)(2,1)}) custom-call(s32[3]{0:T(128)} %pad_add_fusion.1.meta_ref.refs_0_, bf16[32,136,256]{2,1,0:T(8,128)(2,1)} %all-to-all-done.refs_1_, bf16[128,8192]{1,0:T(8,128)(2,1)} %bitcast.25, bf16[16,8192]{1,0:T(8,128)(2,1)} %bitcast.22, bf16[16,128]{1,0:T(8,128)(2,1)} %get-tuple-element.40.refs_3_.refs_4_, ...), custom_call_target="tpu_custom_call" | custom-call | flops 8000000000 | bytes 24000000 | tf_op jit(solution)/shard_map/own/pallas_call | solution.py:96
  77.1 4.6 %all-to-all-start.1 = ((bf16[8,128,128]{2,1,0:T(8,128)(2,1)}), bf16[8,128,128]{2,1,0:T(8,128)(2,1)S(1)}, u32[]{:S(2)}, u32[]{:S(2)}) async-start(bf16[8,128,128]{2,1,0:T(8,128)(2,1)} %get-tuple-element.48), calls=%async_computation.1 | async-start | bytes 524288 | tf_op jit(solution)/shard_map/all_to_all | solution.py:618
  81.7 0.6 pad_add_fusion.refs_0_
  82.3 9.5 %all-to-all-done.1.refs_1_ = bf16[8,128,128]{2,1,0:T(8,128)(2,1)S(1)} async-done(((bf16[8,128,128]{2,1,0:T(8,128)(2,1)}), bf16[8,128,128]{2,1,0:T(8,128)(2,1)S(1)}, u32[]{:S(2)}, u32[]{:S(2)}) %all-to-all-start.1) | async-done | bytes 262176 | tf_op jit(solution)/shard_map/all_to_all | solution.py:618
  91.8 0.7 copy-done
  92.5 7.3 %given.1 = (f32[16,144,256]{2,1,0:T(8,128)}, bf16[16,128]{1,0:T(8,128)(2,1)}, bf16[128,128]{1,0:T(8,128)(2,1)}, bf16[128,128]{1,0:T(8,128)(2,1)}, bf16[2,128,16]{2,1,0:T(8,128)(2,1)}) custom-call(s32[2]{0:T(128)} %pad_add_fusion.refs_0_, bf16[8,128,128]{2,1,0:T(8,128)(2,1)} %copy-done, bf16[192,128]{1,0:T(8,128)(2,1)} %side.1.refs_2_, ...), custom_call_target="tpu_custom_call" | custom-call | flops 5000000000 | bytes 15000000 | tf_op jit(solution)/shard_map/given/pallas_call | solution.py:96
  99.8 3.0 %collective-permute-start.22 = (f32[16,144,256]{2,1,0:T(8,128)}, f32[16,144,256]{2,1,0:T(8,128)}, u32[]{:S(2)}, u32[]{:S(2)}) collective-permute-start(f32[16,144,256]{2,1,0:T(8,128)} %get-tuple-element.63), channel_id=1, source_target_pairs={{0,1},{1,0},{2,3},{3,2},{4,5},{5,4},{6,7},{7,6},{8,9},{9,8},{10,11... | collective-permute-start | bytes 7077896 | tf_op jit(solution)/shard_map/ppermute | solution.py:624
  102.8 4.0 %kept.1 = f32[16,144,256]{2,1,0:T(8,128)} custom-call(s32[1]{0:T(128)} %bitcast.refs_0_, bf16[16,128]{1,0:T(8,128)(2,1)} %get-tuple-element.59.refs_1_, bf16[128,128]{1,0:T(8,128)(2,1)} %get-tuple-element.60.refs_2_, bf16[128,128]{1,0:T(8,128)(2,1)} %get-tuple-element.61.refs_3_, bf16[2,128,16]{2,1,0:T(8,128)(2,1)} %get-tuple-element.62.refs_4_, ...), custom_call_target="tpu_custom_call" | custom-call | flops 4000000000 | bytes 12000000 | tf_op jit(solution)/shard_map/kept/pallas_call | solution.py:96
  106.8 0.5 collective-permute-done.22
  107.3 2.7 %add_convert_fusion = bf16[16,144,256]{2,1,0:T(8,128)(2,1)S(1)} fusion(f32[16,144,256]{2,1,0:T(8,128)} %kept.1, f32[16,144,256]{2,1,0:T(8,128)} %collective-permute-done.22), kind=kLoop, calls=%fused_computation | loop fusion | flops 1179648 | bytes 5898240 | tf_op jit(solution)/shard_map/convert_element_type | solution.py:626
  110.0 24.9 %all_to_all.25 = bf16[16,144,256]{2,1,0:T(8,128)(2,1)S(1)} all-to-all(bf16[16,144,256]{2,1,0:T(8,128)(2,1)S(1)} %add_convert_fusion), channel_id=1, replica_groups=mesh['section'=8,'y'=4,'x'=4,'core'=2] {'y','x'}, dimensions={0} | all-to-all | bytes 2359296 | tf_op jit(solution)/shard_map/all_to_all | solution.py:626
  134.8 0.8 convert_reduce_fusion
  135.6 3.4 %all-to-all-start.3 = ((f32[8,16,256]{2,1,0:T(8,128)}), f32[8,16,256]{2,1,0:T(8,128)S(1)}, u32[]{:S(2)}, u32[]{:S(2)}) async-start(f32[8,16,256]{2,1,0:T(8,128)} %bitcast.9), calls=%async_computation.3 | async-start | bytes 262144 | tf_op jit(solution)/shard_map/all_to_all | solution.py:630
  139.0 7.8 %all-to-all-done.3 = f32[8,16,256]{2,1,0:T(8,128)S(1)} async-done(((f32[8,16,256]{2,1,0:T(8,128)}), f32[8,16,256]{2,1,0:T(8,128)S(1)}, u32[]{:S(2)}, u32[]{:S(2)}) %all-to-all-start.3) | async-done | bytes 131104 | tf_op jit(solution)/shard_map/all_to_all | solution.py:630
  147.0 12.1 %all_to_all.26 = f32[16,32,256]{2,1,0:T(8,128)S(1)} all-to-all(f32[16,32,256]{2,1,0:T(8,128)S(1)} %broadcast_in_dim.13), channel_id=1, replica_groups=mesh['section'=8,'y'=4,'x'=4,'core'=2] {'y','x'}, dimensions={0} | all-to-all | bytes 1048576 | tf_op jit(solution)/shard_map/all_to_all | solution.py:632
  159.1 3.8 %collective-permute-start.23 = (f32[32,4096]{1,0:T(8,128)S(1)}, f32[32,4096]{1,0:T(8,128)S(1)}, u32[]{:S(2)}, u32[]{:S(2)}) collective-permute-start(f32[32,4096]{1,0:T(8,128)S(1)} %bitcast.19), channel_id=1, source_target_pairs={{0,1},{1,0},{2,3},{3,2},{4,5},{5,4},{6,7},{7,6},{8,9},{9,8},{10,11... | collective-permute-start | bytes 1572872 | tf_op jit(solution)/shard_map/ppermute | solution.py:634
  162.9 1.5 collective-permute-done.23
  164.5 1.0 fusion.2
  (74 shorter events, 0.5 us)
Async XLA Ops:
  1.6 28.6 %copy-start.1 = (bf16[16,4096]{1,0:T(8,128)(2,1)}, bf16[16,4096]{1,0:T(8,128)(2,1)S(1)}, u32[]{:S(2)}) copy-start(bf16[16,4096]{1,0:T(8,128)(2,1)S(1)} %dynamic-slice_bitcast_fusion.refs_12_) | copy-start | bytes 393220
  1.6 11.7 %collective-permute-start.1 = (bf16[16,4096]{1,0:T(8,128)(2,1)S(1)}, bf16[16,4096]{1,0:T(8,128)(2,1)S(1)}, u32[]{:S(2)}, u32[]{:S(2)}) collective-permute-start(bf16[16,4096]{1,0:T(8,128)(2,1)S(1)} %dynamic-slice_bitcast_fusion.refs_12_), channel_id=1, source_target_pairs={{0,224},{32,0},{64,32},{96,64},{128,96},{160,128},{192,160},{224,1... | collective-permute-start | bytes 393224 | tf_op jit(solution)/shard_map/ppermute | solution.py:46
  8.0 5.2 %collective-permute-start = (bf16[16,4096]{1,0:T(8,128)(2,1)S(1)}, bf16[16,4096]{1,0:T(8,128)(2,1)S(1)}, u32[]{:S(2)}, u32[]{:S(2)}) collective-permute-start(bf16[16,4096]{1,0:T(8,128)(2,1)S(1)} %dynamic-slice_bitcast_fusion.refs_12_), channel_id=1, source_target_pairs={{0,32},{32,64},{64,96},{96,128},{128,160},{160,192},{192,224},{224... | collective-permute-start | bytes 393224 | tf_op jit(solution)/shard_map/ppermute | solution.py:46
  13.2 18.4 %copy-start.2 = (bf16[16,4096]{1,0:T(8,128)(2,1)}, bf16[16,4096]{1,0:T(8,128)(2,1)S(1)}, u32[]{:S(2)}) copy-start(bf16[16,4096]{1,0:T(8,128)(2,1)S(1)} %collective-permute-done.1.refs_5_) | copy-start | bytes 393220
  13.2 18.5 %copy-start.3 = (bf16[16,4096]{1,0:T(8,128)(2,1)}, bf16[16,4096]{1,0:T(8,128)(2,1)S(1)}, u32[]{:S(2)}) copy-start(bf16[16,4096]{1,0:T(8,128)(2,1)S(1)} %collective-permute-done.refs_11_) | copy-start | bytes 393220
  13.3 54.8 %all-to-all-start = ((bf16[32,136,256]{2,1,0:T(8,128)(2,1)}), bf16[32,136,256]{2,1,0:T(8,128)(2,1)}, u32[]{:S(2)}, u32[]{:S(2)}) async-start(bf16[32,136,256]{2,1,0:T(8,128)(2,1)} %order.1), calls=%async_computation | async-start | bytes 4456448 | tf_op jit(solution)/shard_map/all_to_all | solution.py:601
  22.3 6.8 %collective-permute-start.3 = (bf16[16,4096]{1,0:T(8,128)(2,1)S(1)}, bf16[16,4096]{1,0:T(8,128)(2,1)S(1)}, u32[]{:S(2)}, u32[]{:S(2)}) collective-permute-start(bf16[16,4096]{1,0:T(8,128)(2,1)S(1)} %collective-permute-done.1.refs_5_), channel_id=1, source_target_pairs={{0,224},{32,0},{64,32},{96,64},{128,96},{160,128},{192,160},{224,1... | collective-permute-start | bytes 393224 | tf_op jit(solution)/shard_map/ppermute | solution.py:59
  24.4 5.8 %collective-permute-start.2 = (bf16[16,4096]{1,0:T(8,128)(2,1)S(1)}, bf16[16,4096]{1,0:T(8,128)(2,1)S(1)}, u32[]{:S(2)}, u32[]{:S(2)}) collective-permute-start(bf16[16,4096]{1,0:T(8,128)(2,1)S(1)} %collective-permute-done.refs_11_), channel_id=1, source_target_pairs={{0,32},{32,64},{64,96},{96,128},{128,160},{160,192},{192,224},{224... | collective-permute-start | bytes 393224 | tf_op jit(solution)/shard_map/ppermute | solution.py:56
  29.2 16.4 %copy-start.4 = (bf16[16,4096]{1,0:T(8,128)(2,1)}, bf16[16,4096]{1,0:T(8,128)(2,1)S(1)}, u32[]{:S(2)}) copy-start(bf16[16,4096]{1,0:T(8,128)(2,1)S(1)} %collective-permute-done.3.refs_6_) | copy-start | bytes 393220
  30.2 15.4 %copy-start.5 = (bf16[16,4096]{1,0:T(8,128)(2,1)}, bf16[16,4096]{1,0:T(8,128)(2,1)S(1)}, u32[]{:S(2)}) copy-start(bf16[16,4096]{1,0:T(8,128)(2,1)S(1)} %collective-permute-done.2.refs_10_) | copy-start | bytes 393220
  30.2 5.4 %collective-permute-start.5 = (bf16[16,4096]{1,0:T(8,128)(2,1)S(1)}, bf16[16,4096]{1,0:T(8,128)(2,1)S(1)}, u32[]{:S(2)}, u32[]{:S(2)}) collective-permute-start(bf16[16,4096]{1,0:T(8,128)(2,1)S(1)} %collective-permute-done.2.refs_10_), channel_id=1, source_target_pairs={{0,32},{32,64},{64,96},{96,128},{128,160},{160,192},{192,224},{224... | collective-permute-start | bytes 393224 | tf_op jit(solution)/shard_map/ppermute | solution.py:56
  30.2 5.4 %collective-permute-start.14 = (bf16[16,4096]{1,0:T(8,128)(2,1)S(1)}, bf16[16,4096]{1,0:T(8,128)(2,1)S(1)}, u32[]{:S(2)}, u32[]{:S(2)}) collective-permute-start(bf16[16,4096]{1,0:T(8,128)(2,1)S(1)} %dynamic-slice_bitcast_fusion.refs_12_), channel_id=1, source_target_pairs={{0,1},{1,0},{2,3},{3,2},{4,5},{5,4},{6,7},{7,6},{8,9},{9,8},{10,11... | collective-permute-start | bytes 393224 | tf_op jit(solution)/shard_map/ppermute | solution.py:608
  31.6 6.2 %collective-permute-start.7 = (bf16[16,4096]{1,0:T(8,128)(2,1)S(1)}, bf16[16,4096]{1,0:T(8,128)(2,1)S(1)}, u32[]{:S(2)}, u32[]{:S(2)}) collective-permute-start(bf16[16,4096]{1,0:T(8,128)(2,1)S(1)} %collective-permute-done.1.refs_5_), channel_id=1, source_target_pairs={{0,1},{1,0},{2,3},{3,2},{4,5},{5,4},{6,7},{7,6},{8,9},{9,8},{10,11... | collective-permute-start | bytes 393224 | tf_op jit(solution)/shard_map/ppermute | solution.py:608
  31.7 6.2 %collective-permute-start.13 = (bf16[16,4096]{1,0:T(8,128)(2,1)S(1)}, bf16[16,4096]{1,0:T(8,128)(2,1)S(1)}, u32[]{:S(2)}, u32[]{:S(2)}) collective-permute-start(bf16[16,4096]{1,0:T(8,128)(2,1)S(1)} %collective-permute-done.refs_11_), channel_id=1, source_target_pairs={{0,1},{1,0},{2,3},{3,2},{4,5},{5,4},{6,7},{7,6},{8,9},{9,8},{10,11... | collective-permute-start | bytes 393224 | tf_op jit(solution)/shard_map/ppermute | solution.py:608
  32.1 6.2 %collective-permute-start.4 = (bf16[16,4096]{1,0:T(8,128)(2,1)S(1)}, bf16[16,4096]{1,0:T(8,128)(2,1)S(1)}, u32[]{:S(2)}, u32[]{:S(2)}) collective-permute-start(bf16[16,4096]{1,0:T(8,128)(2,1)S(1)} %collective-permute-done.3.refs_6_), channel_id=1, source_target_pairs={{0,224},{32,0},{64,32},{96,64},{128,96},{160,128},{192,160},{224,1... | collective-permute-start | bytes 393224 | tf_op jit(solution)/shard_map/ppermute | solution.py:59
  35.6 9.9 %copy-start.6 = (bf16[16,4096]{1,0:T(8,128)(2,1)}, bf16[16,4096]{1,0:T(8,128)(2,1)S(1)}, u32[]{:S(2)}) copy-start(bf16[16,4096]{1,0:T(8,128)(2,1)S(1)} %collective-permute-done.5.refs_9_) | copy-start | bytes 393220
  35.6 5.4 %collective-permute-start.6 = (bf16[16,4096]{1,0:T(8,128)(2,1)S(1)}, bf16[16,4096]{1,0:T(8,128)(2,1)S(1)}, u32[]{:S(2)}, u32[]{:S(2)}) collective-permute-start(bf16[16,4096]{1,0:T(8,128)(2,1)S(1)} %collective-permute-done.5.refs_9_), channel_id=1, source_target_pairs={{0,32},{32,64},{64,96},{96,128},{128,160},{160,192},{192,224},{224... | collective-permute-start | bytes 393224 | tf_op jit(solution)/shard_map/ppermute | solution.py:56
  35.6 9.9 %copy-start.7 = (bf16[16,4096]{1,0:T(8,128)(2,1)}, bf16[16,4096]{1,0:T(8,128)(2,1)S(1)}, u32[]{:S(2)}) copy-start(bf16[16,4096]{1,0:T(8,128)(2,1)S(1)} %collective-permute-done.14.refs_20_) | copy-start | bytes 393220
  35.6 8.3 %collective-permute-start.8 = (bf16[16,4096]{1,0:T(8,128)(2,1)S(1)}, bf16[16,4096]{1,0:T(8,128)(2,1)S(1)}, u32[]{:S(2)}, u32[]{:S(2)}) collective-permute-start(bf16[16,4096]{1,0:T(8,128)(2,1)S(1)} %collective-permute-done.3.refs_6_), channel_id=1, source_target_pairs={{0,1},{1,0},{2,3},{3,2},{4,5},{5,4},{6,7},{7,6},{8,9},{9,8},{10,11... | collective-permute-start | bytes 393224 | tf_op jit(solution)/shard_map/ppermute | solution.py:608
  37.8 6.1 %copy-start.8 = (bf16[16,4096]{1,0:T(8,128)(2,1)}, bf16[16,4096]{1,0:T(8,128)(2,1)S(1)}, u32[]{:S(2)}) copy-start(bf16[16,4096]{1,0:T(8,128)(2,1)S(1)} %collective-permute-done.7.refs_13_) | copy-start | bytes 393220
  37.8 6.1 %collective-permute-start.12 = (bf16[16,4096]{1,0:T(8,128)(2,1)S(1)}, bf16[16,4096]{1,0:T(8,128)(2,1)S(1)}, u32[]{:S(2)}, u32[]{:S(2)}) collective-permute-start(bf16[16,4096]{1,0:T(8,128)(2,1)S(1)} %collective-permute-done.2.refs_10_), channel_id=1, source_target_pairs={{0,1},{1,0},{2,3},{3,2},{4,5},{5,4},{6,7},{7,6},{8,9},{9,8},{10,11... | collective-permute-start | bytes 393224 | tf_op jit(solution)/shard_map/ppermute | solution.py:608
  37.9 6.9 %copy-start.9 = (bf16[16,4096]{1,0:T(8,128)(2,1)}, bf16[16,4096]{1,0:T(8,128)(2,1)S(1)}, u32[]{:S(2)}) copy-start(bf16[16,4096]{1,0:T(8,128)(2,1)S(1)} %collective-permute-done.13.refs_19_) | copy-start | bytes 393220
  37.9 6.0 %collective-permute-start.11 = (bf16[16,4096]{1,0:T(8,128)(2,1)S(1)}, bf16[16,4096]{1,0:T(8,128)(2,1)S(1)}, u32[]{:S(2)}, u32[]{:S(2)}) collective-permute-start(bf16[16,4096]{1,0:T(8,128)(2,1)S(1)} %collective-permute-done.5.refs_9_), channel_id=1, source_target_pairs={{0,1},{1,0},{2,3},{3,2},{4,5},{5,4},{6,7},{7,6},{8,9},{9,8},{10,11... | collective-permute-start | bytes 393224 | tf_op jit(solution)/shard_map/ppermute | solution.py:608
  38.3 6.5 %copy-start.10 = (bf16[16,4096]{1,0:T(8,128)(2,1)}, bf16[16,4096]{1,0:T(8,128)(2,1)S(1)}, u32[]{:S(2)}) copy-start(bf16[16,4096]{1,0:T(8,128)(2,1)S(1)} %collective-permute-done.4.refs_7_) | copy-start | bytes 393220
  38.3 5.6 %collective-permute-start.9 = (bf16[16,4096]{1,0:T(8,128)(2,1)S(1)}, bf16[16,4096]{1,0:T(8,128)(2,1)S(1)}, u32[]{:S(2)}, u32[]{:S(2)}) collective-permute-start(bf16[16,4096]{1,0:T(8,128)(2,1)S(1)} %collective-permute-done.4.refs_7_), channel_id=1, source_target_pairs={{0,1},{1,0},{2,3},{3,2},{4,5},{5,4},{6,7},{7,6},{8,9},{9,8},{10,11... | collective-permute-start | bytes 393224 | tf_op jit(solution)/shard_map/ppermute | solution.py:608
  41.0 3.8 %copy-start.11 = (bf16[16,4096]{1,0:T(8,128)(2,1)}, bf16[16,4096]{1,0:T(8,128)(2,1)S(1)}, u32[]{:S(2)}) copy-start(bf16[16,4096]{1,0:T(8,128)(2,1)S(1)} %collective-permute-done.6.refs_8_) | copy-start | bytes 393220
  41.0 3.8 %collective-permute-start.10 = (bf16[16,4096]{1,0:T(8,128)(2,1)S(1)}, bf16[16,4096]{1,0:T(8,128)(2,1)S(1)}, u32[]{:S(2)}, u32[]{:S(2)}) collective-permute-start(bf16[16,4096]{1,0:T(8,128)(2,1)S(1)} %collective-permute-done.6.refs_8_), channel_id=1, source_target_pairs={{0,1},{1,0},{2,3},{3,2},{4,5},{5,4},{6,7},{7,6},{8,9},{9,8},{10,11... | collective-permute-start | bytes 393224 | tf_op jit(solution)/shard_map/ppermute | solution.py:608
  43.9 1.7 %copy-start.12 = (bf16[16,4096]{1,0:T(8,128)(2,1)}, bf16[16,4096]{1,0:T(8,128)(2,1)S(1)}, u32[]{:S(2)}) copy-start(bf16[16,4096]{1,0:T(8,128)(2,1)S(1)} %collective-permute-done.8.refs_14_) | copy-start | bytes 393220
  43.9 1.7 %copy-start.13 = (bf16[16,4096]{1,0:T(8,128)(2,1)}, bf16[16,4096]{1,0:T(8,128)(2,1)S(1)}, u32[]{:S(2)}) copy-start(bf16[16,4096]{1,0:T(8,128)(2,1)S(1)} %collective-permute-done.12.refs_18_) | copy-start | bytes 393220
  43.9 1.6 copy-start.14
  50.9 7.3 %collective-permute-start.21 = (bf16[192,128]{1,0:T(8,128)(2,1)}, bf16[192,128]{1,0:T(8,128)(2,1)S(1)}, u32[]{:S(2)}, u32[]{:S(2)}) collective-permute-start(bf16[192,128]{1,0:T(8,128)(2,1)} %side.1.refs_2_), channel_id=1, source_target_pairs={{0,32},{32,64},{64,96},{96,128},{128,160},{160,192},{192,224},{224... | collective-permute-start | bytes 147464 | tf_op jit(solution)/shard_map/ppermute | solution.py:613
  51.2 9.3 %collective-permute-start.20 = (bf16[192,128]{1,0:T(8,128)(2,1)}, bf16[192,128]{1,0:T(8,128)(2,1)S(1)}, u32[]{:S(2)}, u32[]{:S(2)}) collective-permute-start(bf16[192,128]{1,0:T(8,128)(2,1)} %side.1.refs_2_), channel_id=1, source_target_pairs={{0,64},{32,96},{64,128},{96,160},{128,192},{160,224},{192,0},{224,... | collective-permute-start | bytes 147464 | tf_op jit(solution)/shard_map/ppermute | solution.py:613
  51.3 10.6 %collective-permute-start.19 = (bf16[192,128]{1,0:T(8,128)(2,1)}, bf16[192,128]{1,0:T(8,128)(2,1)S(1)}, u32[]{:S(2)}, u32[]{:S(2)}) collective-permute-start(bf16[192,128]{1,0:T(8,128)(2,1)} %side.1.refs_2_), channel_id=1, source_target_pairs={{0,96},{32,128},{64,160},{96,192},{128,224},{160,0},{192,32},{224,... | collective-permute-start | bytes 147464 | tf_op jit(solution)/shard_map/ppermute | solution.py:613
  52.6 9.3 %collective-permute-start.18 = (bf16[192,128]{1,0:T(8,128)(2,1)}, bf16[192,128]{1,0:T(8,128)(2,1)S(1)}, u32[]{:S(2)}, u32[]{:S(2)}) collective-permute-start(bf16[192,128]{1,0:T(8,128)(2,1)} %side.1.refs_2_), channel_id=1, source_target_pairs={{0,128},{32,160},{64,192},{96,224},{128,0},{160,32},{192,64},{224,... | collective-permute-start | bytes 147464 | tf_op jit(solution)/shard_map/ppermute | solution.py:613
  56.8 5.3 %collective-permute-start.17 = (bf16[192,128]{1,0:T(8,128)(2,1)}, bf16[192,128]{1,0:T(8,128)(2,1)S(1)}, u32[]{:S(2)}, u32[]{:S(2)}) collective-permute-start(bf16[192,128]{1,0:T(8,128)(2,1)} %side.1.refs_2_), channel_id=1, source_target_pairs={{0,160},{32,192},{64,224},{96,0},{128,32},{160,64},{192,96},{224,1... | collective-permute-start | bytes 147464 | tf_op jit(solution)/shard_map/ppermute | solution.py:613
  58.2 18.8 %copy-start.17 = (bf16[192,128]{1,0:T(8,128)(2,1)}, bf16[192,128]{1,0:T(8,128)(2,1)S(1)}, u32[]{:S(2)}) copy-start(bf16[192,128]{1,0:T(8,128)(2,1)S(1)} %collective-permute-done.21.refs_9_) | copy-start | bytes 147460
  58.2 7.8 %collective-permute-start.16 = (bf16[192,128]{1,0:T(8,128)(2,1)}, bf16[192,128]{1,0:T(8,128)(2,1)S(1)}, u32[]{:S(2)}, u32[]{:S(2)}) collective-permute-start(bf16[192,128]{1,0:T(8,128)(2,1)} %side.1.refs_2_), channel_id=1, source_target_pairs={{0,192},{32,224},{64,0},{96,32},{128,64},{160,96},{192,128},{224,1... | collective-permute-start | bytes 147464 | tf_op jit(solution)/shard_map/ppermute | solution.py:613
  60.5 16.6 %copy-start.18 = (bf16[192,128]{1,0:T(8,128)(2,1)}, bf16[192,128]{1,0:T(8,128)(2,1)S(1)}, u32[]{:S(2)}) copy-start(bf16[192,128]{1,0:T(8,128)(2,1)S(1)} %collective-permute-done.20.refs_8_) | copy-start | bytes 147460
  60.5 7.6 %collective-permute-start.15 = (bf16[192,128]{1,0:T(8,128)(2,1)}, bf16[192,128]{1,0:T(8,128)(2,1)S(1)}, u32[]{:S(2)}, u32[]{:S(2)}) collective-permute-start(bf16[192,128]{1,0:T(8,128)(2,1)} %side.1.refs_2_), channel_id=1, source_target_pairs={{0,224},{32,0},{64,32},{96,64},{128,96},{160,128},{192,160},{224,1... | collective-permute-start | bytes 147464 | tf_op jit(solution)/shard_map/ppermute | solution.py:613
  61.9 15.2 %copy-start.19 = (bf16[192,128]{1,0:T(8,128)(2,1)}, bf16[192,128]{1,0:T(8,128)(2,1)S(1)}, u32[]{:S(2)}) copy-start(bf16[192,128]{1,0:T(8,128)(2,1)S(1)} %collective-permute-done.19.refs_7_) | copy-start | bytes 147460
  61.9 15.2 %copy-start.20 = (bf16[192,128]{1,0:T(8,128)(2,1)}, bf16[192,128]{1,0:T(8,128)(2,1)S(1)}, u32[]{:S(2)}) copy-start(bf16[192,128]{1,0:T(8,128)(2,1)S(1)} %collective-permute-done.18.refs_6_) | copy-start | bytes 147460
  62.2 14.9 %copy-start.21 = (bf16[192,128]{1,0:T(8,128)(2,1)}, bf16[192,128]{1,0:T(8,128)(2,1)S(1)}, u32[]{:S(2)}) copy-start(bf16[192,128]{1,0:T(8,128)(2,1)S(1)} %collective-permute-done.17.refs_5_) | copy-start | bytes 147460
  66.0 11.1 %copy-start.22 = (bf16[192,128]{1,0:T(8,128)(2,1)}, bf16[192,128]{1,0:T(8,128)(2,1)S(1)}, u32[]{:S(2)}) copy-start(bf16[192,128]{1,0:T(8,128)(2,1)S(1)} %collective-permute-done.16.refs_4_) | copy-start | bytes 147460
  68.1 9.0 %copy-start.23 = (bf16[192,128]{1,0:T(8,128)(2,1)}, bf16[192,128]{1,0:T(8,128)(2,1)S(1)}, u32[]{:S(2)}) copy-start(bf16[192,128]{1,0:T(8,128)(2,1)S(1)} %collective-permute-done.15.refs_3_) | copy-start | bytes 147460
  77.1 14.7 %all-to-all-start.1 = ((bf16[8,128,128]{2,1,0:T(8,128)(2,1)}), bf16[8,128,128]{2,1,0:T(8,128)(2,1)S(1)}, u32[]{:S(2)}, u32[]{:S(2)}) async-start(bf16[8,128,128]{2,1,0:T(8,128)(2,1)} %get-tuple-element.48), calls=%async_computation.1 | async-start | bytes 524288 | tf_op jit(solution)/shard_map/all_to_all | solution.py:618
  99.8 7.5 %collective-permute-start.22 = (f32[16,144,256]{2,1,0:T(8,128)}, f32[16,144,256]{2,1,0:T(8,128)}, u32[]{:S(2)}, u32[]{:S(2)}) collective-permute-start(f32[16,144,256]{2,1,0:T(8,128)} %get-tuple-element.63), channel_id=1, source_target_pairs={{0,1},{1,0},{2,3},{3,2},{4,5},{5,4},{6,7},{7,6},{8,9},{9,8},{10,11... | collective-permute-start | bytes 7077896 | tf_op jit(solution)/shard_map/ppermute | solution.py:624
  135.6 11.2 %all-to-all-start.3 = ((f32[8,16,256]{2,1,0:T(8,128)}), f32[8,16,256]{2,1,0:T(8,128)S(1)}, u32[]{:S(2)}, u32[]{:S(2)}) async-start(f32[8,16,256]{2,1,0:T(8,128)} %bitcast.9), calls=%async_computation.3 | async-start | bytes 262144 | tf_op jit(solution)/shard_map/all_to_all | solution.py:630
  159.1 5.4 %collective-permute-start.23 = (f32[32,4096]{1,0:T(8,128)S(1)}, f32[32,4096]{1,0:T(8,128)S(1)}, u32[]{:S(2)}, u32[]{:S(2)}) collective-permute-start(f32[32,4096]{1,0:T(8,128)S(1)} %bitcast.19), channel_id=1, source_target_pairs={{0,1},{1,0},{2,3},{3,2},{4,5},{5,4},{6,7},{7,6},{8,9},{9,8},{10,11... | collective-permute-start | bytes 1572872 | tf_op jit(solution)/shard_map/ppermute | solution.py:634
  (3 other events, 2.3 us)

commit v7 on v5

--- a/solution.py
+++ b/solution.py
@@ -273,11 +273,13 @@
     irms_hi = irms.astype(bf16).astype(f32)
     row = lax.broadcasted_iota(jnp.int32, (rank, tokens), 0)
     last = jnp.where(row == 0, irms_hi, jnp.where(row == 1, irms - irms_hi, 0.0)).astype(bf16)
-    out_ref[:rows, :] = (total[:, :tokens] * irms).astype(bf16)
-    out_ref[rows : rows + rank, :] = lrt_in[1][...]
-    out_ref[rows + rank : rows + 2 * rank, :] = w_hi
-    out_ref[rows + 2 * rank : rows + 3 * rank, :] = w_lo
-    out_ref[rows + 3 * rank :, :] = last
+    scaled_up = (total[:, :tokens] * irms).astype(bf16)
+    for i in range(out_ref.shape[0]):
+        out_ref[i, :rows, :] = scaled_up
+        out_ref[i, rows : rows + rank, :] = lrt_in[1][...]
+        out_ref[i, rows + rank : rows + 2 * rank, :] = w_hi
+        out_ref[i, rows + 2 * rank : rows + 3 * rank, :] = w_lo
+        out_ref[i, rows + 3 * rank :, :] = last
 
 
 def up_scratch(mine):
@@ -291,7 +293,7 @@
     (side,) = call(
         functools.partial(side_kernel, layers),
         "side",
-        (jax.ShapeDtypeStruct(((layers + 4) * rank, stream.shape[0]), bf16),),
+        (jax.ShapeDtypeStruct((layers, (layers + 4) * rank, stream.shape[0]), bf16),),
         (meta,),
         (stream, dg, lrt, irms, *mine, *other),
         (1, 1, 1, 1) + (0,) * (2 * layers),
@@ -402,7 +404,7 @@
     )
 
 
-def solve(width, rank, me, own_ref, side_ref, low_ref, lrt_ref, coef_ref, k_ref, acc, lrt_all):
+def solve(width, rank, me, own_ref, side_ref, low_ref, lrt_ref, coef_ref, k_ref, acc):
     layers, rows, _ = own_ref.shape
     acc[...] = jnp.zeros_like(acc)
     for j in range(layers):
@@ -412,35 +414,33 @@
             low = rank * (layers - 1 - j)
             acc[0 : rank * (j + 1), :] += own_ref[me + j, low:rows, :].astype(f32)
 
-    def inverse_rms(j):
-        hi = side_ref[j, rows + 3 * rank : rows + 3 * rank + 1, :].astype(f32)
-        return hi + side_ref[j, rows + 3 * rank + 1 : rows + 3 * rank + 2, :].astype(f32)
-
-    def mean_of(grad, j):
-        lrt = side_ref[j, rows : rows + rank, :].astype(f32)
+    def inverse_rms(t):
+        hi = side_ref[t, rows + 3 * rank : rows + 3 * rank + 1, :].astype(f32)
+        return hi + side_ref[t, rows + 3 * rank + 1 : rows + 3 * rank + 2, :].astype(f32)
+
+    def mean_of(grad, t):
+        lrt = side_ref[t, rows : rows + rank, :].astype(f32)
         return jnp.sum(grad.astype(f32) * lrt, axis=0, keepdims=True) * (1.0 / width)
 
     for j in range(layers - 1, 0, -1):
 
         @pl.when(me + j < layers)
         def _(j=j):
+            t = me + j
             low = rank * (layers - 1 - j)
             grad = acc[rank * j : rank * (j + 1), :].astype(bf16)
-            mean = mean_of(grad, j)
-            w_hi = side_ref[j, rows + rank : rows + 2 * rank, :]
-            w_lo = side_ref[j, rows + 2 * rank : rows + 3 * rank, :]
+            mean = mean_of(grad, t)
+            w_hi = side_ref[t, rows + rank : rows + 2 * rank, :]
+            w_lo = side_ref[t, rows + 2 * rank : rows + 3 * rank, :]
             term = tn(w_hi, grad) + tn(w_lo, grad)
-            scaled_up = side_ref[j, low : rows - rank, :].astype(f32)
-            acc[0 : rank * j, :] += inverse_rms(j) * (term[low : rows - rank, :] - mean * scaled_up)
+            scaled_up = side_ref[t, low : rows - rank, :].astype(f32)
+            acc[0 : rank * j, :] += inverse_rms(t) * (term[low : rows - rank, :] - mean * scaled_up)
 
     grad = acc[0:rank, :].astype(bf16)
     low_ref[...] = grad
-    irms = inverse_rms(0)
-    mean = mean_of(grad, 0)
-    for j in range(layers):
-        where = lax.rem(me + j, layers) * rank
-        lrt_all[pl.ds(pl.multiple_of(where, rank), rank), :] = side_ref[j, rows : rows + rank, :]
-    lrt_f = lrt_all[...].astype(f32)
+    irms = inverse_rms(me)
+    mean = mean_of(grad, me)
+    lrt_f = side_ref[:, rows : rows + rank, :].reshape(layers * rank, -1).astype(f32)
     layer = lax.broadcasted_iota(jnp.int32, lrt_f.shape, 0) // rank
     lrt_ref[...] = jnp.where(layer <= me, lrt_f, 0.0).astype(bf16)
     below = jnp.where(layer < me, lrt_f, 0.0)
@@ -487,20 +487,18 @@
     ]
 
 
-def given_kernel(rank, count, meta_ref, own_up_in, *refs):
-    sides, large = refs[:count], refs[count : count + 4]
-    out_ref, low_ref, lrt_ref, coef_ref, k_ref, acc, lrt_all, side_ref, side_sem, buffer, out_sem = refs[count + 4 :]
+def given_kernel(rank, meta_ref, own_up_in, side_in, *refs):
+    large, (out_ref, low_ref, lrt_ref, coef_ref, k_ref, acc, buffer, out_sem) = refs[:4], refs[4:]
     start, me = meta_ref[0], meta_ref[1]
     loads = part_loads(start, large, buffer.shape[0], buffer.shape[2])
-    whole(own_up_in).start()
-    for i, side in enumerate(sides):
-        pltpu.make_async_copy(side, side_ref.at[i], side_sem).start()
+    for item in (own_up_in, side_in):
+        whole(item).start()
     for load in loads:
         for item in load:
             item.start()
-    whole(own_up_in).wait()
-    pltpu.make_async_copy(side_ref, side_ref, side_sem).wait()
-    solve(large[0][0].shape[1], rank, me, own_up_in[1], side_ref, low_ref, lrt_ref, coef_ref, k_ref, acc, lrt_all)
+    for item in (own_up_in, side_in):
+        whole(item).wait()
+    solve(large[0][0].shape[1], rank, me, own_up_in[1], side_in[1], low_ref, lrt_ref, coef_ref, k_ref, acc)
     part(start, loads, low_ref[...], lrt_ref[...], coef_ref[...], k_ref, *large, out_ref, buffer, out_sem)
 
 
@@ -524,10 +522,10 @@
 
 
 def given_part(meta, chunks, chunk, rank, own_up, sides, *large):
-    layers, rows, tokens = own_up.shape
+    _, rows, tokens = own_up.shape
     shape, scratch = part_shapes(chunks, chunk, rows, rank)
     return call(
-        functools.partial(given_kernel, rank, layers),
+        functools.partial(given_kernel, rank),
         "given",
         (
             shape,
@@ -537,14 +535,9 @@
             jax.ShapeDtypeStruct((2, rows, rank), bf16),
         ),
         (meta,),
-        (own_up, *sides, *large),
-        (1,) + (0,) * layers + (4,) * 4,
-        (
-            pltpu.VMEM((rows, tokens), f32),
-            pltpu.VMEM((rows, tokens), bf16),
-            pltpu.VMEM((layers,) + sides[0].shape, bf16),
-            pltpu.SemaphoreType.DMA,
-        )
+        (own_up, sides, *large),
+        (1, 1) + (4,) * 4,
+        (pltpu.VMEM((rows, tokens), f32),)
         + scratch,
         in_place_outs=1,
     )
@@ -600,11 +593,7 @@
     other = [lax.ppermute(block, "core", swap) for block in mine]
 
     side = side_of(meta, stream, dg, lrt, irms, mine, other)
-    sides = [side]
-    for j in range(1, layers):
-        sides.append(lax.ppermute(side, SEC, [(t, (t - j) % layers) for t in range(layers)]))
-
-    refs, _ = lax.optimization_barrier((refs, side))
+    sides = lax.all_to_all(side, SEC, 0, 0, tiled=True)
 
     own, own_up = own_gradient(meta, refs, stream, up, lrt, mine, other)
     own_up = lax.all_to_all(own_up, SEC, 0, 0, tiled=True)

time: 158 us -> 160 us (1.013)
  waiting for transfers between devices: 20.2 us -> 33.4 us
  starting transfers between devices: 56.8 us -> 44.8 us
    ppermute x7 -> x0, starting transfers between devices: 14.8 us -> none  [shards(): lax.ppermute(side, SEC, [(t, (t - j) % layers) for t in range(layers)])]
    all_to_all x1, waiting for transfers between devices: 0.01 us -> 11.5 us  [shards(): own_up = lax.all_to_all(own_up, SEC, 0, 0, tiled=True)]
    all_to_all x0 -> x1, waiting for transfers between devices: none -> 5.93 us  [shards(): sides = lax.all_to_all(side, SEC, 0, 0, tiled=True)]
    ppermute x7 -> x0, waiting for transfers between devices: 4.33 us -> none  [shards(): lax.ppermute(side, SEC, [(t, (t - j) % layers) for t in range(layers)])]
    all_to_all x0 -> x1, starting transfers between devices: none -> 3.47 us  [shards(): sides = lax.all_to_all(side, SEC, 0, 0, tiled=True)]
  transfers between devices with their start and end apart: 27 -> 21, of which waited for: 9 -> 9; matrix products, arithmetic and copies ran while one was open for 0% -> 0% of each run, Pallas kernels for 9% -> 15%
where the time goes in v7:
time: 160 us; the launch traced here: 159 us
  starting transfers between devices  44.8 us (28%)
  blocking collectives  36.7 us (23%)
  Pallas kernels  33.7 us (21%)
  waiting for transfers between devices  33.4 us (21%)
  other arithmetic  5.85 us (4%)
  local copies, waits for them, and re-layouts  2.39 us (1%)
  between operations  2.24 us (1%)
    pallas_call x5, Pallas kernels, call(): pl.pallas_call(body, out_shape=out_shape, in_specs=[smem()] * count + [in...  30.5 us
    all_to_all x1, blocking collectives, shards(): lax.all_to_all((kept + received).astype(bf16), CHIPS, 0, 0, tiled=True)  24.6 us
    all_to_all x1, blocking collectives, shards(): lax.all_to_all(jnp.broadcast_to(final, (chips,) + final.shape), CHIPS, 0,...  12.1 us
    all_to_all x1, waiting for transfers between devices, shards(): own_up = lax.all_to_all(own_up, SEC, 0, 0, tiled=True)  11.5 us
    ppermute x3, starting transfers between devices, ring_gather(): bwd = lax.ppermute(bwd, axis, down)  11.2 us
    ppermute x8, starting transfers between devices, shards(): other = [lax.ppermute(block, 'core', swap) for block in mine]  10.2 us
    all_to_all x1, starting transfers between devices, shards(): refs = lax.all_to_all(ordered, DP, split_axis=0, concat_axis=0, tiled=True)  8.65 us
    all_to_all x1, waiting for transfers between devices, shards(): lax.all_to_all(grad_up.reshape(layers, rank, chunk), SEC, 0, 0, tiled=True)  7.84 us
  transfers between devices with their start and end apart: 21, of which 9 were waited for; matrix products, arithmetic and copies ran while one was open for 0% of the time, Pallas kernels for 15%

profile of v7, /device:TPU:1, one launch (start us, length us, event | category | flops | bytes accessed | tf_op | source)
XLA Modules:
  0.0 159.0 jit_solution(6687510228482611530)
XLA Ops:
  1.9 0.9 dynamic-slice_bitcast_fusion.refs_12_
  2.9 0.6 pad_add_fusion.1.meta_ref.refs_0_
  3.5 3.2 %order.1 = bf16[32,136,256]{2,1,0:T(8,128)(2,1)} custom-call(s32[32]{0:T(128)} %position_ref, s32[3]{0:T(128)} %pad_add_fusion.1.meta_ref.refs_0_, bf16[32,128,256]{2,1,0:T(8,128)(2,1)} %bitcast.18), custom_call_target="tpu_custom_call" | custom-call | tf_op jit(solution)/shard_map/order/pallas_call | solution.py:162
  6.7 8.6 %all-to-all-start = ((bf16[32,136,256]{2,1,0:T(8,128)(2,1)}), bf16[32,136,256]{2,1,0:T(8,128)(2,1)}, u32[]{:S(2)}, u32[]{:S(2)}) async-start(bf16[32,136,256]{2,1,0:T(8,128)(2,1)} %order.1), calls=%async_computation | async-start | bytes 4456448 | tf_op jit(solution)/shard_map/all_to_all | solution.py:586
  15.4 5.7 %collective-permute-start.1 = (bf16[16,4096]{1,0:T(8,128)(2,1)S(1)}, bf16[16,4096]{1,0:T(8,128)(2,1)S(1)}, u32[]{:S(2)}, u32[]{:S(2)}) collective-permute-start(bf16[16,4096]{1,0:T(8,128)(2,1)S(1)} %dynamic-slice_bitcast_fusion.refs_12_), channel_id=1, source_target_pairs={{0,224},{32,0},{64,32},{96,64},{128,96},{160,128},{192,160},{224,1... | collective-permute-start | bytes 393224 | tf_op jit(solution)/shard_map/ppermute | solution.py:53
  21.0 0.0 collective-permute-start
  21.0 4.8 %forward.1 = (bf16[128,8192]{1,0:T(8,128)(2,1)}, bf16[16,128]{1,0:T(8,128)(2,1)}, f32[8,128]{1,0:T(8,128)}, bf16[2,16,8192]{2,1,0:T(8,128)(2,1)}) custom-call(bf16[128,8192]{1,0:T(8,128)(2,1)} %bitcast.23, bf16[16,8192]{1,0:T(8,128)(2,1)} %bitcast.28, f32[1,8192]{1,0:T(1,128)} %refs_2_), custom_call_target="tpu_custom_call" | custom-call | flops 4000000000 | bytes 12000000 | tf_op jit(solution)/shard_map/forward/pallas_call | solution.py:90
  25.8 1.0 collective-permute-done.refs_11_
  26.8 0.0 collective-permute-start.4
  26.8 2.7 %collective-permute-start.2 = (bf16[16,4096]{1,0:T(8,128)(2,1)S(1)}, bf16[16,4096]{1,0:T(8,128)(2,1)S(1)}, u32[]{:S(2)}, u32[]{:S(2)}) collective-permute-start(bf16[16,4096]{1,0:T(8,128)(2,1)S(1)} %collective-permute-done.1.refs_5_), channel_id=1, source_target_pairs={{0,224},{32,0},{64,32},{96,64},{128,96},{160,128},{192,160},{224,1... | collective-permute-start | bytes 393224 | tf_op jit(solution)/shard_map/ppermute | solution.py:53
  29.5 2.8 %collective-permute-done.4.refs_10_ = bf16[16,4096]{1,0:T(8,128)(2,1)S(1)} collective-permute-done((bf16[16,4096]{1,0:T(8,128)(2,1)S(1)}, bf16[16,4096]{1,0:T(8,128)(2,1)S(1)}, u32[]{:S(2)}, u32[]{:S(2)}) %collective-permute-start.4) | collective-permute-done | bytes 131104 | tf_op jit(solution)/shard_map/ppermute | solution.py:50
  32.3 2.2 %collective-permute-start.14 = (bf16[16,4096]{1,0:T(8,128)(2,1)S(1)}, bf16[16,4096]{1,0:T(8,128)(2,1)S(1)}, u32[]{:S(2)}, u32[]{:S(2)}) collective-permute-start(bf16[16,4096]{1,0:T(8,128)(2,1)S(1)} %dynamic-slice_bitcast_fusion.refs_12_), channel_id=1, source_target_pairs={{0,1},{1,0},{2,3},{3,2},{4,5},{5,4},{6,7},{7,6},{8,9},{9,8},{10,11... | collective-permute-start | bytes 393224 | tf_op jit(solution)/shard_map/ppermute | solution.py:593
  34.4 0.1 collective-permute-start.7
  34.5 0.4 collective-permute-start.13
  34.9 0.0 collective-permute-done.2.refs_6_
  34.9 2.9 %collective-permute-start.3 = (bf16[16,4096]{1,0:T(8,128)(2,1)S(1)}, bf16[16,4096]{1,0:T(8,128)(2,1)S(1)}, u32[]{:S(2)}, u32[]{:S(2)}) collective-permute-start(bf16[16,4096]{1,0:T(8,128)(2,1)S(1)} %collective-permute-done.2.refs_6_), channel_id=1, source_target_pairs={{0,224},{32,0},{64,32},{96,64},{128,96},{160,128},{192,160},{224,1... | collective-permute-start | bytes 393224 | tf_op jit(solution)/shard_map/ppermute | solution.py:53
  37.8 0.0 collective-permute-done.5.refs_9_
  37.8 0.0 collective-permute-start.6
  37.9 2.8 %collective-permute-start.8 = (bf16[16,4096]{1,0:T(8,128)(2,1)S(1)}, bf16[16,4096]{1,0:T(8,128)(2,1)S(1)}, u32[]{:S(2)}, u32[]{:S(2)}) collective-permute-start(bf16[16,4096]{1,0:T(8,128)(2,1)S(1)} %collective-permute-done.2.refs_6_), channel_id=1, source_target_pairs={{0,1},{1,0},{2,3},{3,2},{4,5},{5,4},{6,7},{7,6},{8,9},{9,8},{10,11... | collective-permute-start | bytes 393224 | tf_op jit(solution)/shard_map/ppermute | solution.py:593
  40.6 0.1 collective-permute-start.12
  40.7 0.4 collective-permute-start.11
  41.1 0.4 collective-permute-start.9
  41.5 1.3 collective-permute-done.6.refs_8_
  42.9 3.8 %collective-permute-start.10 = (bf16[16,4096]{1,0:T(8,128)(2,1)S(1)}, bf16[16,4096]{1,0:T(8,128)(2,1)S(1)}, u32[]{:S(2)}, u32[]{:S(2)}) collective-permute-start(bf16[16,4096]{1,0:T(8,128)(2,1)S(1)} %collective-permute-done.6.refs_8_), channel_id=1, source_target_pairs={{0,1},{1,0},{2,3},{3,2},{4,5},{5,4},{6,7},{7,6},{8,9},{9,8},{10,11... | collective-permute-start | bytes 393224 | tf_op jit(solution)/shard_map/ppermute | solution.py:593
  46.8 0.9 collective-permute-done.10.refs_16_
  47.7 0.6 copy-done.17
  48.4 5.5 %side.1 = bf16[8,192,128]{2,1,0:T(8,128)(2,1)} custom-call(s32[3]{0:T(128)} %pad_add_fusion.1.meta_ref.refs_0_, bf16[128,8192]{1,0:T(8,128)(2,1)} %bitcast.24, bf16[2,16,8192]{2,1,0:T(8,128)(2,1)} %get-tuple-element.31.refs_2_.refs_6_.refs_8_, bf16[16,128]{1,0:T(8,128)(2,1)} %get-tuple-element.26.refs_4_.refs_3_, f32[8,128]{1,0:T(8,128)} %get-tuple-element.32.refs_4_, ...), custom_call_target="tpu_custom_call" | custom-call | flops 5000000000 | bytes 15000000 | tf_op jit(solution)/shard_map/side/pallas_call | solution.py:90
  53.9 3.5 %all-to-all-start.2 = ((bf16[8,192,128]{2,1,0:T(8,128)(2,1)}), bf16[8,192,128]{2,1,0:T(8,128)(2,1)S(1)}, u32[]{:S(2)}, u32[]{:S(2)}) async-start(bf16[8,192,128]{2,1,0:T(8,128)(2,1)} %side.1), calls=%async_computation.2 | async-start | bytes 786432 | tf_op jit(solution)/shard_map/all_to_all | solution.py:596
  57.3 9.1 %own.1 = (bf16[128,8192]{1,0:T(8,128)(2,1)}, bf16[8,128,128]{2,1,0:T(8,128)(2,1)}) custom-call(s32[3]{0:T(128)} %pad_add_fusion.1.meta_ref.refs_0_, bf16[32,136,256]{2,1,0:T(8,128)(2,1)} %all-to-all-done.refs_1_, bf16[128,8192]{1,0:T(8,128)(2,1)} %bitcast.25, bf16[16,8192]{1,0:T(8,128)(2,1)} %bitcast.22, bf16[16,128]{1,0:T(8,128)(2,1)} %get-tuple-element.26.refs_4_.refs_3_, ...), custom_call_target="tpu_custom_call" | custom-call | flops 8000000000 | bytes 24000000 | tf_op jit(solution)/shard_map/own/pallas_call | solution.py:90
  66.5 5.9 %all-to-all-done.2.refs_2_ = bf16[8,192,128]{2,1,0:T(8,128)(2,1)S(1)} async-done(((bf16[8,192,128]{2,1,0:T(8,128)(2,1)}), bf16[8,192,128]{2,1,0:T(8,128)(2,1)S(1)}, u32[]{:S(2)}, u32[]{:S(2)}) %all-to-all-start.2) | async-done | bytes 393248 | tf_op jit(solution)/shard_map/all_to_all | solution.py:596
  72.4 3.4 %all-to-all-start.1 = ((bf16[8,128,128]{2,1,0:T(8,128)(2,1)}), bf16[8,128,128]{2,1,0:T(8,128)(2,1)S(1)}, u32[]{:S(2)}, u32[]{:S(2)}) async-start(bf16[8,128,128]{2,1,0:T(8,128)(2,1)} %get-tuple-element.30), calls=%async_computation.1 | async-start | bytes 524288 | tf_op jit(solution)/shard_map/all_to_all | solution.py:599
  75.8 0.6 pad_add_fusion.refs_0_
  76.4 11.5 %all-to-all-done.1.refs_1_ = bf16[8,128,128]{2,1,0:T(8,128)(2,1)S(1)} async-done(((bf16[8,128,128]{2,1,0:T(8,128)(2,1)}), bf16[8,128,128]{2,1,0:T(8,128)(2,1)S(1)}, u32[]{:S(2)}, u32[]{:S(2)}) %all-to-all-start.1) | async-done | bytes 262176 | tf_op jit(solution)/shard_map/all_to_all | solution.py:599
  88.0 0.7 copy-done.1
  88.7 7.2 %given.1 = (f32[16,144,256]{2,1,0:T(8,128)}, bf16[16,128]{1,0:T(8,128)(2,1)}, bf16[128,128]{1,0:T(8,128)(2,1)}, bf16[128,128]{1,0:T(8,128)(2,1)}, bf16[2,128,16]{2,1,0:T(8,128)(2,1)}) custom-call(s32[2]{0:T(128)} %pad_add_fusion.refs_0_, bf16[8,128,128]{2,1,0:T(8,128)(2,1)} %copy-done.1, bf16[8,192,128]{2,1,0:T(8,128)(2,1)} %copy-done, ...), custom_call_target="tpu_custom_call" | custom-call | flops 5000000000 | bytes 15000000 | tf_op jit(solution)/shard_map/given/pallas_call | solution.py:90
  95.9 0.7 collective-permute-start.15
  96.5 4.0 %kept.1 = f32[16,144,256]{2,1,0:T(8,128)} custom-call(s32[1]{0:T(128)} %bitcast.refs_0_, bf16[16,128]{1,0:T(8,128)(2,1)} %get-tuple-element.35.refs_1_, bf16[128,128]{1,0:T(8,128)(2,1)} %get-tuple-element.36.refs_2_, bf16[128,128]{1,0:T(8,128)(2,1)} %get-tuple-element.37.refs_3_, bf16[2,128,16]{2,1,0:T(8,128)(2,1)} %get-tuple-element.38.refs_4_, ...), custom_call_target="tpu_custom_call" | custom-call | flops 4000000000 | bytes 12000000 | tf_op jit(solution)/shard_map/kept/pallas_call | solution.py:90
  100.5 0.5 collective-permute-done.15
  101.0 2.7 %add_convert_fusion = bf16[16,144,256]{2,1,0:T(8,128)(2,1)S(1)} fusion(f32[16,144,256]{2,1,0:T(8,128)} %kept.1, f32[16,144,256]{2,1,0:T(8,128)} %collective-permute-done.15), kind=kLoop, calls=%fused_computation | loop fusion | flops 1179648 | bytes 5898240 | tf_op jit(solution)/shard_map/convert_element_type | solution.py:607
  103.7 24.6 %all_to_all.30 = bf16[16,144,256]{2,1,0:T(8,128)(2,1)S(1)} all-to-all(bf16[16,144,256]{2,1,0:T(8,128)(2,1)S(1)} %add_convert_fusion), channel_id=1, replica_groups=mesh['section'=8,'y'=4,'x'=4,'core'=2] {'y','x'}, dimensions={0} | all-to-all | bytes 2359296 | tf_op jit(solution)/shard_map/all_to_all | solution.py:607
  128.3 0.8 convert_reduce_fusion
  129.1 3.4 %all-to-all-start.4 = ((f32[8,16,256]{2,1,0:T(8,128)}), f32[8,16,256]{2,1,0:T(8,128)S(1)}, u32[]{:S(2)}, u32[]{:S(2)}) async-start(f32[8,16,256]{2,1,0:T(8,128)} %bitcast.9), calls=%async_computation.4 | async-start | bytes 262144 | tf_op jit(solution)/shard_map/all_to_all | solution.py:611
  132.5 7.8 %all-to-all-done.4 = f32[8,16,256]{2,1,0:T(8,128)S(1)} async-done(((f32[8,16,256]{2,1,0:T(8,128)}), f32[8,16,256]{2,1,0:T(8,128)S(1)}, u32[]{:S(2)}, u32[]{:S(2)}) %all-to-all-start.4) | async-done | bytes 131104 | tf_op jit(solution)/shard_map/all_to_all | solution.py:611
  140.4 12.1 %all_to_all.31 = f32[16,32,256]{2,1,0:T(8,128)S(1)} all-to-all(f32[16,32,256]{2,1,0:T(8,128)S(1)} %broadcast_in_dim.13), channel_id=1, replica_groups=mesh['section'=8,'y'=4,'x'=4,'core'=2] {'y','x'}, dimensions={0} | all-to-all | bytes 1048576 | tf_op jit(solution)/shard_map/all_to_all | solution.py:613
  152.5 3.8 %collective-permute-start.16 = (f32[32,4096]{1,0:T(8,128)S(1)}, f32[32,4096]{1,0:T(8,128)S(1)}, u32[]{:S(2)}, u32[]{:S(2)}) collective-permute-start(f32[32,4096]{1,0:T(8,128)S(1)} %bitcast.19), channel_id=1, source_target_pairs={{0,1},{1,0},{2,3},{3,2},{4,5},{5,4},{6,7},{7,6},{8,9},{9,8},{10,11... | collective-permute-start | bytes 1572872 | tf_op jit(solution)/shard_map/ppermute | solution.py:615
  156.4 1.5 collective-permute-done.16
  157.9 0.1 broadcast_select_fusion
  158.0 1.0 fusion.2
  (50 shorter events, 0.2 us)
Async XLA Ops:
  2.9 29.4 %copy-start.2 = (bf16[16,4096]{1,0:T(8,128)(2,1)}, bf16[16,4096]{1,0:T(8,128)(2,1)S(1)}, u32[]{:S(2)}) copy-start(bf16[16,4096]{1,0:T(8,128)(2,1)S(1)} %dynamic-slice_bitcast_fusion.refs_12_) | copy-start | bytes 393220
  6.7 47.1 %all-to-all-start = ((bf16[32,136,256]{2,1,0:T(8,128)(2,1)}), bf16[32,136,256]{2,1,0:T(8,128)(2,1)}, u32[]{:S(2)}, u32[]{:S(2)}) async-start(bf16[32,136,256]{2,1,0:T(8,128)(2,1)} %order.1), calls=%async_computation | async-start | bytes 4456448 | tf_op jit(solution)/shard_map/all_to_all | solution.py:586
  15.4 10.4 %collective-permute-start.1 = (bf16[16,4096]{1,0:T(8,128)(2,1)S(1)}, bf16[16,4096]{1,0:T(8,128)(2,1)S(1)}, u32[]{:S(2)}, u32[]{:S(2)}) collective-permute-start(bf16[16,4096]{1,0:T(8,128)(2,1)S(1)} %dynamic-slice_bitcast_fusion.refs_12_), channel_id=1, source_target_pairs={{0,224},{32,0},{64,32},{96,64},{128,96},{160,128},{192,160},{224,1... | collective-permute-start | bytes 393224 | tf_op jit(solution)/shard_map/ppermute | solution.py:53
  21.0 5.8 %collective-permute-start = (bf16[16,4096]{1,0:T(8,128)(2,1)S(1)}, bf16[16,4096]{1,0:T(8,128)(2,1)S(1)}, u32[]{:S(2)}, u32[]{:S(2)}) collective-permute-start(bf16[16,4096]{1,0:T(8,128)(2,1)S(1)} %dynamic-slice_bitcast_fusion.refs_12_), channel_id=1, source_target_pairs={{0,32},{32,64},{64,96},{96,128},{128,160},{160,192},{192,224},{224... | collective-permute-start | bytes 393224 | tf_op jit(solution)/shard_map/ppermute | solution.py:50
  25.8 22.5 %copy-start.3 = (bf16[16,4096]{1,0:T(8,128)(2,1)}, bf16[16,4096]{1,0:T(8,128)(2,1)S(1)}, u32[]{:S(2)}) copy-start(bf16[16,4096]{1,0:T(8,128)(2,1)S(1)} %collective-permute-done.1.refs_5_) | copy-start | bytes 393220
  26.8 21.5 %copy-start.4 = (bf16[16,4096]{1,0:T(8,128)(2,1)}, bf16[16,4096]{1,0:T(8,128)(2,1)S(1)}, u32[]{:S(2)}) copy-start(bf16[16,4096]{1,0:T(8,128)(2,1)S(1)} %collective-permute-done.refs_11_) | copy-start | bytes 393220
  26.8 5.4 %collective-permute-start.4 = (bf16[16,4096]{1,0:T(8,128)(2,1)S(1)}, bf16[16,4096]{1,0:T(8,128)(2,1)S(1)}, u32[]{:S(2)}, u32[]{:S(2)}) collective-permute-start(bf16[16,4096]{1,0:T(8,128)(2,1)S(1)} %collective-permute-done.refs_11_), channel_id=1, source_target_pairs={{0,32},{32,64},{64,96},{96,128},{128,160},{160,192},{192,224},{224... | collective-permute-start | bytes 393224 | tf_op jit(solution)/shard_map/ppermute | solution.py:50
  26.8 8.1 %collective-permute-start.2 = (bf16[16,4096]{1,0:T(8,128)(2,1)S(1)}, bf16[16,4096]{1,0:T(8,128)(2,1)S(1)}, u32[]{:S(2)}, u32[]{:S(2)}) collective-permute-start(bf16[16,4096]{1,0:T(8,128)(2,1)S(1)} %collective-permute-done.1.refs_5_), channel_id=1, source_target_pairs={{0,224},{32,0},{64,32},{96,64},{128,96},{160,128},{192,160},{224,1... | collective-permute-start | bytes 393224 | tf_op jit(solution)/shard_map/ppermute | solution.py:53
  32.2 16.1 %copy-start.5 = (bf16[16,4096]{1,0:T(8,128)(2,1)}, bf16[16,4096]{1,0:T(8,128)(2,1)S(1)}, u32[]{:S(2)}) copy-start(bf16[16,4096]{1,0:T(8,128)(2,1)S(1)} %collective-permute-done.4.refs_10_) | copy-start | bytes 393220
  32.2 5.6 %collective-permute-start.5 = (bf16[16,4096]{1,0:T(8,128)(2,1)S(1)}, bf16[16,4096]{1,0:T(8,128)(2,1)S(1)}, u32[]{:S(2)}, u32[]{:S(2)}) collective-permute-start(bf16[16,4096]{1,0:T(8,128)(2,1)S(1)} %collective-permute-done.4.refs_10_), channel_id=1, source_target_pairs={{0,32},{32,64},{64,96},{96,128},{128,160},{160,192},{192,224},{224... | collective-permute-start | bytes 393224 | tf_op jit(solution)/shard_map/ppermute | solution.py:50
  32.3 5.6 %collective-permute-start.14 = (bf16[16,4096]{1,0:T(8,128)(2,1)S(1)}, bf16[16,4096]{1,0:T(8,128)(2,1)S(1)}, u32[]{:S(2)}, u32[]{:S(2)}) collective-permute-start(bf16[16,4096]{1,0:T(8,128)(2,1)S(1)} %dynamic-slice_bitcast_fusion.refs_12_), channel_id=1, source_target_pairs={{0,1},{1,0},{2,3},{3,2},{4,5},{5,4},{6,7},{7,6},{8,9},{9,8},{10,11... | collective-permute-start | bytes 393224 | tf_op jit(solution)/shard_map/ppermute | solution.py:593
  34.4 6.2 %collective-permute-start.7 = (bf16[16,4096]{1,0:T(8,128)(2,1)S(1)}, bf16[16,4096]{1,0:T(8,128)(2,1)S(1)}, u32[]{:S(2)}, u32[]{:S(2)}) collective-permute-start(bf16[16,4096]{1,0:T(8,128)(2,1)S(1)} %collective-permute-done.1.refs_5_), channel_id=1, source_target_pairs={{0,1},{1,0},{2,3},{3,2},{4,5},{5,4},{6,7},{7,6},{8,9},{9,8},{10,11... | collective-permute-start | bytes 393224 | tf_op jit(solution)/shard_map/ppermute | solution.py:593
  34.5 6.2 %collective-permute-start.13 = (bf16[16,4096]{1,0:T(8,128)(2,1)S(1)}, bf16[16,4096]{1,0:T(8,128)(2,1)S(1)}, u32[]{:S(2)}, u32[]{:S(2)}) collective-permute-start(bf16[16,4096]{1,0:T(8,128)(2,1)S(1)} %collective-permute-done.refs_11_), channel_id=1, source_target_pairs={{0,1},{1,0},{2,3},{3,2},{4,5},{5,4},{6,7},{7,6},{8,9},{9,8},{10,11... | collective-permute-start | bytes 393224 | tf_op jit(solution)/shard_map/ppermute | solution.py:593
  34.9 13.4 %copy-start.6 = (bf16[16,4096]{1,0:T(8,128)(2,1)}, bf16[16,4096]{1,0:T(8,128)(2,1)S(1)}, u32[]{:S(2)}) copy-start(bf16[16,4096]{1,0:T(8,128)(2,1)S(1)} %collective-permute-done.2.refs_6_) | copy-start | bytes 393220
  34.9 6.2 %collective-permute-start.3 = (bf16[16,4096]{1,0:T(8,128)(2,1)S(1)}, bf16[16,4096]{1,0:T(8,128)(2,1)S(1)}, u32[]{:S(2)}, u32[]{:S(2)}) collective-permute-start(bf16[16,4096]{1,0:T(8,128)(2,1)S(1)} %collective-permute-done.2.refs_6_), channel_id=1, source_target_pairs={{0,224},{32,0},{64,32},{96,64},{128,96},{160,128},{192,160},{224,1... | collective-permute-start | bytes 393224 | tf_op jit(solution)/shard_map/ppermute | solution.py:53
  37.8 10.5 %copy-start.7 = (bf16[16,4096]{1,0:T(8,128)(2,1)}, bf16[16,4096]{1,0:T(8,128)(2,1)S(1)}, u32[]{:S(2)}) copy-start(bf16[16,4096]{1,0:T(8,128)(2,1)S(1)} %collective-permute-done.5.refs_9_) | copy-start | bytes 393220
  37.8 5.0 %collective-permute-start.6 = (bf16[16,4096]{1,0:T(8,128)(2,1)S(1)}, bf16[16,4096]{1,0:T(8,128)(2,1)S(1)}, u32[]{:S(2)}, u32[]{:S(2)}) collective-permute-start(bf16[16,4096]{1,0:T(8,128)(2,1)S(1)} %collective-permute-done.5.refs_9_), channel_id=1, source_target_pairs={{0,32},{32,64},{64,96},{96,128},{128,160},{160,192},{192,224},{224... | collective-permute-start | bytes 393224 | tf_op jit(solution)/shard_map/ppermute | solution.py:50
  37.8 10.5 %copy-start.8 = (bf16[16,4096]{1,0:T(8,128)(2,1)}, bf16[16,4096]{1,0:T(8,128)(2,1)S(1)}, u32[]{:S(2)}) copy-start(bf16[16,4096]{1,0:T(8,128)(2,1)S(1)} %collective-permute-done.14.refs_20_) | copy-start | bytes 393220
  37.9 8.8 %collective-permute-start.8 = (bf16[16,4096]{1,0:T(8,128)(2,1)S(1)}, bf16[16,4096]{1,0:T(8,128)(2,1)S(1)}, u32[]{:S(2)}, u32[]{:S(2)}) collective-permute-start(bf16[16,4096]{1,0:T(8,128)(2,1)S(1)} %collective-permute-done.2.refs_6_), channel_id=1, source_target_pairs={{0,1},{1,0},{2,3},{3,2},{4,5},{5,4},{6,7},{7,6},{8,9},{9,8},{10,11... | collective-permute-start | bytes 393224 | tf_op jit(solution)/shard_map/ppermute | solution.py:593
  40.6 6.1 %copy-start.9 = (bf16[16,4096]{1,0:T(8,128)(2,1)}, bf16[16,4096]{1,0:T(8,128)(2,1)S(1)}, u32[]{:S(2)}) copy-start(bf16[16,4096]{1,0:T(8,128)(2,1)S(1)} %collective-permute-done.7.refs_13_) | copy-start | bytes 393220
  40.6 6.1 %collective-permute-start.12 = (bf16[16,4096]{1,0:T(8,128)(2,1)S(1)}, bf16[16,4096]{1,0:T(8,128)(2,1)S(1)}, u32[]{:S(2)}, u32[]{:S(2)}) collective-permute-start(bf16[16,4096]{1,0:T(8,128)(2,1)S(1)} %collective-permute-done.4.refs_10_), channel_id=1, source_target_pairs={{0,1},{1,0},{2,3},{3,2},{4,5},{5,4},{6,7},{7,6},{8,9},{9,8},{10,11... | collective-permute-start | bytes 393224 | tf_op jit(solution)/shard_map/ppermute | solution.py:593
  40.7 6.9 %copy-start.10 = (bf16[16,4096]{1,0:T(8,128)(2,1)}, bf16[16,4096]{1,0:T(8,128)(2,1)S(1)}, u32[]{:S(2)}) copy-start(bf16[16,4096]{1,0:T(8,128)(2,1)S(1)} %collective-permute-done.13.refs_19_) | copy-start | bytes 393220
  40.7 6.0 %collective-permute-start.11 = (bf16[16,4096]{1,0:T(8,128)(2,1)S(1)}, bf16[16,4096]{1,0:T(8,128)(2,1)S(1)}, u32[]{:S(2)}, u32[]{:S(2)}) collective-permute-start(bf16[16,4096]{1,0:T(8,128)(2,1)S(1)} %collective-permute-done.5.refs_9_), channel_id=1, source_target_pairs={{0,1},{1,0},{2,3},{3,2},{4,5},{5,4},{6,7},{7,6},{8,9},{9,8},{10,11... | collective-permute-start | bytes 393224 | tf_op jit(solution)/shard_map/ppermute | solution.py:593
  41.1 6.5 %copy-start.11 = (bf16[16,4096]{1,0:T(8,128)(2,1)}, bf16[16,4096]{1,0:T(8,128)(2,1)S(1)}, u32[]{:S(2)}) copy-start(bf16[16,4096]{1,0:T(8,128)(2,1)S(1)} %collective-permute-done.3.refs_7_) | copy-start | bytes 393220
  41.1 5.6 %collective-permute-start.9 = (bf16[16,4096]{1,0:T(8,128)(2,1)S(1)}, bf16[16,4096]{1,0:T(8,128)(2,1)S(1)}, u32[]{:S(2)}, u32[]{:S(2)}) collective-permute-start(bf16[16,4096]{1,0:T(8,128)(2,1)S(1)} %collective-permute-done.3.refs_7_), channel_id=1, source_target_pairs={{0,1},{1,0},{2,3},{3,2},{4,5},{5,4},{6,7},{7,6},{8,9},{9,8},{10,11... | collective-permute-start | bytes 393224 | tf_op jit(solution)/shard_map/ppermute | solution.py:593
  42.9 4.8 %copy-start.12 = (bf16[16,4096]{1,0:T(8,128)(2,1)}, bf16[16,4096]{1,0:T(8,128)(2,1)S(1)}, u32[]{:S(2)}) copy-start(bf16[16,4096]{1,0:T(8,128)(2,1)S(1)} %collective-permute-done.6.refs_8_) | copy-start | bytes 393220
  42.9 4.8 %collective-permute-start.10 = (bf16[16,4096]{1,0:T(8,128)(2,1)S(1)}, bf16[16,4096]{1,0:T(8,128)(2,1)S(1)}, u32[]{:S(2)}, u32[]{:S(2)}) collective-permute-start(bf16[16,4096]{1,0:T(8,128)(2,1)S(1)} %collective-permute-done.6.refs_8_), channel_id=1, source_target_pairs={{0,1},{1,0},{2,3},{3,2},{4,5},{5,4},{6,7},{7,6},{8,9},{9,8},{10,11... | collective-permute-start | bytes 393224 | tf_op jit(solution)/shard_map/ppermute | solution.py:593
  46.7 1.7 %copy-start.13 = (bf16[16,4096]{1,0:T(8,128)(2,1)}, bf16[16,4096]{1,0:T(8,128)(2,1)S(1)}, u32[]{:S(2)}) copy-start(bf16[16,4096]{1,0:T(8,128)(2,1)S(1)} %collective-permute-done.8.refs_14_) | copy-start | bytes 393220
  46.7 1.0 copy-start.14
  46.7 1.0 copy-start.16
  46.8 1.0 copy-start.15
  47.7 0.7 copy-start.17
  53.9 18.5 %all-to-all-start.2 = ((bf16[8,192,128]{2,1,0:T(8,128)(2,1)}), bf16[8,192,128]{2,1,0:T(8,128)(2,1)S(1)}, u32[]{:S(2)}, u32[]{:S(2)}) async-start(bf16[8,192,128]{2,1,0:T(8,128)(2,1)} %side.1), calls=%async_computation.2 | async-start | bytes 786432 | tf_op jit(solution)/shard_map/all_to_all | solution.py:596
  72.4 15.6 %copy-start = (bf16[8,192,128]{2,1,0:T(8,128)(2,1)}, bf16[8,192,128]{2,1,0:T(8,128)(2,1)S(1)}, u32[]{:S(2)}) copy-start(bf16[8,192,128]{2,1,0:T(8,128)(2,1)S(1)} %all-to-all-done.2.refs_2_) | copy-start | bytes 1179652
  72.4 15.6 %all-to-all-start.1 = ((bf16[8,128,128]{2,1,0:T(8,128)(2,1)}), bf16[8,128,128]{2,1,0:T(8,128)(2,1)S(1)}, u32[]{:S(2)}, u32[]{:S(2)}) async-start(bf16[8,128,128]{2,1,0:T(8,128)(2,1)} %get-tuple-element.30), calls=%async_computation.1 | async-start | bytes 524288 | tf_op jit(solution)/shard_map/all_to_all | solution.py:599
  88.0 0.7 copy-start.1
  95.9 5.2 %collective-permute-start.15 = (f32[16,144,256]{2,1,0:T(8,128)}, f32[16,144,256]{2,1,0:T(8,128)}, u32[]{:S(2)}, u32[]{:S(2)}) collective-permute-start(f32[16,144,256]{2,1,0:T(8,128)} %get-tuple-element.39), channel_id=1, source_target_pairs={{0,1},{1,0},{2,3},{3,2},{4,5},{5,4},{6,7},{7,6},{8,9},{9,8},{10,11... | collective-permute-start | bytes 7077896 | tf_op jit(solution)/shard_map/ppermute | solution.py:605
  129.1 11.2 %all-to-all-start.4 = ((f32[8,16,256]{2,1,0:T(8,128)}), f32[8,16,256]{2,1,0:T(8,128)S(1)}, u32[]{:S(2)}, u32[]{:S(2)}) async-start(f32[8,16,256]{2,1,0:T(8,128)} %bitcast.9), calls=%async_computation.4 | async-start | bytes 262144 | tf_op jit(solution)/shard_map/all_to_all | solution.py:611
  152.5 5.4 %collective-permute-start.16 = (f32[32,4096]{1,0:T(8,128)S(1)}, f32[32,4096]{1,0:T(8,128)S(1)}, u32[]{:S(2)}, u32[]{:S(2)}) collective-permute-start(f32[32,4096]{1,0:T(8,128)S(1)} %bitcast.19), channel_id=1, source_target_pairs={{0,1},{1,0},{2,3},{3,2},{4,5},{5,4},{6,7},{7,6},{8,9},{9,8},{10,11... | collective-permute-start | bytes 1572872 | tf_op jit(solution)/shard_map/ppermute | solution.py:615

commit v8 on v7

--- a/solution.py
+++ b/solution.py
@@ -102,7 +102,7 @@
 
 
 PIECES = 8
-COST = dict(forward=4, side=5, own=8, given=5, kept=4)
+COST = dict(forward=4, own=8, given=5, kept=4)
 
 
 def gather_into(blocks, buffer, sem):
@@ -237,74 +237,17 @@
     )
 
 
-def side_kernel(count, meta_ref, stream_in, dg_in, lrt_in, irms_in, *refs):
-    mine, other, (out_ref, up_ref, up_sem) = refs[:count], refs[count : 2 * count], refs[2 * count :]
-    core = meta_ref[0]
-    rank, half = mine[0].shape
-    tokens = stream_in[1].shape[0]
-    rows = count * rank
-    chunk = min(1024, half)
-    ready = [gather_into(mine, up_ref.at[0], up_sem.at[0])]
-    for item in (stream_in, dg_in):
-        whole(item).start()
-    ready.append(gather_into(other, up_ref.at[1], up_sem.at[1]))
-    for item in (lrt_in, irms_in):
-        whole(item).start()
-    for item in (stream_in, dg_in):
-        whole(item).wait()
-    stream_ref, dg_ref = stream_in[1], dg_in[1]
-    total = jnp.zeros((rows, tokens + 2 * rank), f32)
-    for which, base in enumerate((core, 1 - core)):
-        ready[which].wait()
-
-        def step(i, acc, which=which, base=base):
-            local = pl.ds(pl.multiple_of(i * chunk, chunk), chunk)
-            columns = pl.ds(pl.multiple_of(base * half + i * chunk, chunk), chunk)
-            right = jnp.concatenate([stream_ref[:, columns], dg_ref[0, :, columns], dg_ref[1, :, columns]], axis=0)
-            return acc + nt(up_ref[which, :, local], right)
-
-        total = lax.fori_loop(0, half // chunk, step, total, unroll=2)
-    whole(lrt_in).wait()
-    whole(irms_in).wait()
-    irms = irms_in[1][0:1, :]
-    w = total[:, tokens : tokens + rank] + total[:, tokens + rank :]
-    w = jnp.concatenate([w, jnp.zeros((rows, 128 - rank), f32)], axis=1).T[:rank, :]
-    w_hi, w_lo = split2(w)
-    irms_hi = irms.astype(bf16).astype(f32)
-    row = lax.broadcasted_iota(jnp.int32, (rank, tokens), 0)
-    last = jnp.where(row == 0, irms_hi, jnp.where(row == 1, irms - irms_hi, 0.0)).astype(bf16)
-    scaled_up = (total[:, :tokens] * irms).astype(bf16)
-    for i in range(out_ref.shape[0]):
-        out_ref[i, :rows, :] = scaled_up
-        out_ref[i, rows : rows + rank, :] = lrt_in[1][...]
-        out_ref[i, rows + rank : rows + 2 * rank, :] = w_hi
-        out_ref[i, rows + 2 * rank : rows + 3 * rank, :] = w_lo
-        out_ref[i, rows + 3 * rank :, :] = last
-
-
 def up_scratch(mine):
     rank, half = mine[0].shape
     return (pltpu.VMEM((2, len(mine) * rank, half), bf16), pltpu.SemaphoreType.DMA((2,)))
 
 
-def side_of(meta, stream, dg, lrt, irms, mine, other):
-    layers = len(mine)
-    rank = lrt.shape[0]
-    (side,) = call(
-        functools.partial(side_kernel, layers),
-        "side",
-        (jax.ShapeDtypeStruct((layers, (layers + 4) * rank, stream.shape[0]), bf16),),
-        (meta,),
-        (stream, dg, lrt, irms, *mine, *other),
-        (1, 1, 1, 1) + (0,) * (2 * layers),
-        up_scratch(mine),
-    )
-    return side
-
-
-def own_kernel(count, meta_ref, refs_in, stream_in, up_in, lrt_in, *refs):
+def own_kernel(count, meta_ref, refs_in, stream_in, up_in, lrt_in, dg_in, irms_in, *refs):
     mine, other = refs[:count], refs[count : 2 * count]
-    own_ref, proj_ref, output_ref, ups_ref, up_sem = refs[2 * count :]
+    own_ref, out_ref, output_ref, ups_ref, up_sem = refs[2 * count :]
+    rank = lrt_in[1].shape[0]
+    rows = count * rank
+    dg_ref = dg_in[1]
     core, flag, valid = meta_ref[0], meta_ref[1], meta_ref[2]
     refs_ref, stream_ref, up_ref = refs_in[1], stream_in[1], up_in[1]
     tiles, padded, chunk = refs_ref.shape
@@ -322,6 +265,9 @@
         stream_loads[i].start()
         ref_loads[i].start()
     ready = [gather_into(blocks, ups_ref.at[i], up_sem.at[i]) for i, blocks in enumerate((mine, other))]
+    for item in (dg_in, irms_in):
+        whole(item).start()
+        ready.append(whole(item))
     whole(lrt_in).wait()
     whole(up_in).wait()
     low_rank = lrt_in[1][...].astype(f32).T.astype(bf16)
@@ -351,7 +297,7 @@
     def finish(make):
         for wait in ready:
             wait.wait()
-        total = jnp.zeros(proj_ref.shape[1:], f32)
+        total = jnp.zeros((rows, 2 * tokens + 2 * rank), f32)
         for which, base in enumerate((core, 1 - core)):
 
             def step(i, acc, which=which, base=base):
@@ -362,13 +308,28 @@
                     own = make(output_ref[:, columns], refs_ref[j, :tokens, :].astype(f32)).astype(bf16)
                     own_ref[:, columns] = own
                     parts.append(own)
-                local = pl.ds(pl.multiple_of(i * group * chunk, group * chunk), group * chunk)
-                return acc + nt(ups_ref[which, :, local], jnp.concatenate(parts, axis=1))
+                size = group * chunk
+                local = pl.ds(pl.multiple_of(i * size, size), size)
+                columns = pl.ds(pl.multiple_of(base * half + i * size, size), size)
+                right = [jnp.concatenate(parts, axis=1), stream_ref[:, columns], dg_ref[0, :, columns], dg_ref[1, :, columns]]
+                return acc + nt(ups_ref[which, :, local], jnp.concatenate(right, axis=0))
 
             total = lax.fori_loop(0, per_half // group, step, total, unroll=2)
-        total = total.astype(bf16)
-        for i in range(proj_ref.shape[0]):
-            proj_ref[i] = total
+
+        irms = irms_in[1][0:1, :]
+        own_up = total[:, :tokens].astype(bf16)
+        scaled_up = (total[:, tokens : 2 * tokens] * irms).astype(bf16)
+        w = total[:, 2 * tokens : 2 * tokens + rank] + total[:, 2 * tokens + rank :]
+        w = jnp.concatenate([w, jnp.zeros((rows, 128 - rank), f32)], axis=1).T[:rank, :]
+        w_hi, w_lo = split2(w)
+        irms_hi = irms.astype(bf16).astype(f32)
+        row = lax.broadcasted_iota(jnp.int32, (rank, tokens), 0)
+        last = jnp.where(row == 0, irms_hi, jnp.where(row == 1, irms - irms_hi, 0.0)).astype(bf16)
+        for i in range(out_ref.shape[0]):
+            low = 0
+            for value in (scaled_up, lrt_in[1][...], w_hi, w_lo, last, own_up):
+                out_ref[i, low : low + value.shape[0], :] = value
+                low += value.shape[0]
 
     @pl.when(flag == 1)
     def _():
@@ -388,31 +349,34 @@
         finish(lambda o, r: coef * (o - r))
 
 
-def own_gradient(meta, refs, stream, up, lrt, mine, other):
+def own_gradient(meta, refs, stream, up, lrt, dg, irms, mine, other):
     layers = len(mine)
+    rank = up.shape[0]
     return call(
         functools.partial(own_kernel, layers),
         "own",
         (
             jax.ShapeDtypeStruct(stream.shape, bf16),
-            jax.ShapeDtypeStruct((layers, layers * up.shape[0], stream.shape[0]), bf16),
+            jax.ShapeDtypeStruct((layers, (2 * layers + 4) * rank, stream.shape[0]), bf16),
         ),
         (meta,),
-        (refs, stream, up, lrt, *mine, *other),
-        (PIECES, PIECES, 1, 1) + (0,) * (2 * layers),
+        (refs, stream, up, lrt, dg, irms, *mine, *other),
+        (PIECES, PIECES, 1, 1, 1, 1) + (0,) * (2 * layers),
         (pltpu.VMEM(stream.shape, f32),) + up_scratch(mine),
     )
 
 
-def solve(width, rank, me, own_ref, side_ref, low_ref, lrt_ref, coef_ref, k_ref, acc):
-    layers, rows, _ = own_ref.shape
+def solve(width, rank, me, side_ref, low_ref, lrt_ref, coef_ref, k_ref, acc):
+    layers = side_ref.shape[0]
+    rows = layers * rank
+    first = rows + 4 * rank
     acc[...] = jnp.zeros_like(acc)
     for j in range(layers):
 
         @pl.when(me + j < layers)
         def _(j=j):
             low = rank * (layers - 1 - j)
-            acc[0 : rank * (j + 1), :] += own_ref[me + j, low:rows, :].astype(f32)
+            acc[0 : rank * (j + 1), :] += side_ref[me + j, first + low : first + rows, :].astype(f32)
 
     def inverse_rms(t):
         hi = side_ref[t, rows + 3 * rank : rows + 3 * rank + 1, :].astype(f32)
@@ -487,18 +451,16 @@
     ]
 
 
-def given_kernel(rank, meta_ref, own_up_in, side_in, *refs):
+def given_kernel(rank, meta_ref, side_in, *refs):
     large, (out_ref, low_ref, lrt_ref, coef_ref, k_ref, acc, buffer, out_sem) = refs[:4], refs[4:]
     start, me = meta_ref[0], meta_ref[1]
     loads = part_loads(start, large, buffer.shape[0], buffer.shape[2])
-    for item in (own_up_in, side_in):
-        whole(item).start()
+    whole(side_in).start()
     for load in loads:
         for item in load:
             item.start()
-    for item in (own_up_in, side_in):
-        whole(item).wait()
-    solve(large[0][0].shape[1], rank, me, own_up_in[1], side_in[1], low_ref, lrt_ref, coef_ref, k_ref, acc)
+    whole(side_in).wait()
+    solve(large[0][0].shape[1], rank, me, side_in[1], low_ref, lrt_ref, coef_ref, k_ref, acc)
     part(start, loads, low_ref[...], lrt_ref[...], coef_ref[...], k_ref, *large, out_ref, buffer, out_sem)
 
 
@@ -521,8 +483,9 @@
     return jax.ShapeDtypeStruct(shape, f32), (pltpu.VMEM(shape, f32), pltpu.SemaphoreType.DMA((4,)))
 
 
-def given_part(meta, chunks, chunk, rank, own_up, sides, *large):
-    _, rows, tokens = own_up.shape
+def given_part(meta, chunks, chunk, rank, sides, *large):
+    layers, _, tokens = sides.shape
+    rows = layers * rank
     shape, scratch = part_shapes(chunks, chunk, rows, rank)
     return call(
         functools.partial(given_kernel, rank),
@@ -535,8 +498,8 @@
             jax.ShapeDtypeStruct((2, rows, rank), bf16),
         ),
         (meta,),
-        (own_up, sides, *large),
-        (1, 1) + (4,) * 4,
+        (sides, *large),
+        (1,) + (4,) * 4,
         (pltpu.VMEM((rows, tokens), f32),)
         + scratch,
         in_place_outs=1,
@@ -592,16 +555,13 @@
     mine = ring_gather(up_half, SEC, lrt)[::-1]
     other = [lax.ppermute(block, "core", swap) for block in mine]
 
-    side = side_of(meta, stream, dg, lrt, irms, mine, other)
+    own, side = own_gradient(meta, refs, stream, up, lrt, dg, irms, mine, other)
     sides = lax.all_to_all(side, SEC, 0, 0, tiled=True)
-
-    own, own_up = own_gradient(meta, refs, stream, up, lrt, mine, other)
-    own_up = lax.all_to_all(own_up, SEC, 0, 0, tiled=True)
 
     large = (own, stream, normed, dg)
     away = jnp.stack([(1 - core) * half, me]).astype(jnp.int32)
     here = (core * half)[None].astype(jnp.int32)
-    given, *coefs = given_part(away, chips, chunk, rank, own_up, sides, *large)
+    given, *coefs = given_part(away, chips, chunk, rank, sides, *large)
     received = lax.ppermute(given, "core", swap)
     kept = kept_part(here, chips, chunk, *coefs, *large)
     blocks = lax.all_to_all((kept + received).astype(bf16), CHIPS, 0, 0, tiled=True)

time: 160 us -> 154 us (0.963)
  Pallas kernels: 33.7 us -> 28.8 us
    all_to_all x1 -> x0, waiting for transfers between devices: 11.5 us -> none  [shards(): own_up = lax.all_to_all(own_up, SEC, 0, 0, tiled=True)]
    all_to_all x1, waiting for transfers between devices: 5.93 us -> 17.3 us  [shards(): sides = lax.all_to_all(side, SEC, 0, 0, tiled=True)]
    pallas_call x5 -> x4, Pallas kernels: 30.5 us -> 25.7 us  [call(): pl.pallas_call(body, out_shape=out_shape, in_specs=[smem()] * count + [in...]
    all_to_all x1 -> x0, starting transfers between devices: 3.41 us -> none  [shards(): own_up = lax.all_to_all(own_up, SEC, 0, 0, tiled=True)]
    ppermute x1, starting transfers between devices: 0.68 us -> 3.53 us  [shards(): received = lax.ppermute(given, 'core', swap)]
  transfers between devices with their start and end apart: 21 -> 20, of which waited for: 9 -> 7; matrix products, arithmetic and copies ran while one was open for 0% -> 0% of each run, Pallas kernels for 15% -> 6%
where the time goes in v8:
time: 154 us; the launch traced here: 153 us
  starting transfers between devices  45.5 us (30%)
  blocking collectives  35.3 us (23%)
  waiting for transfers between devices  32.3 us (21%)
  Pallas kernels  28.8 us (19%)
  other arithmetic  5.82 us (4%)
  local copies, waits for them, and re-layouts  3.19 us (2%)
  between operations  2.21 us (1%)
    pallas_call x4, Pallas kernels, call(): pl.pallas_call(body, out_shape=out_shape, in_specs=[smem()] * count + [in...  25.7 us
    all_to_all x1, blocking collectives, shards(): lax.all_to_all((kept + received).astype(bf16), CHIPS, 0, 0, tiled=True)  23.2 us
    all_to_all x1, waiting for transfers between devices, shards(): sides = lax.all_to_all(side, SEC, 0, 0, tiled=True)  17.3 us
    all_to_all x1, blocking collectives, shards(): lax.all_to_all(jnp.broadcast_to(final, (chips,) + final.shape), CHIPS, 0,...  12.1 us
    ppermute x3, starting transfers between devices, ring_gather(): bwd = lax.ppermute(bwd, axis, down)  11.2 us
    ppermute x8, starting transfers between devices, shards(): other = [lax.ppermute(block, 'core', swap) for block in mine]  10.2 us
    all_to_all x1, starting transfers between devices, shards(): refs = lax.all_to_all(ordered, DP, split_axis=0, concat_axis=0, tiled=True)  8.65 us
    all_to_all x1, waiting for transfers between devices, shards(): lax.all_to_all(grad_up.reshape(layers, rank, chunk), SEC, 0, 0, tiled=True)  7.84 us
  transfers between devices with their start and end apart: 20, of which 7 were waited for; matrix products, arithmetic and copies ran while one was open for 0% of the time, Pallas kernels for 6%

profile of v8, /device:TPU:1, one launch (start us, length us, event | category | flops | bytes accessed | tf_op | source)
XLA Modules:
  0.0 153.1 jit_solution(6491280888503708294)
XLA Ops:
  1.9 0.9 dynamic-slice_bitcast_fusion.refs_14_
  2.9 0.6 pad_add_fusion.1.meta_ref.refs_0_
  3.5 3.2 %order.1 = bf16[32,136,256]{2,1,0:T(8,128)(2,1)} custom-call(s32[32]{0:T(128)} %position_ref, s32[3]{0:T(128)} %pad_add_fusion.1.meta_ref.refs_0_, bf16[32,128,256]{2,1,0:T(8,128)(2,1)} %bitcast.18), custom_call_target="tpu_custom_call" | custom-call | tf_op jit(solution)/shard_map/order/pallas_call | solution.py:162
  6.7 8.6 %all-to-all-start = ((bf16[32,136,256]{2,1,0:T(8,128)(2,1)}), bf16[32,136,256]{2,1,0:T(8,128)(2,1)}, u32[]{:S(2)}, u32[]{:S(2)}) async-start(bf16[32,136,256]{2,1,0:T(8,128)(2,1)} %order.1), calls=%async_computation | async-start | bytes 4456448 | tf_op jit(solution)/shard_map/all_to_all | solution.py:549
  15.3 5.7 %collective-permute-start.1 = (bf16[16,4096]{1,0:T(8,128)(2,1)S(1)}, bf16[16,4096]{1,0:T(8,128)(2,1)S(1)}, u32[]{:S(2)}, u32[]{:S(2)}) collective-permute-start(bf16[16,4096]{1,0:T(8,128)(2,1)S(1)} %dynamic-slice_bitcast_fusion.refs_14_), channel_id=1, source_target_pairs={{0,224},{32,0},{64,32},{96,64},{128,96},{160,128},{192,160},{224,1... | collective-permute-start | bytes 393224 | tf_op jit(solution)/shard_map/ppermute | solution.py:53
  21.0 0.0 collective-permute-start
  21.0 4.8 %forward.1 = (bf16[128,8192]{1,0:T(8,128)(2,1)}, bf16[16,128]{1,0:T(8,128)(2,1)}, f32[8,128]{1,0:T(8,128)}, bf16[2,16,8192]{2,1,0:T(8,128)(2,1)}) custom-call(bf16[128,8192]{1,0:T(8,128)(2,1)} %bitcast.23, bf16[16,8192]{1,0:T(8,128)(2,1)} %bitcast.27, f32[1,8192]{1,0:T(1,128)} %refs_2_), custom_call_target="tpu_custom_call" | custom-call | flops 4000000000 | bytes 12000000 | tf_op jit(solution)/shard_map/forward/pallas_call | solution.py:90
  25.7 0.0 copy-start.2
  25.8 1.0 collective-permute-done.refs_13_
  26.8 0.0 collective-permute-start.4
  26.8 2.7 %collective-permute-start.2 = (bf16[16,4096]{1,0:T(8,128)(2,1)S(1)}, bf16[16,4096]{1,0:T(8,128)(2,1)S(1)}, u32[]{:S(2)}, u32[]{:S(2)}) collective-permute-start(bf16[16,4096]{1,0:T(8,128)(2,1)S(1)} %collective-permute-done.1.refs_7_), channel_id=1, source_target_pairs={{0,224},{32,0},{64,32},{96,64},{128,96},{160,128},{192,160},{224,1... | collective-permute-start | bytes 393224 | tf_op jit(solution)/shard_map/ppermute | solution.py:53
  29.4 2.8 %collective-permute-done.4.refs_12_ = bf16[16,4096]{1,0:T(8,128)(2,1)S(1)} collective-permute-done((bf16[16,4096]{1,0:T(8,128)(2,1)S(1)}, bf16[16,4096]{1,0:T(8,128)(2,1)S(1)}, u32[]{:S(2)}, u32[]{:S(2)}) %collective-permute-start.4) | collective-permute-done | bytes 131104 | tf_op jit(solution)/shard_map/ppermute | solution.py:50
  32.2 0.0 collective-permute-start.5
  32.2 2.2 %collective-permute-start.14 = (bf16[16,4096]{1,0:T(8,128)(2,1)S(1)}, bf16[16,4096]{1,0:T(8,128)(2,1)S(1)}, u32[]{:S(2)}, u32[]{:S(2)}) collective-permute-start(bf16[16,4096]{1,0:T(8,128)(2,1)S(1)} %dynamic-slice_bitcast_fusion.refs_14_), channel_id=1, source_target_pairs={{0,1},{1,0},{2,3},{3,2},{4,5},{5,4},{6,7},{7,6},{8,9},{9,8},{10,11... | collective-permute-start | bytes 393224 | tf_op jit(solution)/shard_map/ppermute | solution.py:556
  34.4 0.1 collective-permute-start.7
  34.5 0.4 collective-permute-start.13
  34.9 0.0 collective-permute-done.2.refs_8_
  34.9 2.9 %collective-permute-start.3 = (bf16[16,4096]{1,0:T(8,128)(2,1)S(1)}, bf16[16,4096]{1,0:T(8,128)(2,1)S(1)}, u32[]{:S(2)}, u32[]{:S(2)}) collective-permute-start(bf16[16,4096]{1,0:T(8,128)(2,1)S(1)} %collective-permute-done.2.refs_8_), channel_id=1, source_target_pairs={{0,224},{32,0},{64,32},{96,64},{128,96},{160,128},{192,160},{224,1... | collective-permute-start | bytes 393224 | tf_op jit(solution)/shard_map/ppermute | solution.py:53
  37.8 0.0 collective-permute-done.5.refs_11_
  37.8 0.0 collective-permute-start.6
  37.8 2.8 %collective-permute-start.8 = (bf16[16,4096]{1,0:T(8,128)(2,1)S(1)}, bf16[16,4096]{1,0:T(8,128)(2,1)S(1)}, u32[]{:S(2)}, u32[]{:S(2)}) collective-permute-start(bf16[16,4096]{1,0:T(8,128)(2,1)S(1)} %collective-permute-done.2.refs_8_), channel_id=1, source_target_pairs={{0,1},{1,0},{2,3},{3,2},{4,5},{5,4},{6,7},{7,6},{8,9},{9,8},{10,11... | collective-permute-start | bytes 393224 | tf_op jit(solution)/shard_map/ppermute | solution.py:556
  40.6 0.1 collective-permute-start.12
  40.7 0.4 collective-permute-start.11
  41.1 0.4 collective-permute-start.9
  41.5 1.3 collective-permute-done.6.refs_10_
  42.8 3.8 %collective-permute-start.10 = (bf16[16,4096]{1,0:T(8,128)(2,1)S(1)}, bf16[16,4096]{1,0:T(8,128)(2,1)}, u32[]{:S(2)}, u32[]{:S(2)}) collective-permute-start(bf16[16,4096]{1,0:T(8,128)(2,1)S(1)} %collective-permute-done.6.refs_10_), channel_id=1, source_target_pairs={{0,1},{1,0},{2,3},{3,2},{4,5},{5,4},{6,7},{7,6},{8,9},{9,8},{10,11... | collective-permute-start | bytes 393224 | tf_op jit(solution)/shard_map/ppermute | solution.py:556
  46.7 0.6 copy-done.13
  47.3 0.0 copy-done.15
  47.4 0.6 copy-done.14
  48.1 10.5 %own.1 = (bf16[128,8192]{1,0:T(8,128)(2,1)}, bf16[8,320,128]{2,1,0:T(8,128)(2,1)}) custom-call(s32[3]{0:T(128)} %pad_add_fusion.1.meta_ref.refs_0_, bf16[32,136,256]{2,1,0:T(8,128)(2,1)} %all-to-all-done.refs_1_, bf16[128,8192]{1,0:T(8,128)(2,1)} %bitcast.24, bf16[16,8192]{1,0:T(8,128)(2,1)} %bitcast.22, bf16[16,128]{1,0:T(8,128)(2,1)} %get-tuple-element.26.refs_4_, ...), custom_call_target="tpu_custom_call" | custom-call | flops 8000000000 | bytes 24000000 | tf_op jit(solution)/shard_map/own/pallas_call | solution.py:90
  58.6 4.8 %all-to-all-start.1 = ((bf16[8,320,128]{2,1,0:T(8,128)(2,1)}), bf16[8,320,128]{2,1,0:T(8,128)(2,1)S(1)}, u32[]{:S(2)}, u32[]{:S(2)}) async-start(bf16[8,320,128]{2,1,0:T(8,128)(2,1)} %get-tuple-element.32), calls=%async_computation.1 | async-start | bytes 1310720 | tf_op jit(solution)/shard_map/all_to_all | solution.py:559
  63.4 0.6 pad_add_fusion.refs_0_
  64.0 17.3 %all-to-all-done.1.refs_1_ = bf16[8,320,128]{2,1,0:T(8,128)(2,1)S(1)} async-done(((bf16[8,320,128]{2,1,0:T(8,128)(2,1)}), bf16[8,320,128]{2,1,0:T(8,128)(2,1)S(1)}, u32[]{:S(2)}, u32[]{:S(2)}) %all-to-all-start.1) | async-done | bytes 655392 | tf_op jit(solution)/shard_map/all_to_all | solution.py:559
  81.3 0.8 copy-done
  82.1 6.4 %given.1 = (f32[16,144,256]{2,1,0:T(8,128)}, bf16[16,128]{1,0:T(8,128)(2,1)}, bf16[128,128]{1,0:T(8,128)(2,1)}, bf16[128,128]{1,0:T(8,128)(2,1)}, bf16[2,128,16]{2,1,0:T(8,128)(2,1)}) custom-call(s32[2]{0:T(128)} %pad_add_fusion.refs_0_, bf16[8,320,128]{2,1,0:T(8,128)(2,1)} %copy-done, bf16[128,8192]{1,0:T(8,128)(2,1)} %get-tuple-element.33.refs_2_.refs_5_, ...), custom_call_target="tpu_custom_call" | custom-call | flops 5000000000 | bytes 15000000 | tf_op jit(solution)/shard_map/given/pallas_call | solution.py:90
  88.5 3.5 %collective-permute-start.15 = (f32[16,144,256]{2,1,0:T(8,128)}, f32[16,144,256]{2,1,0:T(8,128)}, u32[]{:S(2)}, u32[]{:S(2)}) collective-permute-start(f32[16,144,256]{2,1,0:T(8,128)} %get-tuple-element.39), channel_id=1, source_target_pairs={{0,1},{1,0},{2,3},{3,2},{4,5},{5,4},{6,7},{7,6},{8,9},{9,8},{10,11... | collective-permute-start | bytes 7077896 | tf_op jit(solution)/shard_map/ppermute | solution.py:565
  92.0 4.0 %kept.1 = f32[16,144,256]{2,1,0:T(8,128)} custom-call(s32[1]{0:T(128)} %bitcast.refs_0_, bf16[16,128]{1,0:T(8,128)(2,1)} %get-tuple-element.35.refs_1_, bf16[128,128]{1,0:T(8,128)(2,1)} %get-tuple-element.36.refs_2_, bf16[128,128]{1,0:T(8,128)(2,1)} %get-tuple-element.37.refs_3_, bf16[2,128,16]{2,1,0:T(8,128)(2,1)} %get-tuple-element.38.refs_4_, ...), custom_call_target="tpu_custom_call" | custom-call | flops 4000000000 | bytes 12000000 | tf_op jit(solution)/shard_map/kept/pallas_call | solution.py:90
  96.0 0.5 collective-permute-done.15
  96.5 2.7 %add_convert_fusion = bf16[16,144,256]{2,1,0:T(8,128)(2,1)S(1)} fusion(f32[16,144,256]{2,1,0:T(8,128)} %kept.1, f32[16,144,256]{2,1,0:T(8,128)} %collective-permute-done.15), kind=kLoop, calls=%fused_computation | loop fusion | flops 1179648 | bytes 5898240 | tf_op jit(solution)/shard_map/convert_element_type | solution.py:567
  99.2 23.2 %all_to_all.25 = bf16[16,144,256]{2,1,0:T(8,128)(2,1)S(1)} all-to-all(bf16[16,144,256]{2,1,0:T(8,128)(2,1)S(1)} %add_convert_fusion), channel_id=1, replica_groups=mesh['section'=8,'y'=4,'x'=4,'core'=2] {'y','x'}, dimensions={0} | all-to-all | bytes 2359296 | tf_op jit(solution)/shard_map/all_to_all | solution.py:567
  122.4 0.8 convert_reduce_fusion
  123.2 3.4 %all-to-all-start.3 = ((f32[8,16,256]{2,1,0:T(8,128)}), f32[8,16,256]{2,1,0:T(8,128)S(1)}, u32[]{:S(2)}, u32[]{:S(2)}) async-start(f32[8,16,256]{2,1,0:T(8,128)} %bitcast.9), calls=%async_computation.3 | async-start | bytes 262144 | tf_op jit(solution)/shard_map/all_to_all | solution.py:571
  126.6 7.8 %all-to-all-done.3 = f32[8,16,256]{2,1,0:T(8,128)S(1)} async-done(((f32[8,16,256]{2,1,0:T(8,128)}), f32[8,16,256]{2,1,0:T(8,128)S(1)}, u32[]{:S(2)}, u32[]{:S(2)}) %all-to-all-start.3) | async-done | bytes 131104 | tf_op jit(solution)/shard_map/all_to_all | solution.py:571
  134.5 12.1 %all_to_all.26 = f32[16,32,256]{2,1,0:T(8,128)S(1)} all-to-all(f32[16,32,256]{2,1,0:T(8,128)S(1)} %broadcast_in_dim.13), channel_id=1, replica_groups=mesh['section'=8,'y'=4,'x'=4,'core'=2] {'y','x'}, dimensions={0} | all-to-all | bytes 1048576 | tf_op jit(solution)/shard_map/all_to_all | solution.py:573
  146.6 3.8 %collective-permute-start.16 = (f32[32,4096]{1,0:T(8,128)S(1)}, f32[32,4096]{1,0:T(8,128)S(1)}, u32[]{:S(2)}, u32[]{:S(2)}) collective-permute-start(f32[32,4096]{1,0:T(8,128)S(1)} %bitcast.19), channel_id=1, source_target_pairs={{0,1},{1,0},{2,3},{3,2},{4,5},{5,4},{6,7},{7,6},{8,9},{9,8},{10,11... | collective-permute-start | bytes 1572872 | tf_op jit(solution)/shard_map/ppermute | solution.py:575
  150.5 1.5 %collective-permute-done.16 = f32[32,4096]{1,0:T(8,128)S(1)} collective-permute-done((f32[32,4096]{1,0:T(8,128)S(1)}, f32[32,4096]{1,0:T(8,128)S(1)}, u32[]{:S(2)}, u32[]{:S(2)}) %collective-permute-start.16) | collective-permute-done | bytes 524320 | tf_op jit(solution)/shard_map/ppermute | solution.py:575
  152.0 0.1 broadcast_select_fusion
  152.1 1.0 fusion.2
  (43 shorter events, 0.2 us)
Async XLA Ops:
  2.9 29.3 %copy-start.1 = (bf16[16,4096]{1,0:T(8,128)(2,1)}, bf16[16,4096]{1,0:T(8,128)(2,1)S(1)}, u32[]{:S(2)}) copy-start(bf16[16,4096]{1,0:T(8,128)(2,1)S(1)} %dynamic-slice_bitcast_fusion.refs_14_) | copy-start | bytes 393220
  6.7 41.4 %all-to-all-start = ((bf16[32,136,256]{2,1,0:T(8,128)(2,1)}), bf16[32,136,256]{2,1,0:T(8,128)(2,1)}, u32[]{:S(2)}, u32[]{:S(2)}) async-start(bf16[32,136,256]{2,1,0:T(8,128)(2,1)} %order.1), calls=%async_computation | async-start | bytes 4456448 | tf_op jit(solution)/shard_map/all_to_all | solution.py:549
  15.3 10.4 %collective-permute-start.1 = (bf16[16,4096]{1,0:T(8,128)(2,1)S(1)}, bf16[16,4096]{1,0:T(8,128)(2,1)S(1)}, u32[]{:S(2)}, u32[]{:S(2)}) collective-permute-start(bf16[16,4096]{1,0:T(8,128)(2,1)S(1)} %dynamic-slice_bitcast_fusion.refs_14_), channel_id=1, source_target_pairs={{0,224},{32,0},{64,32},{96,64},{128,96},{160,128},{192,160},{224,1... | collective-permute-start | bytes 393224 | tf_op jit(solution)/shard_map/ppermute | solution.py:53
  21.0 5.8 %collective-permute-start = (bf16[16,4096]{1,0:T(8,128)(2,1)S(1)}, bf16[16,4096]{1,0:T(8,128)(2,1)S(1)}, u32[]{:S(2)}, u32[]{:S(2)}) collective-permute-start(bf16[16,4096]{1,0:T(8,128)(2,1)S(1)} %dynamic-slice_bitcast_fusion.refs_14_), channel_id=1, source_target_pairs={{0,32},{32,64},{64,96},{96,128},{128,160},{160,192},{192,224},{224... | collective-permute-start | bytes 393224 | tf_op jit(solution)/shard_map/ppermute | solution.py:50
  25.7 22.3 %copy-start.2 = (bf16[16,4096]{1,0:T(8,128)(2,1)}, bf16[16,4096]{1,0:T(8,128)(2,1)S(1)}, u32[]{:S(2)}) copy-start(bf16[16,4096]{1,0:T(8,128)(2,1)S(1)} %collective-permute-done.1.refs_7_) | copy-start | bytes 393220
  26.8 21.3 %copy-start.3 = (bf16[16,4096]{1,0:T(8,128)(2,1)}, bf16[16,4096]{1,0:T(8,128)(2,1)S(1)}, u32[]{:S(2)}) copy-start(bf16[16,4096]{1,0:T(8,128)(2,1)S(1)} %collective-permute-done.refs_13_) | copy-start | bytes 393220
  26.8 5.4 %collective-permute-start.4 = (bf16[16,4096]{1,0:T(8,128)(2,1)S(1)}, bf16[16,4096]{1,0:T(8,128)(2,1)S(1)}, u32[]{:S(2)}, u32[]{:S(2)}) collective-permute-start(bf16[16,4096]{1,0:T(8,128)(2,1)S(1)} %collective-permute-done.refs_13_), channel_id=1, source_target_pairs={{0,32},{32,64},{64,96},{96,128},{128,160},{160,192},{192,224},{224... | collective-permute-start | bytes 393224 | tf_op jit(solution)/shard_map/ppermute | solution.py:50
  26.8 8.1 %collective-permute-start.2 = (bf16[16,4096]{1,0:T(8,128)(2,1)S(1)}, bf16[16,4096]{1,0:T(8,128)(2,1)S(1)}, u32[]{:S(2)}, u32[]{:S(2)}) collective-permute-start(bf16[16,4096]{1,0:T(8,128)(2,1)S(1)} %collective-permute-done.1.refs_7_), channel_id=1, source_target_pairs={{0,224},{32,0},{64,32},{96,64},{128,96},{160,128},{192,160},{224,1... | collective-permute-start | bytes 393224 | tf_op jit(solution)/shard_map/ppermute | solution.py:53
  32.2 15.9 %copy-start.4 = (bf16[16,4096]{1,0:T(8,128)(2,1)}, bf16[16,4096]{1,0:T(8,128)(2,1)S(1)}, u32[]{:S(2)}) copy-start(bf16[16,4096]{1,0:T(8,128)(2,1)S(1)} %collective-permute-done.4.refs_12_) | copy-start | bytes 393220
  32.2 5.6 %collective-permute-start.5 = (bf16[16,4096]{1,0:T(8,128)(2,1)S(1)}, bf16[16,4096]{1,0:T(8,128)(2,1)S(1)}, u32[]{:S(2)}, u32[]{:S(2)}) collective-permute-start(bf16[16,4096]{1,0:T(8,128)(2,1)S(1)} %collective-permute-done.4.refs_12_), channel_id=1, source_target_pairs={{0,32},{32,64},{64,96},{96,128},{128,160},{160,192},{192,224},{224... | collective-permute-start | bytes 393224 | tf_op jit(solution)/shard_map/ppermute | solution.py:50
  32.2 5.6 %collective-permute-start.14 = (bf16[16,4096]{1,0:T(8,128)(2,1)S(1)}, bf16[16,4096]{1,0:T(8,128)(2,1)S(1)}, u32[]{:S(2)}, u32[]{:S(2)}) collective-permute-start(bf16[16,4096]{1,0:T(8,128)(2,1)S(1)} %dynamic-slice_bitcast_fusion.refs_14_), channel_id=1, source_target_pairs={{0,1},{1,0},{2,3},{3,2},{4,5},{5,4},{6,7},{7,6},{8,9},{9,8},{10,11... | collective-permute-start | bytes 393224 | tf_op jit(solution)/shard_map/ppermute | solution.py:556
  34.4 6.2 %collective-permute-start.7 = (bf16[16,4096]{1,0:T(8,128)(2,1)S(1)}, bf16[16,4096]{1,0:T(8,128)(2,1)S(1)}, u32[]{:S(2)}, u32[]{:S(2)}) collective-permute-start(bf16[16,4096]{1,0:T(8,128)(2,1)S(1)} %collective-permute-done.1.refs_7_), channel_id=1, source_target_pairs={{0,1},{1,0},{2,3},{3,2},{4,5},{5,4},{6,7},{7,6},{8,9},{9,8},{10,11... | collective-permute-start | bytes 393224 | tf_op jit(solution)/shard_map/ppermute | solution.py:556
  34.5 6.2 %collective-permute-start.13 = (bf16[16,4096]{1,0:T(8,128)(2,1)S(1)}, bf16[16,4096]{1,0:T(8,128)(2,1)S(1)}, u32[]{:S(2)}, u32[]{:S(2)}) collective-permute-start(bf16[16,4096]{1,0:T(8,128)(2,1)S(1)} %collective-permute-done.refs_13_), channel_id=1, source_target_pairs={{0,1},{1,0},{2,3},{3,2},{4,5},{5,4},{6,7},{7,6},{8,9},{9,8},{10,11... | collective-permute-start | bytes 393224 | tf_op jit(solution)/shard_map/ppermute | solution.py:556
  34.9 13.2 %copy-start.5 = (bf16[16,4096]{1,0:T(8,128)(2,1)}, bf16[16,4096]{1,0:T(8,128)(2,1)S(1)}, u32[]{:S(2)}) copy-start(bf16[16,4096]{1,0:T(8,128)(2,1)S(1)} %collective-permute-done.2.refs_8_) | copy-start | bytes 393220
  34.9 6.2 %collective-permute-start.3 = (bf16[16,4096]{1,0:T(8,128)(2,1)S(1)}, bf16[16,4096]{1,0:T(8,128)(2,1)S(1)}, u32[]{:S(2)}, u32[]{:S(2)}) collective-permute-start(bf16[16,4096]{1,0:T(8,128)(2,1)S(1)} %collective-permute-done.2.refs_8_), channel_id=1, source_target_pairs={{0,224},{32,0},{64,32},{96,64},{128,96},{160,128},{192,160},{224,1... | collective-permute-start | bytes 393224 | tf_op jit(solution)/shard_map/ppermute | solution.py:53
  37.8 10.3 %copy-start.6 = (bf16[16,4096]{1,0:T(8,128)(2,1)}, bf16[16,4096]{1,0:T(8,128)(2,1)S(1)}, u32[]{:S(2)}) copy-start(bf16[16,4096]{1,0:T(8,128)(2,1)S(1)} %collective-permute-done.5.refs_11_) | copy-start | bytes 393220
  37.8 5.0 %collective-permute-start.6 = (bf16[16,4096]{1,0:T(8,128)(2,1)S(1)}, bf16[16,4096]{1,0:T(8,128)(2,1)S(1)}, u32[]{:S(2)}, u32[]{:S(2)}) collective-permute-start(bf16[16,4096]{1,0:T(8,128)(2,1)S(1)} %collective-permute-done.5.refs_11_), channel_id=1, source_target_pairs={{0,32},{32,64},{64,96},{96,128},{128,160},{160,192},{192,224},{224... | collective-permute-start | bytes 393224 | tf_op jit(solution)/shard_map/ppermute | solution.py:50
  37.8 10.3 %copy-start.7 = (bf16[16,4096]{1,0:T(8,128)(2,1)}, bf16[16,4096]{1,0:T(8,128)(2,1)S(1)}, u32[]{:S(2)}) copy-start(bf16[16,4096]{1,0:T(8,128)(2,1)S(1)} %collective-permute-done.14.refs_22_) | copy-start | bytes 393220
  37.8 8.8 %collective-permute-start.8 = (bf16[16,4096]{1,0:T(8,128)(2,1)S(1)}, bf16[16,4096]{1,0:T(8,128)(2,1)S(1)}, u32[]{:S(2)}, u32[]{:S(2)}) collective-permute-start(bf16[16,4096]{1,0:T(8,128)(2,1)S(1)} %collective-permute-done.2.refs_8_), channel_id=1, source_target_pairs={{0,1},{1,0},{2,3},{3,2},{4,5},{5,4},{6,7},{7,6},{8,9},{9,8},{10,11... | collective-permute-start | bytes 393224 | tf_op jit(solution)/shard_map/ppermute | solution.py:556
  40.6 6.1 %copy-start.8 = (bf16[16,4096]{1,0:T(8,128)(2,1)}, bf16[16,4096]{1,0:T(8,128)(2,1)S(1)}, u32[]{:S(2)}) copy-start(bf16[16,4096]{1,0:T(8,128)(2,1)S(1)} %collective-permute-done.7.refs_15_) | copy-start | bytes 393220
  40.6 6.1 %collective-permute-start.12 = (bf16[16,4096]{1,0:T(8,128)(2,1)S(1)}, bf16[16,4096]{1,0:T(8,128)(2,1)S(1)}, u32[]{:S(2)}, u32[]{:S(2)}) collective-permute-start(bf16[16,4096]{1,0:T(8,128)(2,1)S(1)} %collective-permute-done.4.refs_12_), channel_id=1, source_target_pairs={{0,1},{1,0},{2,3},{3,2},{4,5},{5,4},{6,7},{7,6},{8,9},{9,8},{10,11... | collective-permute-start | bytes 393224 | tf_op jit(solution)/shard_map/ppermute | solution.py:556
  40.7 6.0 %copy-start.9 = (bf16[16,4096]{1,0:T(8,128)(2,1)}, bf16[16,4096]{1,0:T(8,128)(2,1)S(1)}, u32[]{:S(2)}) copy-start(bf16[16,4096]{1,0:T(8,128)(2,1)S(1)} %collective-permute-done.13.refs_21_) | copy-start | bytes 393220
  40.7 6.0 %collective-permute-start.11 = (bf16[16,4096]{1,0:T(8,128)(2,1)S(1)}, bf16[16,4096]{1,0:T(8,128)(2,1)S(1)}, u32[]{:S(2)}, u32[]{:S(2)}) collective-permute-start(bf16[16,4096]{1,0:T(8,128)(2,1)S(1)} %collective-permute-done.5.refs_11_), channel_id=1, source_target_pairs={{0,1},{1,0},{2,3},{3,2},{4,5},{5,4},{6,7},{7,6},{8,9},{9,8},{10,11... | collective-permute-start | bytes 393224 | tf_op jit(solution)/shard_map/ppermute | solution.py:556
  41.1 5.6 %copy-start.10 = (bf16[16,4096]{1,0:T(8,128)(2,1)}, bf16[16,4096]{1,0:T(8,128)(2,1)S(1)}, u32[]{:S(2)}) copy-start(bf16[16,4096]{1,0:T(8,128)(2,1)S(1)} %collective-permute-done.3.refs_9_) | copy-start | bytes 393220
  41.1 5.6 %collective-permute-start.9 = (bf16[16,4096]{1,0:T(8,128)(2,1)S(1)}, bf16[16,4096]{1,0:T(8,128)(2,1)S(1)}, u32[]{:S(2)}, u32[]{:S(2)}) collective-permute-start(bf16[16,4096]{1,0:T(8,128)(2,1)S(1)} %collective-permute-done.3.refs_9_), channel_id=1, source_target_pairs={{0,1},{1,0},{2,3},{3,2},{4,5},{5,4},{6,7},{7,6},{8,9},{9,8},{10,11... | collective-permute-start | bytes 393224 | tf_op jit(solution)/shard_map/ppermute | solution.py:556
  42.8 3.9 %copy-start.11 = (bf16[16,4096]{1,0:T(8,128)(2,1)}, bf16[16,4096]{1,0:T(8,128)(2,1)S(1)}, u32[]{:S(2)}) copy-start(bf16[16,4096]{1,0:T(8,128)(2,1)S(1)} %collective-permute-done.6.refs_10_) | copy-start | bytes 393220
  42.8 5.2 %collective-permute-start.10 = (bf16[16,4096]{1,0:T(8,128)(2,1)S(1)}, bf16[16,4096]{1,0:T(8,128)(2,1)}, u32[]{:S(2)}, u32[]{:S(2)}) collective-permute-start(bf16[16,4096]{1,0:T(8,128)(2,1)S(1)} %collective-permute-done.6.refs_10_), channel_id=1, source_target_pairs={{0,1},{1,0},{2,3},{3,2},{4,5},{5,4},{6,7},{7,6},{8,9},{9,8},{10,11... | collective-permute-start | bytes 393224 | tf_op jit(solution)/shard_map/ppermute | solution.py:556
  46.6 1.5 copy-start.12
  46.6 0.7 copy-start.13
  46.7 0.7 copy-start.15
  47.4 0.6 copy-start.14
  58.6 22.7 %all-to-all-start.1 = ((bf16[8,320,128]{2,1,0:T(8,128)(2,1)}), bf16[8,320,128]{2,1,0:T(8,128)(2,1)S(1)}, u32[]{:S(2)}, u32[]{:S(2)}) async-start(bf16[8,320,128]{2,1,0:T(8,128)(2,1)} %get-tuple-element.32), calls=%async_computation.1 | async-start | bytes 1310720 | tf_op jit(solution)/shard_map/all_to_all | solution.py:559
  81.3 0.8 copy-start
  88.5 8.0 %collective-permute-start.15 = (f32[16,144,256]{2,1,0:T(8,128)}, f32[16,144,256]{2,1,0:T(8,128)}, u32[]{:S(2)}, u32[]{:S(2)}) collective-permute-start(f32[16,144,256]{2,1,0:T(8,128)} %get-tuple-element.39), channel_id=1, source_target_pairs={{0,1},{1,0},{2,3},{3,2},{4,5},{5,4},{6,7},{7,6},{8,9},{9,8},{10,11... | collective-permute-start | bytes 7077896 | tf_op jit(solution)/shard_map/ppermute | solution.py:565
  123.2 11.2 %all-to-all-start.3 = ((f32[8,16,256]{2,1,0:T(8,128)}), f32[8,16,256]{2,1,0:T(8,128)S(1)}, u32[]{:S(2)}, u32[]{:S(2)}) async-start(f32[8,16,256]{2,1,0:T(8,128)} %bitcast.9), calls=%async_computation.3 | async-start | bytes 262144 | tf_op jit(solution)/shard_map/all_to_all | solution.py:571
  146.6 5.4 %collective-permute-start.16 = (f32[32,4096]{1,0:T(8,128)S(1)}, f32[32,4096]{1,0:T(8,128)S(1)}, u32[]{:S(2)}, u32[]{:S(2)}) collective-permute-start(f32[32,4096]{1,0:T(8,128)S(1)} %bitcast.19), channel_id=1, source_target_pairs={{0,1},{1,0},{2,3},{3,2},{4,5},{5,4},{6,7},{7,6},{8,9},{9,8},{10,11... | collective-permute-start | bytes 1572872 | tf_op jit(solution)/shard_map/ppermute | solution.py:575

commit v9 on v8

--- a/solution.py
+++ b/solution.py
@@ -323,11 +323,11 @@
         w = jnp.concatenate([w, jnp.zeros((rows, 128 - rank), f32)], axis=1).T[:rank, :]
         w_hi, w_lo = split2(w)
         irms_hi = irms.astype(bf16).astype(f32)
-        row = lax.broadcasted_iota(jnp.int32, (rank, tokens), 0)
+        row = lax.broadcasted_iota(jnp.int32, (8, tokens), 0)
         last = jnp.where(row == 0, irms_hi, jnp.where(row == 1, irms - irms_hi, 0.0)).astype(bf16)
         for i in range(out_ref.shape[0]):
             low = 0
-            for value in (scaled_up, lrt_in[1][...], w_hi, w_lo, last, own_up):
+            for value in (scaled_up[: rows - rank], lrt_in[1][...], w_hi, w_lo, own_up, last):
                 out_ref[i, low : low + value.shape[0], :] = value
                 low += value.shape[0]
 
@@ -357,7 +357,7 @@
         "own",
         (
             jax.ShapeDtypeStruct(stream.shape, bf16),
-            jax.ShapeDtypeStruct((layers, (2 * layers + 4) * rank, stream.shape[0]), bf16),
+            jax.ShapeDtypeStruct((layers, (2 * layers + 2) * rank + 8, stream.shape[0]), bf16),
         ),
         (meta,),
         (refs, stream, up, lrt, dg, irms, *mine, *other),
@@ -369,7 +369,9 @@
 def solve(width, rank, me, side_ref, low_ref, lrt_ref, coef_ref, k_ref, acc):
     layers = side_ref.shape[0]
     rows = layers * rank
-    first = rows + 4 * rank
+    side = rows - rank
+    first = side + 3 * rank
+    last = first + rows
     acc[...] = jnp.zeros_like(acc)
     for j in range(layers):
 
@@ -379,11 +381,11 @@
             acc[0 : rank * (j + 1), :] += side_ref[me + j, first + low : first + rows, :].astype(f32)
 
     def inverse_rms(t):
-        hi = side_ref[t, rows + 3 * rank : rows + 3 * rank + 1, :].astype(f32)
-        return hi + side_ref[t, rows + 3 * rank + 1 : rows + 3 * rank + 2, :].astype(f32)
+        hi = side_ref[t, last : last + 1, :].astype(f32)
+        return hi + side_ref[t, last + 1 : last + 2, :].astype(f32)
 
     def mean_of(grad, t):
-        lrt = side_ref[t, rows : rows + rank, :].astype(f32)
+        lrt = side_ref[t, side : side + rank, :].astype(f32)
         return jnp.sum(grad.astype(f32) * lrt, axis=0, keepdims=True) * (1.0 / width)
 
     for j in range(layers - 1, 0, -1):
@@ -394,8 +396,8 @@
             low = rank * (layers - 1 - j)
             grad = acc[rank * j : rank * (j + 1), :].astype(bf16)
             mean = mean_of(grad, t)
-            w_hi = side_ref[t, rows + rank : rows + 2 * rank, :]
-            w_lo = side_ref[t, rows + 2 * rank : rows + 3 * rank, :]
+            w_hi = side_ref[t, side + rank : side + 2 * rank, :]
+            w_lo = side_ref[t, side + 2 * rank : side + 3 * rank, :]
             term = tn(w_hi, grad) + tn(w_lo, grad)
             scaled_up = side_ref[t, low : rows - rank, :].astype(f32)
             acc[0 : rank * j, :] += inverse_rms(t) * (term[low : rows - rank, :] - mean * scaled_up)
@@ -404,7 +406,7 @@
     low_ref[...] = grad
     irms = inverse_rms(me)
     mean = mean_of(grad, me)
-    lrt_f = side_ref[:, rows : rows + rank, :].reshape(layers * rank, -1).astype(f32)
+    lrt_f = side_ref[:, side : side + rank, :].reshape(layers * rank, -1).astype(f32)
     layer = lax.broadcasted_iota(jnp.int32, lrt_f.shape, 0) // rank
     lrt_ref[...] = jnp.where(layer <= me, lrt_f, 0.0).astype(bf16)
     below = jnp.where(layer < me, lrt_f, 0.0)

time: 154 us -> 153 us (level)
  no operation moved by 1% of the time
where the time goes in v9:
time: 153 us; the launch traced here: 152 us
  starting transfers between devices  45.7 us (30%)
  blocking collectives  35.3 us (23%)
  waiting for transfers between devices  31 us (20%)
  Pallas kernels  28.8 us (19%)
  other arithmetic  5.78 us (4%)
  local copies, waits for them, and re-layouts  3.18 us (2%)
  between operations  2.21 us (1%)
    pallas_call x4, Pallas kernels, call(): pl.pallas_call(body, out_shape=out_shape, in_specs=[smem()] * count + [in...  25.7 us
    all_to_all x1, blocking collectives, shards(): lax.all_to_all((kept + received).astype(bf16), CHIPS, 0, 0, tiled=True)  23.2 us
    all_to_all x1, waiting for transfers between devices, shards(): sides = lax.all_to_all(side, SEC, 0, 0, tiled=True)  16 us
    all_to_all x1, blocking collectives, shards(): lax.all_to_all(jnp.broadcast_to(final, (chips,) + final.shape), CHIPS, 0,...  12.1 us
    ppermute x3, starting transfers between devices, ring_gather(): bwd = lax.ppermute(bwd, axis, down)  11.2 us
    ppermute x8, starting transfers between devices, shards(): other = [lax.ppermute(block, 'core', swap) for block in mine]  10.2 us
    all_to_all x1, starting transfers between devices, shards(): refs = lax.all_to_all(ordered, DP, split_axis=0, concat_axis=0, tiled=True)  8.65 us
    all_to_all x1, waiting for transfers between devices, shards(): lax.all_to_all(grad_up.reshape(layers, rank, chunk), SEC, 0, 0, tiled=True)  7.84 us
  transfers between devices with their start and end apart: 20, of which 7 were waited for; matrix products, arithmetic and copies ran while one was open for 0% of the time, Pallas kernels for 6%

profile of v9, /device:TPU:1, one launch (start us, length us, event | category | flops | bytes accessed | tf_op | source)
XLA Modules:
  0.0 152.0 jit_solution(7302627720220400964)
XLA Ops:
  1.9 0.9 dynamic-slice_bitcast_fusion.refs_14_
  2.9 0.6 pad_add_fusion.1.meta_ref.refs_0_
  3.5 3.2 %order.1 = bf16[32,136,256]{2,1,0:T(8,128)(2,1)} custom-call(s32[32]{0:T(128)} %position_ref, s32[3]{0:T(128)} %pad_add_fusion.1.meta_ref.refs_0_, bf16[32,128,256]{2,1,0:T(8,128)(2,1)} %bitcast.18), custom_call_target="tpu_custom_call" | custom-call | tf_op jit(solution)/shard_map/order/pallas_call | solution.py:162
  6.7 8.6 %all-to-all-start = ((bf16[32,136,256]{2,1,0:T(8,128)(2,1)}), bf16[32,136,256]{2,1,0:T(8,128)(2,1)}, u32[]{:S(2)}, u32[]{:S(2)}) async-start(bf16[32,136,256]{2,1,0:T(8,128)(2,1)} %order.1), calls=%async_computation | async-start | bytes 4456448 | tf_op jit(solution)/shard_map/all_to_all | solution.py:551
  15.3 5.7 %collective-permute-start.1 = (bf16[16,4096]{1,0:T(8,128)(2,1)S(1)}, bf16[16,4096]{1,0:T(8,128)(2,1)S(1)}, u32[]{:S(2)}, u32[]{:S(2)}) collective-permute-start(bf16[16,4096]{1,0:T(8,128)(2,1)S(1)} %dynamic-slice_bitcast_fusion.refs_14_), channel_id=1, source_target_pairs={{0,224},{32,0},{64,32},{96,64},{128,96},{160,128},{192,160},{224,1... | collective-permute-start | bytes 393224 | tf_op jit(solution)/shard_map/ppermute | solution.py:53
  21.0 0.0 collective-permute-start
  21.0 4.8 %forward.1 = (bf16[128,8192]{1,0:T(8,128)(2,1)}, bf16[16,128]{1,0:T(8,128)(2,1)}, f32[8,128]{1,0:T(8,128)}, bf16[2,16,8192]{2,1,0:T(8,128)(2,1)}) custom-call(bf16[128,8192]{1,0:T(8,128)(2,1)} %bitcast.23, bf16[16,8192]{1,0:T(8,128)(2,1)} %bitcast.27, f32[1,8192]{1,0:T(1,128)} %refs_2_), custom_call_target="tpu_custom_call" | custom-call | flops 4000000000 | bytes 12000000 | tf_op jit(solution)/shard_map/forward/pallas_call | solution.py:90
  25.7 0.0 copy-start.2
  25.8 1.0 collective-permute-done.refs_13_
  26.8 0.0 collective-permute-start.4
  26.8 2.7 %collective-permute-start.2 = (bf16[16,4096]{1,0:T(8,128)(2,1)S(1)}, bf16[16,4096]{1,0:T(8,128)(2,1)S(1)}, u32[]{:S(2)}, u32[]{:S(2)}) collective-permute-start(bf16[16,4096]{1,0:T(8,128)(2,1)S(1)} %collective-permute-done.1.refs_7_), channel_id=1, source_target_pairs={{0,224},{32,0},{64,32},{96,64},{128,96},{160,128},{192,160},{224,1... | collective-permute-start | bytes 393224 | tf_op jit(solution)/shard_map/ppermute | solution.py:53
  29.4 2.8 %collective-permute-done.4.refs_12_ = bf16[16,4096]{1,0:T(8,128)(2,1)S(1)} collective-permute-done((bf16[16,4096]{1,0:T(8,128)(2,1)S(1)}, bf16[16,4096]{1,0:T(8,128)(2,1)S(1)}, u32[]{:S(2)}, u32[]{:S(2)}) %collective-permute-start.4) | collective-permute-done | bytes 131104 | tf_op jit(solution)/shard_map/ppermute | solution.py:50
  32.2 0.0 collective-permute-start.5
  32.2 2.2 %collective-permute-start.14 = (bf16[16,4096]{1,0:T(8,128)(2,1)S(1)}, bf16[16,4096]{1,0:T(8,128)(2,1)S(1)}, u32[]{:S(2)}, u32[]{:S(2)}) collective-permute-start(bf16[16,4096]{1,0:T(8,128)(2,1)S(1)} %dynamic-slice_bitcast_fusion.refs_14_), channel_id=1, source_target_pairs={{0,1},{1,0},{2,3},{3,2},{4,5},{5,4},{6,7},{7,6},{8,9},{9,8},{10,11... | collective-permute-start | bytes 393224 | tf_op jit(solution)/shard_map/ppermute | solution.py:558
  34.4 0.1 collective-permute-start.7
  34.5 0.4 collective-permute-start.13
  34.9 0.0 collective-permute-done.2.refs_8_
  34.9 2.9 %collective-permute-start.3 = (bf16[16,4096]{1,0:T(8,128)(2,1)S(1)}, bf16[16,4096]{1,0:T(8,128)(2,1)S(1)}, u32[]{:S(2)}, u32[]{:S(2)}) collective-permute-start(bf16[16,4096]{1,0:T(8,128)(2,1)S(1)} %collective-permute-done.2.refs_8_), channel_id=1, source_target_pairs={{0,224},{32,0},{64,32},{96,64},{128,96},{160,128},{192,160},{224,1... | collective-permute-start | bytes 393224 | tf_op jit(solution)/shard_map/ppermute | solution.py:53
  37.8 0.0 collective-permute-done.5.refs_11_
  37.8 0.0 collective-permute-start.6
  37.8 2.8 %collective-permute-start.8 = (bf16[16,4096]{1,0:T(8,128)(2,1)S(1)}, bf16[16,4096]{1,0:T(8,128)(2,1)S(1)}, u32[]{:S(2)}, u32[]{:S(2)}) collective-permute-start(bf16[16,4096]{1,0:T(8,128)(2,1)S(1)} %collective-permute-done.2.refs_8_), channel_id=1, source_target_pairs={{0,1},{1,0},{2,3},{3,2},{4,5},{5,4},{6,7},{7,6},{8,9},{9,8},{10,11... | collective-permute-start | bytes 393224 | tf_op jit(solution)/shard_map/ppermute | solution.py:558
  40.6 0.1 collective-permute-start.12
  40.7 0.4 collective-permute-start.11
  41.1 0.4 collective-permute-start.9
  41.5 1.3 collective-permute-done.6.refs_10_
  42.8 3.8 %collective-permute-start.10 = (bf16[16,4096]{1,0:T(8,128)(2,1)S(1)}, bf16[16,4096]{1,0:T(8,128)(2,1)}, u32[]{:S(2)}, u32[]{:S(2)}) collective-permute-start(bf16[16,4096]{1,0:T(8,128)(2,1)S(1)} %collective-permute-done.6.refs_10_), channel_id=1, source_target_pairs={{0,1},{1,0},{2,3},{3,2},{4,5},{5,4},{6,7},{7,6},{8,9},{9,8},{10,11... | collective-permute-start | bytes 393224 | tf_op jit(solution)/shard_map/ppermute | solution.py:558
  46.7 0.6 copy-done.13
  47.3 0.0 copy-done.15
  47.4 0.6 copy-done.14
  48.1 10.5 %own.1 = (bf16[128,8192]{1,0:T(8,128)(2,1)}, bf16[8,296,128]{2,1,0:T(8,128)(2,1)}) custom-call(s32[3]{0:T(128)} %pad_add_fusion.1.meta_ref.refs_0_, bf16[32,136,256]{2,1,0:T(8,128)(2,1)} %all-to-all-done.refs_1_, bf16[128,8192]{1,0:T(8,128)(2,1)} %bitcast.24, bf16[16,8192]{1,0:T(8,128)(2,1)} %bitcast.22, bf16[16,128]{1,0:T(8,128)(2,1)} %get-tuple-element.26.refs_4_, ...), custom_call_target="tpu_custom_call" | custom-call | flops 8000000000 | bytes 24000000 | tf_op jit(solution)/shard_map/own/pallas_call | solution.py:90
  58.6 4.8 %all-to-all-start.1 = ((bf16[8,296,128]{2,1,0:T(8,128)(2,1)}), bf16[8,296,128]{2,1,0:T(8,128)(2,1)S(1)}, u32[]{:S(2)}, u32[]{:S(2)}) async-start(bf16[8,296,128]{2,1,0:T(8,128)(2,1)} %get-tuple-element.32), calls=%async_computation.1 | async-start | bytes 1212416 | tf_op jit(solution)/shard_map/all_to_all | solution.py:561
  63.4 0.6 pad_add_fusion.refs_0_
  63.9 16.0 %all-to-all-done.1.refs_1_ = bf16[8,296,128]{2,1,0:T(8,128)(2,1)S(1)} async-done(((bf16[8,296,128]{2,1,0:T(8,128)(2,1)}), bf16[8,296,128]{2,1,0:T(8,128)(2,1)S(1)}, u32[]{:S(2)}, u32[]{:S(2)}) %all-to-all-start.1) | async-done | bytes 606240 | tf_op jit(solution)/shard_map/all_to_all | solution.py:561
  79.9 0.8 copy-done
  80.8 6.4 %given.1 = (f32[16,144,256]{2,1,0:T(8,128)}, bf16[16,128]{1,0:T(8,128)(2,1)}, bf16[128,128]{1,0:T(8,128)(2,1)}, bf16[128,128]{1,0:T(8,128)(2,1)}, bf16[2,128,16]{2,1,0:T(8,128)(2,1)}) custom-call(s32[2]{0:T(128)} %pad_add_fusion.refs_0_, bf16[8,296,128]{2,1,0:T(8,128)(2,1)} %copy-done, bf16[128,8192]{1,0:T(8,128)(2,1)} %get-tuple-element.33.refs_2_.refs_5_, ...), custom_call_target="tpu_custom_call" | custom-call | flops 5000000000 | bytes 15000000 | tf_op jit(solution)/shard_map/given/pallas_call | solution.py:90
  87.2 3.7 %collective-permute-start.15 = (f32[16,144,256]{2,1,0:T(8,128)}, f32[16,144,256]{2,1,0:T(8,128)}, u32[]{:S(2)}, u32[]{:S(2)}) collective-permute-start(f32[16,144,256]{2,1,0:T(8,128)} %get-tuple-element.39), channel_id=1, source_target_pairs={{0,1},{1,0},{2,3},{3,2},{4,5},{5,4},{6,7},{7,6},{8,9},{9,8},{10,11... | collective-permute-start | bytes 7077896 | tf_op jit(solution)/shard_map/ppermute | solution.py:567
  90.9 4.0 %kept.1 = f32[16,144,256]{2,1,0:T(8,128)} custom-call(s32[1]{0:T(128)} %bitcast.refs_0_, bf16[16,128]{1,0:T(8,128)(2,1)} %get-tuple-element.35.refs_1_, bf16[128,128]{1,0:T(8,128)(2,1)} %get-tuple-element.36.refs_2_, bf16[128,128]{1,0:T(8,128)(2,1)} %get-tuple-element.37.refs_3_, bf16[2,128,16]{2,1,0:T(8,128)(2,1)} %get-tuple-element.38.refs_4_, ...), custom_call_target="tpu_custom_call" | custom-call | flops 4000000000 | bytes 12000000 | tf_op jit(solution)/shard_map/kept/pallas_call | solution.py:90
  94.9 0.5 collective-permute-done.15
  95.4 2.7 %add_convert_fusion = bf16[16,144,256]{2,1,0:T(8,128)(2,1)S(1)} fusion(f32[16,144,256]{2,1,0:T(8,128)} %kept.1, f32[16,144,256]{2,1,0:T(8,128)} %collective-permute-done.15), kind=kLoop, calls=%fused_computation | loop fusion | flops 1179648 | bytes 5898240 | tf_op jit(solution)/shard_map/convert_element_type | solution.py:569
  98.0 23.2 %all_to_all.25 = bf16[16,144,256]{2,1,0:T(8,128)(2,1)S(1)} all-to-all(bf16[16,144,256]{2,1,0:T(8,128)(2,1)S(1)} %add_convert_fusion), channel_id=1, replica_groups=mesh['section'=8,'y'=4,'x'=4,'core'=2] {'y','x'}, dimensions={0} | all-to-all | bytes 2359296 | tf_op jit(solution)/shard_map/all_to_all | solution.py:569
  121.3 0.8 convert_reduce_fusion
  122.1 3.4 %all-to-all-start.3 = ((f32[8,16,256]{2,1,0:T(8,128)}), f32[8,16,256]{2,1,0:T(8,128)S(1)}, u32[]{:S(2)}, u32[]{:S(2)}) async-start(f32[8,16,256]{2,1,0:T(8,128)} %bitcast.9), calls=%async_computation.3 | async-start | bytes 262144 | tf_op jit(solution)/shard_map/all_to_all | solution.py:573
  125.5 7.8 %all-to-all-done.3 = f32[8,16,256]{2,1,0:T(8,128)S(1)} async-done(((f32[8,16,256]{2,1,0:T(8,128)}), f32[8,16,256]{2,1,0:T(8,128)S(1)}, u32[]{:S(2)}, u32[]{:S(2)}) %all-to-all-start.3) | async-done | bytes 131104 | tf_op jit(solution)/shard_map/all_to_all | solution.py:573
  133.4 12.1 %all_to_all.26 = f32[16,32,256]{2,1,0:T(8,128)S(1)} all-to-all(f32[16,32,256]{2,1,0:T(8,128)S(1)} %broadcast_in_dim.13), channel_id=1, replica_groups=mesh['section'=8,'y'=4,'x'=4,'core'=2] {'y','x'}, dimensions={0} | all-to-all | bytes 1048576 | tf_op jit(solution)/shard_map/all_to_all | solution.py:575
  145.5 3.8 %collective-permute-start.16 = (f32[32,4096]{1,0:T(8,128)S(1)}, f32[32,4096]{1,0:T(8,128)S(1)}, u32[]{:S(2)}, u32[]{:S(2)}) collective-permute-start(f32[32,4096]{1,0:T(8,128)S(1)} %bitcast.19), channel_id=1, source_target_pairs={{0,1},{1,0},{2,3},{3,2},{4,5},{5,4},{6,7},{7,6},{8,9},{9,8},{10,11... | collective-permute-start | bytes 1572872 | tf_op jit(solution)/shard_map/ppermute | solution.py:577
  149.4 1.5 %collective-permute-done.16 = f32[32,4096]{1,0:T(8,128)S(1)} collective-permute-done((f32[32,4096]{1,0:T(8,128)S(1)}, f32[32,4096]{1,0:T(8,128)S(1)}, u32[]{:S(2)}, u32[]{:S(2)}) %collective-permute-start.16) | collective-permute-done | bytes 524320 | tf_op jit(solution)/shard_map/ppermute | solution.py:577
  150.9 0.1 broadcast_select_fusion
  151.0 1.0 fusion.2
  (43 shorter events, 0.2 us)
Async XLA Ops:
  2.9 29.3 %copy-start.1 = (bf16[16,4096]{1,0:T(8,128)(2,1)}, bf16[16,4096]{1,0:T(8,128)(2,1)S(1)}, u32[]{:S(2)}) copy-start(bf16[16,4096]{1,0:T(8,128)(2,1)S(1)} %dynamic-slice_bitcast_fusion.refs_14_) | copy-start | bytes 393220
  6.7 41.4 %all-to-all-start = ((bf16[32,136,256]{2,1,0:T(8,128)(2,1)}), bf16[32,136,256]{2,1,0:T(8,128)(2,1)}, u32[]{:S(2)}, u32[]{:S(2)}) async-start(bf16[32,136,256]{2,1,0:T(8,128)(2,1)} %order.1), calls=%async_computation | async-start | bytes 4456448 | tf_op jit(solution)/shard_map/all_to_all | solution.py:551
  15.3 10.4 %collective-permute-start.1 = (bf16[16,4096]{1,0:T(8,128)(2,1)S(1)}, bf16[16,4096]{1,0:T(8,128)(2,1)S(1)}, u32[]{:S(2)}, u32[]{:S(2)}) collective-permute-start(bf16[16,4096]{1,0:T(8,128)(2,1)S(1)} %dynamic-slice_bitcast_fusion.refs_14_), channel_id=1, source_target_pairs={{0,224},{32,0},{64,32},{96,64},{128,96},{160,128},{192,160},{224,1... | collective-permute-start | bytes 393224 | tf_op jit(solution)/shard_map/ppermute | solution.py:53
  21.0 5.8 %collective-permute-start = (bf16[16,4096]{1,0:T(8,128)(2,1)S(1)}, bf16[16,4096]{1,0:T(8,128)(2,1)S(1)}, u32[]{:S(2)}, u32[]{:S(2)}) collective-permute-start(bf16[16,4096]{1,0:T(8,128)(2,1)S(1)} %dynamic-slice_bitcast_fusion.refs_14_), channel_id=1, source_target_pairs={{0,32},{32,64},{64,96},{96,128},{128,160},{160,192},{192,224},{224... | collective-permute-start | bytes 393224 | tf_op jit(solution)/shard_map/ppermute | solution.py:50
  25.7 22.3 %copy-start.2 = (bf16[16,4096]{1,0:T(8,128)(2,1)}, bf16[16,4096]{1,0:T(8,128)(2,1)S(1)}, u32[]{:S(2)}) copy-start(bf16[16,4096]{1,0:T(8,128)(2,1)S(1)} %collective-permute-done.1.refs_7_) | copy-start | bytes 393220
  26.8 21.3 %copy-start.3 = (bf16[16,4096]{1,0:T(8,128)(2,1)}, bf16[16,4096]{1,0:T(8,128)(2,1)S(1)}, u32[]{:S(2)}) copy-start(bf16[16,4096]{1,0:T(8,128)(2,1)S(1)} %collective-permute-done.refs_13_) | copy-start | bytes 393220
  26.8 5.4 %collective-permute-start.4 = (bf16[16,4096]{1,0:T(8,128)(2,1)S(1)}, bf16[16,4096]{1,0:T(8,128)(2,1)S(1)}, u32[]{:S(2)}, u32[]{:S(2)}) collective-permute-start(bf16[16,4096]{1,0:T(8,128)(2,1)S(1)} %collective-permute-done.refs_13_), channel_id=1, source_target_pairs={{0,32},{32,64},{64,96},{96,128},{128,160},{160,192},{192,224},{224... | collective-permute-start | bytes 393224 | tf_op jit(solution)/shard_map/ppermute | solution.py:50
  26.8 8.1 %collective-permute-start.2 = (bf16[16,4096]{1,0:T(8,128)(2,1)S(1)}, bf16[16,4096]{1,0:T(8,128)(2,1)S(1)}, u32[]{:S(2)}, u32[]{:S(2)}) collective-permute-start(bf16[16,4096]{1,0:T(8,128)(2,1)S(1)} %collective-permute-done.1.refs_7_), channel_id=1, source_target_pairs={{0,224},{32,0},{64,32},{96,64},{128,96},{160,128},{192,160},{224,1... | collective-permute-start | bytes 393224 | tf_op jit(solution)/shard_map/ppermute | solution.py:53
  32.2 15.9 %copy-start.4 = (bf16[16,4096]{1,0:T(8,128)(2,1)}, bf16[16,4096]{1,0:T(8,128)(2,1)S(1)}, u32[]{:S(2)}) copy-start(bf16[16,4096]{1,0:T(8,128)(2,1)S(1)} %collective-permute-done.4.refs_12_) | copy-start | bytes 393220
  32.2 5.6 %collective-permute-start.5 = (bf16[16,4096]{1,0:T(8,128)(2,1)S(1)}, bf16[16,4096]{1,0:T(8,128)(2,1)S(1)}, u32[]{:S(2)}, u32[]{:S(2)}) collective-permute-start(bf16[16,4096]{1,0:T(8,128)(2,1)S(1)} %collective-permute-done.4.refs_12_), channel_id=1, source_target_pairs={{0,32},{32,64},{64,96},{96,128},{128,160},{160,192},{192,224},{224... | collective-permute-start | bytes 393224 | tf_op jit(solution)/shard_map/ppermute | solution.py:50
  32.2 5.6 %collective-permute-start.14 = (bf16[16,4096]{1,0:T(8,128)(2,1)S(1)}, bf16[16,4096]{1,0:T(8,128)(2,1)S(1)}, u32[]{:S(2)}, u32[]{:S(2)}) collective-permute-start(bf16[16,4096]{1,0:T(8,128)(2,1)S(1)} %dynamic-slice_bitcast_fusion.refs_14_), channel_id=1, source_target_pairs={{0,1},{1,0},{2,3},{3,2},{4,5},{5,4},{6,7},{7,6},{8,9},{9,8},{10,11... | collective-permute-start | bytes 393224 | tf_op jit(solution)/shard_map/ppermute | solution.py:558
  34.4 6.2 %collective-permute-start.7 = (bf16[16,4096]{1,0:T(8,128)(2,1)S(1)}, bf16[16,4096]{1,0:T(8,128)(2,1)S(1)}, u32[]{:S(2)}, u32[]{:S(2)}) collective-permute-start(bf16[16,4096]{1,0:T(8,128)(2,1)S(1)} %collective-permute-done.1.refs_7_), channel_id=1, source_target_pairs={{0,1},{1,0},{2,3},{3,2},{4,5},{5,4},{6,7},{7,6},{8,9},{9,8},{10,11... | collective-permute-start | bytes 393224 | tf_op jit(solution)/shard_map/ppermute | solution.py:558
  34.5 6.2 %collective-permute-start.13 = (bf16[16,4096]{1,0:T(8,128)(2,1)S(1)}, bf16[16,4096]{1,0:T(8,128)(2,1)S(1)}, u32[]{:S(2)}, u32[]{:S(2)}) collective-permute-start(bf16[16,4096]{1,0:T(8,128)(2,1)S(1)} %collective-permute-done.refs_13_), channel_id=1, source_target_pairs={{0,1},{1,0},{2,3},{3,2},{4,5},{5,4},{6,7},{7,6},{8,9},{9,8},{10,11... | collective-permute-start | bytes 393224 | tf_op jit(solution)/shard_map/ppermute | solution.py:558
  34.9 13.2 %copy-start.5 = (bf16[16,4096]{1,0:T(8,128)(2,1)}, bf16[16,4096]{1,0:T(8,128)(2,1)S(1)}, u32[]{:S(2)}) copy-start(bf16[16,4096]{1,0:T(8,128)(2,1)S(1)} %collective-permute-done.2.refs_8_) | copy-start | bytes 393220
  34.9 6.2 %collective-permute-start.3 = (bf16[16,4096]{1,0:T(8,128)(2,1)S(1)}, bf16[16,4096]{1,0:T(8,128)(2,1)S(1)}, u32[]{:S(2)}, u32[]{:S(2)}) collective-permute-start(bf16[16,4096]{1,0:T(8,128)(2,1)S(1)} %collective-permute-done.2.refs_8_), channel_id=1, source_target_pairs={{0,224},{32,0},{64,32},{96,64},{128,96},{160,128},{192,160},{224,1... | collective-permute-start | bytes 393224 | tf_op jit(solution)/shard_map/ppermute | solution.py:53
  37.8 10.3 %copy-start.6 = (bf16[16,4096]{1,0:T(8,128)(2,1)}, bf16[16,4096]{1,0:T(8,128)(2,1)S(1)}, u32[]{:S(2)}) copy-start(bf16[16,4096]{1,0:T(8,128)(2,1)S(1)} %collective-permute-done.5.refs_11_) | copy-start | bytes 393220
  37.8 5.0 %collective-permute-start.6 = (bf16[16,4096]{1,0:T(8,128)(2,1)S(1)}, bf16[16,4096]{1,0:T(8,128)(2,1)S(1)}, u32[]{:S(2)}, u32[]{:S(2)}) collective-permute-start(bf16[16,4096]{1,0:T(8,128)(2,1)S(1)} %collective-permute-done.5.refs_11_), channel_id=1, source_target_pairs={{0,32},{32,64},{64,96},{96,128},{128,160},{160,192},{192,224},{224... | collective-permute-start | bytes 393224 | tf_op jit(solution)/shard_map/ppermute | solution.py:50
  37.8 10.3 %copy-start.7 = (bf16[16,4096]{1,0:T(8,128)(2,1)}, bf16[16,4096]{1,0:T(8,128)(2,1)S(1)}, u32[]{:S(2)}) copy-start(bf16[16,4096]{1,0:T(8,128)(2,1)S(1)} %collective-permute-done.14.refs_22_) | copy-start | bytes 393220
  37.8 8.8 %collective-permute-start.8 = (bf16[16,4096]{1,0:T(8,128)(2,1)S(1)}, bf16[16,4096]{1,0:T(8,128)(2,1)S(1)}, u32[]{:S(2)}, u32[]{:S(2)}) collective-permute-start(bf16[16,4096]{1,0:T(8,128)(2,1)S(1)} %collective-permute-done.2.refs_8_), channel_id=1, source_target_pairs={{0,1},{1,0},{2,3},{3,2},{4,5},{5,4},{6,7},{7,6},{8,9},{9,8},{10,11... | collective-permute-start | bytes 393224 | tf_op jit(solution)/shard_map/ppermute | solution.py:558
  40.6 6.1 %copy-start.8 = (bf16[16,4096]{1,0:T(8,128)(2,1)}, bf16[16,4096]{1,0:T(8,128)(2,1)S(1)}, u32[]{:S(2)}) copy-start(bf16[16,4096]{1,0:T(8,128)(2,1)S(1)} %collective-permute-done.7.refs_15_) | copy-start | bytes 393220
  40.6 6.1 %collective-permute-start.12 = (bf16[16,4096]{1,0:T(8,128)(2,1)S(1)}, bf16[16,4096]{1,0:T(8,128)(2,1)S(1)}, u32[]{:S(2)}, u32[]{:S(2)}) collective-permute-start(bf16[16,4096]{1,0:T(8,128)(2,1)S(1)} %collective-permute-done.4.refs_12_), channel_id=1, source_target_pairs={{0,1},{1,0},{2,3},{3,2},{4,5},{5,4},{6,7},{7,6},{8,9},{9,8},{10,11... | collective-permute-start | bytes 393224 | tf_op jit(solution)/shard_map/ppermute | solution.py:558
  40.7 6.0 %copy-start.9 = (bf16[16,4096]{1,0:T(8,128)(2,1)}, bf16[16,4096]{1,0:T(8,128)(2,1)S(1)}, u32[]{:S(2)}) copy-start(bf16[16,4096]{1,0:T(8,128)(2,1)S(1)} %collective-permute-done.13.refs_21_) | copy-start | bytes 393220
  40.7 6.0 %collective-permute-start.11 = (bf16[16,4096]{1,0:T(8,128)(2,1)S(1)}, bf16[16,4096]{1,0:T(8,128)(2,1)S(1)}, u32[]{:S(2)}, u32[]{:S(2)}) collective-permute-start(bf16[16,4096]{1,0:T(8,128)(2,1)S(1)} %collective-permute-done.5.refs_11_), channel_id=1, source_target_pairs={{0,1},{1,0},{2,3},{3,2},{4,5},{5,4},{6,7},{7,6},{8,9},{9,8},{10,11... | collective-permute-start | bytes 393224 | tf_op jit(solution)/shard_map/ppermute | solution.py:558
  41.1 5.6 %copy-start.10 = (bf16[16,4096]{1,0:T(8,128)(2,1)}, bf16[16,4096]{1,0:T(8,128)(2,1)S(1)}, u32[]{:S(2)}) copy-start(bf16[16,4096]{1,0:T(8,128)(2,1)S(1)} %collective-permute-done.3.refs_9_) | copy-start | bytes 393220
  41.1 5.6 %collective-permute-start.9 = (bf16[16,4096]{1,0:T(8,128)(2,1)S(1)}, bf16[16,4096]{1,0:T(8,128)(2,1)S(1)}, u32[]{:S(2)}, u32[]{:S(2)}) collective-permute-start(bf16[16,4096]{1,0:T(8,128)(2,1)S(1)} %collective-permute-done.3.refs_9_), channel_id=1, source_target_pairs={{0,1},{1,0},{2,3},{3,2},{4,5},{5,4},{6,7},{7,6},{8,9},{9,8},{10,11... | collective-permute-start | bytes 393224 | tf_op jit(solution)/shard_map/ppermute | solution.py:558
  42.8 3.9 %copy-start.11 = (bf16[16,4096]{1,0:T(8,128)(2,1)}, bf16[16,4096]{1,0:T(8,128)(2,1)S(1)}, u32[]{:S(2)}) copy-start(bf16[16,4096]{1,0:T(8,128)(2,1)S(1)} %collective-permute-done.6.refs_10_) | copy-start | bytes 393220
  42.8 5.2 %collective-permute-start.10 = (bf16[16,4096]{1,0:T(8,128)(2,1)S(1)}, bf16[16,4096]{1,0:T(8,128)(2,1)}, u32[]{:S(2)}, u32[]{:S(2)}) collective-permute-start(bf16[16,4096]{1,0:T(8,128)(2,1)S(1)} %collective-permute-done.6.refs_10_), channel_id=1, source_target_pairs={{0,1},{1,0},{2,3},{3,2},{4,5},{5,4},{6,7},{7,6},{8,9},{9,8},{10,11... | collective-permute-start | bytes 393224 | tf_op jit(solution)/shard_map/ppermute | solution.py:558
  46.6 1.5 copy-start.12
  46.6 0.7 copy-start.13
  46.7 0.7 copy-start.15
  47.4 0.6 copy-start.14
  58.6 21.3 %all-to-all-start.1 = ((bf16[8,296,128]{2,1,0:T(8,128)(2,1)}), bf16[8,296,128]{2,1,0:T(8,128)(2,1)S(1)}, u32[]{:S(2)}, u32[]{:S(2)}) async-start(bf16[8,296,128]{2,1,0:T(8,128)(2,1)} %get-tuple-element.32), calls=%async_computation.1 | async-start | bytes 1212416 | tf_op jit(solution)/shard_map/all_to_all | solution.py:561
  79.9 0.8 copy-start
  87.2 8.2 %collective-permute-start.15 = (f32[16,144,256]{2,1,0:T(8,128)}, f32[16,144,256]{2,1,0:T(8,128)}, u32[]{:S(2)}, u32[]{:S(2)}) collective-permute-start(f32[16,144,256]{2,1,0:T(8,128)} %get-tuple-element.39), channel_id=1, source_target_pairs={{0,1},{1,0},{2,3},{3,2},{4,5},{5,4},{6,7},{7,6},{8,9},{9,8},{10,11... | collective-permute-start | bytes 7077896 | tf_op jit(solution)/shard_map/ppermute | solution.py:567
  122.1 11.2 %all-to-all-start.3 = ((f32[8,16,256]{2,1,0:T(8,128)}), f32[8,16,256]{2,1,0:T(8,128)S(1)}, u32[]{:S(2)}, u32[]{:S(2)}) async-start(f32[8,16,256]{2,1,0:T(8,128)} %bitcast.9), calls=%async_computation.3 | async-start | bytes 262144 | tf_op jit(solution)/shard_map/all_to_all | solution.py:573
  145.5 5.4 %collective-permute-start.16 = (f32[32,4096]{1,0:T(8,128)S(1)}, f32[32,4096]{1,0:T(8,128)S(1)}, u32[]{:S(2)}, u32[]{:S(2)}) collective-permute-start(f32[32,4096]{1,0:T(8,128)S(1)} %bitcast.19), channel_id=1, source_target_pairs={{0,1},{1,0},{2,3},{3,2},{4,5},{5,4},{6,7},{7,6},{8,9},{9,8},{10,11... | collective-permute-start | bytes 1572872 | tf_op jit(solution)/shard_map/ppermute | solution.py:577
